TPU v7x, 128 devices: a whole 4x4x4 slice. The times are simulated.
128 devices in a mesh: tenant: 16 (over z, y_lo, core), row: 8 (over x, y_hi).
Axes of the slice: x: 4, y: 4 (y_hi: 2, y_lo: 2; y = y_hi * 2 + y_lo), z: 4, core: 2. Of those that a mesh axis runs over, the one named last changes fastest.
Arguments:
- b_factors: float32 [128, 16, 8192], P('tenant', None, 'row'), may hold values from -6 to 6
- a_factors: float32 [128, 16, 8192], P('tenant', None, 'row'), may hold values from -6 to 6
- u_start: float32 [8192, 256], P('row'), may hold values from -0.0625 to 0.0625
- v_start: float32 [8192, 256], P('row'), may hold values from -0.0625 to 0.0625
Outputs:
- u_scaled: float32 [8192, 256], P('row')
- v_scaled: float32 [8192, 256], P('row')
- core_left: float32 [128, 16, 256], P('tenant')
- core_right: float32 [128, 16, 256], P('tenant')
All inputs are finite; a program needn't handle non-finite values.
Results may differ from a plain program's by a relative error of at most 0.0003.
Values sent between devices are 32-bit elements; how exact they have to be, the bound alone decides.
No kernel may reach another device: no remote copies, remote signals or barrier semaphores. Data moves between devices by JAX's collectives and lax.ppermute only.
A program may use at most 64 MiB of HBM per device.

v0:
```python
import math

import jax
import jax.numpy as jnp
from jax import lax
from jax.sharding import PartitionSpec as P

D = 8192


HIGH = lax.Precision.HIGHEST


def padded_to(lines, count):
    spare = -len(lines) % count
    return jnp.pad(lines, [(0, spare)] + [(0, 0)] * (lines.ndim - 1))


def joined_along(tiles, dim):
    lengths = list(tiles.shape[1:])
    lengths[dim] *= tiles.shape[0]
    return jnp.moveaxis(tiles, 0, dim).reshape(lengths)


def copy_for_each(x, axis):
    copies = jnp.broadcast_to(x, (lax.axis_size(axis), *x.shape))
    return lax.all_to_all(copies, axis, split_axis=0, concat_axis=0, tiled=True)


def gathered_copies(x, axis, dim):
    return joined_along(copy_for_each(x, axis), dim)


def cut_along(x, dim, count):
    lengths = x.shape
    tiles = x.reshape(*lengths[:dim], count, lengths[dim] // count, *lengths[dim + 1 :])
    return jnp.moveaxis(tiles, dim, 0)


def sum_at_owner(x, axis, dim):
    count = lax.axis_size(axis)
    tiles = lax.all_to_all(cut_along(x, dim, count), axis, 0, 0, tiled=True)
    return jnp.sum(tiles, axis=0)


def nested_sum(x, axes):
    lines = x.reshape(-1, x.shape[-1])
    padded = padded_to(lines, lax.axis_size(axes))
    whole = gathered_copies(sum_at_owner(padded, axes, 0), axes, 0)
    return lax.slice_in_dim(whole, 0, len(lines)).reshape(x.shape)


def taken_together(x, axis):
    everything = copy_for_each(x, axis)
    return jnp.sum(everything, axis=0)


def packed_total(arrays, axis):
    ends = [0]
    for a in arrays:
        ends.append(ends[-1] + a.size)
    subtotal = taken_together(jnp.concatenate([a.ravel() for a in arrays]), axis)
    return tuple((subtotal[b:e].reshape(a.shape) for a, b, e in zip(arrays, ends, ends[1:])))


def project(factors, basis):
    return jnp.einsum("trd,dk->trk", factors, basis, precision=HIGH)


def normalize(matrix, gram):
    lower = jnp.linalg.cholesky(gram)
    return lax.linalg.triangular_solve(lower, matrix, left_side=False, lower=True, transpose_a=True)


def refresh(loading, coeffs):
    local_sum = jnp.einsum("trd,trk->dk", loading, coeffs, precision=HIGH)
    total = nested_sum(local_sum, "tenant")
    gram = taken_together(jnp.dot(total.T, total, precision=HIGH), "row")
    return normalize(total, gram)


def local(b_factors, a_factors, u_start, v_start):
    left, right = packed_total((project(b_factors, u_start), project(a_factors, v_start)), "row")
    weight = jnp.einsum("trk,tsk->trs", right, right, precision=HIGH)
    coeffs = jnp.einsum("trs,tsk->trk", weight, left, precision=HIGH)
    basis_u = refresh(b_factors, coeffs)
    left = taken_together(project(b_factors, basis_u), "row")
    weight = jnp.einsum("trk,tsk->trs", left, left, precision=HIGH)
    coeffs = jnp.einsum("trs,tsk->trk", weight, right, precision=HIGH)
    basis_v = refresh(a_factors, coeffs)
    right = taken_together(project(a_factors, basis_v), "row")
    scale = math.sqrt(D)
    return (basis_u * scale, basis_v * scale, left, right)


def solution(mesh):
    in_specs = (P("tenant", None, "row"), P("tenant", None, "row"), P("row", None), P("row", None))
    out_specs = (P("row", None), P("row", None), P("tenant", None, None), P("tenant", None, None))
    return jax.shard_map(local, mesh=mesh, in_specs=in_specs, out_specs=out_specs, check_vma=False)
```

profile of v0, /device:TPU:8, one launch (start us, length us, event | category | flops | bytes accessed | tf_op | source)
XLA Modules:
  0.0 385.8 jit_solution(6752987593848051979)
XLA Ops:
  0.7 1.2 copy-done
  1.9 1.7 fusion.4
  4.5 2.4 broadcast_in_dim.22
  6.9 6.0 %all-to-all-start = ((f32[8,1,65536]{2,1,0:T(1,128)}), f32[8,1,65536]{2,1,0:T(1,128)S(1)}, u32[]{:S(2)}, u32[]{:S(2)}) async-start(f32[8,1,65536]{2,1,0:T(1,128)} %broadcast_in_dim.22), calls=%async_computation | async-start | bytes 4194304 | tf_op jit(solution)/shard_map/all_to_all | solution.py:27
  12.9 31.2 %all-to-all-done = f32[8,1,65536]{2,1,0:T(1,128)S(1)} async-done(((f32[8,1,65536]{2,1,0:T(1,128)}), f32[8,1,65536]{2,1,0:T(1,128)S(1)}, u32[]{:S(2)}, u32[]{:S(2)}) %all-to-all-start) | async-done | bytes 2097184 | tf_op jit(solution)/shard_map/all_to_all | solution.py:27
  44.1 1.5 reduce_sum.63
  46.2 2.1 convolution_bitcast_fusion.1
  48.7 21.9 %all_to_all.48 = f32[16,64,256]{2,1,0:T(8,128)S(1)} all-to-all(f32[16,64,256]{2,1,0:T(8,128)S(1)} %bitcast.128), channel_id=1, replica_groups=mesh['tenant'=16,'row'=8] {'tenant'}, dimensions={0} | all-to-all | bytes 2097152 | tf_op jit(solution)/shard_map/all_to_all | solution.py:42
  70.8 19.1 %all_to_all.46 = f32[16,64,256]{2,1,0:T(8,128)S(1)} all-to-all(f32[16,64,256]{2,1,0:T(8,128)S(1)} %broadcast_in_dim.23), channel_id=1, replica_groups=mesh['tenant'=16,'row'=8] {'tenant'}, dimensions={0} | all-to-all | bytes 2097152 | tf_op jit(solution)/shard_map/all_to_all | solution.py:27
  89.8 1.8 convolution_bitcast_fusion.3
  91.7 1.5 broadcast_in_dim.24
  93.1 4.6 %all-to-all-start.3 = ((f32[8,256,256]{2,1,0:T(8,128)}), f32[8,256,256]{2,1,0:T(8,128)}, u32[]{:S(2)}, u32[]{:S(2)}) async-start(f32[8,256,256]{2,1,0:T(8,128)} %broadcast_in_dim.24), calls=%async_computation.3 | async-start | bytes 4194304 | tf_op jit(solution)/shard_map/all_to_all | solution.py:27
  97.8 32.0 %all-to-all-done.3 = f32[8,256,256]{2,1,0:T(8,128)} async-done(((f32[8,256,256]{2,1,0:T(8,128)}), f32[8,256,256]{2,1,0:T(8,128)}, u32[]{:S(2)}, u32[]{:S(2)}) %all-to-all-start.3) | async-done | bytes 2097184 | tf_op jit(solution)/shard_map/all_to_all | solution.py:27
  129.8 1.8 reduce_sum.65
  131.7 11.7 %cholesky.130 = f32[128,128]{1,0:T(8,128)S(1)} custom-call(f32[128,128]{1,0:T(8,128)S(1)} %cholesky.194), custom_call_target="Cholesky" | custom-call | tf_op jit(solution)/shard_map/jit(cholesky)/cholesky | solution.py:71
  143.5 9.8 %custom-call.13 = f32[1,128,128]{1,2,0:T(8,128)S(1)} custom-call(f32[1,128,128]{2,1,0:T(8,128)S(1)} %get-tuple-element.67), custom_call_target="InvertDiagBlocksLowerTriangular" | custom-call | tf_op jit(solution)/shard_map/jit(cholesky)/cholesky | solution.py:71
  153.8 11.7 %cholesky.147 = f32[128,128]{1,0:T(8,128)S(1)} custom-call(f32[128,128]{1,0:T(8,128)S(1)} %convolution_subtract_fusion.3), custom_call_target="Cholesky" | custom-call | tf_op jit(solution)/shard_map/jit(cholesky)/cholesky | solution.py:71
  167.6 4.0 %while.4 = (s32[]{:T(128)}, f32[256,256]{1,0:T(8,128)S(1)}, s32[2,2]{1,0:T(2,128)S(1)}, f32[2,128,128]{2,1,0:T(8,128)S(1)}, s32[]{:T(128)}) while((s32[]{:T(128)}, f32[256,256]{1,0:T(8,128)S(1)}, s32[2,2]{1,0:T(2,128)S(1)}, f32[2,128,128]{2,1,0:T(8,128)S(1)}, s32[]{:T(128)}) %tuple.52), condition=%wide.while_cond, body=%wide.while_body.sunk | while | flops 2 | bytes 131181 | solution.py:72
  168.2 1.4 bitcast_dynamic-update-slice_fusion.4
  170.2 1.4 bitcast_dynamic-update-slice_fusion.4
  171.6 20.8 %custom-call.14 = f32[2,128,128]{1,2,0:T(8,128)} custom-call(f32[2,128,128]{2,1,0:T(8,128)S(1)} %get-tuple-element.20), custom_call_target="InvertDiagBlocksLowerTriangular" | custom-call | tf_op jit(solution)/shard_map/triangular_solve/custom-call.0 | solution.py:72
  192.5 1.6 fusion.10
  196.5 1.2 convolution_bitcast_fusion.5
  197.8 20.0 %all_to_all.49 = f32[8,8,16,256]{3,2,1,0:T(8,128)S(1)} all-to-all(f32[8,8,16,256]{3,2,1,0:T(8,128)S(1)} %broadcast_in_dim.25), channel_id=1, replica_groups=mesh['tenant'=16,'row'=8] {'row'}, dimensions={0} | all-to-all | bytes 2097152 | tf_op jit(solution)/shard_map/all_to_all | solution.py:27
  218.4 2.0 convolution_bitcast_fusion
  220.4 1.6 copy.34
  222.0 19.5 %all_to_all.50 = f32[16,64,256]{2,1,0:T(8,128)} all-to-all(f32[16,64,256]{2,1,0:T(8,128)S(1)} %bitcast.129), channel_id=1, replica_groups=mesh['tenant'=16,'row'=8] {'tenant'}, dimensions={0} | all-to-all | bytes 2097152 | tf_op jit(solution)/shard_map/all_to_all | solution.py:42
  241.5 1.3 reduce_sum.67
  242.9 19.1 %all_to_all.47 = f32[16,64,256]{2,1,0:T(8,128)S(1)} all-to-all(f32[16,64,256]{2,1,0:T(8,128)S(1)} %broadcast_in_dim.26), channel_id=1, replica_groups=mesh['tenant'=16,'row'=8] {'tenant'}, dimensions={0} | all-to-all | bytes 2097152 | tf_op jit(solution)/shard_map/all_to_all | solution.py:27
  262.0 1.8 convolution_bitcast_fusion.2
  264.0 32.0 %all_to_all.51 = f32[8,256,256]{2,1,0:T(8,128)} all-to-all(f32[8,256,256]{2,1,0:T(8,128)S(1)} %broadcast_in_dim.27), channel_id=1, replica_groups=mesh['tenant'=16,'row'=8] {'row'}, dimensions={0} | all-to-all | bytes 4194304 | tf_op jit(solution)/shard_map/all_to_all | solution.py:27
  296.0 1.8 reduce_sum.68
  298.0 11.7 %cholesky.164 = f32[128,128]{1,0:T(8,128)S(1)} custom-call(f32[128,128]{1,0:T(8,128)S(1)} %cholesky.197), custom_call_target="Cholesky" | custom-call | tf_op jit(solution)/shard_map/jit(cholesky)/cholesky | solution.py:71
  309.7 9.8 %custom-call.15 = f32[1,128,128]{1,2,0:T(8,128)S(1)} custom-call(f32[1,128,128]{2,1,0:T(8,128)S(1)} %get-tuple-element.63), custom_call_target="InvertDiagBlocksLowerTriangular" | custom-call | tf_op jit(solution)/shard_map/jit(cholesky)/cholesky | solution.py:71
  320.0 11.7 %cholesky.181 = f32[128,128]{1,0:T(8,128)S(1)} custom-call(f32[128,128]{1,0:T(8,128)S(1)} %convolution_subtract_fusion.2), custom_call_target="Cholesky" | custom-call | tf_op jit(solution)/shard_map/jit(cholesky)/cholesky | solution.py:71
  334.4 4.0 %while.5 = (s32[]{:T(128)}, f32[256,256]{1,0:T(8,128)S(1)}, s32[2,2]{1,0:T(2,128)S(1)}, f32[2,128,128]{2,1,0:T(8,128)S(1)}, s32[]{:T(128)}) while((s32[]{:T(128)}, f32[256,256]{1,0:T(8,128)S(1)}, s32[2,2]{1,0:T(2,128)S(1)}, f32[2,128,128]{2,1,0:T(8,128)S(1)}, s32[]{:T(128)}) %tuple.58), condition=%wide.while_cond.clone, body=%wide.while_body.clone.sunk | while | flops 2 | bytes 131181 | solution.py:72
  335.0 1.4 bitcast_dynamic-update-slice_fusion.5
  337.0 1.4 bitcast_dynamic-update-slice_fusion.5
  338.4 19.9 %custom-call.16 = f32[2,128,128]{1,2,0:T(8,128)S(1)} custom-call(f32[2,128,128]{2,1,0:T(8,128)S(1)} %get-tuple-element.21), custom_call_target="InvertDiagBlocksLowerTriangular" | custom-call | tf_op jit(solution)/shard_map/triangular_solve/custom-call.0 | solution.py:72
  360.6 2.3 convolution_bitcast_fusion.4
  362.9 1.2 broadcast_in_dim.28
  364.0 4.2 %all-to-all-start.8 = ((f32[8,8,16,256]{3,2,1,0:T(8,128)}), f32[8,8,16,256]{3,2,1,0:T(8,128)}, u32[]{:S(2)}, u32[]{:S(2)}) async-start(f32[8,8,16,256]{3,2,1,0:T(8,128)} %broadcast_in_dim.28), calls=%async_computation.8 | async-start | bytes 2097152 | tf_op jit(solution)/shard_map/all_to_all | solution.py:27
  368.3 1.1 fusion.7
  369.4 2.5 copy.37
  371.9 1.1 fusion.6
  373.0 2.5 copy.38
  375.5 8.1 %all-to-all-done.8 = f32[8,8,16,256]{3,2,1,0:T(8,128)} async-done(((f32[8,8,16,256]{3,2,1,0:T(8,128)}), f32[8,8,16,256]{3,2,1,0:T(8,128)}, u32[]{:S(2)}, u32[]{:S(2)}) %all-to-all-start.8) | async-done | bytes 1048608 | tf_op jit(solution)/shard_map/all_to_all | solution.py:27
  383.6 2.0 reduce_sum.69
  (73 shorter events, 13.4 us)
Async XLA Ops:
  0.6 1.2 copy-start
  0.6 3.0 copy-start.7
  1.9 1.8 copy-start.4
  6.9 37.2 %all-to-all-start = ((f32[8,1,65536]{2,1,0:T(1,128)}), f32[8,1,65536]{2,1,0:T(1,128)S(1)}, u32[]{:S(2)}, u32[]{:S(2)}) async-start(f32[8,1,65536]{2,1,0:T(1,128)} %broadcast_in_dim.22), calls=%async_computation | async-start | bytes 4194304 | tf_op jit(solution)/shard_map/all_to_all | solution.py:27
  93.1 36.6 %all-to-all-start.3 = ((f32[8,256,256]{2,1,0:T(8,128)}), f32[8,256,256]{2,1,0:T(8,128)}, u32[]{:S(2)}, u32[]{:S(2)}) async-start(f32[8,256,256]{2,1,0:T(8,128)} %broadcast_in_dim.24), calls=%async_computation.3 | async-start | bytes 4194304 | tf_op jit(solution)/shard_map/all_to_all | solution.py:27
  171.6 24.8 %copy-start.3 = (f32[8,16,1024]{2,1,0:T(8,128)S(1)}, f32[8,16,1024]{2,1,0:T(8,128)}, u32[]{:S(2)}) copy-start(f32[8,16,1024]{2,1,0:T(8,128)} %param.7) | copy-start | bytes 1572868
  192.5 2.6 copy-start.8
  195.7 0.8 copy-start.1
  197.8 20.6 %copy-start.5 = (f32[8,16,1024]{2,1,0:T(8,128)S(1)}, f32[8,16,1024]{2,1,0:T(8,128)}, u32[]{:S(2)}) copy-start(f32[8,16,1024]{2,1,0:T(8,128)} %param.8) | copy-start | bytes 1572868
  217.9 4.1 %copy-start.6 = (f32[8,16,256]{2,1,0:T(8,128)}, f32[8,16,256]{2,1,0:T(8,128)S(1)}, u32[]{:S(2)}) copy-start(f32[8,16,256]{2,1,0:T(8,128)S(1)} %reduce_sum.66) | copy-start | bytes 393220
  360.6 7.7 %copy-start.2 = (f32[1024,128]{0,1:T(8,128)S(1)}, f32[1024,128]{0,1:T(8,128)}, u32[]{:S(2)}) copy-start(f32[1024,128]{0,1:T(8,128)} %copy-done.1) | copy-start | bytes 1572868
  364.0 19.6 %all-to-all-start.8 = ((f32[8,8,16,256]{3,2,1,0:T(8,128)}), f32[8,8,16,256]{3,2,1,0:T(8,128)}, u32[]{:S(2)}, u32[]{:S(2)}) async-start(f32[8,8,16,256]{3,2,1,0:T(8,128)} %broadcast_in_dim.28), calls=%async_computation.8 | async-start | bytes 2097152 | tf_op jit(solution)/shard_map/all_to_all | solution.py:27
where the time goes:
time: 393 us; the launch traced here: 386 us
  blocking collectives  132 us (34%)
  other arithmetic  120 us (31%)
  waiting for transfers between devices  71.3 us (18%)
  local copies, waits for them, and re-layouts  23.1 us (6%)
  matrix products  20.9 us (5%)
  starting transfers between devices  14.9 us (4%)
  between operations  3.99 us (1%)
    all_to_all x4, blocking collectives, copy_for_each(): return lax.all_to_all(copies, axis, split_axis=0, concat_axis=0, tiled=True)  90.1 us
    all_to_all x3, waiting for transfers between devices, copy_for_each(): return lax.all_to_all(copies, axis, split_axis=0, concat_axis=0, tiled=True)  71.3 us
    another operation x13, other arithmetic, normalize(): lower = jnp.linalg.cholesky(gram)  68.5 us
    all_to_all x2, blocking collectives, sum_at_owner(): tiles = lax.all_to_all(cut_along(x, dim, count), axis, 0, 0, tiled=True)  41.5 us
    another operation x5, other arithmetic, normalize(): lax.linalg.triangular_solve(lower, matrix, left_side=False, lower=True, t...  40.8 us
    all_to_all x3, starting transfers between devices, copy_for_each(): return lax.all_to_all(copies, axis, split_axis=0, concat_axis=0, tiled=True)  14.9 us
    another operation x15, local copies, waits for them, and re-layouts, normalize(): lax.linalg.triangular_solve(lower, matrix, left_side=False, lower=True, t...  7.99 us
  transfers between devices with their start and end apart: 3, of which 3 were waited for; matrix products, arithmetic and copies ran while one was open for 2% of the time, Pallas kernels for 0%

commit v1 on v0

v1 whole, which is shorter than its diff:
```python
import math

import jax
import jax.numpy as jnp
from jax import lax
from jax.sharding import PartitionSpec as P

D = 8192
RANK = 16
HIGH = lax.Precision.HIGH


def chip_groups(count):
    return [[2 * chip + core for chip in range(count // 2)] for core in range(2)]


def sibling_pairs(count):
    return [(i, i ^ 1) for i in range(count)]


def exchanged(tiles, axis, groups=None):
    return lax.all_to_all(tiles, axis, 0, 0, axis_index_groups=groups, tiled=True)


def sum_at_owner(tiles, axis, groups=None):
    return jnp.sum(exchanged(tiles, axis, groups), axis=0)


def gathered(x, axis, count, groups=None):
    return exchanged(jnp.broadcast_to(x, (count, *x.shape)), axis, groups)


def tenant_total(factors, coeffs):
    count = lax.axis_size("tenant")
    core = lax.axis_index("tenant") % 2
    half = factors.shape[1] // 2
    chips = count // 2

    def part(which):
        columns = lax.dynamic_slice_in_dim(factors, which * half, half, 1)
        return jnp.einsum("td,tk->dk", columns, coeffs, precision=HIGH)

    other = lax.ppermute(part(1 - core), "tenant", sibling_pairs(count))
    mine = part(core) + other
    groups = chip_groups(count)
    tile = sum_at_owner(mine.reshape(chips, half // chips, -1), "tenant", groups)
    mine = gathered(tile, "tenant", chips, groups).reshape(half, -1)
    other = lax.ppermute(mine, "tenant", sibling_pairs(count))
    return jnp.where(core == 0, jnp.concatenate([mine, other]), jnp.concatenate([other, mine]))


def row_total(arrays):
    count = lax.axis_size("row")
    tiles = jnp.concatenate([a.reshape(count, -1, a.shape[-1]) for a in arrays], axis=1)
    whole = gathered(sum_at_owner(tiles, "row"), "row", count)
    ends = [0]
    for a in arrays:
        ends.append(ends[-1] + a.size // count // a.shape[-1])
    return [whole[:, b:e].reshape(a.shape) for a, b, e in zip(arrays, ends, ends[1:])]


def weighted(side, other):
    side = side.reshape(-1, RANK, side.shape[-1])
    other = other.reshape(side.shape)
    weight = jnp.einsum("trk,tsk->trs", side, side, precision=HIGH)
    return jnp.einsum("trs,tsk->trk", weight, other, precision=HIGH).reshape(-1, other.shape[-1])


def refresh(factors, coeffs):
    total = tenant_total(factors, coeffs)
    cores, gram = row_total(
        (
            jnp.dot(factors, total, precision=HIGH),
            jnp.einsum("dk,dl->kl", total, total, precision=HIGH),
        )
    )
    lower = jnp.linalg.cholesky(gram)
    both = jnp.concatenate([total, cores])
    both = lax.linalg.triangular_solve(lower, both, left_side=False, lower=True, transpose_a=True)
    return both[: len(total)], both[len(total) :]


def local(b_factors, a_factors, u_start, v_start):
    shape = (*b_factors.shape[:2], u_start.shape[1])
    b = b_factors.reshape(-1, b_factors.shape[2])
    a = a_factors.reshape(-1, a_factors.shape[2])
    count = lax.axis_size("row")
    left = jnp.dot(b, u_start, precision=HIGH).reshape(count, -1, shape[2])
    right = jnp.dot(a, v_start, precision=HIGH).reshape(count, -1, shape[2])
    owned = sum_at_owner(jnp.concatenate([left, right], axis=1), "row")
    left, right = jnp.split(owned, 2)
    pair = gathered(jnp.concatenate([weighted(right, left), right]), "row", count)
    coeffs, right = (x.reshape(-1, shape[2]) for x in jnp.split(pair, 2, axis=1))
    basis_u, left = refresh(b, coeffs)
    basis_v, right = refresh(a, weighted(left, right))
    scale = math.sqrt(D)
    return (basis_u * scale, basis_v * scale, left.reshape(shape), right.reshape(shape))


def solution(mesh):
    in_specs = (P("tenant", None, "row"), P("tenant", None, "row"), P("row", None), P("row", None))
    out_specs = (P("row", None), P("row", None), P("tenant", None, None), P("tenant", None, None))
    return jax.shard_map(local, mesh=mesh, in_specs=in_specs, out_specs=out_specs, check_vma=False)
```

time: 393 us -> 294 us (0.75)
  blocking collectives: 132 us -> 80.7 us
  waiting for transfers between devices: 71.3 us -> 39.4 us
  matrix products: 20.9 us -> 13.2 us
  other arithmetic: 120 us -> 113 us
    all_to_all x6, blocking collectives: 132 us -> 80.7 us  [exchanged(): lax.all_to_all(tiles, axis, 0, 0, axis_index_groups=groups, tiled=True)]
    all_to_all x3 -> x4, waiting for transfers between devices: 71.3 us -> 31.7 us  [exchanged(): lax.all_to_all(tiles, axis, 0, 0, axis_index_groups=groups, tiled=True)]
    ppermute x0 -> x4, waiting for transfers between devices: none -> 7.73 us  [the longest x2 3.95 us: tenant_total(): other = lax.ppermute(mine, 'tenant', sibling_pairs(count))]
    dot_general x12 -> x14, matrix products: 14.6 us -> 7.09 us  [the longest x2 2 us: refresh(): jnp.einsum('dk,dl->kl', total, total, precision=HIGH)]
    reduce_sum x7 -> x5, other arithmetic: 8.42 us -> 1.14 us  [sum_at_owner(): return jnp.sum(exchanged(tiles, axis, groups), axis=0)]
    all_to_all x3 -> x4, starting transfers between devices: 14.9 us -> 17.9 us  [exchanged(): lax.all_to_all(tiles, axis, 0, 0, axis_index_groups=groups, tiled=True)]
    another operation x18 -> x20, other arithmetic: 109 us -> 109 us  [the longest x13 68.7 us: refresh(): lower = jnp.linalg.cholesky(gram)]
  transfers between devices with their start and end apart: 3 -> 8, of which waited for: 3 -> 8; matrix products, arithmetic and copies ran while one was open for 2% -> 1% of each run, Pallas kernels for 0% -> 0%
where the time goes in v1:
time: 294 us; the launch traced here: 288 us
  other arithmetic  113 us (38%)
  blocking collectives  80.7 us (27%)
  waiting for transfers between devices  39.4 us (13%)
  local copies, waits for them, and re-layouts  19.2 us (7%)
  starting transfers between devices  18 us (6%)
  matrix products  13.2 us (4%)
  between operations  4.11 us (1%)
    all_to_all x6, blocking collectives, exchanged(): lax.all_to_all(tiles, axis, 0, 0, axis_index_groups=groups, tiled=True)  80.7 us
    another operation x13, other arithmetic, refresh(): lower = jnp.linalg.cholesky(gram)  68.7 us
    another operation x7, other arithmetic, refresh(): lax.linalg.triangular_solve(lower, both, left_side=False, lower=True, tra...  39.9 us
    all_to_all x4, waiting for transfers between devices, exchanged(): lax.all_to_all(tiles, axis, 0, 0, axis_index_groups=groups, tiled=True)  31.7 us
    all_to_all x4, starting transfers between devices, exchanged(): lax.all_to_all(tiles, axis, 0, 0, axis_index_groups=groups, tiled=True)  17.9 us
    another operation x15, local copies, waits for them, and re-layouts, refresh(): lax.linalg.triangular_solve(lower, both, left_side=False, lower=True, tra...  8.05 us
  transfers between devices with their start and end apart: 8, of which 8 were waited for; matrix products, arithmetic and copies ran while one was open for 1% of the time, Pallas kernels for 0%

profile of v1, /device:TPU:8, one launch (start us, length us, event | category | flops | bytes accessed | tf_op | source)
XLA Modules:
  0.0 287.9 jit_solution(4261515183368053085)
XLA Ops:
  0.7 1.2 copy-done
  1.9 1.5 fusion.6
  4.6 6.2 %all-to-all-start = ((f32[8,32,256]{2,1,0:T(8,128)}), f32[8,32,256]{2,1,0:T(8,128)S(1)}, u32[]{:S(2)}, u32[]{:S(2)}) async-start(f32[8,32,256]{2,1,0:T(8,128)} %pad_maximum_fusion.4), calls=%async_computation | async-start | bytes 524288 | tf_op jit(solution)/shard_map/all_to_all | solution.py:22
  10.7 8.7 %all-to-all-done = f32[8,32,256]{2,1,0:T(8,128)S(1)} async-done(((f32[8,32,256]{2,1,0:T(8,128)}), f32[8,32,256]{2,1,0:T(8,128)S(1)}, u32[]{:S(2)}, u32[]{:S(2)}) %all-to-all-start) | async-done | bytes 262176 | tf_op jit(solution)/shard_map/all_to_all | solution.py:22
  20.5 3.4 %all-to-all-start.1 = ((f32[8,32,256]{2,1,0:T(8,128)}), f32[8,32,256]{2,1,0:T(8,128)S(1)}, u32[]{:S(2)}, u32[]{:S(2)}) async-start(f32[8,32,256]{2,1,0:T(8,128)} %broadcast_in_dim.16), calls=%async_computation.1 | async-start | bytes 524288 | tf_op jit(solution)/shard_map/all_to_all | solution.py:22
  23.9 8.4 %all-to-all-done.1 = f32[8,32,256]{2,1,0:T(8,128)S(1)} async-done(((f32[8,32,256]{2,1,0:T(8,128)}), f32[8,32,256]{2,1,0:T(8,128)S(1)}, u32[]{:S(2)}, u32[]{:S(2)}) %all-to-all-start.1) | async-done | bytes 262176 | tf_op jit(solution)/shard_map/all_to_all | solution.py:22
  32.8 1.9 collective-permute-done
  35.2 15.8 %all_to_all.52 = f32[8,64,256]{2,1,0:T(8,128)S(1)} all-to-all(f32[8,64,256]{2,1,0:T(8,128)S(1)} %bitcast.127), channel_id=1, replica_groups={{0,16,32,48,64,80,96,112},{8,24,40,56,72,88,104,120},{1,17,33,49,65,81,..., dimensions={0} | all-to-all | bytes 1048576 | tf_op jit(solution)/shard_map/all_to_all | solution.py:22
  51.0 12.1 %all_to_all.50 = f32[8,64,256]{2,1,0:T(8,128)S(1)} all-to-all(f32[8,64,256]{2,1,0:T(8,128)S(1)} %broadcast_in_dim.17), channel_id=1, replica_groups={{0,16,32,48,64,80,96,112},{8,24,40,56,72,88,104,120},{1,17,33,49,65,81,..., dimensions={0} | all-to-all | bytes 1048576 | tf_op jit(solution)/shard_map/all_to_all | solution.py:22
  63.1 2.0 collective-permute-done.1
  65.2 1.3 maximum_select_fusion
  66.9 1.0 fusion.57
  68.0 13.2 %all_to_all.53 = f32[8,48,256]{2,1,0:T(8,128)S(1)} all-to-all(f32[8,48,256]{2,1,0:T(8,128)S(1)} %pad_maximum_fusion.2), channel_id=1, replica_groups=mesh['tenant'=16,'row'=8] {'row'}, dimensions={0} | all-to-all | bytes 786432 | tf_op jit(solution)/shard_map/all_to_all | solution.py:22
  81.2 0.8 broadcast_in_dim.18
  81.9 4.0 %all-to-all-start.5 = ((f32[8,48,256]{2,1,0:T(8,128)}), f32[8,48,256]{2,1,0:T(8,128)S(1)}, u32[]{:S(2)}, u32[]{:S(2)}) async-start(f32[8,48,256]{2,1,0:T(8,128)} %broadcast_in_dim.18), calls=%async_computation.5 | async-start | bytes 786432 | tf_op jit(solution)/shard_map/all_to_all | solution.py:22
  85.9 8.9 %all-to-all-done.5 = f32[8,48,256]{2,1,0:T(8,128)S(1)} async-done(((f32[8,48,256]{2,1,0:T(8,128)}), f32[8,48,256]{2,1,0:T(8,128)S(1)}, u32[]{:S(2)}, u32[]{:S(2)}) %all-to-all-start.5) | async-done | bytes 393248 | tf_op jit(solution)/shard_map/all_to_all | solution.py:22
  95.1 11.7 %cholesky.130 = f32[128,128]{1,0:T(8,128)S(1)} custom-call(f32[128,128]{1,0:T(8,128)S(1)} %cholesky.194), custom_call_target="Cholesky" | custom-call | tf_op jit(solution)/shard_map/jit(cholesky)/cholesky | solution.py:77
  106.8 9.8 %custom-call.13 = f32[1,128,128]{1,2,0:T(8,128)S(1)} custom-call(f32[1,128,128]{2,1,0:T(8,128)S(1)} %get-tuple-element.57), custom_call_target="InvertDiagBlocksLowerTriangular" | custom-call | tf_op jit(solution)/shard_map/jit(cholesky)/cholesky | solution.py:77
  117.1 11.7 %cholesky.147 = f32[128,128]{1,0:T(8,128)S(1)} custom-call(f32[128,128]{1,0:T(8,128)S(1)} %convolution_subtract_fusion.1), custom_call_target="Cholesky" | custom-call | tf_op jit(solution)/shard_map/jit(cholesky)/cholesky | solution.py:77
  131.1 4.1 %while.4 = (s32[]{:T(128)}, f32[256,256]{1,0:T(8,128)S(1)}, s32[2,2]{1,0:T(2,128)S(1)}, f32[2,128,128]{2,1,0:T(8,128)S(1)}, s32[]{:T(128)}) while((s32[]{:T(128)}, f32[256,256]{1,0:T(8,128)S(1)}, s32[2,2]{1,0:T(2,128)S(1)}, f32[2,128,128]{2,1,0:T(8,128)S(1)}, s32[]{:T(128)}) %tuple.49), condition=%wide.while_cond, body=%wide.while_body.sunk | while | flops 2 | bytes 131189 | solution.py:79
  131.7 1.4 bitcast_dynamic-update-slice_fusion.4
  133.7 1.4 bitcast_dynamic-update-slice_fusion.4
  135.2 19.8 %custom-call.14 = f32[2,128,128]{1,2,0:T(8,128)S(1)} custom-call(f32[2,128,128]{2,1,0:T(8,128)S(1)} %get-tuple-element.20), custom_call_target="InvertDiagBlocksLowerTriangular" | custom-call | tf_op jit(solution)/shard_map/triangular_solve/custom-call.0 | solution.py:79
  155.8 1.1 fusion.36
  159.3 1.9 collective-permute-done.2
  161.7 13.7 %all_to_all.54 = f32[8,64,256]{2,1,0:T(8,128)S(1)} all-to-all(f32[8,64,256]{2,1,0:T(8,128)S(1)} %bitcast.126), channel_id=1, replica_groups={{0,16,32,48,64,80,96,112},{8,24,40,56,72,88,104,120},{1,17,33,49,65,81,..., dimensions={0} | all-to-all | bytes 1048576 | tf_op jit(solution)/shard_map/all_to_all | solution.py:22
  175.4 12.2 %all_to_all.51 = f32[8,64,256]{2,1,0:T(8,128)S(1)} all-to-all(f32[8,64,256]{2,1,0:T(8,128)S(1)} %broadcast_in_dim.19), channel_id=1, replica_groups={{0,16,32,48,64,80,96,112},{8,24,40,56,72,88,104,120},{1,17,33,49,65,81,..., dimensions={0} | all-to-all | bytes 1048576 | tf_op jit(solution)/shard_map/all_to_all | solution.py:22
  187.7 1.9 collective-permute-done.3
  190.1 1.0 fusion.60
  191.2 13.7 %all_to_all.55 = f32[8,48,256]{2,1,0:T(8,128)} all-to-all(f32[8,48,256]{2,1,0:T(8,128)S(1)} %pad_maximum_fusion.3), channel_id=1, replica_groups=mesh['tenant'=16,'row'=8] {'row'}, dimensions={0} | all-to-all | bytes 786432 | tf_op jit(solution)/shard_map/all_to_all | solution.py:22
  204.8 1.0 reduce_sum.49
  205.9 0.8 broadcast_in_dim.20
  206.7 4.3 %all-to-all-start.9 = ((f32[8,48,256]{2,1,0:T(8,128)}), f32[8,48,256]{2,1,0:T(8,128)}, u32[]{:S(2)}, u32[]{:S(2)}) async-start(f32[8,48,256]{2,1,0:T(8,128)} %broadcast_in_dim.20), calls=%async_computation.9 | async-start | bytes 786432 | tf_op jit(solution)/shard_map/all_to_all | solution.py:22
  211.0 1.1 fusion.3
  212.1 2.5 copy.20
  214.6 5.7 %all-to-all-done.9 = f32[8,48,256]{2,1,0:T(8,128)} async-done(((f32[8,48,256]{2,1,0:T(8,128)}), f32[8,48,256]{2,1,0:T(8,128)}, u32[]{:S(2)}, u32[]{:S(2)}) %all-to-all-start.9) | async-done | bytes 393248 | tf_op jit(solution)/shard_map/all_to_all | solution.py:22
  220.3 1.0 slice.107
  221.5 11.7 %cholesky.164 = f32[128,128]{1,0:T(8,128)S(1)} custom-call(f32[128,128]{1,0:T(8,128)S(1)} %cholesky.197), custom_call_target="Cholesky" | custom-call | tf_op jit(solution)/shard_map/jit(cholesky)/cholesky | solution.py:77
  233.9 9.8 %custom-call.15 = f32[1,128,128]{1,2,0:T(8,128)S(1)} custom-call(f32[1,128,128]{2,1,0:T(8,128)S(1)} %get-tuple-element.53), custom_call_target="InvertDiagBlocksLowerTriangular" | custom-call | tf_op jit(solution)/shard_map/jit(cholesky)/cholesky | solution.py:77
  244.2 11.7 %cholesky.181 = f32[128,128]{1,0:T(8,128)S(1)} custom-call(f32[128,128]{1,0:T(8,128)S(1)} %convolution_subtract_fusion), custom_call_target="Cholesky" | custom-call | tf_op jit(solution)/shard_map/jit(cholesky)/cholesky | solution.py:77
  258.0 4.0 %while.5 = (s32[]{:T(128)}, f32[256,256]{1,0:T(8,128)S(1)}, s32[2,2]{1,0:T(2,128)S(1)}, f32[2,128,128]{2,1,0:T(8,128)S(1)}, s32[]{:T(128)}) while((s32[]{:T(128)}, f32[256,256]{1,0:T(8,128)S(1)}, s32[2,2]{1,0:T(2,128)S(1)}, f32[2,128,128]{2,1,0:T(8,128)S(1)}, s32[]{:T(128)}) %tuple.55), condition=%wide.while_cond.clone, body=%wide.while_body.clone.sunk | while | flops 2 | bytes 131189 | solution.py:79
  258.6 1.4 bitcast_dynamic-update-slice_fusion.5
  260.6 1.4 bitcast_dynamic-update-slice_fusion.5
  261.9 19.9 %custom-call.16 = f32[2,128,128]{1,2,0:T(8,128)S(1)} custom-call(f32[2,128,128]{2,1,0:T(8,128)S(1)} %get-tuple-element.21), custom_call_target="InvertDiagBlocksLowerTriangular" | custom-call | tf_op jit(solution)/shard_map/triangular_solve/custom-call.0 | solution.py:79
  281.9 0.9 slice.109
  283.5 1.1 fusion.32
  285.6 1.3 copy.21
  286.9 0.8 copy.19
  (89 shorter events, 15.5 us)
Async XLA Ops:
  0.6 1.2 copy-start
  0.6 2.8 copy-start.2
  1.9 1.6 copy-start.8
  4.6 27.7 %copy-start.1 = (f32[8,16,1024]{2,1,0:T(8,128)S(1)}, f32[8,16,1024]{2,1,0:T(8,128)}, u32[]{:S(2)}) copy-start(f32[8,16,1024]{2,1,0:T(8,128)} %param.7) | copy-start | bytes 1572868
  4.6 14.9 %all-to-all-start = ((f32[8,32,256]{2,1,0:T(8,128)}), f32[8,32,256]{2,1,0:T(8,128)S(1)}, u32[]{:S(2)}, u32[]{:S(2)}) async-start(f32[8,32,256]{2,1,0:T(8,128)} %pad_maximum_fusion.4), calls=%async_computation | async-start | bytes 524288 | tf_op jit(solution)/shard_map/all_to_all | solution.py:22
  20.5 11.8 %all-to-all-start.1 = ((f32[8,32,256]{2,1,0:T(8,128)}), f32[8,32,256]{2,1,0:T(8,128)S(1)}, u32[]{:S(2)}, u32[]{:S(2)}) async-start(f32[8,32,256]{2,1,0:T(8,128)} %broadcast_in_dim.16), calls=%async_computation.1 | async-start | bytes 524288 | tf_op jit(solution)/shard_map/all_to_all | solution.py:22
  32.3 2.9 copy-start.6
  32.7 2.0 collective-permute-start
  63.1 2.0 collective-permute-start.1
  81.9 12.9 %all-to-all-start.5 = ((f32[8,48,256]{2,1,0:T(8,128)}), f32[8,48,256]{2,1,0:T(8,128)S(1)}, u32[]{:S(2)}, u32[]{:S(2)}) async-start(f32[8,48,256]{2,1,0:T(8,128)} %broadcast_in_dim.18), calls=%async_computation.5 | async-start | bytes 786432 | tf_op jit(solution)/shard_map/all_to_all | solution.py:22
  157.6 1.0 copy-start.7
  157.7 1.2 copy-start.3
  157.8 3.9 %copy-start.5 = (f32[128,256]{1,0:T(8,128)}, f32[128,256]{1,0:T(8,128)S(1)}, u32[]{:S(2)}) copy-start(f32[128,256]{1,0:T(8,128)S(1)} %copy.17) | copy-start | bytes 393220
  159.2 2.0 collective-permute-start.2
  187.7 2.0 copy-start.4
  187.7 1.9 collective-permute-start.3
  206.7 13.7 %all-to-all-start.9 = ((f32[8,48,256]{2,1,0:T(8,128)}), f32[8,48,256]{2,1,0:T(8,128)}, u32[]{:S(2)}, u32[]{:S(2)}) async-start(f32[8,48,256]{2,1,0:T(8,128)} %broadcast_in_dim.20), calls=%async_computation.9 | async-start | bytes 786432 | tf_op jit(solution)/shard_map/all_to_all | solution.py:22

commit v2 on v1

v2 whole, which is shorter than its diff:
```python
import math

import jax
import jax.numpy as jnp
from jax import lax
from jax.experimental import pallas as pl
from jax.experimental.pallas import tpu as pltpu
from jax.sharding import PartitionSpec as P

D = 8192
RANK = 16
LANES = 128
SUBLANES = 8
PANEL = 32


def pieces(x):
    high = x.astype(jnp.bfloat16)
    rest = x - high.astype(jnp.float32)
    middle = rest.astype(jnp.bfloat16)
    return high, middle, (rest - middle.astype(jnp.float32)).astype(jnp.bfloat16)


def float32_product(x, y):
    xh, xm, xl = pieces(x)
    yh, ym, yl = pieces(y)
    xs = jnp.concatenate([xh, xh, xm, xh, xl, xm])
    ys = jnp.concatenate([yh, ym, yh, yl, yh, ym])
    return lax.dot_general(xs, ys, (((0,), (0,)), ((), ())), preferred_element_type=jnp.float32)


def wide(x, width):
    return jnp.concatenate([x] * (width // LANES), axis=1)


def eliminate(rows, units, start):
    width = rows[0].shape[1]
    tile = (SUBLANES, LANES)
    for m, first in enumerate(range(start, start + PANEL, SUBLANES)):
        r = [jnp.broadcast_to(rows[m][i : i + 1], rows[m].shape) for i in range(SUBLANES)]
        e = [jnp.broadcast_to(units[m][i : i + 1], tile) for i in range(SUBLANES)]
        later = range(m + 1, len(rows))

        def column(x, j):
            return jnp.broadcast_to(x[:, first + j : first + j + 1], tile)

        d = [[column(r[i], j) for j in range(SUBLANES)] for i in range(SUBLANES)]
        c = {g: [column(rows[g], j) for j in range(SUBLANES)] for g in later}
        sub = lax.broadcasted_iota(jnp.int32, rows[m].shape, 0)
        sub_tile = lax.broadcasted_iota(jnp.int32, tile, 0)
        done, done_unit = jnp.zeros_like(rows[m]), jnp.zeros_like(units[m])
        for j in range(SUBLANES):
            inverse = lax.rsqrt(d[j][j])
            p, q = r[j] * wide(inverse, width), e[j] * inverse
            done = jnp.where(sub == j, p, done)
            done_unit = jnp.where(sub_tile == j, q, done_unit)
            below = range(j + 1, SUBLANES)
            factor = {i: d[j][i] * inverse for i in below}
            for i in below:
                for other in range(i, SUBLANES):
                    d[i][other] -= factor[i] * factor[other]
                r[i] -= wide(factor[i], width) * p
                e[i] -= factor[i] * q
            for g in later:
                scale = c[g][j] * inverse
                for i in below:
                    c[g][i] -= scale * factor[i]
                rows[g] -= wide(scale, width) * p
                units[g] -= scale * q
        rows[m], units[m] = done, done_unit
    return jnp.concatenate(rows), jnp.concatenate(units)


def split(x):
    high = x.astype(jnp.bfloat16)
    return high, (x - high.astype(jnp.float32)).astype(jnp.bfloat16)


def product(x, y, x_dim=1, y_dim=0):
    dims = (((x_dim,), (y_dim,)), ((), ()))
    xh, xl = split(x)
    yh, yl = split(y)

    def part(p, q):
        return lax.dot_general(p, q, dims, preferred_element_type=jnp.float32)

    return part(xh, yh) + (part(xh, yl) + part(xl, yh))


def matrix(x):
    return x.reshape(-1, x.shape[-1])


def factor_in_place(out_ref):
    n = out_ref.shape[0]
    sub = lax.broadcasted_iota(jnp.int32, (SUBLANES, LANES), 0)
    lane = lax.broadcasted_iota(jnp.int32, (SUBLANES, LANES), 1)
    column = lax.broadcasted_iota(jnp.int32, (n, n), 1)
    for start in range(0, n, PANEL):
        end = start + PANEL
        tile = start // LANES
        rows, units = [], []
        for g in range(0, PANEL, SUBLANES):
            rows.append(out_ref[pl.ds(start + g, SUBLANES), :])
            units.append(jnp.where(lane == sub + (start % LANES + g), 1.0, 0.0))
        rows, units = eliminate(rows, units, start)
        blank = jnp.zeros_like(units)
        units = jnp.concatenate([units if t == tile else blank for t in range(n // LANES)], axis=1)
        inside = (column >= start) & (column < end)
        solved = jnp.where(inside[:PANEL], units, rows)
        out_ref[pl.ds(start, PANEL), :] = jnp.where(column[:PANEL] < end, solved, 0.0)
        if end < n:
            aligned = end // LANES * LANES
            update = float32_product(rows[:, aligned:], solved)[end - aligned :]
            rest = out_ref[pl.ds(end, n - end), :]
            out_ref[pl.ds(end, n - end), :] = jnp.where(inside[end:], 0.0, rest) - update


def call(kernel, shapes, *operands, **options):
    shapes = [jax.ShapeDtypeStruct(shape, jnp.float32) for shape in shapes]
    return pl.pallas_call(
        kernel,
        out_shape=shapes if len(shapes) > 1 else shapes[0],
        compiler_params=pltpu.CompilerParams(vmem_limit_bytes=32 << 20),
        name=kernel.__name__,
        **options,
    )(*operands)


def projections(b_ref, a_ref, u_ref, v_ref, out_ref):
    left = product(b_ref[...], u_ref[...]).reshape(-1, RANK, out_ref.shape[2])
    right = product(a_ref[...], v_ref[...]).reshape(left.shape)
    first = pl.program_id(0) == 0

    @pl.when(first)
    def _():
        out_ref[:, :RANK] = left
        out_ref[:, RANK:] = right

    @pl.when(jnp.logical_not(first))
    def _():
        out_ref[:, :RANK] += left
        out_ref[:, RANK:] += right


def owner_coefficients(tiles_ref, out_ref):
    total = jnp.sum(tiles_ref[...], axis=0)
    left, right = total[:RANK], total[RANK:]
    coeffs = product(product(right, right, 1, 1), left)
    out_ref[:, :RANK] = jnp.broadcast_to(coeffs, (len(out_ref), *coeffs.shape))
    out_ref[:, RANK:] = jnp.broadcast_to(right, (len(out_ref), *right.shape))


def owner_sum(tiles_ref, out_ref):
    out_ref[...] = jnp.broadcast_to(jnp.sum(tiles_ref[...], axis=0), out_ref.shape)


def both(x_ref, y_ref):
    return jnp.concatenate([matrix(x_ref[...]), matrix(y_ref[...])])


def both_upper(x_ref, y_ref):
    return jnp.concatenate([matrix(x_ref[:, :RANK]), matrix(y_ref[:, :RANK])])


def both_lower(x_ref, y_ref):
    return jnp.concatenate([matrix(x_ref[:, RANK:]), matrix(y_ref[:, RANK:])])


def load_sum(keep_ref, swap_ref, mine_ref, other_ref, out_ref):
    load = product(both(keep_ref, swap_ref), both_upper(mine_ref, other_ref), 0, 0)
    out_ref[...] = load.reshape(out_ref.shape)


def gram_and_cores(core_ref, keep_ref, swap_ref, basis_ref, mine_ref, other_ref, gram_ref):
    basis = matrix(basis_ref[...])
    cores = product(both(keep_ref, swap_ref), basis)
    gram_ref[...] = product(basis, basis, 0, 0)
    count, half = len(mine_ref), len(gram_ref) // 2
    mine_ref[:, :RANK] = cores[:half].reshape(count, RANK, -1)
    other_ref[:, :RANK] = cores[half:].reshape(count, RANK, -1)
    core = core_ref[0]
    mine_ref[:, RANK:] = gram_ref[pl.ds(core * half, half), :].reshape(count, RANK, -1)
    other_ref[:, RANK:] = gram_ref[pl.ds((1 - core) * half, half), :].reshape(count, RANK, -1)


def inverse_factor(core, mine_ref, other_ref, inverse_ref):
    half = len(inverse_ref) // 2
    inverse_ref[pl.ds(core * half, half), :] = matrix(mine_ref[:, RANK:])
    inverse_ref[pl.ds((1 - core) * half, half), :] = matrix(other_ref[:, RANK:])
    factor_in_place(inverse_ref)


def turn_over(
    core_ref, mine_ref, other_ref, pair_ref, pair_other_ref, keep_ref, swap_ref,
    inverse_ref, left_ref, load_ref,
):
    inverse_factor(core_ref[0], mine_ref, other_ref, inverse_ref)
    left = product(both_upper(mine_ref, other_ref), inverse_ref[...], 1, 1)
    left_ref[...] = left[: len(left) // 2].reshape(left_ref.shape)
    weight = product(left, left, 1, 1)
    tenant = [lax.broadcasted_iota(jnp.int32, weight.shape, d) // RANK for d in range(2)]
    weight = jnp.where(tenant[0] == tenant[1], weight, 0.0)
    coeffs = product(weight, both_lower(pair_ref, pair_other_ref))
    load = product(both(keep_ref, swap_ref), coeffs, 0, 0)
    load_ref[...] = load.reshape(load_ref.shape)


def scaled_basis(core, inverse, mine_ref, other_ref, out_ref):
    half = len(out_ref) // 2
    scale = math.sqrt(D)
    for place, ref in ((core, mine_ref), (1 - core, other_ref)):
        out_ref[pl.ds(place * half, half), :] = product(matrix(ref[...]), inverse, 1, 1) * scale


def left_basis(core_ref, inverse_ref, mine_ref, other_ref, out_ref):
    scaled_basis(core_ref[0], inverse_ref[...], mine_ref, other_ref, out_ref)


def finish(core_ref, mine_ref, other_ref, basis_ref, basis_other_ref, out_ref, right_ref, inverse_ref):
    inverse_factor(core_ref[0], mine_ref, other_ref, inverse_ref)
    inverse = inverse_ref[...]
    right = product(matrix(mine_ref[:, :RANK]), inverse, 1, 1)
    right_ref[...] = right.reshape(right_ref.shape)
    scaled_basis(core_ref[0], inverse, basis_ref, basis_other_ref, out_ref)


def exchanged(tiles, axis, groups=None):
    return lax.all_to_all(tiles, axis, 0, 0, axis_index_groups=groups, tiled=True)


def total(tiles, axis, groups=None, at_owner=owner_sum):
    copies = call(at_owner, [tiles.shape], exchanged(tiles, axis, groups))
    return exchanged(copies, axis, groups)


def from_sibling(x):
    count = lax.axis_size("tenant")
    return lax.ppermute(x, "tenant", [(i, i ^ 1) for i in range(count)])


def tenant_total(load):
    chips = lax.axis_size("tenant") // 2
    groups = [[2 * chip + core for chip in range(chips)] for core in range(2)]
    return total(load, "tenant", groups)


def gram_total(core, halves, basis, rank):
    count = lax.axis_size("row")
    tiles = (count, 2 * RANK, rank)
    mine, other = call(
        gram_and_cores,
        [tiles, tiles],
        core,
        *halves,
        basis,
        in_specs=with_core(3),
        scratch_shapes=[pltpu.VMEM((rank, rank), jnp.float32)],
    )
    return total(mine + from_sibling(other), "row")


def column_halves(factors, core):
    half = factors.shape[1] // 2
    keep = lax.dynamic_slice_in_dim(factors, core * half, half, 1)
    return keep, from_sibling(lax.dynamic_slice_in_dim(factors, (1 - core) * half, half, 1))


def with_core(count):
    return [pl.BlockSpec(memory_space=m) for m in (pltpu.SMEM, *[pltpu.VMEM] * count)]


def local(b_factors, a_factors, u_start, v_start):
    shape = (*b_factors.shape[:2], u_start.shape[1])
    width, rank = u_start.shape
    core = lax.axis_index("tenant") % 2
    flag = jnp.reshape(core, (1,)).astype(jnp.int32)
    b = b_factors.reshape(-1, width)
    a = a_factors.reshape(-1, width)
    b_halves, a_halves = column_halves(b, core), column_halves(a, core)

    step = width // 4
    factor_block = pl.BlockSpec((len(b), step), lambda i: (0, i))
    basis_block = pl.BlockSpec((step, rank), lambda i: (i, 0))
    tiles = (shape[0], 2 * RANK, rank)
    partial = call(
        projections,
        [tiles],
        b,
        a,
        u_start,
        v_start,
        grid=(4,),
        in_specs=[factor_block, factor_block, basis_block, basis_block],
        out_specs=pl.BlockSpec(tiles, lambda i: (0, 0, 0)),
    )
    pair = total(partial, "row", None, owner_coefficients)
    pair_other = from_sibling(pair)

    chips = lax.axis_size("tenant") // 2
    load_shape = (chips, width // 2 // chips, rank)
    load = call(load_sum, [load_shape], *b_halves, pair, pair_other)
    basis = tenant_total(load)
    basis_other = from_sibling(basis)
    mine = gram_total(flag, b_halves, basis, rank)
    inverse, left, load = call(
        turn_over,
        [(rank, rank), shape, load_shape],
        flag,
        mine,
        from_sibling(mine),
        pair,
        pair_other,
        *a_halves,
        in_specs=with_core(6),
    )
    u_scaled = call(
        left_basis, [(width, rank)], flag, inverse, basis, basis_other, in_specs=with_core(3)
    )
    basis = tenant_total(load)
    basis_other = from_sibling(basis)
    mine = gram_total(flag, a_halves, basis, rank)
    v_scaled, right = call(
        finish,
        [(width, rank), shape],
        flag,
        mine,
        from_sibling(mine),
        basis,
        basis_other,
        in_specs=with_core(4),
        scratch_shapes=[pltpu.VMEM((rank, rank), jnp.float32)],
    )
    return u_scaled, v_scaled, left, right


def solution(mesh):
    in_specs = (P("tenant", None, "row"), P("tenant", None, "row"), P("row", None), P("row", None))
    out_specs = (P("row", None), P("row", None), P("tenant", None, None), P("tenant", None, None))
    return jax.shard_map(local, mesh=mesh, in_specs=in_specs, out_specs=out_specs, check_vma=False)
```

time: 294 us -> 168 us (0.57); the launches traced: 288 us -> 165 us
  other arithmetic: 113 us -> 0.78 us
  Pallas kernels: 0 us -> 25.3 us
  local copies, waits for them, and re-layouts: 19.2 us -> 4.62 us
  matrix products: 13.2 us -> 0 us
  blocking collectives: 80.7 us -> 91.3 us
  waiting for transfers between devices: 39.4 us -> 30.9 us
  starting transfers between devices: 18 us -> 11.2 us
  between operations: 4.11 us -> 0.82 us
    another operation x20 -> x0, other arithmetic: 109 us -> none  [the longest x13 68.7 us: refresh(): lower = jnp.linalg.cholesky(gram)]
    pallas_call x0 -> x12, Pallas kernels: none -> 25.3 us  [call(): pl.pallas_call(kernel, out_shape=shapes if len(shapes) > 1 else shapes[0]...]
    all_to_all x6 -> x7, blocking collectives: 80.7 us -> 91.3 us  [exchanged(): lax.all_to_all(tiles, axis, 0, 0, axis_index_groups=groups, tiled=True)]
    another operation x19 -> x0, local copies, waits for them, and re-layouts: 8.1 us -> none  [the longest x15 8.05 us: refresh(): lax.linalg.triangular_solve(lower, both, left_side=False, lower=True, tra...]
    all_to_all x4 -> x3, starting transfers between devices: 17.9 us -> 10.2 us  [exchanged(): lax.all_to_all(tiles, axis, 0, 0, axis_index_groups=groups, tiled=True)]
    dot_general x14 -> x0, matrix products: 7.09 us -> none  [the longest x2 2 us: refresh(): jnp.einsum('dk,dl->kl', total, total, precision=HIGH)]
    all_to_all x4 -> x3, waiting for transfers between devices: 31.7 us -> 24.8 us  [exchanged(): lax.all_to_all(tiles, axis, 0, 0, axis_index_groups=groups, tiled=True)]
    another operation x10 -> x0, matrix products: 6.08 us -> none  [the longest x6 5.14 us: refresh(): lax.linalg.triangular_solve(lower, both, left_side=False, lower=True, tra...]
  transfers between devices with their start and end apart: 8 -> 12, of which waited for: 8 -> 7; matrix products, arithmetic and copies ran while one was open for 1% -> 0% of each run, Pallas kernels for 0% -> 1%
where the time goes in v2:
time: 168 us; the launch traced here: 165 us
  blocking collectives  91.3 us (54%)
  waiting for transfers between devices  30.9 us (18%)
  Pallas kernels  25.3 us (15%)
  starting transfers between devices  11.2 us (7%)
  local copies, waits for them, and re-layouts  4.62 us (3%)
    all_to_all x7, blocking collectives, exchanged(): lax.all_to_all(tiles, axis, 0, 0, axis_index_groups=groups, tiled=True)  91.3 us
    pallas_call x12, Pallas kernels, call(): pl.pallas_call(kernel, out_shape=shapes if len(shapes) > 1 else shapes[0]...  25.3 us
    all_to_all x3, waiting for transfers between devices, exchanged(): lax.all_to_all(tiles, axis, 0, 0, axis_index_groups=groups, tiled=True)  24.8 us
    all_to_all x3, starting transfers between devices, exchanged(): lax.all_to_all(tiles, axis, 0, 0, axis_index_groups=groups, tiled=True)  10.2 us
    ppermute x9, waiting for transfers between devices, from_sibling(): return lax.ppermute(x, 'tenant', [(i, i ^ 1) for i in range(count)])  6.12 us
    unnamed x12, local copies, waits for them, and re-layouts  4.53 us
  transfers between devices with their start and end apart: 12, of which 7 were waited for; matrix products, arithmetic and copies ran while one was open for 0% of the time, Pallas kernels for 1%

profile of v2, /device:TPU:8, one launch (start us, length us, event | category | flops | bytes accessed | tf_op | source)
XLA Modules:
  0.0 164.9 jit_solution(18289764475586561205)
XLA Ops:
  0.6 0.0 copy-start
  0.6 1.0 copy-done
  1.7 1.0 copy-done.2
  2.7 1.2 copy-done.4
  3.9 1.2 copy-done.5
  5.2 1.5 projections.1
  6.7 14.5 %all_to_all.50.tiles_ref = f32[8,32,256]{2,1,0:T(8,128)S(1)} all-to-all(f32[8,32,256]{2,1,0:T(8,128)S(1)} %projections.1), channel_id=1, replica_groups=mesh['tenant'=16,'row'=8] {'row'}, dimensions={0} | all-to-all | bytes 524288 | tf_op jit(solution)/shard_map/all_to_all | solution.py:229
  21.2 1.0 owner_coefficients.1
  22.2 3.4 %all-to-all-start.1 = ((f32[8,32,256]{2,1,0:T(8,128)}), f32[8,32,256]{2,1,0:T(8,128)S(1)}, u32[]{:S(2)}, u32[]{:S(2)}) async-start(f32[8,32,256]{2,1,0:T(8,128)} %owner_coefficients.1), calls=%async_computation.1 | async-start | bytes 524288 | tf_op jit(solution)/shard_map/all_to_all | solution.py:229
  25.6 0.0 copy-done.1
  25.7 0.1 collective-permute-start
  25.8 8.2 %all-to-all-done.1.mine_ref.pair_ref = f32[8,32,256]{2,1,0:T(8,128)S(1)} async-done(((f32[8,32,256]{2,1,0:T(8,128)}), f32[8,32,256]{2,1,0:T(8,128)S(1)}, u32[]{:S(2)}, u32[]{:S(2)}) %all-to-all-start.1) | async-done | bytes 262176 | tf_op jit(solution)/shard_map/all_to_all | solution.py:229
  34.0 0.0 collective-permute-start.1
  34.0 0.0 collective-permute-done.swap_ref
  34.0 1.5 collective-permute-done.1.other_ref.pair_other_ref
  35.5 0.4 load_sum.1
  35.9 15.8 %all_to_all.51.tiles_ref = f32[8,64,256]{2,1,0:T(8,128)S(1)} all-to-all(f32[8,64,256]{2,1,0:T(8,128)S(1)} %load_sum.1), channel_id=1, replica_groups={{0,16,32,48,64,80,96,112},{8,24,40,56,72,88,104,120},{1,17,33,49,65,81,..., dimensions={0} | all-to-all | bytes 1048576 | tf_op jit(solution)/shard_map/all_to_all | solution.py:229
  51.8 12.1 %all_to_all.52.basis_ref.mine_ref = f32[8,64,256]{2,1,0:T(8,128)S(1)} all-to-all(f32[8,64,256]{2,1,0:T(8,128)S(1)} %owner_sum.4), channel_id=1, replica_groups={{0,16,32,48,64,80,96,112},{8,24,40,56,72,88,104,120},{1,17,33,49,65,81,..., dimensions={0} | all-to-all | bytes 1048576 | tf_op jit(solution)/shard_map/all_to_all | solution.py:229
  63.9 0.6 gram_and_cores.2
  64.5 0.1 collective-permute-start.2
  64.6 1.5 collective-permute-done.2
  66.2 11.7 %all_to_all.53.tiles_ref = f32[8,32,256]{2,1,0:T(8,128)S(1)} all-to-all(f32[8,32,256]{2,1,0:T(8,128)S(1)} %add.21), channel_id=1, replica_groups=mesh['tenant'=16,'row'=8] {'row'}, dimensions={0} | all-to-all | bytes 524288 | tf_op jit(solution)/shard_map/all_to_all | solution.py:229
  77.8 0.7 owner_sum.5
  78.6 3.4 %all-to-all-start.5 = ((f32[8,32,256]{2,1,0:T(8,128)}), f32[8,32,256]{2,1,0:T(8,128)S(1)}, u32[]{:S(2)}, u32[]{:S(2)}) async-start(f32[8,32,256]{2,1,0:T(8,128)} %owner_sum.5), calls=%async_computation.5 | async-start | bytes 524288 | tf_op jit(solution)/shard_map/all_to_all | solution.py:229
  82.0 0.0 copy-done.3
  82.0 0.1 collective-permute-start.4
  82.1 8.2 %all-to-all-done.5.mine_ref = f32[8,32,256]{2,1,0:T(8,128)S(1)} async-done(((f32[8,32,256]{2,1,0:T(8,128)}), f32[8,32,256]{2,1,0:T(8,128)S(1)}, u32[]{:S(2)}, u32[]{:S(2)}) %all-to-all-start.5) | async-done | bytes 262176 | tf_op jit(solution)/shard_map/all_to_all | solution.py:229
  90.4 0.0 collective-permute-start.3
  90.4 0.0 collective-permute-done.4.swap_ref
  90.4 1.5 collective-permute-done.3.other_ref
  91.9 9.2 %turn_over.1 = (f32[256,256]{1,0:T(8,128)S(1)}, f32[8,16,256]{2,1,0:T(8,128)}, f32[8,64,256]{2,1,0:T(8,128)S(1)}) custom-call(s32[1]{0:T(128)} %bitcast.core_ref, f32[8,32,256]{2,1,0:T(8,128)S(1)} %all-to-all-done.5.mine_ref, f32[8,32,256]{2,1,0:T(8,128)S(1)} %collective-permute-done.3.other_ref, f32[8,32,256]{2,1,0:T(8,128)S(1)} %all-to-all-done.1.mine_ref.pair_ref, ...), custom_call_target="tpu_custom_call" | custom-call | tf_op jit(solution)/shard_map/turn_over/pallas_call | solution.py:121
  101.1 13.7 %all_to_all.54.tiles_ref = f32[8,64,256]{2,1,0:T(8,128)S(1)} all-to-all(f32[8,64,256]{2,1,0:T(8,128)S(1)} %get-tuple-element.16), channel_id=1, replica_groups={{0,16,32,48,64,80,96,112},{8,24,40,56,72,88,104,120},{1,17,33,49,65,81,..., dimensions={0} | all-to-all | bytes 1048576 | tf_op jit(solution)/shard_map/all_to_all | solution.py:229
  114.8 12.2 %all_to_all.55.basis_ref = f32[8,64,256]{2,1,0:T(8,128)S(1)} all-to-all(f32[8,64,256]{2,1,0:T(8,128)S(1)} %owner_sum.6), channel_id=1, replica_groups={{0,16,32,48,64,80,96,112},{8,24,40,56,72,88,104,120},{1,17,33,49,65,81,..., dimensions={0} | all-to-all | bytes 1048576 | tf_op jit(solution)/shard_map/all_to_all | solution.py:229
  127.1 0.6 gram_and_cores.3
  127.7 0.1 collective-permute-start.6
  127.8 1.5 collective-permute-done.6
  129.3 0.7 add.22
  130.1 3.4 %all-to-all-start.8 = ((f32[8,32,256]{2,1,0:T(8,128)}), f32[8,32,256]{2,1,0:T(8,128)S(1)}, u32[]{:S(2)}, u32[]{:S(2)}) async-start(f32[8,32,256]{2,1,0:T(8,128)} %add.22), calls=%async_computation.8 | async-start | bytes 524288 | tf_op jit(solution)/shard_map/all_to_all | solution.py:229
  133.5 0.2 collective-permute-start.5
  133.7 0.4 collective-permute-start.8
  134.1 8.4 %all-to-all-done.8.tiles_ref = f32[8,32,256]{2,1,0:T(8,128)S(1)} async-done(((f32[8,32,256]{2,1,0:T(8,128)}), f32[8,32,256]{2,1,0:T(8,128)S(1)}, u32[]{:S(2)}, u32[]{:S(2)}) %all-to-all-start.8) | async-done | bytes 262176 | tf_op jit(solution)/shard_map/all_to_all | solution.py:229
  142.4 11.3 %all_to_all.56.mine_ref = f32[8,32,256]{2,1,0:T(8,128)S(1)} all-to-all(f32[8,32,256]{2,1,0:T(8,128)S(1)} %owner_sum.7), channel_id=1, replica_groups=mesh['tenant'=16,'row'=8] {'row'}, dimensions={0} | all-to-all | bytes 524288 | tf_op jit(solution)/shard_map/all_to_all | solution.py:229
  153.7 0.0 collective-permute-start.7
  153.7 0.0 collective-permute-done.5.other_ref
  153.8 1.6 left_basis.1
  155.4 0.0 collective-permute-done.8.basis_other_ref
  155.4 0.0 collective-permute-done.7.other_ref
  155.4 9.5 %finish.1 = (f32[1024,256]{1,0:T(8,128)}, f32[8,16,256]{2,1,0:T(8,128)}) custom-call(s32[1]{0:T(128)} %bitcast.core_ref, f32[8,32,256]{2,1,0:T(8,128)S(1)} %all_to_all.56.mine_ref, f32[8,32,256]{2,1,0:T(8,128)S(1)} %collective-permute-done.7.other_ref, f32[8,64,256]{2,1,0:T(8,128)S(1)} %all_to_all.55.basis_ref, ...), custom_call_target="tpu_custom_call" | custom-call | tf_op jit(solution)/shard_map/finish/pallas_call | solution.py:121
  (11 shorter events, 0.2 us)
Async XLA Ops:
  0.6 1.0 copy-start
  1.7 1.0 copy-start.2
  2.7 1.2 copy-start.4
  3.9 1.2 copy-start.5
  21.2 4.4 %copy-start.1 = (f32[8,16,1024]{2,1,0:T(8,128)S(1)}, f32[8,16,1024]{2,1,0:T(8,128)}, u32[]{:S(2)}) copy-start(f32[8,16,1024]{2,1,0:T(8,128)} %param.4) | copy-start | bytes 1572868
  22.2 11.8 %all-to-all-start.1 = ((f32[8,32,256]{2,1,0:T(8,128)}), f32[8,32,256]{2,1,0:T(8,128)S(1)}, u32[]{:S(2)}, u32[]{:S(2)}) async-start(f32[8,32,256]{2,1,0:T(8,128)} %owner_coefficients.1), calls=%async_computation.1 | async-start | bytes 524288 | tf_op jit(solution)/shard_map/all_to_all | solution.py:229
  25.7 8.3 %collective-permute-start = (f32[128,512]{1,0:T(8,128)S(1)}, f32[128,512]{1,0:T(8,128)S(1)}, u32[]{:S(2)}, u32[]{:S(2)}) collective-permute-start(f32[128,512]{1,0:T(8,128)S(1)} %get-tuple-element.24), channel_id=1, source_target_pairs={{0,8},{8,0},{16,24},{24,16},{32,40},{40,32},{48,56},{56,48},{64,72... | collective-permute-start | bytes 786440 | tf_op jit(solution)/shard_map/ppermute | solution.py:239
  34.0 1.5 collective-permute-start.1
  64.5 1.6 collective-permute-start.2
  77.8 4.2 %copy-start.3 = (f32[8,16,1024]{2,1,0:T(8,128)S(1)}, f32[8,16,1024]{2,1,0:T(8,128)}, u32[]{:S(2)}) copy-start(f32[8,16,1024]{2,1,0:T(8,128)} %param.5) | copy-start | bytes 1572868
  78.6 11.8 %all-to-all-start.5 = ((f32[8,32,256]{2,1,0:T(8,128)}), f32[8,32,256]{2,1,0:T(8,128)S(1)}, u32[]{:S(2)}, u32[]{:S(2)}) async-start(f32[8,32,256]{2,1,0:T(8,128)} %owner_sum.5), calls=%async_computation.5 | async-start | bytes 524288 | tf_op jit(solution)/shard_map/all_to_all | solution.py:229
  82.0 8.3 %collective-permute-start.4 = (f32[128,512]{1,0:T(8,128)S(1)}, f32[128,512]{1,0:T(8,128)S(1)}, u32[]{:S(2)}, u32[]{:S(2)}) collective-permute-start(f32[128,512]{1,0:T(8,128)S(1)} %get-tuple-element.22), channel_id=1, source_target_pairs={{0,8},{8,0},{16,24},{24,16},{32,40},{40,32},{48,56},{56,48},{64,72... | collective-permute-start | bytes 786440 | tf_op jit(solution)/shard_map/ppermute | solution.py:239
  90.4 1.5 collective-permute-start.3
  127.7 1.6 collective-permute-start.6
  130.1 12.4 %all-to-all-start.8 = ((f32[8,32,256]{2,1,0:T(8,128)}), f32[8,32,256]{2,1,0:T(8,128)S(1)}, u32[]{:S(2)}, u32[]{:S(2)}) async-start(f32[8,32,256]{2,1,0:T(8,128)} %add.22), calls=%async_computation.8 | async-start | bytes 524288 | tf_op jit(solution)/shard_map/all_to_all | solution.py:229
  133.5 20.3 %collective-permute-start.5 = (f32[8,64,256]{2,1,0:T(8,128)S(1)}, f32[8,64,256]{2,1,0:T(8,128)S(1)}, u32[]{:S(2)}, u32[]{:S(2)}) collective-permute-start(f32[8,64,256]{2,1,0:T(8,128)S(1)} %all_to_all.52.basis_ref.mine_ref), channel_id=1, source_target_pairs={{0,8},{8,0},{16,24},{24,16},{32,40},{40,32},{48,56},{56,48},{64,72... | collective-permute-start | bytes 1572872 | tf_op jit(solution)/shard_map/ppermute | solution.py:239
  133.7 21.7 %collective-permute-start.8 = (f32[8,64,256]{2,1,0:T(8,128)S(1)}, f32[8,64,256]{2,1,0:T(8,128)S(1)}, u32[]{:S(2)}, u32[]{:S(2)}) collective-permute-start(f32[8,64,256]{2,1,0:T(8,128)S(1)} %all_to_all.55.basis_ref), channel_id=1, source_target_pairs={{0,8},{8,0},{16,24},{24,16},{32,40},{40,32},{48,56},{56,48},{64,72... | collective-permute-start | bytes 1572872 | tf_op jit(solution)/shard_map/ppermute | solution.py:239
  153.7 1.6 %collective-permute-start.7 = (f32[8,32,256]{2,1,0:T(8,128)S(1)}, f32[8,32,256]{2,1,0:T(8,128)S(1)}, u32[]{:S(2)}, u32[]{:S(2)}) collective-permute-start(f32[8,32,256]{2,1,0:T(8,128)S(1)} %all_to_all.56.mine_ref), channel_id=1, source_target_pairs={{0,8},{8,0},{16,24},{24,16},{32,40},{40,32},{48,56},{56,48},{64,72... | collective-permute-start | bytes 786440 | tf_op jit(solution)/shard_map/ppermute | solution.py:239

commit v3 on v2

--- a/solution.py
+++ b/solution.py
@@ -245,7 +245,7 @@
     return total(load, "tenant", groups)
 
 
-def gram_total(core, halves, basis, rank):
+def gram_total(core, halves, basis, rank, beside=()):
     count = lax.axis_size("row")
     tiles = (count, 2 * RANK, rank)
     mine, other = call(
@@ -257,7 +257,8 @@
         in_specs=with_core(3),
         scratch_shapes=[pltpu.VMEM((rank, rank), jnp.float32)],
     )
-    return total(mine + from_sibling(other), "row")
+    other, beside = lax.optimization_barrier((from_sibling(other), beside))
+    return total(mine + other, "row"), beside
 
 
 def column_halves(factors, core):
@@ -286,10 +287,7 @@
     partial = call(
         projections,
         [tiles],
-        b,
-        a,
-        u_start,
-        v_start,
+        *(pltpu.with_memory_space_constraint(x, pltpu.HBM) for x in (b, a, u_start, v_start)),
         grid=(4,),
         in_specs=[factor_block, factor_block, basis_block, basis_block],
         out_specs=pl.BlockSpec(tiles, lambda i: (0, 0, 0)),
@@ -302,7 +300,7 @@
     load = call(load_sum, [load_shape], *b_halves, pair, pair_other)
     basis = tenant_total(load)
     basis_other = from_sibling(basis)
-    mine = gram_total(flag, b_halves, basis, rank)
+    mine, _ = gram_total(flag, b_halves, basis, rank)
     inverse, left, load = call(
         turn_over,
         [(rank, rank), shape, load_shape],
@@ -315,11 +313,20 @@
         in_specs=with_core(6),
     )
     u_scaled = call(
-        left_basis, [(width, rank)], flag, inverse, basis, basis_other, in_specs=with_core(3)
+        left_basis,
+        [(width, rank)],
+        flag,
+        inverse,
+        basis,
+        basis_other,
+        in_specs=with_core(3),
+        cost_estimate=pl.CostEstimate(
+            flops=6 * width * rank * rank, bytes_accessed=8 * width * rank, transcendentals=0
+        ),
     )
     basis = tenant_total(load)
     basis_other = from_sibling(basis)
-    mine = gram_total(flag, a_halves, basis, rank)
+    mine, u_scaled = gram_total(flag, a_halves, basis, rank, u_scaled)
     v_scaled, right = call(
         finish,
         [(width, rank), shape],

time: 168 us -> 167 us (level)
  blocking collectives: 91.3 us -> 79.5 us
  waiting for transfers between devices: 30.9 us -> 39.6 us
  starting transfers between devices: 11.2 us -> 15.9 us
  local copies, waits for them, and re-layouts: 4.62 us -> 0.09 us
  Pallas kernels: 25.3 us -> 28 us
    all_to_all x7 -> x6, blocking collectives: 91.3 us -> 79.5 us  [exchanged(): lax.all_to_all(tiles, axis, 0, 0, axis_index_groups=groups, tiled=True)]
    all_to_all x3 -> x4, waiting for transfers between devices: 24.8 us -> 33.4 us  [exchanged(): lax.all_to_all(tiles, axis, 0, 0, axis_index_groups=groups, tiled=True)]
    all_to_all x3 -> x4, starting transfers between devices: 10.2 us -> 14.8 us  [exchanged(): lax.all_to_all(tiles, axis, 0, 0, axis_index_groups=groups, tiled=True)]
    unnamed x12 -> x4, local copies, waits for them, and re-layouts: 4.53 us -> 0.01 us
    pallas_call x12, Pallas kernels: 25.3 us -> 28 us  [call(): pl.pallas_call(kernel, out_shape=shapes if len(shapes) > 1 else shapes[0]...]
  transfers between devices with their start and end apart: 12 -> 13, of which waited for: 7 -> 8; matrix products, arithmetic and copies ran while one was open for 0% -> 0% of each run, Pallas kernels for 1% -> 1%
where the time goes in v3:
time: 167 us; the launch traced here: 165 us
  blocking collectives  79.5 us (48%)
  waiting for transfers between devices  39.6 us (24%)
  Pallas kernels  28 us (17%)
  starting transfers between devices  15.9 us (10%)
    all_to_all x6, blocking collectives, exchanged(): lax.all_to_all(tiles, axis, 0, 0, axis_index_groups=groups, tiled=True)  79.5 us
    all_to_all x4, waiting for transfers between devices, exchanged(): lax.all_to_all(tiles, axis, 0, 0, axis_index_groups=groups, tiled=True)  33.4 us
    pallas_call x12, Pallas kernels, call(): pl.pallas_call(kernel, out_shape=shapes if len(shapes) > 1 else shapes[0]...  28 us
    all_to_all x4, starting transfers between devices, exchanged(): lax.all_to_all(tiles, axis, 0, 0, axis_index_groups=groups, tiled=True)  14.8 us
    ppermute x9, waiting for transfers between devices, from_sibling(): return lax.ppermute(x, 'tenant', [(i, i ^ 1) for i in range(count)])  6.12 us
  transfers between devices with their start and end apart: 13, of which 8 were waited for; matrix products, arithmetic and copies ran while one was open for 0% of the time, Pallas kernels for 1%

profile of v3, /device:TPU:8, one launch (start us, length us, event | category | flops | bytes accessed | tf_op | source)
XLA Modules:
  0.0 164.6 jit_solution(14694847491340850638)
XLA Ops:
  0.6 3.4 %projections.1 = f32[8,32,256]{2,1,0:T(8,128)S(1)} custom-call(f32[128,1024]{1,0:T(8,128)} %bitcast.3, f32[128,1024]{1,0:T(8,128)} %bitcast.5, f32[1024,256]{1,0:T(8,128)} %u_ref.1, f32[1024,256]{1,0:T(8,128)} %v_ref.1), custom_call_target="tpu_custom_call" | custom-call | tf_op jit(solution)/shard_map/projections/pallas_call | solution.py:121
  4.0 14.6 %all_to_all.50.tiles_ref = f32[8,32,256]{2,1,0:T(8,128)S(1)} all-to-all(f32[8,32,256]{2,1,0:T(8,128)S(1)} %projections.1), channel_id=1, replica_groups=mesh['tenant'=16,'row'=8] {'row'}, dimensions={0} | all-to-all | bytes 524288 | tf_op jit(solution)/shard_map/all_to_all | solution.py:229
  18.6 0.0 copy-start
  18.6 1.0 owner_coefficients.1
  19.5 3.4 %all-to-all-start.1 = ((f32[8,32,256]{2,1,0:T(8,128)}), f32[8,32,256]{2,1,0:T(8,128)S(1)}, u32[]{:S(2)}, u32[]{:S(2)}) async-start(f32[8,32,256]{2,1,0:T(8,128)} %owner_coefficients.1), calls=%async_computation.1 | async-start | bytes 524288 | tf_op jit(solution)/shard_map/all_to_all | solution.py:229
  23.0 0.0 copy-done
  23.0 0.1 collective-permute-start.1
  23.1 8.2 %all-to-all-done.1.mine_ref.pair_ref = f32[8,32,256]{2,1,0:T(8,128)S(1)} async-done(((f32[8,32,256]{2,1,0:T(8,128)}), f32[8,32,256]{2,1,0:T(8,128)S(1)}, u32[]{:S(2)}, u32[]{:S(2)}) %all-to-all-start.1) | async-done | bytes 262176 | tf_op jit(solution)/shard_map/all_to_all | solution.py:229
  31.3 0.0 collective-permute-start.2
  31.3 0.0 collective-permute-done.1.swap_ref
  31.3 1.5 collective-permute-done.2.other_ref.pair_other_ref
  32.9 0.4 load_sum.1
  33.3 15.8 %all_to_all.51.tiles_ref = f32[8,64,256]{2,1,0:T(8,128)S(1)} all-to-all(f32[8,64,256]{2,1,0:T(8,128)S(1)} %load_sum.1), channel_id=1, replica_groups={{0,16,32,48,64,80,96,112},{8,24,40,56,72,88,104,120},{1,17,33,49,65,81,..., dimensions={0} | all-to-all | bytes 1048576 | tf_op jit(solution)/shard_map/all_to_all | solution.py:229
  49.1 12.1 %all_to_all.52.basis_ref.mine_ref = f32[8,64,256]{2,1,0:T(8,128)S(1)} all-to-all(f32[8,64,256]{2,1,0:T(8,128)S(1)} %owner_sum.4), channel_id=1, replica_groups={{0,16,32,48,64,80,96,112},{8,24,40,56,72,88,104,120},{1,17,33,49,65,81,..., dimensions={0} | all-to-all | bytes 1048576 | tf_op jit(solution)/shard_map/all_to_all | solution.py:229
  61.2 0.6 gram_and_cores.2
  61.9 0.1 collective-permute-start.3
  62.0 1.5 collective-permute-done.3
  63.5 11.6 %all_to_all.53.tiles_ref = f32[8,32,256]{2,1,0:T(8,128)S(1)} all-to-all(f32[8,32,256]{2,1,0:T(8,128)S(1)} %add.21), channel_id=1, replica_groups=mesh['tenant'=16,'row'=8] {'row'}, dimensions={0} | all-to-all | bytes 524288 | tf_op jit(solution)/shard_map/all_to_all | solution.py:229
  75.2 0.0 copy-start.1
  75.2 0.7 owner_sum.5
  75.9 3.4 %all-to-all-start.5 = ((f32[8,32,256]{2,1,0:T(8,128)}), f32[8,32,256]{2,1,0:T(8,128)S(1)}, u32[]{:S(2)}, u32[]{:S(2)}) async-start(f32[8,32,256]{2,1,0:T(8,128)} %owner_sum.5), calls=%async_computation.5 | async-start | bytes 524288 | tf_op jit(solution)/shard_map/all_to_all | solution.py:229
  79.3 0.0 copy-done.1
  79.4 0.1 collective-permute-start
  79.5 8.2 %all-to-all-done.5.mine_ref = f32[8,32,256]{2,1,0:T(8,128)S(1)} async-done(((f32[8,32,256]{2,1,0:T(8,128)}), f32[8,32,256]{2,1,0:T(8,128)S(1)}, u32[]{:S(2)}, u32[]{:S(2)}) %all-to-all-start.5) | async-done | bytes 262176 | tf_op jit(solution)/shard_map/all_to_all | solution.py:229
  87.7 0.0 collective-permute-start.4
  87.7 0.0 collective-permute-done.swap_ref
  87.7 1.5 collective-permute-done.4.other_ref
  89.2 9.2 %turn_over.1 = (f32[256,256]{1,0:T(8,128)S(1)}, f32[8,16,256]{2,1,0:T(8,128)}, f32[8,64,256]{2,1,0:T(8,128)S(1)}) custom-call(s32[1]{0:T(128)} %bitcast.core_ref, f32[8,32,256]{2,1,0:T(8,128)S(1)} %all-to-all-done.5.mine_ref, f32[8,32,256]{2,1,0:T(8,128)S(1)} %collective-permute-done.4.other_ref, f32[8,32,256]{2,1,0:T(8,128)S(1)} %all-to-all-done.1.mine_ref.pair_ref, ...), custom_call_target="tpu_custom_call" | custom-call | tf_op jit(solution)/shard_map/turn_over/pallas_call | solution.py:121
  98.4 13.7 %all_to_all.54.tiles_ref = f32[8,64,256]{2,1,0:T(8,128)S(1)} all-to-all(f32[8,64,256]{2,1,0:T(8,128)S(1)} %get-tuple-element.17), channel_id=1, replica_groups={{0,16,32,48,64,80,96,112},{8,24,40,56,72,88,104,120},{1,17,33,49,65,81,..., dimensions={0} | all-to-all | bytes 1048576 | tf_op jit(solution)/shard_map/all_to_all | solution.py:229
  112.1 0.8 owner_sum.6
  113.0 4.6 %all-to-all-start.7 = ((f32[8,64,256]{2,1,0:T(8,128)}), f32[8,64,256]{2,1,0:T(8,128)S(1)}, u32[]{:S(2)}, u32[]{:S(2)}) async-start(f32[8,64,256]{2,1,0:T(8,128)} %owner_sum.6), calls=%async_computation.7 | async-start | bytes 1048576 | tf_op jit(solution)/shard_map/all_to_all | solution.py:229
  117.5 0.0 collective-permute-start.6
  117.5 8.7 %all-to-all-done.7.basis_ref = f32[8,64,256]{2,1,0:T(8,128)S(1)} async-done(((f32[8,64,256]{2,1,0:T(8,128)}), f32[8,64,256]{2,1,0:T(8,128)S(1)}, u32[]{:S(2)}, u32[]{:S(2)}) %all-to-all-start.7) | async-done | bytes 524320 | tf_op jit(solution)/shard_map/all_to_all | solution.py:229
  126.2 0.6 gram_and_cores.3
  126.9 0.1 collective-permute-start.5
  127.0 0.0 collective-permute-done.6.other_ref
  127.0 1.6 left_basis.1
  128.6 0.0 collective-permute-done.5
  128.6 0.7 add.22
  129.3 3.4 %all-to-all-start.8 = ((f32[8,32,256]{2,1,0:T(8,128)}), f32[8,32,256]{2,1,0:T(8,128)S(1)}, u32[]{:S(2)}, u32[]{:S(2)}) async-start(f32[8,32,256]{2,1,0:T(8,128)} %add.22), calls=%async_computation.8 | async-start | bytes 524288 | tf_op jit(solution)/shard_map/all_to_all | solution.py:229
  132.8 0.8 collective-permute-start.8
  133.5 8.3 %all-to-all-done.8.tiles_ref = f32[8,32,256]{2,1,0:T(8,128)S(1)} async-done(((f32[8,32,256]{2,1,0:T(8,128)}), f32[8,32,256]{2,1,0:T(8,128)S(1)}, u32[]{:S(2)}, u32[]{:S(2)}) %all-to-all-start.8) | async-done | bytes 262176 | tf_op jit(solution)/shard_map/all_to_all | solution.py:229
  141.9 11.7 %all_to_all.55.mine_ref = f32[8,32,256]{2,1,0:T(8,128)S(1)} all-to-all(f32[8,32,256]{2,1,0:T(8,128)S(1)} %owner_sum.7), channel_id=1, replica_groups=mesh['tenant'=16,'row'=8] {'row'}, dimensions={0} | all-to-all | bytes 524288 | tf_op jit(solution)/shard_map/all_to_all | solution.py:229
  153.5 0.0 collective-permute-start.7
  153.5 0.0 collective-permute-done.8.basis_other_ref
  153.6 1.5 collective-permute-done.7.other_ref
  155.1 9.5 %finish.1 = (f32[1024,256]{1,0:T(8,128)}, f32[8,16,256]{2,1,0:T(8,128)}) custom-call(s32[1]{0:T(128)} %bitcast.core_ref, f32[8,32,256]{2,1,0:T(8,128)S(1)} %all_to_all.55.mine_ref, f32[8,32,256]{2,1,0:T(8,128)S(1)} %collective-permute-done.7.other_ref, f32[8,64,256]{2,1,0:T(8,128)S(1)} %all-to-all-done.7.basis_ref, ...), custom_call_target="tpu_custom_call" | custom-call | tf_op jit(solution)/shard_map/finish/pallas_call | solution.py:121
  (5 shorter events, 0.2 us)
Async XLA Ops:
  18.6 4.4 %copy-start = (f32[8,16,1024]{2,1,0:T(8,128)S(1)}, f32[8,16,1024]{2,1,0:T(8,128)}, u32[]{:S(2)}) copy-start(f32[8,16,1024]{2,1,0:T(8,128)} %param.4) | copy-start | bytes 1572868
  19.5 11.8 %all-to-all-start.1 = ((f32[8,32,256]{2,1,0:T(8,128)}), f32[8,32,256]{2,1,0:T(8,128)S(1)}, u32[]{:S(2)}, u32[]{:S(2)}) async-start(f32[8,32,256]{2,1,0:T(8,128)} %owner_coefficients.1), calls=%async_computation.1 | async-start | bytes 524288 | tf_op jit(solution)/shard_map/all_to_all | solution.py:229
  23.0 8.3 %collective-permute-start.1 = (f32[128,512]{1,0:T(8,128)S(1)}, f32[128,512]{1,0:T(8,128)S(1)}, u32[]{:S(2)}, u32[]{:S(2)}) collective-permute-start(f32[128,512]{1,0:T(8,128)S(1)} %get-tuple-element.26), channel_id=1, source_target_pairs={{0,8},{8,0},{16,24},{24,16},{32,40},{40,32},{48,56},{56,48},{64,72... | collective-permute-start | bytes 786440 | tf_op jit(solution)/shard_map/ppermute | solution.py:239
  31.3 1.5 collective-permute-start.2
  61.9 1.6 collective-permute-start.3
  75.2 4.2 %copy-start.1 = (f32[8,16,1024]{2,1,0:T(8,128)S(1)}, f32[8,16,1024]{2,1,0:T(8,128)}, u32[]{:S(2)}) copy-start(f32[8,16,1024]{2,1,0:T(8,128)} %param.5) | copy-start | bytes 1572868
  75.9 11.8 %all-to-all-start.5 = ((f32[8,32,256]{2,1,0:T(8,128)}), f32[8,32,256]{2,1,0:T(8,128)S(1)}, u32[]{:S(2)}, u32[]{:S(2)}) async-start(f32[8,32,256]{2,1,0:T(8,128)} %owner_sum.5), calls=%async_computation.5 | async-start | bytes 524288 | tf_op jit(solution)/shard_map/all_to_all | solution.py:229
  79.4 8.3 %collective-permute-start = (f32[128,512]{1,0:T(8,128)S(1)}, f32[128,512]{1,0:T(8,128)S(1)}, u32[]{:S(2)}, u32[]{:S(2)}) collective-permute-start(f32[128,512]{1,0:T(8,128)S(1)} %get-tuple-element.28), channel_id=1, source_target_pairs={{0,8},{8,0},{16,24},{24,16},{32,40},{40,32},{48,56},{56,48},{64,72... | collective-permute-start | bytes 786440 | tf_op jit(solution)/shard_map/ppermute | solution.py:239
  87.7 1.5 collective-permute-start.4
  113.0 13.3 %all-to-all-start.7 = ((f32[8,64,256]{2,1,0:T(8,128)}), f32[8,64,256]{2,1,0:T(8,128)S(1)}, u32[]{:S(2)}, u32[]{:S(2)}) async-start(f32[8,64,256]{2,1,0:T(8,128)} %owner_sum.6), calls=%async_computation.7 | async-start | bytes 1048576 | tf_op jit(solution)/shard_map/all_to_all | solution.py:229
  117.5 9.4 %collective-permute-start.6 = (f32[8,64,256]{2,1,0:T(8,128)S(1)}, f32[8,64,256]{2,1,0:T(8,128)S(1)}, u32[]{:S(2)}, u32[]{:S(2)}) collective-permute-start(f32[8,64,256]{2,1,0:T(8,128)S(1)} %all_to_all.52.basis_ref.mine_ref), channel_id=1, source_target_pairs={{0,8},{8,0},{16,24},{24,16},{32,40},{40,32},{48,56},{56,48},{64,72... | collective-permute-start | bytes 1572872 | tf_op jit(solution)/shard_map/ppermute | solution.py:239
  126.9 1.7 %collective-permute-start.5 = (f32[8,32,256]{2,1,0:T(8,128)S(1)}, f32[8,32,256]{2,1,0:T(8,128)S(1)}, u32[]{:S(2)}, u32[]{:S(2)}) collective-permute-start(f32[8,32,256]{2,1,0:T(8,128)S(1)} %get-tuple-element.18), channel_id=1, source_target_pairs={{0,8},{8,0},{16,24},{24,16},{32,40},{40,32},{48,56},{56,48},{64,72... | collective-permute-start | bytes 786440 | tf_op jit(solution)/shard_map/ppermute | solution.py:239
  129.3 12.5 %all-to-all-start.8 = ((f32[8,32,256]{2,1,0:T(8,128)}), f32[8,32,256]{2,1,0:T(8,128)S(1)}, u32[]{:S(2)}, u32[]{:S(2)}) async-start(f32[8,32,256]{2,1,0:T(8,128)} %add.22), calls=%async_computation.8 | async-start | bytes 524288 | tf_op jit(solution)/shard_map/all_to_all | solution.py:229
  132.8 20.8 %collective-permute-start.8 = (f32[8,64,256]{2,1,0:T(8,128)S(1)}, f32[8,64,256]{2,1,0:T(8,128)S(1)}, u32[]{:S(2)}, u32[]{:S(2)}) collective-permute-start(f32[8,64,256]{2,1,0:T(8,128)S(1)} %all-to-all-done.7.basis_ref), channel_id=1, source_target_pairs={{0,8},{8,0},{16,24},{24,16},{32,40},{40,32},{48,56},{56,48},{64,72... | collective-permute-start | bytes 1572872 | tf_op jit(solution)/shard_map/ppermute | solution.py:239
  153.5 1.5 collective-permute-start.7

commit v4 on v3

--- a/solution.py
+++ b/solution.py
@@ -12,6 +12,7 @@
 LANES = 128
 SUBLANES = 8
 PANEL = 32
+STEPS = 4
 
 
 def pieces(x):
@@ -29,45 +30,63 @@
     return lax.dot_general(xs, ys, (((0,), (0,)), ((), ())), preferred_element_type=jnp.float32)
 
 
-def wide(x, width):
-    return jnp.concatenate([x] * (width // LANES), axis=1)
-
-
-def eliminate(rows, units, start):
-    width = rows[0].shape[1]
-    tile = (SUBLANES, LANES)
-    for m, first in enumerate(range(start, start + PANEL, SUBLANES)):
-        r = [jnp.broadcast_to(rows[m][i : i + 1], rows[m].shape) for i in range(SUBLANES)]
-        e = [jnp.broadcast_to(units[m][i : i + 1], tile) for i in range(SUBLANES)]
+def column(x, lane):
+    return jnp.broadcast_to(x[:, lane : lane + 1], (SUBLANES, LANES))
+
+
+def spread(ref, row):
+    return ref[pl.ds(row, SUBLANES, stride=0), :]
+
+
+def eliminate(rows, units, start, rows_ref, columns_ref, factors_ref):
+    sub = lax.broadcasted_iota(jnp.int32, (SUBLANES, LANES), 0)
+    tile = start // LANES
+    for m, first in enumerate(range(start % LANES, start % LANES + PANEL, SUBLANES)):
+        slot = m % 4
+        tiles = [*rows[m], units[m]]
+        if m == 0:
+            pivots = [column(rows[m][tile], first + j) for j in range(SUBLANES)]
+        for j in range(SUBLANES):
+            columns_ref[slot, pl.ds(j * SUBLANES, SUBLANES), :] = pivots[j]
+        for t, x in enumerate(tiles):
+            rows_ref[slot, pl.ds(t * SUBLANES, SUBLANES), :] = x
+        r = [
+            [spread(rows_ref.at[slot], t * SUBLANES + i) for t in range(len(tiles))]
+            for i in range(SUBLANES)
+        ]
+        d = [
+            [spread(columns_ref.at[slot], j * SUBLANES + i) for j in range(SUBLANES)]
+            for i in range(SUBLANES)
+        ]
         later = range(m + 1, len(rows))
-
-        def column(x, j):
-            return jnp.broadcast_to(x[:, first + j : first + j + 1], tile)
-
-        d = [[column(r[i], j) for j in range(SUBLANES)] for i in range(SUBLANES)]
-        c = {g: [column(rows[g], j) for j in range(SUBLANES)] for g in later}
-        sub = lax.broadcasted_iota(jnp.int32, rows[m].shape, 0)
-        sub_tile = lax.broadcasted_iota(jnp.int32, tile, 0)
-        done, done_unit = jnp.zeros_like(rows[m]), jnp.zeros_like(units[m])
+        c = {g: [column(rows[g][tile], first + j) for j in range(SUBLANES)] for g in later}
+        if later:
+            ahead = first + SUBLANES
+            pivots = [column(rows[m + 1][tile], ahead + j) for j in range(SUBLANES)]
+        done = tiles
         for j in range(SUBLANES):
             inverse = lax.rsqrt(d[j][j])
-            p, q = r[j] * wide(inverse, width), e[j] * inverse
-            done = jnp.where(sub == j, p, done)
-            done_unit = jnp.where(sub_tile == j, q, done_unit)
+            p = [x * inverse for x in r[j]]
+            done = [jnp.where(sub == j, x, y) for x, y in zip(p, done)]
             below = range(j + 1, SUBLANES)
             factor = {i: d[j][i] * inverse for i in below}
             for i in below:
                 for other in range(i, SUBLANES):
                     d[i][other] -= factor[i] * factor[other]
-                r[i] -= wide(factor[i], width) * p
-                e[i] -= factor[i] * q
+                r[i] = [x - factor[i] * y for x, y in zip(r[i], p)]
             for g in later:
                 scale = c[g][j] * inverse
+                if g == m + 1:
+                    place = pl.ds(j * SUBLANES, SUBLANES)
+                    factors_ref[slot, place, :] = scale
+                    for k in range(SUBLANES):
+                        pivots[k] -= scale * spread(factors_ref.at[slot], j * SUBLANES + k)
                 for i in below:
                     c[g][i] -= scale * factor[i]
-                rows[g] -= wide(scale, width) * p
-                units[g] -= scale * q
-        rows[m], units[m] = done, done_unit
+                rows[g] = [x - scale * y for x, y in zip(rows[g], p)]
+                units[g] -= scale * p[-1]
+        rows[m], units[m] = done[:-1], done[-1]
+    rows = [jnp.concatenate(tiles, axis=1) for tiles in rows]
     return jnp.concatenate(rows), jnp.concatenate(units)
 
 
@@ -91,7 +110,7 @@
     return x.reshape(-1, x.shape[-1])
 
 
-def factor_in_place(out_ref):
+def factor_in_place(out_ref, *scratch):
     n = out_ref.shape[0]
     sub = lax.broadcasted_iota(jnp.int32, (SUBLANES, LANES), 0)
     lane = lax.broadcasted_iota(jnp.int32, (SUBLANES, LANES), 1)
@@ -101,9 +120,10 @@
         tile = start // LANES
         rows, units = [], []
         for g in range(0, PANEL, SUBLANES):
-            rows.append(out_ref[pl.ds(start + g, SUBLANES), :])
+            place = pl.ds(start + g, SUBLANES)
+            rows.append([out_ref[place, pl.ds(t, LANES)] for t in range(0, n, LANES)])
             units.append(jnp.where(lane == sub + (start % LANES + g), 1.0, 0.0))
-        rows, units = eliminate(rows, units, start)
+        rows, units = eliminate(rows, units, start, *scratch)
         blank = jnp.zeros_like(units)
         units = jnp.concatenate([units if t == tile else blank for t in range(n // LANES)], axis=1)
         inside = (column >= start) & (column < end)
@@ -116,6 +136,15 @@
             out_ref[pl.ds(end, n - end), :] = jnp.where(inside[end:], 0.0, rest) - update
 
 
+def factor_scratch(n):
+    tiles = n // LANES + 1
+    return [
+        pltpu.VMEM((4, tiles * SUBLANES, LANES), jnp.float32),
+        pltpu.VMEM((4, SUBLANES * SUBLANES, LANES), jnp.float32),
+        pltpu.VMEM((4, SUBLANES * SUBLANES, LANES), jnp.float32),
+    ]
+
+
 def call(kernel, shapes, *operands, **options):
     shapes = [jax.ShapeDtypeStruct(shape, jnp.float32) for shape in shapes]
     return pl.pallas_call(
@@ -127,20 +156,32 @@
     )(*operands)
 
 
-def projections(b_ref, a_ref, u_ref, v_ref, out_ref):
-    left = product(b_ref[...], u_ref[...]).reshape(-1, RANK, out_ref.shape[2])
-    right = product(a_ref[...], v_ref[...]).reshape(left.shape)
-    first = pl.program_id(0) == 0
-
-    @pl.when(first)
-    def _():
-        out_ref[:, :RANK] = left
-        out_ref[:, RANK:] = right
-
-    @pl.when(jnp.logical_not(first))
-    def _():
-        out_ref[:, :RANK] += left
-        out_ref[:, RANK:] += right
+def projections(b_hbm, a_hbm, u_hbm, v_hbm, out_ref, b_ref, a_ref, u_ref, v_ref, sems):
+    step = b_ref.shape[1] // STEPS
+    copies = []
+    for i in range(STEPS):
+        part = pl.ds(i * step, step)
+        pairs = (
+            (u_hbm.at[part], u_ref.at[part]),
+            (b_hbm.at[:, part], b_ref.at[:, part]),
+            (v_hbm.at[part], v_ref.at[part]),
+            (a_hbm.at[:, part], a_ref.at[:, part]),
+        )
+        copies.append([pltpu.make_async_copy(*p, sems.at[i, k]) for k, p in enumerate(pairs)])
+    for group in copies:
+        for copy in group:
+            copy.start()
+    left = right = 0.0
+    for i, group in enumerate(copies):
+        part = pl.ds(i * step, step)
+        group[0].wait()
+        group[1].wait()
+        left += product(b_ref[:, part], u_ref[part])
+        group[2].wait()
+        group[3].wait()
+        right += product(a_ref[:, part], v_ref[part])
+    out_ref[:, :RANK] = left.reshape(-1, RANK, left.shape[1])
+    out_ref[:, RANK:] = right.reshape(-1, RANK, right.shape[1])
 
 
 def owner_coefficients(tiles_ref, out_ref):
@@ -184,18 +225,18 @@
     other_ref[:, RANK:] = gram_ref[pl.ds((1 - core) * half, half), :].reshape(count, RANK, -1)
 
 
-def inverse_factor(core, mine_ref, other_ref, inverse_ref):
+def inverse_factor(core, mine_ref, other_ref, inverse_ref, *scratch):
     half = len(inverse_ref) // 2
     inverse_ref[pl.ds(core * half, half), :] = matrix(mine_ref[:, RANK:])
     inverse_ref[pl.ds((1 - core) * half, half), :] = matrix(other_ref[:, RANK:])
-    factor_in_place(inverse_ref)
+    factor_in_place(inverse_ref, *scratch)
 
 
 def turn_over(
     core_ref, mine_ref, other_ref, pair_ref, pair_other_ref, keep_ref, swap_ref,
-    inverse_ref, left_ref, load_ref,
+    inverse_ref, left_ref, load_ref, *scratch,
 ):
-    inverse_factor(core_ref[0], mine_ref, other_ref, inverse_ref)
+    inverse_factor(core_ref[0], mine_ref, other_ref, inverse_ref, *scratch)
     left = product(both_upper(mine_ref, other_ref), inverse_ref[...], 1, 1)
     left_ref[...] = left[: len(left) // 2].reshape(left_ref.shape)
     weight = product(left, left, 1, 1)
@@ -217,8 +258,11 @@
     scaled_basis(core_ref[0], inverse_ref[...], mine_ref, other_ref, out_ref)
 
 
-def finish(core_ref, mine_ref, other_ref, basis_ref, basis_other_ref, out_ref, right_ref, inverse_ref):
-    inverse_factor(core_ref[0], mine_ref, other_ref, inverse_ref)
+def finish(
+    core_ref, mine_ref, other_ref, basis_ref, basis_other_ref,
+    out_ref, right_ref, inverse_ref, *scratch,
+):
+    inverse_factor(core_ref[0], mine_ref, other_ref, inverse_ref, *scratch)
     inverse = inverse_ref[...]
     right = product(matrix(mine_ref[:, :RANK]), inverse, 1, 1)
     right_ref[...] = right.reshape(right_ref.shape)
@@ -280,17 +324,18 @@
     a = a_factors.reshape(-1, width)
     b_halves, a_halves = column_halves(b, core), column_halves(a, core)
 
-    step = width // 4
-    factor_block = pl.BlockSpec((len(b), step), lambda i: (0, i))
-    basis_block = pl.BlockSpec((step, rank), lambda i: (i, 0))
-    tiles = (shape[0], 2 * RANK, rank)
     partial = call(
         projections,
-        [tiles],
-        *(pltpu.with_memory_space_constraint(x, pltpu.HBM) for x in (b, a, u_start, v_start)),
-        grid=(4,),
-        in_specs=[factor_block, factor_block, basis_block, basis_block],
-        out_specs=pl.BlockSpec(tiles, lambda i: (0, 0, 0)),
+        [(shape[0], 2 * RANK, rank)],
+        b,
+        a,
+        u_start,
+        v_start,
+        in_specs=[pl.BlockSpec(memory_space=pltpu.HBM)] * 4,
+        scratch_shapes=[
+            *(pltpu.VMEM(x.shape, x.dtype) for x in (b, a, u_start, v_start)),
+            pltpu.SemaphoreType.DMA((STEPS, 4)),
+        ],
     )
     pair = total(partial, "row", None, owner_coefficients)
     pair_other = from_sibling(pair)
@@ -311,6 +356,7 @@
         pair_other,
         *a_halves,
         in_specs=with_core(6),
+        scratch_shapes=factor_scratch(rank),
     )
     u_scaled = call(
         left_basis,
@@ -336,7 +382,7 @@
         basis,
         basis_other,
         in_specs=with_core(4),
-        scratch_shapes=[pltpu.VMEM((rank, rank), jnp.float32)],
+        scratch_shapes=[pltpu.VMEM((rank, rank), jnp.float32), *factor_scratch(rank)],
     )
     return u_scaled, v_scaled, left, right
 

time: 167 us -> 166 us (level)
  Pallas kernels: 28 us -> 21.9 us
  local copies, waits for them, and re-layouts: 0.09 us -> 4.62 us
    pallas_call x12, Pallas kernels: 28 us -> 21.9 us  [call(): pl.pallas_call(kernel, out_shape=shapes if len(shapes) > 1 else shapes[0]...]
    unnamed x4 -> x12, local copies, waits for them, and re-layouts: 0.01 us -> 4.53 us
where the time goes in v4:
time: 166 us; the launch traced here: 163 us
  blocking collectives  79.5 us (48%)
  waiting for transfers between devices  39.5 us (24%)
  Pallas kernels  21.9 us (13%)
  starting transfers between devices  15.9 us (10%)
  local copies, waits for them, and re-layouts  4.62 us (3%)
    all_to_all x6, blocking collectives, exchanged(): lax.all_to_all(tiles, axis, 0, 0, axis_index_groups=groups, tiled=True)  79.5 us
    all_to_all x4, waiting for transfers between devices, exchanged(): lax.all_to_all(tiles, axis, 0, 0, axis_index_groups=groups, tiled=True)  33.4 us
    pallas_call x12, Pallas kernels, call(): pl.pallas_call(kernel, out_shape=shapes if len(shapes) > 1 else shapes[0]...  21.9 us
    all_to_all x4, starting transfers between devices, exchanged(): lax.all_to_all(tiles, axis, 0, 0, axis_index_groups=groups, tiled=True)  14.8 us
    ppermute x9, waiting for transfers between devices, from_sibling(): return lax.ppermute(x, 'tenant', [(i, i ^ 1) for i in range(count)])  6.12 us
    unnamed x12, local copies, waits for them, and re-layouts  4.53 us
  transfers between devices with their start and end apart: 13, of which 8 were waited for; matrix products, arithmetic and copies ran while one was open for 0% of the time, Pallas kernels for 1%

profile of v4, /device:TPU:8, one launch (start us, length us, event | category | flops | bytes accessed | tf_op | source)
XLA Modules:
  0.0 163.1 jit_solution(15423452016545004119)
XLA Ops:
  0.6 0.0 copy-start
  0.6 1.0 copy-done
  1.7 1.0 copy-done.2
  2.7 1.2 copy-done.4
  3.9 1.2 copy-done.5
  5.2 1.8 %projections.1 = f32[8,32,256]{2,1,0:T(8,128)S(1)} custom-call(f32[128,1024]{1,0:T(8,128)S(1)} %bitcast.3, f32[128,1024]{1,0:T(8,128)S(1)} %bitcast.5, f32[1024,256]{1,0:T(8,128)S(1)} %copy-done.4, f32[1024,256]{1,0:T(8,128)S(1)} %copy-done.5), custom_call_target="tpu_custom_call" | custom-call | tf_op jit(solution)/shard_map/projections/pallas_call | solution.py:150
  7.0 14.5 %all_to_all.50.tiles_ref = f32[8,32,256]{2,1,0:T(8,128)S(1)} all-to-all(f32[8,32,256]{2,1,0:T(8,128)S(1)} %projections.1), channel_id=1, replica_groups=mesh['tenant'=16,'row'=8] {'row'}, dimensions={0} | all-to-all | bytes 524288 | tf_op jit(solution)/shard_map/all_to_all | solution.py:273
  21.5 1.0 owner_coefficients.1
  22.5 3.4 %all-to-all-start.1 = ((f32[8,32,256]{2,1,0:T(8,128)}), f32[8,32,256]{2,1,0:T(8,128)S(1)}, u32[]{:S(2)}, u32[]{:S(2)}) async-start(f32[8,32,256]{2,1,0:T(8,128)} %owner_coefficients.1), calls=%async_computation.1 | async-start | bytes 524288 | tf_op jit(solution)/shard_map/all_to_all | solution.py:273
  26.0 0.1 collective-permute-start.1
  26.1 8.2 %all-to-all-done.1.mine_ref.pair_ref = f32[8,32,256]{2,1,0:T(8,128)S(1)} async-done(((f32[8,32,256]{2,1,0:T(8,128)}), f32[8,32,256]{2,1,0:T(8,128)S(1)}, u32[]{:S(2)}, u32[]{:S(2)}) %all-to-all-start.1) | async-done | bytes 262176 | tf_op jit(solution)/shard_map/all_to_all | solution.py:273
  34.3 0.0 collective-permute-start.2
  34.3 0.0 collective-permute-done.1.swap_ref
  34.3 1.5 collective-permute-done.2.other_ref.pair_other_ref
  35.9 0.4 load_sum.1
  36.3 15.8 %all_to_all.51.tiles_ref = f32[8,64,256]{2,1,0:T(8,128)S(1)} all-to-all(f32[8,64,256]{2,1,0:T(8,128)S(1)} %load_sum.1), channel_id=1, replica_groups={{0,16,32,48,64,80,96,112},{8,24,40,56,72,88,104,120},{1,17,33,49,65,81,..., dimensions={0} | all-to-all | bytes 1048576 | tf_op jit(solution)/shard_map/all_to_all | solution.py:273
  52.1 12.1 %all_to_all.52.basis_ref.mine_ref = f32[8,64,256]{2,1,0:T(8,128)S(1)} all-to-all(f32[8,64,256]{2,1,0:T(8,128)S(1)} %owner_sum.4), channel_id=1, replica_groups={{0,16,32,48,64,80,96,112},{8,24,40,56,72,88,104,120},{1,17,33,49,65,81,..., dimensions={0} | all-to-all | bytes 1048576 | tf_op jit(solution)/shard_map/all_to_all | solution.py:273
  64.2 0.6 gram_and_cores.2
  64.9 0.1 collective-permute-start.3
  65.0 1.5 collective-permute-done.3
  66.5 11.7 %all_to_all.53.tiles_ref = f32[8,32,256]{2,1,0:T(8,128)S(1)} all-to-all(f32[8,32,256]{2,1,0:T(8,128)S(1)} %add.21), channel_id=1, replica_groups=mesh['tenant'=16,'row'=8] {'row'}, dimensions={0} | all-to-all | bytes 524288 | tf_op jit(solution)/shard_map/all_to_all | solution.py:273
  78.2 0.7 owner_sum.5
  78.9 3.4 %all-to-all-start.5 = ((f32[8,32,256]{2,1,0:T(8,128)}), f32[8,32,256]{2,1,0:T(8,128)S(1)}, u32[]{:S(2)}, u32[]{:S(2)}) async-start(f32[8,32,256]{2,1,0:T(8,128)} %owner_sum.5), calls=%async_computation.5 | async-start | bytes 524288 | tf_op jit(solution)/shard_map/all_to_all | solution.py:273
  82.4 0.1 collective-permute-start
  82.5 8.2 %all-to-all-done.5.mine_ref = f32[8,32,256]{2,1,0:T(8,128)S(1)} async-done(((f32[8,32,256]{2,1,0:T(8,128)}), f32[8,32,256]{2,1,0:T(8,128)S(1)}, u32[]{:S(2)}, u32[]{:S(2)}) %all-to-all-start.5) | async-done | bytes 262176 | tf_op jit(solution)/shard_map/all_to_all | solution.py:273
  90.7 0.0 collective-permute-start.4
  90.7 0.0 collective-permute-done.swap_ref
  90.7 1.5 collective-permute-done.4.other_ref
  92.2 7.0 %turn_over.1 = (f32[256,256]{1,0:T(8,128)S(1)}, f32[8,16,256]{2,1,0:T(8,128)}, f32[8,64,256]{2,1,0:T(8,128)S(1)}) custom-call(s32[1]{0:T(128)} %bitcast.core_ref, f32[8,32,256]{2,1,0:T(8,128)S(1)} %all-to-all-done.5.mine_ref, f32[8,32,256]{2,1,0:T(8,128)S(1)} %collective-permute-done.4.other_ref, f32[8,32,256]{2,1,0:T(8,128)S(1)} %all-to-all-done.1.mine_ref.pair_ref, ...), custom_call_target="tpu_custom_call" | custom-call | tf_op jit(solution)/shard_map/turn_over/pallas_call | solution.py:150
  99.2 13.7 %all_to_all.54.tiles_ref = f32[8,64,256]{2,1,0:T(8,128)S(1)} all-to-all(f32[8,64,256]{2,1,0:T(8,128)S(1)} %get-tuple-element.17), channel_id=1, replica_groups={{0,16,32,48,64,80,96,112},{8,24,40,56,72,88,104,120},{1,17,33,49,65,81,..., dimensions={0} | all-to-all | bytes 1048576 | tf_op jit(solution)/shard_map/all_to_all | solution.py:273
  112.9 0.8 owner_sum.6
  113.7 4.6 %all-to-all-start.7 = ((f32[8,64,256]{2,1,0:T(8,128)}), f32[8,64,256]{2,1,0:T(8,128)S(1)}, u32[]{:S(2)}, u32[]{:S(2)}) async-start(f32[8,64,256]{2,1,0:T(8,128)} %owner_sum.6), calls=%async_computation.7 | async-start | bytes 1048576 | tf_op jit(solution)/shard_map/all_to_all | solution.py:273
  118.3 0.0 collective-permute-start.6
  118.3 8.7 %all-to-all-done.7.basis_ref = f32[8,64,256]{2,1,0:T(8,128)S(1)} async-done(((f32[8,64,256]{2,1,0:T(8,128)}), f32[8,64,256]{2,1,0:T(8,128)S(1)}, u32[]{:S(2)}, u32[]{:S(2)}) %all-to-all-start.7) | async-done | bytes 524320 | tf_op jit(solution)/shard_map/all_to_all | solution.py:273
  127.0 0.6 gram_and_cores.3
  127.6 0.1 collective-permute-start.5
  127.7 0.0 collective-permute-done.6.other_ref
  127.7 1.6 %left_basis.1 = f32[1024,256]{1,0:T(8,128)} custom-call(s32[1]{0:T(128)} %bitcast.core_ref, f32[256,256]{1,0:T(8,128)S(1)} %get-tuple-element.19.inverse_ref, f32[8,64,256]{2,1,0:T(8,128)S(1)} %all_to_all.52.basis_ref.mine_ref, f32[8,64,256]{2,1,0:T(8,128)S(1)} %collective-permute-done.6.other_ref), custom_call_target="tpu_custom_call" | custom-call | flops 402653184 | bytes 2097152 | tf_op jit(solution)/shard_map/left_basis/pallas_call | solution.py:150
  129.3 0.0 collective-permute-done.5
  129.4 0.7 add.22
  130.1 3.4 %all-to-all-start.8 = ((f32[8,32,256]{2,1,0:T(8,128)}), f32[8,32,256]{2,1,0:T(8,128)S(1)}, u32[]{:S(2)}, u32[]{:S(2)}) async-start(f32[8,32,256]{2,1,0:T(8,128)} %add.22), calls=%async_computation.8 | async-start | bytes 524288 | tf_op jit(solution)/shard_map/all_to_all | solution.py:273
  133.5 0.8 collective-permute-start.8
  134.3 8.3 %all-to-all-done.8.tiles_ref = f32[8,32,256]{2,1,0:T(8,128)S(1)} async-done(((f32[8,32,256]{2,1,0:T(8,128)}), f32[8,32,256]{2,1,0:T(8,128)S(1)}, u32[]{:S(2)}, u32[]{:S(2)}) %all-to-all-start.8) | async-done | bytes 262176 | tf_op jit(solution)/shard_map/all_to_all | solution.py:273
  142.6 11.7 %all_to_all.55.mine_ref = f32[8,32,256]{2,1,0:T(8,128)S(1)} all-to-all(f32[8,32,256]{2,1,0:T(8,128)S(1)} %owner_sum.7), channel_id=1, replica_groups=mesh['tenant'=16,'row'=8] {'row'}, dimensions={0} | all-to-all | bytes 524288 | tf_op jit(solution)/shard_map/all_to_all | solution.py:273
  154.3 0.0 collective-permute-start.7
  154.3 0.0 collective-permute-done.8.basis_other_ref
  154.3 1.5 collective-permute-done.7.other_ref
  155.8 7.3 %finish.1 = (f32[1024,256]{1,0:T(8,128)}, f32[8,16,256]{2,1,0:T(8,128)}) custom-call(s32[1]{0:T(128)} %bitcast.core_ref, f32[8,32,256]{2,1,0:T(8,128)S(1)} %all_to_all.55.mine_ref, f32[8,32,256]{2,1,0:T(8,128)S(1)} %collective-permute-done.7.other_ref, f32[8,64,256]{2,1,0:T(8,128)S(1)} %all-to-all-done.7.basis_ref, ...), custom_call_target="tpu_custom_call" | custom-call | tf_op jit(solution)/shard_map/finish/pallas_call | solution.py:150
  (12 shorter events, 0.2 us)
Async XLA Ops:
  0.6 1.0 copy-start
  1.7 1.0 copy-start.2
  2.7 1.2 copy-start.4
  3.9 1.2 copy-start.5
  21.5 4.4 %copy-start.1 = (f32[8,16,1024]{2,1,0:T(8,128)S(1)}, f32[8,16,1024]{2,1,0:T(8,128)}, u32[]{:S(2)}) copy-start(f32[8,16,1024]{2,1,0:T(8,128)} %param.4) | copy-start | bytes 1572868
  22.5 11.8 %all-to-all-start.1 = ((f32[8,32,256]{2,1,0:T(8,128)}), f32[8,32,256]{2,1,0:T(8,128)S(1)}, u32[]{:S(2)}, u32[]{:S(2)}) async-start(f32[8,32,256]{2,1,0:T(8,128)} %owner_coefficients.1), calls=%async_computation.1 | async-start | bytes 524288 | tf_op jit(solution)/shard_map/all_to_all | solution.py:273
  26.0 8.3 %collective-permute-start.1 = (f32[128,512]{1,0:T(8,128)S(1)}, f32[128,512]{1,0:T(8,128)S(1)}, u32[]{:S(2)}, u32[]{:S(2)}) collective-permute-start(f32[128,512]{1,0:T(8,128)S(1)} %get-tuple-element.26), channel_id=1, source_target_pairs={{0,8},{8,0},{16,24},{24,16},{32,40},{40,32},{48,56},{56,48},{64,72... | collective-permute-start | bytes 786440 | tf_op jit(solution)/shard_map/ppermute | solution.py:283
  34.3 1.5 collective-permute-start.2
  64.9 1.6 collective-permute-start.3
  78.2 4.2 %copy-start.3 = (f32[8,16,1024]{2,1,0:T(8,128)S(1)}, f32[8,16,1024]{2,1,0:T(8,128)}, u32[]{:S(2)}) copy-start(f32[8,16,1024]{2,1,0:T(8,128)} %param.5) | copy-start | bytes 1572868
  78.9 11.8 %all-to-all-start.5 = ((f32[8,32,256]{2,1,0:T(8,128)}), f32[8,32,256]{2,1,0:T(8,128)S(1)}, u32[]{:S(2)}, u32[]{:S(2)}) async-start(f32[8,32,256]{2,1,0:T(8,128)} %owner_sum.5), calls=%async_computation.5 | async-start | bytes 524288 | tf_op jit(solution)/shard_map/all_to_all | solution.py:273
  82.4 8.3 %collective-permute-start = (f32[128,512]{1,0:T(8,128)S(1)}, f32[128,512]{1,0:T(8,128)S(1)}, u32[]{:S(2)}, u32[]{:S(2)}) collective-permute-start(f32[128,512]{1,0:T(8,128)S(1)} %get-tuple-element.28), channel_id=1, source_target_pairs={{0,8},{8,0},{16,24},{24,16},{32,40},{40,32},{48,56},{56,48},{64,72... | collective-permute-start | bytes 786440 | tf_op jit(solution)/shard_map/ppermute | solution.py:283
  90.7 1.5 collective-permute-start.4
  113.7 13.3 %all-to-all-start.7 = ((f32[8,64,256]{2,1,0:T(8,128)}), f32[8,64,256]{2,1,0:T(8,128)S(1)}, u32[]{:S(2)}, u32[]{:S(2)}) async-start(f32[8,64,256]{2,1,0:T(8,128)} %owner_sum.6), calls=%async_computation.7 | async-start | bytes 1048576 | tf_op jit(solution)/shard_map/all_to_all | solution.py:273
  118.3 9.4 %collective-permute-start.6 = (f32[8,64,256]{2,1,0:T(8,128)S(1)}, f32[8,64,256]{2,1,0:T(8,128)S(1)}, u32[]{:S(2)}, u32[]{:S(2)}) collective-permute-start(f32[8,64,256]{2,1,0:T(8,128)S(1)} %all_to_all.52.basis_ref.mine_ref), channel_id=1, source_target_pairs={{0,8},{8,0},{16,24},{24,16},{32,40},{40,32},{48,56},{56,48},{64,72... | collective-permute-start | bytes 1572872 | tf_op jit(solution)/shard_map/ppermute | solution.py:283
  127.6 1.7 %collective-permute-start.5 = (f32[8,32,256]{2,1,0:T(8,128)S(1)}, f32[8,32,256]{2,1,0:T(8,128)S(1)}, u32[]{:S(2)}, u32[]{:S(2)}) collective-permute-start(f32[8,32,256]{2,1,0:T(8,128)S(1)} %get-tuple-element.18), channel_id=1, source_target_pairs={{0,8},{8,0},{16,24},{24,16},{32,40},{40,32},{48,56},{56,48},{64,72... | collective-permute-start | bytes 786440 | tf_op jit(solution)/shard_map/ppermute | solution.py:283
  130.1 12.5 %all-to-all-start.8 = ((f32[8,32,256]{2,1,0:T(8,128)}), f32[8,32,256]{2,1,0:T(8,128)S(1)}, u32[]{:S(2)}, u32[]{:S(2)}) async-start(f32[8,32,256]{2,1,0:T(8,128)} %add.22), calls=%async_computation.8 | async-start | bytes 524288 | tf_op jit(solution)/shard_map/all_to_all | solution.py:273
  133.5 20.8 %collective-permute-start.8 = (f32[8,64,256]{2,1,0:T(8,128)S(1)}, f32[8,64,256]{2,1,0:T(8,128)S(1)}, u32[]{:S(2)}, u32[]{:S(2)}) collective-permute-start(f32[8,64,256]{2,1,0:T(8,128)S(1)} %all-to-all-done.7.basis_ref), channel_id=1, source_target_pairs={{0,8},{8,0},{16,24},{24,16},{32,40},{40,32},{48,56},{56,48},{64,72... | collective-permute-start | bytes 1572872 | tf_op jit(solution)/shard_map/ppermute | solution.py:283
  154.3 1.5 collective-permute-start.7

commit v5 on v4

--- a/solution.py
+++ b/solution.py
@@ -327,10 +327,7 @@
     partial = call(
         projections,
         [(shape[0], 2 * RANK, rank)],
-        b,
-        a,
-        u_start,
-        v_start,
+        *(pltpu.with_memory_space_constraint(x, pltpu.HBM) for x in (b, a, u_start, v_start)),
         in_specs=[pl.BlockSpec(memory_space=pltpu.HBM)] * 4,
         scratch_shapes=[
             *(pltpu.VMEM(x.shape, x.dtype) for x in (b, a, u_start, v_start)),
@@ -346,12 +343,13 @@
     basis = tenant_total(load)
     basis_other = from_sibling(basis)
     mine, _ = gram_total(flag, b_halves, basis, rank)
+    mine_other, basis_other = lax.optimization_barrier((from_sibling(mine), basis_other))
     inverse, left, load = call(
         turn_over,
         [(rank, rank), shape, load_shape],
         flag,
         mine,
-        from_sibling(mine),
+        mine_other,
         pair,
         pair_other,
         *a_halves,

time: 166 us -> 161 us (0.970)
  blocking collectives: 79.5 us -> 92 us
  waiting for transfers between devices: 39.5 us -> 30.8 us
  local copies, waits for them, and re-layouts: 4.62 us -> 0.08 us
  starting transfers between devices: 15.9 us -> 11.7 us
    all_to_all x6 -> x7, blocking collectives: 79.5 us -> 92 us  [exchanged(): lax.all_to_all(tiles, axis, 0, 0, axis_index_groups=groups, tiled=True)]
    all_to_all x4 -> x3, waiting for transfers between devices: 33.4 us -> 25 us  [exchanged(): lax.all_to_all(tiles, axis, 0, 0, axis_index_groups=groups, tiled=True)]
    all_to_all x4 -> x3, starting transfers between devices: 14.8 us -> 10.2 us  [exchanged(): lax.all_to_all(tiles, axis, 0, 0, axis_index_groups=groups, tiled=True)]
    unnamed x12 -> x4, local copies, waits for them, and re-layouts: 4.53 us -> 0.01 us
  transfers between devices with their start and end apart: 13 -> 12, of which waited for: 8 -> 8; matrix products, arithmetic and copies ran while one was open for 0% -> 0% of each run, Pallas kernels for 1% -> 1%
where the time goes in v5:
time: 161 us; the launch traced here: 158 us
  blocking collectives  92 us (57%)
  waiting for transfers between devices  30.8 us (19%)
  Pallas kernels  21.8 us (14%)
  starting transfers between devices  11.7 us (7%)
    all_to_all x7, blocking collectives, exchanged(): lax.all_to_all(tiles, axis, 0, 0, axis_index_groups=groups, tiled=True)  92 us
    all_to_all x3, waiting for transfers between devices, exchanged(): lax.all_to_all(tiles, axis, 0, 0, axis_index_groups=groups, tiled=True)  25 us
    pallas_call x12, Pallas kernels, call(): pl.pallas_call(kernel, out_shape=shapes if len(shapes) > 1 else shapes[0]...  21.8 us
    all_to_all x3, starting transfers between devices, exchanged(): lax.all_to_all(tiles, axis, 0, 0, axis_index_groups=groups, tiled=True)  10.2 us
    ppermute x9, waiting for transfers between devices, from_sibling(): return lax.ppermute(x, 'tenant', [(i, i ^ 1) for i in range(count)])  5.87 us
  transfers between devices with their start and end apart: 12, of which 8 were waited for; matrix products, arithmetic and copies ran while one was open for 0% of the time, Pallas kernels for 1%

profile of v5, /device:TPU:8, one launch (start us, length us, event | category | flops | bytes accessed | tf_op | source)
XLA Modules:
  0.0 158.0 jit_solution(13712105194033237921)
XLA Ops:
  0.6 2.5 %projections.1 = f32[8,32,256]{2,1,0:T(8,128)S(1)} custom-call(f32[128,1024]{1,0:T(8,128)} %bitcast.3, f32[128,1024]{1,0:T(8,128)} %bitcast.5, f32[1024,256]{1,0:T(8,128)} %u_hbm.1, f32[1024,256]{1,0:T(8,128)} %v_hbm.1), custom_call_target="tpu_custom_call" | custom-call | tf_op jit(solution)/shard_map/projections/pallas_call | solution.py:150
  3.1 14.5 %all_to_all.50.tiles_ref = f32[8,32,256]{2,1,0:T(8,128)S(1)} all-to-all(f32[8,32,256]{2,1,0:T(8,128)S(1)} %projections.1), channel_id=1, replica_groups=mesh['tenant'=16,'row'=8] {'row'}, dimensions={0} | all-to-all | bytes 524288 | tf_op jit(solution)/shard_map/all_to_all | solution.py:273
  17.7 0.0 copy-start
  17.7 1.0 owner_coefficients.1
  18.6 3.4 %all-to-all-start.1 = ((f32[8,32,256]{2,1,0:T(8,128)}), f32[8,32,256]{2,1,0:T(8,128)S(1)}, u32[]{:S(2)}, u32[]{:S(2)}) async-start(f32[8,32,256]{2,1,0:T(8,128)} %owner_coefficients.1), calls=%async_computation.1 | async-start | bytes 524288 | tf_op jit(solution)/shard_map/all_to_all | solution.py:273
  22.1 0.0 copy-done
  22.1 0.1 collective-permute-start.1
  22.2 8.2 %all-to-all-done.1.mine_ref.pair_ref = f32[8,32,256]{2,1,0:T(8,128)S(1)} async-done(((f32[8,32,256]{2,1,0:T(8,128)}), f32[8,32,256]{2,1,0:T(8,128)S(1)}, u32[]{:S(2)}, u32[]{:S(2)}) %all-to-all-start.1) | async-done | bytes 262176 | tf_op jit(solution)/shard_map/all_to_all | solution.py:273
  30.4 0.0 collective-permute-start.2
  30.4 0.0 collective-permute-done.1.swap_ref
  30.4 1.5 collective-permute-done.2.other_ref.pair_other_ref
  32.0 0.4 load_sum.1
  32.4 15.8 %all_to_all.51.tiles_ref = f32[8,64,256]{2,1,0:T(8,128)S(1)} all-to-all(f32[8,64,256]{2,1,0:T(8,128)S(1)} %load_sum.1), channel_id=1, replica_groups={{0,16,32,48,64,80,96,112},{8,24,40,56,72,88,104,120},{1,17,33,49,65,81,..., dimensions={0} | all-to-all | bytes 1048576 | tf_op jit(solution)/shard_map/all_to_all | solution.py:273
  48.2 12.1 %all_to_all.52.basis_ref.mine_ref = f32[8,64,256]{2,1,0:T(8,128)S(1)} all-to-all(f32[8,64,256]{2,1,0:T(8,128)S(1)} %owner_sum.4), channel_id=1, replica_groups={{0,16,32,48,64,80,96,112},{8,24,40,56,72,88,104,120},{1,17,33,49,65,81,..., dimensions={0} | all-to-all | bytes 1048576 | tf_op jit(solution)/shard_map/all_to_all | solution.py:273
  60.4 0.6 gram_and_cores.2
  61.0 0.1 collective-permute-start.3
  61.1 1.5 collective-permute-done.3
  62.6 11.6 %all_to_all.53.tiles_ref = f32[8,32,256]{2,1,0:T(8,128)S(1)} all-to-all(f32[8,32,256]{2,1,0:T(8,128)S(1)} %add.21), channel_id=1, replica_groups=mesh['tenant'=16,'row'=8] {'row'}, dimensions={0} | all-to-all | bytes 524288 | tf_op jit(solution)/shard_map/all_to_all | solution.py:273
  74.3 0.0 copy-start.1
  74.3 0.7 owner_sum.5
  75.0 3.4 %all-to-all-start.5 = ((f32[8,32,256]{2,1,0:T(8,128)}), f32[8,32,256]{2,1,0:T(8,128)S(1)}, u32[]{:S(2)}, u32[]{:S(2)}) async-start(f32[8,32,256]{2,1,0:T(8,128)} %owner_sum.5), calls=%async_computation.5 | async-start | bytes 524288 | tf_op jit(solution)/shard_map/all_to_all | solution.py:273
  78.4 0.1 collective-permute-start.5
  78.5 8.3 %all-to-all-done.5.mine_ref = f32[8,32,256]{2,1,0:T(8,128)S(1)} async-done(((f32[8,32,256]{2,1,0:T(8,128)}), f32[8,32,256]{2,1,0:T(8,128)S(1)}, u32[]{:S(2)}, u32[]{:S(2)}) %all-to-all-start.5) | async-done | bytes 262176 | tf_op jit(solution)/shard_map/all_to_all | solution.py:273
  86.8 0.0 collective-permute-start.4
  86.8 0.0 copy-done.1
  86.8 0.6 collective-permute-start
  87.4 0.0 collective-permute-done.5.other_ref
  87.4 0.9 collective-permute-done.4.other_ref
  88.3 0.4 collective-permute-done.swap_ref
  88.7 7.0 %turn_over.1 = (f32[256,256]{1,0:T(8,128)S(1)}, f32[8,16,256]{2,1,0:T(8,128)}, f32[8,64,256]{2,1,0:T(8,128)S(1)}) custom-call(s32[1]{0:T(128)} %bitcast.core_ref, f32[8,32,256]{2,1,0:T(8,128)S(1)} %all-to-all-done.5.mine_ref, f32[8,32,256]{2,1,0:T(8,128)S(1)} %collective-permute-done.4.other_ref, f32[8,32,256]{2,1,0:T(8,128)S(1)} %all-to-all-done.1.mine_ref.pair_ref, ...), custom_call_target="tpu_custom_call" | custom-call | tf_op jit(solution)/shard_map/turn_over/pallas_call | solution.py:150
  95.7 13.8 %all_to_all.54.tiles_ref = f32[8,64,256]{2,1,0:T(8,128)S(1)} all-to-all(f32[8,64,256]{2,1,0:T(8,128)S(1)} %get-tuple-element.20), channel_id=1, replica_groups={{0,16,32,48,64,80,96,112},{8,24,40,56,72,88,104,120},{1,17,33,49,65,81,..., dimensions={0} | all-to-all | bytes 1048576 | tf_op jit(solution)/shard_map/all_to_all | solution.py:273
  109.5 12.4 %all_to_all.55.basis_ref = f32[8,64,256]{2,1,0:T(8,128)S(1)} all-to-all(f32[8,64,256]{2,1,0:T(8,128)S(1)} %owner_sum.6), channel_id=1, replica_groups={{0,16,32,48,64,80,96,112},{8,24,40,56,72,88,104,120},{1,17,33,49,65,81,..., dimensions={0} | all-to-all | bytes 1048576 | tf_op jit(solution)/shard_map/all_to_all | solution.py:273
  121.9 0.6 gram_and_cores.3
  122.5 0.1 collective-permute-start.6
  122.6 1.6 %left_basis.1 = f32[1024,256]{1,0:T(8,128)} custom-call(s32[1]{0:T(128)} %bitcast.core_ref, f32[256,256]{1,0:T(8,128)S(1)} %get-tuple-element.22.inverse_ref, f32[8,64,256]{2,1,0:T(8,128)S(1)} %all_to_all.52.basis_ref.mine_ref, f32[8,64,256]{2,1,0:T(8,128)S(1)} %collective-permute-done.5.other_ref), custom_call_target="tpu_custom_call" | custom-call | flops 402653184 | bytes 2097152 | tf_op jit(solution)/shard_map/left_basis/pallas_call | solution.py:150
  124.3 0.0 collective-permute-done.6
  124.3 0.7 add.22
  125.0 3.4 %all-to-all-start.8 = ((f32[8,32,256]{2,1,0:T(8,128)}), f32[8,32,256]{2,1,0:T(8,128)S(1)}, u32[]{:S(2)}, u32[]{:S(2)}) async-start(f32[8,32,256]{2,1,0:T(8,128)} %add.22), calls=%async_computation.8 | async-start | bytes 524288 | tf_op jit(solution)/shard_map/all_to_all | solution.py:273
  128.4 0.6 collective-permute-start.8
  129.0 8.5 %all-to-all-done.8.tiles_ref = f32[8,32,256]{2,1,0:T(8,128)S(1)} async-done(((f32[8,32,256]{2,1,0:T(8,128)}), f32[8,32,256]{2,1,0:T(8,128)S(1)}, u32[]{:S(2)}, u32[]{:S(2)}) %all-to-all-start.8) | async-done | bytes 262176 | tf_op jit(solution)/shard_map/all_to_all | solution.py:273
  137.5 11.7 %all_to_all.56.mine_ref = f32[8,32,256]{2,1,0:T(8,128)S(1)} all-to-all(f32[8,32,256]{2,1,0:T(8,128)S(1)} %owner_sum.7), channel_id=1, replica_groups=mesh['tenant'=16,'row'=8] {'row'}, dimensions={0} | all-to-all | bytes 524288 | tf_op jit(solution)/shard_map/all_to_all | solution.py:273
  149.2 0.0 collective-permute-start.7
  149.2 0.0 collective-permute-done.8.basis_other_ref
  149.2 1.5 collective-permute-done.7.other_ref
  150.8 7.3 %finish.1 = (f32[1024,256]{1,0:T(8,128)}, f32[8,16,256]{2,1,0:T(8,128)}) custom-call(s32[1]{0:T(128)} %bitcast.core_ref, f32[8,32,256]{2,1,0:T(8,128)S(1)} %all_to_all.56.mine_ref, f32[8,32,256]{2,1,0:T(8,128)S(1)} %collective-permute-done.7.other_ref, f32[8,64,256]{2,1,0:T(8,128)S(1)} %all_to_all.55.basis_ref, ...), custom_call_target="tpu_custom_call" | custom-call | tf_op jit(solution)/shard_map/finish/pallas_call | solution.py:150
  (6 shorter events, 0.2 us)
Async XLA Ops:
  17.7 4.4 %copy-start = (f32[8,16,1024]{2,1,0:T(8,128)S(1)}, f32[8,16,1024]{2,1,0:T(8,128)}, u32[]{:S(2)}) copy-start(f32[8,16,1024]{2,1,0:T(8,128)} %param.4) | copy-start | bytes 1572868
  18.6 11.8 %all-to-all-start.1 = ((f32[8,32,256]{2,1,0:T(8,128)}), f32[8,32,256]{2,1,0:T(8,128)S(1)}, u32[]{:S(2)}, u32[]{:S(2)}) async-start(f32[8,32,256]{2,1,0:T(8,128)} %owner_coefficients.1), calls=%async_computation.1 | async-start | bytes 524288 | tf_op jit(solution)/shard_map/all_to_all | solution.py:273
  22.1 8.3 %collective-permute-start.1 = (f32[128,512]{1,0:T(8,128)S(1)}, f32[128,512]{1,0:T(8,128)S(1)}, u32[]{:S(2)}, u32[]{:S(2)}) collective-permute-start(f32[128,512]{1,0:T(8,128)S(1)} %get-tuple-element.30), channel_id=1, source_target_pairs={{0,8},{8,0},{16,24},{24,16},{32,40},{40,32},{48,56},{56,48},{64,72... | collective-permute-start | bytes 786440 | tf_op jit(solution)/shard_map/ppermute | solution.py:283
  30.4 1.5 collective-permute-start.2
  61.0 1.6 %collective-permute-start.3 = (f32[8,32,256]{2,1,0:T(8,128)S(1)}, f32[8,32,256]{2,1,0:T(8,128)S(1)}, u32[]{:S(2)}, u32[]{:S(2)}) collective-permute-start(f32[8,32,256]{2,1,0:T(8,128)S(1)} %get-tuple-element.18), channel_id=1, source_target_pairs={{0,8},{8,0},{16,24},{24,16},{32,40},{40,32},{48,56},{56,48},{64,72... | collective-permute-start | bytes 786440 | tf_op jit(solution)/shard_map/ppermute | solution.py:283
  74.3 12.5 %copy-start.1 = (f32[8,16,1024]{2,1,0:T(8,128)S(1)}, f32[8,16,1024]{2,1,0:T(8,128)}, u32[]{:S(2)}) copy-start(f32[8,16,1024]{2,1,0:T(8,128)} %param.5) | copy-start | bytes 1572868
  75.0 11.8 %all-to-all-start.5 = ((f32[8,32,256]{2,1,0:T(8,128)}), f32[8,32,256]{2,1,0:T(8,128)S(1)}, u32[]{:S(2)}, u32[]{:S(2)}) async-start(f32[8,32,256]{2,1,0:T(8,128)} %owner_sum.5), calls=%async_computation.5 | async-start | bytes 524288 | tf_op jit(solution)/shard_map/all_to_all | solution.py:273
  78.4 9.0 %collective-permute-start.5 = (f32[8,64,256]{2,1,0:T(8,128)S(1)}, f32[8,64,256]{2,1,0:T(8,128)S(1)}, u32[]{:S(2)}, u32[]{:S(2)}) collective-permute-start(f32[8,64,256]{2,1,0:T(8,128)S(1)} %all_to_all.52.basis_ref.mine_ref), channel_id=1, source_target_pairs={{0,8},{8,0},{16,24},{24,16},{32,40},{40,32},{48,56},{56,48},{64,72... | collective-permute-start | bytes 1572872 | tf_op jit(solution)/shard_map/ppermute | solution.py:283
  86.8 1.5 collective-permute-start.4
  86.8 1.9 %collective-permute-start = (f32[128,512]{1,0:T(8,128)S(1)}, f32[128,512]{1,0:T(8,128)S(1)}, u32[]{:S(2)}, u32[]{:S(2)}) collective-permute-start(f32[128,512]{1,0:T(8,128)S(1)} %get-tuple-element.32), channel_id=1, source_target_pairs={{0,8},{8,0},{16,24},{24,16},{32,40},{40,32},{48,56},{56,48},{64,72... | collective-permute-start | bytes 786440 | tf_op jit(solution)/shard_map/ppermute | solution.py:283
  122.5 1.7 %collective-permute-start.6 = (f32[8,32,256]{2,1,0:T(8,128)S(1)}, f32[8,32,256]{2,1,0:T(8,128)S(1)}, u32[]{:S(2)}, u32[]{:S(2)}) collective-permute-start(f32[8,32,256]{2,1,0:T(8,128)S(1)} %get-tuple-element.21), channel_id=1, source_target_pairs={{0,8},{8,0},{16,24},{24,16},{32,40},{40,32},{48,56},{56,48},{64,72... | collective-permute-start | bytes 786440 | tf_op jit(solution)/shard_map/ppermute | solution.py:283
  125.0 12.5 %all-to-all-start.8 = ((f32[8,32,256]{2,1,0:T(8,128)}), f32[8,32,256]{2,1,0:T(8,128)S(1)}, u32[]{:S(2)}, u32[]{:S(2)}) async-start(f32[8,32,256]{2,1,0:T(8,128)} %add.22), calls=%async_computation.8 | async-start | bytes 524288 | tf_op jit(solution)/shard_map/all_to_all | solution.py:273
  128.4 20.8 %collective-permute-start.8 = (f32[8,64,256]{2,1,0:T(8,128)S(1)}, f32[8,64,256]{2,1,0:T(8,128)S(1)}, u32[]{:S(2)}, u32[]{:S(2)}) collective-permute-start(f32[8,64,256]{2,1,0:T(8,128)S(1)} %all_to_all.55.basis_ref), channel_id=1, source_target_pairs={{0,8},{8,0},{16,24},{24,16},{32,40},{40,32},{48,56},{56,48},{64,72... | collective-permute-start | bytes 1572872 | tf_op jit(solution)/shard_map/ppermute | solution.py:283
  149.2 1.5 collective-permute-start.7

commit v6 on v5

--- a/solution.py
+++ b/solution.py
@@ -5,6 +5,7 @@
 from jax import lax
 from jax.experimental import pallas as pl
 from jax.experimental.pallas import tpu as pltpu
+from jax.sharding import Mesh
 from jax.sharding import PartitionSpec as P
 
 D = 8192
@@ -13,6 +14,9 @@
 SUBLANES = 8
 PANEL = 32
 STEPS = 4
+ROW = ("y_lo", "row")
+QUARTER = ("y_lo", "core")
+STEPS_AWAY = (0, 2, 1, 3)
 
 
 def pieces(x):
@@ -196,33 +200,46 @@
     out_ref[...] = jnp.broadcast_to(jnp.sum(tiles_ref[...], axis=0), out_ref.shape)
 
 
-def both(x_ref, y_ref):
-    return jnp.concatenate([matrix(x_ref[...]), matrix(y_ref[...])])
-
-
-def both_upper(x_ref, y_ref):
-    return jnp.concatenate([matrix(x_ref[:, :RANK]), matrix(y_ref[:, :RANK])])
-
-
-def both_lower(x_ref, y_ref):
-    return jnp.concatenate([matrix(x_ref[:, RANK:]), matrix(y_ref[:, RANK:])])
-
-
-def load_sum(keep_ref, swap_ref, mine_ref, other_ref, out_ref):
-    load = product(both(keep_ref, swap_ref), both_upper(mine_ref, other_ref), 0, 0)
-    out_ref[...] = load.reshape(out_ref.shape)
-
-
-def gram_and_cores(core_ref, keep_ref, swap_ref, basis_ref, mine_ref, other_ref, gram_ref):
-    basis = matrix(basis_ref[...])
-    cores = product(both(keep_ref, swap_ref), basis)
+def stacked(refs):
+    return jnp.concatenate([ref[...] for ref in refs])
+
+
+def by_distance(quarter, ref):
+    count = len(ref) // 2
+    half = quarter // 2
+    return [pl.ds(place * count, count) for place in (half, 1 - half)]
+
+
+def tenants(quarter, refs, first):
+    rows = pl.ds(first, RANK)
+    tiles = [ref[place, rows] for ref in refs for place in by_distance(quarter, ref)]
+    return jnp.concatenate([matrix(x) for x in tiles])
+
+
+def load_sum(quarter_ref, f0, f1, f2, f3, mine_ref, other_ref, *out_refs):
+    coeffs = tenants(quarter_ref[0], (mine_ref, other_ref), 0)
+    store_load(product(stacked((f0, f1, f2, f3)), coeffs, 0, 0), out_refs)
+
+
+def store_load(load, out_refs):
+    count = len(out_refs[0])
+    for i, ref in enumerate(out_refs):
+        ref[...] = load[i * count : (i + 1) * count]
+
+
+def gram_and_cores(quarter_ref, f0, f1, f2, f3, x_ref, y_ref, mine_ref, other_ref, gram_ref):
+    basis = stacked((x_ref, y_ref))
+    cores = product(stacked((f0, f1, f2, f3)), basis)
     gram_ref[...] = product(basis, basis, 0, 0)
-    count, half = len(mine_ref), len(gram_ref) // 2
-    mine_ref[:, :RANK] = cores[:half].reshape(count, RANK, -1)
-    other_ref[:, :RANK] = cores[half:].reshape(count, RANK, -1)
-    core = core_ref[0]
-    mine_ref[:, RANK:] = gram_ref[pl.ds(core * half, half), :].reshape(count, RANK, -1)
-    other_ref[:, RANK:] = gram_ref[pl.ds((1 - core) * half, half), :].reshape(count, RANK, -1)
+    quarter = quarter_ref[0]
+    core, half = quarter % 2, len(gram_ref) // 2
+    block = len(cores) // 4
+    for i, (ref, which) in enumerate(((mine_ref, core), (other_ref, 1 - core))):
+        for j, place in enumerate(by_distance(quarter, ref)):
+            rows = cores[(2 * i + j) * block : (2 * i + j + 1) * block]
+            ref[place, :RANK] = rows.reshape(-1, RANK, rows.shape[1])
+        rows = gram_ref[pl.ds(which * half, half), :]
+        ref[:, RANK:] = rows.reshape(len(ref), -1, rows.shape[1])
 
 
 def inverse_factor(core, mine_ref, other_ref, inverse_ref, *scratch):
@@ -233,96 +250,114 @@
 
 
 def turn_over(
-    core_ref, mine_ref, other_ref, pair_ref, pair_other_ref, keep_ref, swap_ref,
-    inverse_ref, left_ref, load_ref, *scratch,
+    quarter_ref, mine_ref, other_ref, pair_ref, pair_other_ref, f0, f1, f2, f3,
+    inverse_ref, left_ref, x_ref, y_ref, *scratch,
 ):
-    inverse_factor(core_ref[0], mine_ref, other_ref, inverse_ref, *scratch)
-    left = product(both_upper(mine_ref, other_ref), inverse_ref[...], 1, 1)
-    left_ref[...] = left[: len(left) // 2].reshape(left_ref.shape)
-    weight = product(left, left, 1, 1)
-    tenant = [lax.broadcasted_iota(jnp.int32, weight.shape, d) // RANK for d in range(2)]
-    weight = jnp.where(tenant[0] == tenant[1], weight, 0.0)
-    coeffs = product(weight, both_lower(pair_ref, pair_other_ref))
-    load = product(both(keep_ref, swap_ref), coeffs, 0, 0)
-    load_ref[...] = load.reshape(load_ref.shape)
-
-
-def scaled_basis(core, inverse, mine_ref, other_ref, out_ref):
-    half = len(out_ref) // 2
+    quarter = quarter_ref[0]
+    inverse_factor(quarter % 2, mine_ref, other_ref, inverse_ref, *scratch)
+    left = product(tenants(quarter, (mine_ref, other_ref), 0), inverse_ref[...], 1, 1)
+    right = tenants(quarter, (pair_ref, pair_other_ref), RANK)
+    own = left[: len(left) // 4]
+    left_ref[...] = own.reshape(left_ref.shape)
+    half = len(left) // 2
+    tenant = [lax.broadcasted_iota(jnp.int32, (half, half), d) // RANK for d in range(2)]
+    coeffs = []
+    for part in (slice(0, half), slice(half, None)):
+        weight = jnp.where(tenant[0] == tenant[1], product(left[part], left[part], 1, 1), 0.0)
+        coeffs.append(product(weight, right[part]))
+    load = product(stacked((f0, f1, f2, f3)), jnp.concatenate(coeffs), 0, 0)
+    store_load(load, (x_ref, y_ref))
+
+
+def scaled_basis(quarter, inverse, refs, out_ref):
     scale = math.sqrt(D)
-    for place, ref in ((core, mine_ref), (1 - core, other_ref)):
-        out_ref[pl.ds(place * half, half), :] = product(matrix(ref[...]), inverse, 1, 1) * scale
-
-
-def left_basis(core_ref, inverse_ref, mine_ref, other_ref, out_ref):
-    scaled_basis(core_ref[0], inverse_ref[...], mine_ref, other_ref, out_ref)
+    for step, ref in zip(STEPS_AWAY, refs):
+        rows = pl.ds((quarter ^ step) * len(ref), len(ref))
+        out_ref[rows, :] = product(ref[...], inverse, 1, 1) * scale
+
+
+def left_basis(quarter_ref, inverse_ref, q0, q1, q2, q3, out_ref):
+    scaled_basis(quarter_ref[0], inverse_ref[...], (q0, q1, q2, q3), out_ref)
 
 
 def finish(
-    core_ref, mine_ref, other_ref, basis_ref, basis_other_ref,
-    out_ref, right_ref, inverse_ref, *scratch,
+    quarter_ref, mine_ref, other_ref, q0, q1, q2, q3, out_ref, right_ref, inverse_ref, *scratch
 ):
-    inverse_factor(core_ref[0], mine_ref, other_ref, inverse_ref, *scratch)
+    quarter = quarter_ref[0]
+    inverse_factor(quarter % 2, mine_ref, other_ref, inverse_ref, *scratch)
     inverse = inverse_ref[...]
-    right = product(matrix(mine_ref[:, :RANK]), inverse, 1, 1)
-    right_ref[...] = right.reshape(right_ref.shape)
-    scaled_basis(core_ref[0], inverse, basis_ref, basis_other_ref, out_ref)
-
-
-def exchanged(tiles, axis, groups=None):
-    return lax.all_to_all(tiles, axis, 0, 0, axis_index_groups=groups, tiled=True)
-
-
-def total(tiles, axis, groups=None, at_owner=owner_sum):
-    copies = call(at_owner, [tiles.shape], exchanged(tiles, axis, groups))
-    return exchanged(copies, axis, groups)
+    own = matrix(mine_ref[by_distance(quarter, mine_ref)[0], :RANK])
+    right_ref[...] = product(own, inverse, 1, 1).reshape(right_ref.shape)
+    scaled_basis(quarter, inverse, (q0, q1, q2, q3), out_ref)
+
+
+def exchanged(tiles, axis):
+    return lax.all_to_all(tiles, axis, 0, 0, tiled=True)
+
+
+def from_peer(x, axis, step):
+    count = lax.axis_size(axis)
+    return lax.ppermute(x, axis, [(i, i ^ step) for i in range(count)])
+
+
+def row_total(tiles):
+    tiles = exchanged(tiles, ROW)
+    return exchanged(call(owner_sum, [tiles.shape], tiles), ROW)
+
+
+def plane_total(x, y):
+    for x_step, y_step in ((1, 3), (3, 1)):
+        x, y = x + from_peer(x, "z", x_step), y + from_peer(y, "z", y_step)
+    return x, y
 
 
 def from_sibling(x):
-    count = lax.axis_size("tenant")
-    return lax.ppermute(x, "tenant", [(i, i ^ 1) for i in range(count)])
-
-
-def tenant_total(load):
-    chips = lax.axis_size("tenant") // 2
-    groups = [[2 * chip + core for chip in range(chips)] for core in range(2)]
-    return total(load, "tenant", groups)
-
-
-def gram_total(core, halves, basis, rank, beside=()):
-    count = lax.axis_size("row")
-    tiles = (count, 2 * RANK, rank)
+    return from_peer(x, "core", 1)
+
+
+def column_quarters(factors, quarter):
+    size = factors.shape[1] // 4
+
+    def columns(step):
+        return lax.dynamic_slice_in_dim(factors, (quarter ^ step) * size, size, 1)
+
+    moved = [from_peer(columns(step), QUARTER, step) for step in STEPS_AWAY[1:]]
+    return columns(0), *moved
+
+
+def basis_quarters(x, y):
+    mine = jnp.concatenate([x, y])
+    across = from_peer(mine, "y_lo", 1)
+    return mine, across, from_sibling(mine), from_sibling(across)
+
+
+def with_quarter(count):
+    return [pl.BlockSpec(memory_space=m) for m in (pltpu.SMEM, *[pltpu.VMEM] * count)]
+
+
+def gram_total(quarter, factors, parts, rank, beside=()):
+    tiles = (lax.axis_size(ROW), RANK + rank // 2 // lax.axis_size(ROW), rank)
     mine, other = call(
         gram_and_cores,
         [tiles, tiles],
-        core,
-        *halves,
-        basis,
-        in_specs=with_core(3),
+        quarter,
+        *factors,
+        *parts,
+        in_specs=with_quarter(6),
         scratch_shapes=[pltpu.VMEM((rank, rank), jnp.float32)],
     )
     other, beside = lax.optimization_barrier((from_sibling(other), beside))
-    return total(mine + other, "row"), beside
-
-
-def column_halves(factors, core):
-    half = factors.shape[1] // 2
-    keep = lax.dynamic_slice_in_dim(factors, core * half, half, 1)
-    return keep, from_sibling(lax.dynamic_slice_in_dim(factors, (1 - core) * half, half, 1))
-
-
-def with_core(count):
-    return [pl.BlockSpec(memory_space=m) for m in (pltpu.SMEM, *[pltpu.VMEM] * count)]
+    return row_total(mine + other), beside
 
 
 def local(b_factors, a_factors, u_start, v_start):
     shape = (*b_factors.shape[:2], u_start.shape[1])
     width, rank = u_start.shape
-    core = lax.axis_index("tenant") % 2
-    flag = jnp.reshape(core, (1,)).astype(jnp.int32)
+    place = lax.axis_index(QUARTER)
+    quarter = jnp.reshape(place, (1,)).astype(jnp.int32)
     b = b_factors.reshape(-1, width)
     a = a_factors.reshape(-1, width)
-    b_halves, a_halves = column_halves(b, core), column_halves(a, core)
+    b_quarters, a_quarters = column_quarters(b, place), column_quarters(a, place)
 
     partial = call(
         projections,
@@ -334,58 +369,60 @@
             pltpu.SemaphoreType.DMA((STEPS, 4)),
         ],
     )
-    pair = total(partial, "row", None, owner_coefficients)
+    copies = (lax.axis_size(ROW), 2 * RANK, rank)
+    pair = exchanged(call(owner_coefficients, [copies], exchanged(partial, "row")), ROW)
     pair_other = from_sibling(pair)
 
-    chips = lax.axis_size("tenant") // 2
-    load_shape = (chips, width // 2 // chips, rank)
-    load = call(load_sum, [load_shape], *b_halves, pair, pair_other)
-    basis = tenant_total(load)
-    basis_other = from_sibling(basis)
-    mine, _ = gram_total(flag, b_halves, basis, rank)
-    mine_other, basis_other = lax.optimization_barrier((from_sibling(mine), basis_other))
-    inverse, left, load = call(
+    part = (width // 8, rank)
+    parts = call(
+        load_sum, [part, part], quarter, *b_quarters, pair, pair_other, in_specs=with_quarter(6)
+    )
+    parts = plane_total(*parts)
+    basis = basis_quarters(*parts)
+    mine, _ = gram_total(quarter, b_quarters, parts, rank)
+    inverse, left, *parts = call(
         turn_over,
-        [(rank, rank), shape, load_shape],
-        flag,
+        [(rank, rank), shape, part, part],
+        quarter,
         mine,
-        mine_other,
+        from_sibling(mine),
         pair,
         pair_other,
-        *a_halves,
-        in_specs=with_core(6),
+        *a_quarters,
+        in_specs=with_quarter(8),
         scratch_shapes=factor_scratch(rank),
     )
     u_scaled = call(
         left_basis,
         [(width, rank)],
-        flag,
+        quarter,
         inverse,
-        basis,
-        basis_other,
-        in_specs=with_core(3),
+        *basis,
+        in_specs=with_quarter(5),
         cost_estimate=pl.CostEstimate(
             flops=6 * width * rank * rank, bytes_accessed=8 * width * rank, transcendentals=0
         ),
     )
-    basis = tenant_total(load)
-    basis_other = from_sibling(basis)
-    mine, u_scaled = gram_total(flag, a_halves, basis, rank, u_scaled)
+    parts = plane_total(*parts)
+    basis = basis_quarters(*parts)
+    mine, u_scaled = gram_total(quarter, a_quarters, parts, rank, u_scaled)
     v_scaled, right = call(
         finish,
         [(width, rank), shape],
-        flag,
+        quarter,
         mine,
         from_sibling(mine),
-        basis,
-        basis_other,
-        in_specs=with_core(4),
+        *basis,
+        in_specs=with_quarter(6),
         scratch_shapes=[pltpu.VMEM((rank, rank), jnp.float32), *factor_scratch(rank)],
     )
     return u_scaled, v_scaled, left, right
 
 
 def solution(mesh):
-    in_specs = (P("tenant", None, "row"), P("tenant", None, "row"), P("row", None), P("row", None))
-    out_specs = (P("row", None), P("row", None), P("tenant", None, None), P("tenant", None, None))
+    count, rows = mesh.devices.shape
+    mesh = Mesh(mesh.devices.reshape(count // 4, 2, 2, rows), ("z", "y_lo", "core", "row"))
+    tenant = ("z", "y_lo", "core")
+    in_specs = (P(tenant, None, "row"), P(tenant, None, "row"), P("row", None), P("row", None))
+    out_specs = (P("row", None), P("row", None), P(tenant, None, None), P(tenant, None, None))
     return jax.shard_map(local, mesh=mesh, in_specs=in_specs, out_specs=out_specs, check_vma=False)

time: 161 us -> 156 us (0.969)
  blocking collectives: 92 us -> 67.6 us
  starting transfers between devices: 11.7 us -> 26 us
  waiting for transfers between devices: 30.8 us -> 38.3 us
    ppermute x9 -> x25, waiting for transfers between devices: 5.87 us -> 30.5 us  [from_peer(): return lax.ppermute(x, axis, [(i, i ^ step) for i in range(count)])]
    all_to_all x7 -> x5, blocking collectives: 92 us -> 67.6 us  [exchanged(): return lax.all_to_all(tiles, axis, 0, 0, tiled=True)]
    ppermute x9 -> x25, starting transfers between devices: 1.51 us -> 21.2 us  [from_peer(): return lax.ppermute(x, axis, [(i, i ^ step) for i in range(count)])]
    all_to_all x3 -> x1, waiting for transfers between devices: 25 us -> 7.85 us  [exchanged(): return lax.all_to_all(tiles, axis, 0, 0, tiled=True)]
    all_to_all x3 -> x1, starting transfers between devices: 10.2 us -> 4.85 us  [exchanged(): return lax.all_to_all(tiles, axis, 0, 0, tiled=True)]
    pallas_call x12 -> x10, Pallas kernels: 21.8 us -> 21.3 us  [call(): pl.pallas_call(kernel, out_shape=shapes if len(shapes) > 1 else shapes[0]...]
  transfers between devices with their start and end apart: 12 -> 26, of which waited for: 8 -> 16; matrix products, arithmetic and copies ran while one was open for 0% -> 0% of each run, Pallas kernels for 1% -> 1%
where the time goes in v6:
time: 156 us; the launch traced here: 154 us
  blocking collectives  67.6 us (43%)
  waiting for transfers between devices  38.3 us (25%)
  starting transfers between devices  26 us (17%)
  Pallas kernels  21.3 us (14%)
    all_to_all x5, blocking collectives, exchanged(): return lax.all_to_all(tiles, axis, 0, 0, tiled=True)  67.6 us
    ppermute x25, waiting for transfers between devices, from_peer(): return lax.ppermute(x, axis, [(i, i ^ step) for i in range(count)])  30.5 us
    pallas_call x10, Pallas kernels, call(): pl.pallas_call(kernel, out_shape=shapes if len(shapes) > 1 else shapes[0]...  21.3 us
    ppermute x25, starting transfers between devices, from_peer(): return lax.ppermute(x, axis, [(i, i ^ step) for i in range(count)])  21.2 us
    all_to_all x1, waiting for transfers between devices, exchanged(): return lax.all_to_all(tiles, axis, 0, 0, tiled=True)  7.85 us
    all_to_all x1, starting transfers between devices, exchanged(): return lax.all_to_all(tiles, axis, 0, 0, tiled=True)  4.85 us
  transfers between devices with their start and end apart: 26, of which 16 were waited for; matrix products, arithmetic and copies ran while one was open for 0% of the time, Pallas kernels for 1%

profile of v6, /device:TPU:8, one launch (start us, length us, event | category | flops | bytes accessed | tf_op | source)
XLA Modules:
  0.0 154.4 jit_solution(4775193528124835593)
XLA Ops:
  0.6 2.5 %projections.1 = f32[8,32,256]{2,1,0:T(8,128)S(1)} custom-call(f32[128,1024]{1,0:T(8,128)} %bitcast.3, f32[128,1024]{1,0:T(8,128)} %bitcast.5, f32[1024,256]{1,0:T(8,128)} %u_hbm.1, f32[1024,256]{1,0:T(8,128)} %v_hbm.1), custom_call_target="tpu_custom_call" | custom-call | tf_op jit(solution)/shard_map/projections/pallas_call | solution.py:154
  3.1 14.5 %all_to_all.30.tiles_ref = f32[8,32,256]{2,1,0:T(8,128)S(1)} all-to-all(f32[8,32,256]{2,1,0:T(8,128)S(1)} %projections.1), channel_id=1, replica_groups=mesh['z'=4,'y_lo'=2,'core'=2,'row'=8] {'row'}, dimensions={0} | all-to-all | bytes 524288 | tf_op jit(solution)/shard_map/all_to_all | solution.py:295
  17.7 0.3 owner_coefficients.1
  18.0 12.9 %all_to_all.31.mine_ref.pair_ref = f32[16,32,256]{2,1,0:T(8,128)S(1)} all-to-all(f32[16,32,256]{2,1,0:T(8,128)S(1)} %owner_coefficients.1), channel_id=1, replica_groups=mesh['z'=4,'y_lo'=2,'core'=2,'row'=8] {'y_lo','row'}, dimensions={0} | all-to-all | bytes 1048576 | tf_op jit(solution)/shard_map/all_to_all | solution.py:295
  30.9 1.6 %collective-permute-start.5 = (f32[128,256]{1,0:T(8,128)S(1)}, f32[128,256]{1,0:T(8,128)S(1)}, u32[]{:S(2)}, u32[]{:S(2)}) collective-permute-start(f32[128,256]{1,0:T(8,128)S(1)} %get-tuple-element.32), channel_id=1, source_target_pairs={{0,24},{8,16},{16,8},{24,0},{1,25},{9,17},{17,9},{25,1},{2,26},{10... | collective-permute-start | bytes 393224 | tf_op jit(solution)/shard_map/ppermute | solution.py:300
  32.5 0.6 collective-permute-start.3
  33.1 3.3 %collective-permute-done.5.f3 = f32[128,256]{1,0:T(8,128)S(1)} collective-permute-done((f32[128,256]{1,0:T(8,128)S(1)}, f32[128,256]{1,0:T(8,128)S(1)}, u32[]{:S(2)}, u32[]{:S(2)}) %collective-permute-start.5) | collective-permute-done | bytes 131104 | tf_op jit(solution)/shard_map/ppermute | solution.py:300
  36.4 3.2 %collective-permute-done.3.f1 = f32[128,256]{1,0:T(8,128)S(1)} collective-permute-done((f32[128,256]{1,0:T(8,128)S(1)}, f32[128,256]{1,0:T(8,128)S(1)}, u32[]{:S(2)}, u32[]{:S(2)}) %collective-permute-start.3) | collective-permute-done | bytes 131104 | tf_op jit(solution)/shard_map/ppermute | solution.py:300
  39.6 0.4 load_sum.1
  40.0 2.0 %collective-permute-start.7 = (f32[128,256]{1,0:T(8,128)S(1)}, f32[128,256]{1,0:T(8,128)S(1)}, u32[]{:S(2)}, u32[]{:S(2)}) collective-permute-start(f32[128,256]{1,0:T(8,128)S(1)} %get-tuple-element.18), channel_id=1, source_target_pairs={{0,32},{32,0},{64,96},{96,64},{1,33},{33,1},{65,97},{97,65},{2,34}... | collective-permute-start | bytes 393224 | tf_op jit(solution)/shard_map/ppermute | solution.py:300
  42.0 2.5 %collective-permute-start.9 = (f32[128,256]{1,0:T(8,128)S(1)}, f32[128,256]{1,0:T(8,128)S(1)}, u32[]{:S(2)}, u32[]{:S(2)}) collective-permute-start(f32[128,256]{1,0:T(8,128)S(1)} %get-tuple-element.19), channel_id=1, source_target_pairs={{0,96},{32,64},{64,32},{96,0},{1,97},{33,65},{65,33},{97,1},{2,98}... | collective-permute-start | bytes 393224 | tf_op jit(solution)/shard_map/ppermute | solution.py:300
  44.5 0.6 collective-permute-done.7
  45.1 4.0 %collective-permute-start.8 = (f32[128,256]{1,0:T(8,128)S(1)}, f32[128,256]{1,0:T(8,128)S(1)}, u32[]{:S(2)}, u32[]{:S(2)}) collective-permute-start(f32[128,256]{1,0:T(8,128)S(1)} %add.54), channel_id=1, source_target_pairs={{0,96},{32,64},{64,32},{96,0},{1,97},{33,65},{65,33},{97,1},{2,98}... | collective-permute-start | bytes 393224 | tf_op jit(solution)/shard_map/ppermute | solution.py:300
  49.2 0.1 collective-permute-start.10
  49.3 2.8 %collective-permute-done.8 = f32[128,256]{1,0:T(8,128)S(1)} collective-permute-done((f32[128,256]{1,0:T(8,128)S(1)}, f32[128,256]{1,0:T(8,128)S(1)}, u32[]{:S(2)}, u32[]{:S(2)}) %collective-permute-start.8) | collective-permute-done | bytes 131104 | tf_op jit(solution)/shard_map/ppermute | solution.py:300
  52.1 2.1 %collective-permute-done.10 = f32[128,256]{1,0:T(8,128)S(1)} collective-permute-done((f32[128,256]{1,0:T(8,128)S(1)}, f32[128,256]{1,0:T(8,128)S(1)}, u32[]{:S(2)}, u32[]{:S(2)}) %collective-permute-start.10) | collective-permute-done | bytes 131104 | tf_op jit(solution)/shard_map/ppermute | solution.py:300
  54.3 0.5 gram_and_cores.2
  54.9 1.7 %collective-permute-done.11 = f32[16,24,256]{2,1,0:T(8,128)S(1)} collective-permute-done((f32[16,24,256]{2,1,0:T(8,128)S(1)}, f32[16,24,256]{2,1,0:T(8,128)S(1)}, u32[]{:S(2)}, u32[]{:S(2)}) %collective-permute-start.11) | collective-permute-done | bytes 393248 | tf_op jit(solution)/shard_map/ppermute | solution.py:300
  56.7 13.7 %all_to_all.32.tiles_ref = f32[16,24,256]{2,1,0:T(8,128)S(1)} all-to-all(f32[16,24,256]{2,1,0:T(8,128)S(1)} %add.58), channel_id=1, replica_groups=mesh['z'=4,'y_lo'=2,'core'=2,'row'=8] {'y_lo','row'}, dimensions={0} | all-to-all | bytes 786432 | tf_op jit(solution)/shard_map/all_to_all | solution.py:295
  70.4 12.8 %all_to_all.33.mine_ref = f32[16,24,256]{2,1,0:T(8,128)S(1)} all-to-all(f32[16,24,256]{2,1,0:T(8,128)S(1)} %owner_sum.2), channel_id=1, replica_groups=mesh['z'=4,'y_lo'=2,'core'=2,'row'=8] {'y_lo','row'}, dimensions={0} | all-to-all | bytes 786432 | tf_op jit(solution)/shard_map/all_to_all | solution.py:295
  83.2 1.6 %collective-permute-start.2 = (f32[128,256]{1,0:T(8,128)S(1)}, f32[128,256]{1,0:T(8,128)S(1)}, u32[]{:S(2)}, u32[]{:S(2)}) collective-permute-start(f32[128,256]{1,0:T(8,128)S(1)} %get-tuple-element.36), channel_id=1, source_target_pairs={{0,24},{8,16},{16,8},{24,0},{1,25},{9,17},{17,9},{25,1},{2,26},{10... | collective-permute-start | bytes 393224 | tf_op jit(solution)/shard_map/ppermute | solution.py:300
  84.9 0.6 collective-permute-start
  85.5 3.3 %collective-permute-done.2.f3 = f32[128,256]{1,0:T(8,128)S(1)} collective-permute-done((f32[128,256]{1,0:T(8,128)S(1)}, f32[128,256]{1,0:T(8,128)S(1)}, u32[]{:S(2)}, u32[]{:S(2)}) %collective-permute-start.2) | collective-permute-done | bytes 131104 | tf_op jit(solution)/shard_map/ppermute | solution.py:300
  88.7 3.2 %collective-permute-done.f1 = f32[128,256]{1,0:T(8,128)S(1)} collective-permute-done((f32[128,256]{1,0:T(8,128)S(1)}, f32[128,256]{1,0:T(8,128)S(1)}, u32[]{:S(2)}, u32[]{:S(2)}) %collective-permute-start) | collective-permute-done | bytes 131104 | tf_op jit(solution)/shard_map/ppermute | solution.py:300
  91.9 7.3 %turn_over.1 = (f32[256,256]{1,0:T(8,128)S(1)}, f32[8,16,256]{2,1,0:T(8,128)}, f32[128,256]{1,0:T(8,128)S(1)}, f32[128,256]{1,0:T(8,128)S(1)}) custom-call(s32[1]{0:T(128)} %bitcast.quarter_ref, f32[16,24,256]{2,1,0:T(8,128)S(1)} %all_to_all.33.mine_ref, f32[16,24,256]{2,1,0:T(8,128)S(1)} %collective-permute-done.12.other_ref, ...), custom_call_target="tpu_custom_call" | custom-call | tf_op jit(solution)/shard_map/turn_over/pallas_call | solution.py:154
  99.3 0.1 collective-permute-start.13
  99.4 2.5 %collective-permute-start.15 = (f32[128,256]{1,0:T(8,128)S(1)}, f32[128,256]{1,0:T(8,128)S(1)}, u32[]{:S(2)}, u32[]{:S(2)}) collective-permute-start(f32[128,256]{1,0:T(8,128)S(1)} %get-tuple-element.23), channel_id=1, source_target_pairs={{0,96},{32,64},{64,32},{96,0},{1,97},{33,65},{65,33},{97,1},{2,98}... | collective-permute-start | bytes 393224 | tf_op jit(solution)/shard_map/ppermute | solution.py:300
  102.0 1.5 collective-permute-start.18
  103.5 0.9 collective-permute-done.13
  104.4 1.6 %collective-permute-start.14 = (f32[128,256]{1,0:T(8,128)S(1)}, f32[128,256]{1,0:T(8,128)S(1)}, u32[]{:S(2)}, u32[]{:S(2)}) collective-permute-start(f32[128,256]{1,0:T(8,128)S(1)} %add.59), channel_id=1, source_target_pairs={{0,96},{32,64},{64,32},{96,0},{1,97},{33,65},{65,33},{97,1},{2,98}... | collective-permute-start | bytes 393224 | tf_op jit(solution)/shard_map/ppermute | solution.py:300
  106.0 0.7 collective-permute-start.16
  106.7 3.9 %collective-permute-done.14 = f32[128,256]{1,0:T(8,128)S(1)} collective-permute-done((f32[128,256]{1,0:T(8,128)S(1)}, f32[128,256]{1,0:T(8,128)S(1)}, u32[]{:S(2)}, u32[]{:S(2)}) %collective-permute-start.14) | collective-permute-done | bytes 131104 | tf_op jit(solution)/shard_map/ppermute | solution.py:300
  110.7 0.4 collective-permute-done.16
  111.1 0.5 gram_and_cores.3
  111.7 0.5 collective-permute-start.19
  112.2 0.1 collective-permute-start.20
  112.3 1.5 collective-permute-done.19.q2
  113.8 0.4 collective-permute-done.20.q3
  114.1 1.6 %left_basis.1 = f32[1024,256]{1,0:T(8,128)} custom-call(s32[1]{0:T(128)} %bitcast.quarter_ref, f32[256,256]{1,0:T(8,128)S(1)} %get-tuple-element.25.inverse_ref, f32[256,256]{1,0:T(8,128)S(1)} %pad_maximum_fusion.q0, f32[256,256]{1,0:T(8,128)S(1)} %collective-permute-done.18.q1, f32[256,256]{1,0:T(8,128)S(1)} %collective-permute-done.19.q2, ...), custom_call_target="tpu_custom_call" | custom-call | flops 402653184 | bytes 2097152 | tf_op jit(solution)/shard_map/left_basis/pallas_call | solution.py:154
  115.8 13.7 %all_to_all.34.tiles_ref = f32[16,24,256]{2,1,0:T(8,128)S(1)} all-to-all(f32[16,24,256]{2,1,0:T(8,128)S(1)} %add.63), channel_id=1, replica_groups=mesh['z'=4,'y_lo'=2,'core'=2,'row'=8] {'y_lo','row'}, dimensions={0} | all-to-all | bytes 786432 | tf_op jit(solution)/shard_map/all_to_all | solution.py:295
  129.5 0.8 owner_sum.3
  130.3 4.8 %all-to-all-start.5 = ((f32[16,24,256]{2,1,0:T(8,128)}), f32[16,24,256]{2,1,0:T(8,128)S(1)}, u32[]{:S(2)}, u32[]{:S(2)}) async-start(f32[16,24,256]{2,1,0:T(8,128)} %owner_sum.3), calls=%async_computation.5 | async-start | bytes 786432 | tf_op jit(solution)/shard_map/all_to_all | solution.py:295
  135.2 0.3 collective-permute-start.22
  135.5 7.9 %all-to-all-done.5.mine_ref = f32[16,24,256]{2,1,0:T(8,128)S(1)} async-done(((f32[16,24,256]{2,1,0:T(8,128)}), f32[16,24,256]{2,1,0:T(8,128)S(1)}, u32[]{:S(2)}, u32[]{:S(2)}) %all-to-all-start.5) | async-done | bytes 393248 | tf_op jit(solution)/shard_map/all_to_all | solution.py:295
  143.3 0.5 collective-permute-start.23
  143.8 1.7 %collective-permute-done.22.q1 = f32[256,256]{1,0:T(8,128)S(1)} collective-permute-done((f32[256,256]{1,0:T(8,128)S(1)}, f32[256,256]{1,0:T(8,128)S(1)}, u32[]{:S(2)}, u32[]{:S(2)}) %collective-permute-start.22) | collective-permute-done | bytes 262176 | tf_op jit(solution)/shard_map/ppermute | solution.py:300
  145.6 1.5 collective-permute-done.24.q3
  147.1 7.3 %finish.1 = (f32[1024,256]{1,0:T(8,128)}, f32[8,16,256]{2,1,0:T(8,128)}) custom-call(s32[1]{0:T(128)} %bitcast.quarter_ref, f32[16,24,256]{2,1,0:T(8,128)S(1)} %all-to-all-done.5.mine_ref, f32[16,24,256]{2,1,0:T(8,128)S(1)} %collective-permute-done.21.other_ref, f32[256,256]{1,0:T(8,128)S(1)} %pad_maximum_fusion.1.q0, ...), custom_call_target="tpu_custom_call" | custom-call | tf_op jit(solution)/shard_map/finish/pallas_call | solution.py:154
  (37 shorter events, 0.6 us)
Async XLA Ops:
  18.0 12.9 %copy-start = (f32[8,16,1024]{2,1,0:T(8,128)S(1)}, f32[8,16,1024]{2,1,0:T(8,128)}, u32[]{:S(2)}) copy-start(f32[8,16,1024]{2,1,0:T(8,128)} %param.4) | copy-start | bytes 1572868
  30.8 8.7 %collective-permute-start.6 = (f32[16,32,256]{2,1,0:T(8,128)S(1)}, f32[16,32,256]{2,1,0:T(8,128)S(1)}, u32[]{:S(2)}, u32[]{:S(2)}) collective-permute-start(f32[16,32,256]{2,1,0:T(8,128)S(1)} %all_to_all.31.mine_ref.pair_ref), channel_id=1, source_target_pairs={{0,8},{8,0},{1,9},{9,1},{2,10},{10,2},{3,11},{11,3},{4,12},{12,4},... | collective-permute-start | bytes 1572872 | tf_op jit(solution)/shard_map/ppermute | solution.py:300
  30.9 5.5 %collective-permute-start.5 = (f32[128,256]{1,0:T(8,128)S(1)}, f32[128,256]{1,0:T(8,128)S(1)}, u32[]{:S(2)}, u32[]{:S(2)}) collective-permute-start(f32[128,256]{1,0:T(8,128)S(1)} %get-tuple-element.32), channel_id=1, source_target_pairs={{0,24},{8,16},{16,8},{24,0},{1,25},{9,17},{17,9},{25,1},{2,26},{10... | collective-permute-start | bytes 393224 | tf_op jit(solution)/shard_map/ppermute | solution.py:300
  32.5 3.9 %collective-permute-start.4 = (f32[128,256]{1,0:T(8,128)S(1)}, f32[128,256]{1,0:T(8,128)S(1)}, u32[]{:S(2)}, u32[]{:S(2)}) collective-permute-start(f32[128,256]{1,0:T(8,128)S(1)} %get-tuple-element.33), channel_id=1, source_target_pairs={{0,8},{8,0},{16,24},{24,16},{1,9},{9,1},{17,25},{25,17},{2,10},{10... | collective-permute-start | bytes 393224 | tf_op jit(solution)/shard_map/ppermute | solution.py:300
  32.5 7.0 %collective-permute-start.3 = (f32[128,256]{1,0:T(8,128)S(1)}, f32[128,256]{1,0:T(8,128)S(1)}, u32[]{:S(2)}, u32[]{:S(2)}) collective-permute-start(f32[128,256]{1,0:T(8,128)S(1)} %get-tuple-element.34), channel_id=1, source_target_pairs={{0,16},{8,24},{16,0},{24,8},{1,17},{9,25},{17,1},{25,9},{2,18},{10... | collective-permute-start | bytes 393224 | tf_op jit(solution)/shard_map/ppermute | solution.py:300
  40.0 5.1 %collective-permute-start.7 = (f32[128,256]{1,0:T(8,128)S(1)}, f32[128,256]{1,0:T(8,128)S(1)}, u32[]{:S(2)}, u32[]{:S(2)}) collective-permute-start(f32[128,256]{1,0:T(8,128)S(1)} %get-tuple-element.18), channel_id=1, source_target_pairs={{0,32},{32,0},{64,96},{96,64},{1,33},{33,1},{65,97},{97,65},{2,34}... | collective-permute-start | bytes 393224 | tf_op jit(solution)/shard_map/ppermute | solution.py:300
  42.0 7.2 %collective-permute-start.9 = (f32[128,256]{1,0:T(8,128)S(1)}, f32[128,256]{1,0:T(8,128)S(1)}, u32[]{:S(2)}, u32[]{:S(2)}) collective-permute-start(f32[128,256]{1,0:T(8,128)S(1)} %get-tuple-element.19), channel_id=1, source_target_pairs={{0,96},{32,64},{64,32},{96,0},{1,97},{33,65},{65,33},{97,1},{2,98}... | collective-permute-start | bytes 393224 | tf_op jit(solution)/shard_map/ppermute | solution.py:300
  45.1 7.0 %collective-permute-start.8 = (f32[128,256]{1,0:T(8,128)S(1)}, f32[128,256]{1,0:T(8,128)S(1)}, u32[]{:S(2)}, u32[]{:S(2)}) collective-permute-start(f32[128,256]{1,0:T(8,128)S(1)} %add.54), channel_id=1, source_target_pairs={{0,96},{32,64},{64,32},{96,0},{1,97},{33,65},{65,33},{97,1},{2,98}... | collective-permute-start | bytes 393224 | tf_op jit(solution)/shard_map/ppermute | solution.py:300
  49.2 5.0 %collective-permute-start.10 = (f32[128,256]{1,0:T(8,128)S(1)}, f32[128,256]{1,0:T(8,128)S(1)}, u32[]{:S(2)}, u32[]{:S(2)}) collective-permute-start(f32[128,256]{1,0:T(8,128)S(1)} %add.56), channel_id=1, source_target_pairs={{0,32},{32,0},{64,96},{96,64},{1,33},{33,1},{65,97},{97,65},{2,34}... | collective-permute-start | bytes 393224 | tf_op jit(solution)/shard_map/ppermute | solution.py:300
  54.8 1.8 %collective-permute-start.11 = (f32[16,24,256]{2,1,0:T(8,128)S(1)}, f32[16,24,256]{2,1,0:T(8,128)S(1)}, u32[]{:S(2)}, u32[]{:S(2)}) collective-permute-start(f32[16,24,256]{2,1,0:T(8,128)S(1)} %get-tuple-element.21), channel_id=1, source_target_pairs={{0,8},{8,0},{1,9},{9,1},{2,10},{10,2},{3,11},{11,3},{4,12},{12,4},... | collective-permute-start | bytes 1179656 | tf_op jit(solution)/shard_map/ppermute | solution.py:300
  70.4 12.8 %copy-start.1 = (f32[8,16,1024]{2,1,0:T(8,128)S(1)}, f32[8,16,1024]{2,1,0:T(8,128)}, u32[]{:S(2)}) copy-start(f32[8,16,1024]{2,1,0:T(8,128)} %param.5) | copy-start | bytes 1572868
  83.2 8.7 %collective-permute-start.12 = (f32[16,24,256]{2,1,0:T(8,128)S(1)}, f32[16,24,256]{2,1,0:T(8,128)S(1)}, u32[]{:S(2)}, u32[]{:S(2)}) collective-permute-start(f32[16,24,256]{2,1,0:T(8,128)S(1)} %all_to_all.33.mine_ref), channel_id=1, source_target_pairs={{0,8},{8,0},{1,9},{9,1},{2,10},{10,2},{3,11},{11,3},{4,12},{12,4},... | collective-permute-start | bytes 1179656 | tf_op jit(solution)/shard_map/ppermute | solution.py:300
  83.2 5.5 %collective-permute-start.2 = (f32[128,256]{1,0:T(8,128)S(1)}, f32[128,256]{1,0:T(8,128)S(1)}, u32[]{:S(2)}, u32[]{:S(2)}) collective-permute-start(f32[128,256]{1,0:T(8,128)S(1)} %get-tuple-element.36), channel_id=1, source_target_pairs={{0,24},{8,16},{16,8},{24,0},{1,25},{9,17},{17,9},{25,1},{2,26},{10... | collective-permute-start | bytes 393224 | tf_op jit(solution)/shard_map/ppermute | solution.py:300
  84.9 3.9 %collective-permute-start.1 = (f32[128,256]{1,0:T(8,128)S(1)}, f32[128,256]{1,0:T(8,128)S(1)}, u32[]{:S(2)}, u32[]{:S(2)}) collective-permute-start(f32[128,256]{1,0:T(8,128)S(1)} %get-tuple-element.37), channel_id=1, source_target_pairs={{0,8},{8,0},{16,24},{24,16},{1,9},{9,1},{17,25},{25,17},{2,10},{10... | collective-permute-start | bytes 393224 | tf_op jit(solution)/shard_map/ppermute | solution.py:300
  84.9 7.0 %collective-permute-start = (f32[128,256]{1,0:T(8,128)S(1)}, f32[128,256]{1,0:T(8,128)S(1)}, u32[]{:S(2)}, u32[]{:S(2)}) collective-permute-start(f32[128,256]{1,0:T(8,128)S(1)} %get-tuple-element.38), channel_id=1, source_target_pairs={{0,16},{8,24},{16,0},{24,8},{1,17},{9,25},{17,1},{25,9},{2,18},{10... | collective-permute-start | bytes 393224 | tf_op jit(solution)/shard_map/ppermute | solution.py:300
  99.3 5.1 %collective-permute-start.13 = (f32[128,256]{1,0:T(8,128)S(1)}, f32[128,256]{1,0:T(8,128)S(1)}, u32[]{:S(2)}, u32[]{:S(2)}) collective-permute-start(f32[128,256]{1,0:T(8,128)S(1)} %get-tuple-element.22), channel_id=1, source_target_pairs={{0,32},{32,0},{64,96},{96,64},{1,33},{33,1},{65,97},{97,65},{2,34}... | collective-permute-start | bytes 393224 | tf_op jit(solution)/shard_map/ppermute | solution.py:300
  99.4 6.6 %collective-permute-start.15 = (f32[128,256]{1,0:T(8,128)S(1)}, f32[128,256]{1,0:T(8,128)S(1)}, u32[]{:S(2)}, u32[]{:S(2)}) collective-permute-start(f32[128,256]{1,0:T(8,128)S(1)} %get-tuple-element.23), channel_id=1, source_target_pairs={{0,96},{32,64},{64,32},{96,0},{1,97},{33,65},{65,33},{97,1},{2,98}... | collective-permute-start | bytes 393224 | tf_op jit(solution)/shard_map/ppermute | solution.py:300
  102.0 10.2 %collective-permute-start.18 = (f32[256,256]{1,0:T(8,128)S(1)}, f32[256,256]{1,0:T(8,128)S(1)}, u32[]{:S(2)}, u32[]{:S(2)}) collective-permute-start(f32[256,256]{1,0:T(8,128)S(1)} %pad_maximum_fusion.q0), channel_id=1, source_target_pairs={{0,16},{16,0},{1,17},{17,1},{2,18},{18,2},{3,19},{19,3},{4,20},{20... | collective-permute-start | bytes 786440 | tf_op jit(solution)/shard_map/ppermute | solution.py:300
  104.4 6.3 %collective-permute-start.14 = (f32[128,256]{1,0:T(8,128)S(1)}, f32[128,256]{1,0:T(8,128)S(1)}, u32[]{:S(2)}, u32[]{:S(2)}) collective-permute-start(f32[128,256]{1,0:T(8,128)S(1)} %add.59), channel_id=1, source_target_pairs={{0,96},{32,64},{64,32},{96,0},{1,97},{33,65},{65,33},{97,1},{2,98}... | collective-permute-start | bytes 393224 | tf_op jit(solution)/shard_map/ppermute | solution.py:300
  106.0 5.0 %collective-permute-start.16 = (f32[128,256]{1,0:T(8,128)S(1)}, f32[128,256]{1,0:T(8,128)S(1)}, u32[]{:S(2)}, u32[]{:S(2)}) collective-permute-start(f32[128,256]{1,0:T(8,128)S(1)} %add.61), channel_id=1, source_target_pairs={{0,32},{32,0},{64,96},{96,64},{1,33},{33,1},{65,97},{97,65},{2,34}... | collective-permute-start | bytes 393224 | tf_op jit(solution)/shard_map/ppermute | solution.py:300
  111.6 4.2 %collective-permute-start.17 = (f32[16,24,256]{2,1,0:T(8,128)S(1)}, f32[16,24,256]{2,1,0:T(8,128)S(1)}, u32[]{:S(2)}, u32[]{:S(2)}) collective-permute-start(f32[16,24,256]{2,1,0:T(8,128)S(1)} %get-tuple-element.24), channel_id=1, source_target_pairs={{0,8},{8,0},{1,9},{9,1},{2,10},{10,2},{3,11},{11,3},{4,12},{12,4},... | collective-permute-start | bytes 1179656 | tf_op jit(solution)/shard_map/ppermute | solution.py:300
  111.7 2.1 %collective-permute-start.19 = (f32[256,256]{1,0:T(8,128)S(1)}, f32[256,256]{1,0:T(8,128)S(1)}, u32[]{:S(2)}, u32[]{:S(2)}) collective-permute-start(f32[256,256]{1,0:T(8,128)S(1)} %pad_maximum_fusion.q0), channel_id=1, source_target_pairs={{0,8},{8,0},{1,9},{9,1},{2,10},{10,2},{3,11},{11,3},{4,12},{12,4},... | collective-permute-start | bytes 786440 | tf_op jit(solution)/shard_map/ppermute | solution.py:300
  112.2 2.0 %collective-permute-start.20 = (f32[256,256]{1,0:T(8,128)S(1)}, f32[256,256]{1,0:T(8,128)S(1)}, u32[]{:S(2)}, u32[]{:S(2)}) collective-permute-start(f32[256,256]{1,0:T(8,128)S(1)} %collective-permute-done.18.q1), channel_id=1, source_target_pairs={{0,8},{8,0},{1,9},{9,1},{2,10},{10,2},{3,11},{11,3},{4,12},{12,4},... | collective-permute-start | bytes 786440 | tf_op jit(solution)/shard_map/ppermute | solution.py:300
  130.3 13.0 %all-to-all-start.5 = ((f32[16,24,256]{2,1,0:T(8,128)}), f32[16,24,256]{2,1,0:T(8,128)S(1)}, u32[]{:S(2)}, u32[]{:S(2)}) async-start(f32[16,24,256]{2,1,0:T(8,128)} %owner_sum.3), calls=%async_computation.5 | async-start | bytes 786432 | tf_op jit(solution)/shard_map/all_to_all | solution.py:295
  135.2 10.4 %collective-permute-start.22 = (f32[256,256]{1,0:T(8,128)S(1)}, f32[256,256]{1,0:T(8,128)S(1)}, u32[]{:S(2)}, u32[]{:S(2)}) collective-permute-start(f32[256,256]{1,0:T(8,128)S(1)} %pad_maximum_fusion.1.q0), channel_id=1, source_target_pairs={{0,16},{16,0},{1,17},{17,1},{2,18},{18,2},{3,19},{19,3},{4,20},{20... | collective-permute-start | bytes 786440 | tf_op jit(solution)/shard_map/ppermute | solution.py:300
  143.3 3.8 %collective-permute-start.21 = (f32[16,24,256]{2,1,0:T(8,128)S(1)}, f32[16,24,256]{2,1,0:T(8,128)S(1)}, u32[]{:S(2)}, u32[]{:S(2)}) collective-permute-start(f32[16,24,256]{2,1,0:T(8,128)S(1)} %all-to-all-done.5.mine_ref), channel_id=1, source_target_pairs={{0,8},{8,0},{1,9},{9,1},{2,10},{10,2},{3,11},{11,3},{4,12},{12,4},... | collective-permute-start | bytes 1179656 | tf_op jit(solution)/shard_map/ppermute | solution.py:300
  143.3 2.2 %collective-permute-start.23 = (f32[256,256]{1,0:T(8,128)S(1)}, f32[256,256]{1,0:T(8,128)S(1)}, u32[]{:S(2)}, u32[]{:S(2)}) collective-permute-start(f32[256,256]{1,0:T(8,128)S(1)} %pad_maximum_fusion.1.q0), channel_id=1, source_target_pairs={{0,8},{8,0},{1,9},{9,1},{2,10},{10,2},{3,11},{11,3},{4,12},{12,4},... | collective-permute-start | bytes 786440 | tf_op jit(solution)/shard_map/ppermute | solution.py:300
  145.6 1.5 collective-permute-start.24

commit v7 on v6

--- a/solution.py
+++ b/solution.py
@@ -300,9 +300,17 @@
     return lax.ppermute(x, axis, [(i, i ^ step) for i in range(count)])
 
 
-def row_total(tiles):
-    tiles = exchanged(tiles, ROW)
-    return exchanged(call(owner_sum, [tiles.shape], tiles), ROW)
+def together(x, others):
+    return lax.optimization_barrier((x, others))
+
+
+def row_total(tiles, parts, others):
+    basis = jnp.concatenate(parts)
+    tiles, across = together(exchanged(tiles, ROW), from_peer(basis, "y_lo", 1))
+    whole = exchanged(call(owner_sum, [tiles.shape], tiles), ROW)
+    quarters = (from_sibling(basis), from_sibling(across))
+    whole, (quarters, others) = together(whole, (quarters, others))
+    return whole, (basis, across, *quarters), others
 
 
 def plane_total(x, y):
@@ -325,17 +333,11 @@
     return columns(0), *moved
 
 
-def basis_quarters(x, y):
-    mine = jnp.concatenate([x, y])
-    across = from_peer(mine, "y_lo", 1)
-    return mine, across, from_sibling(mine), from_sibling(across)
-
-
 def with_quarter(count):
     return [pl.BlockSpec(memory_space=m) for m in (pltpu.SMEM, *[pltpu.VMEM] * count)]
 
 
-def gram_total(quarter, factors, parts, rank, beside=()):
+def gram_total(quarter, factors, parts, rank, beside=(), others=()):
     tiles = (lax.axis_size(ROW), RANK + rank // 2 // lax.axis_size(ROW), rank)
     mine, other = call(
         gram_and_cores,
@@ -346,8 +348,8 @@
         in_specs=with_quarter(6),
         scratch_shapes=[pltpu.VMEM((rank, rank), jnp.float32)],
     )
-    other, beside = lax.optimization_barrier((from_sibling(other), beside))
-    return row_total(mine + other), beside
+    other, beside = together(from_sibling(other), beside)
+    return *row_total(mine + other, parts, others), beside
 
 
 def local(b_factors, a_factors, u_start, v_start):
@@ -371,6 +373,7 @@
     )
     copies = (lax.axis_size(ROW), 2 * RANK, rank)
     pair = exchanged(call(owner_coefficients, [copies], exchanged(partial, "row")), ROW)
+    pair, b_quarters = together(pair, b_quarters)
     pair_other = from_sibling(pair)
 
     part = (width // 8, rank)
@@ -378,8 +381,9 @@
         load_sum, [part, part], quarter, *b_quarters, pair, pair_other, in_specs=with_quarter(6)
     )
     parts = plane_total(*parts)
-    basis = basis_quarters(*parts)
-    mine, _ = gram_total(quarter, b_quarters, parts, rank)
+    mine, basis, a_quarters, _ = gram_total(
+        quarter, b_quarters, parts, rank, others=a_quarters
+    )
     inverse, left, *parts = call(
         turn_over,
         [(rank, rank), shape, part, part],
@@ -404,8 +408,7 @@
         ),
     )
     parts = plane_total(*parts)
-    basis = basis_quarters(*parts)
-    mine, u_scaled = gram_total(quarter, a_quarters, parts, rank, u_scaled)
+    mine, basis, _, u_scaled = gram_total(quarter, a_quarters, parts, rank, u_scaled)
     v_scaled, right = call(
         finish,
         [(width, rank), shape],

time: 156 us -> 166 us (1.064)
  blocking collectives: 67.6 us -> 14.5 us
  waiting for transfers between devices: 38.3 us -> 70.5 us
  starting transfers between devices: 26 us -> 52.7 us
    all_to_all x5 -> x1, blocking collectives: 67.6 us -> 14.5 us  [exchanged(): return lax.all_to_all(tiles, axis, 0, 0, tiled=True)]
    ppermute x25, waiting for transfers between devices: 30.5 us -> 63.7 us  [from_peer(): return lax.ppermute(x, axis, [(i, i ^ step) for i in range(count)])]
    all_to_all x1 -> x5, starting transfers between devices: 4.85 us -> 34.4 us  [exchanged(): return lax.all_to_all(tiles, axis, 0, 0, tiled=True)]
    ppermute x25, starting transfers between devices: 21.2 us -> 18.3 us  [from_peer(): return lax.ppermute(x, axis, [(i, i ^ step) for i in range(count)])]
    all_to_all x1 -> x5, waiting for transfers between devices: 7.85 us -> 6.79 us  [exchanged(): return lax.all_to_all(tiles, axis, 0, 0, tiled=True)]
  transfers between devices with their start and end apart: 26 -> 30, of which waited for: 16 -> 20; matrix products, arithmetic and copies ran while one was open for 0% -> 0% of each run, Pallas kernels for 1% -> 1%
where the time goes in v7:
time: 166 us; the launch traced here: 163 us
  waiting for transfers between devices  70.5 us (42%)
  starting transfers between devices  52.7 us (32%)
  Pallas kernels  22.9 us (14%)
  blocking collectives  14.5 us (9%)
  other arithmetic  1.78 us (1%)
    ppermute x25, waiting for transfers between devices, from_peer(): return lax.ppermute(x, axis, [(i, i ^ step) for i in range(count)])  63.7 us
    all_to_all x5, starting transfers between devices, exchanged(): return lax.all_to_all(tiles, axis, 0, 0, tiled=True)  34.4 us
    pallas_call x10, Pallas kernels, call(): pl.pallas_call(kernel, out_shape=shapes if len(shapes) > 1 else shapes[0]...  22.9 us
    ppermute x25, starting transfers between devices, from_peer(): return lax.ppermute(x, axis, [(i, i ^ step) for i in range(count)])  18.3 us
    all_to_all x1, blocking collectives, exchanged(): return lax.all_to_all(tiles, axis, 0, 0, tiled=True)  14.5 us
    all_to_all x5, waiting for transfers between devices, exchanged(): return lax.all_to_all(tiles, axis, 0, 0, tiled=True)  6.79 us
  transfers between devices with their start and end apart: 30, of which 20 were waited for; matrix products, arithmetic and copies ran while one was open for 0% of the time, Pallas kernels for 1%

profile of v7, /device:TPU:8, one launch (start us, length us, event | category | flops | bytes accessed | tf_op | source)
XLA Modules:
  0.0 163.3 jit_solution(14916724443057711354)
XLA Ops:
  0.6 2.5 %projections.1 = f32[8,32,256]{2,1,0:T(8,128)S(1)} custom-call(f32[128,1024]{1,0:T(8,128)} %bitcast.3, f32[128,1024]{1,0:T(8,128)} %bitcast.5, f32[1024,256]{1,0:T(8,128)} %u_hbm.1, f32[1024,256]{1,0:T(8,128)} %v_hbm.1), custom_call_target="tpu_custom_call" | custom-call | tf_op jit(solution)/shard_map/projections/pallas_call | solution.py:154
  3.1 14.5 %all_to_all.30.tiles_ref = f32[8,32,256]{2,1,0:T(8,128)S(1)} all-to-all(f32[8,32,256]{2,1,0:T(8,128)S(1)} %projections.1), channel_id=1, replica_groups=mesh['z'=4,'y_lo'=2,'core'=2,'row'=8] {'row'}, dimensions={0} | all-to-all | bytes 524288 | tf_op jit(solution)/shard_map/all_to_all | solution.py:295
  17.7 1.1 owner_coefficients.1
  18.8 4.9 %all-to-all-start.1 = ((f32[16,32,256]{2,1,0:T(8,128)}), f32[16,32,256]{2,1,0:T(8,128)S(1)}, u32[]{:S(2)}, u32[]{:S(2)}) async-start(f32[16,32,256]{2,1,0:T(8,128)} %owner_coefficients.1), calls=%async_computation.1 | async-start | bytes 1048576 | tf_op jit(solution)/shard_map/all_to_all | solution.py:295
  23.8 0.3 collective-permute-start.1
  24.1 1.8 %collective-permute-start = (f32[128,256]{1,0:T(8,128)S(1)}, f32[128,256]{1,0:T(8,128)S(1)}, u32[]{:S(2)}, u32[]{:S(2)}) collective-permute-start(f32[128,256]{1,0:T(8,128)S(1)} %get-tuple-element.76), channel_id=1, source_target_pairs={{0,16},{8,24},{16,0},{24,8},{1,17},{9,25},{17,1},{25,9},{2,18},{10... | collective-permute-start | bytes 393224 | tf_op jit(solution)/shard_map/ppermute | solution.py:300
  25.9 7.1 %collective-permute-done.2.f3 = f32[128,256]{1,0:T(8,128)S(1)} collective-permute-done((f32[128,256]{1,0:T(8,128)S(1)}, f32[128,256]{1,0:T(8,128)S(1)}, u32[]{:S(2)}, u32[]{:S(2)}) %collective-permute-start.2) | collective-permute-done | bytes 131104 | tf_op jit(solution)/shard_map/ppermute | solution.py:300
  33.0 2.4 %collective-permute-done.f1 = f32[128,256]{1,0:T(8,128)S(1)} collective-permute-done((f32[128,256]{1,0:T(8,128)S(1)}, f32[128,256]{1,0:T(8,128)S(1)}, u32[]{:S(2)}, u32[]{:S(2)}) %collective-permute-start) | collective-permute-done | bytes 131104 | tf_op jit(solution)/shard_map/ppermute | solution.py:300
  35.6 1.8 %collective-permute-done.3.other_ref.pair_other_ref = f32[16,32,256]{2,1,0:T(8,128)S(1)} collective-permute-done((f32[16,32,256]{2,1,0:T(8,128)S(1)}, f32[16,32,256]{2,1,0:T(8,128)S(1)}, u32[]{:S(2)}, u32[]{:S(2)}) %collective-permute-start.3) | collective-permute-done | bytes 524320 | tf_op jit(solution)/shard_map/ppermute | solution.py:300
  37.4 0.4 load_sum.1
  37.8 2.0 %collective-permute-start.4 = (f32[128,256]{1,0:T(8,128)S(1)}, f32[128,256]{1,0:T(8,128)S(1)}, u32[]{:S(2)}, u32[]{:S(2)}) collective-permute-start(f32[128,256]{1,0:T(8,128)S(1)} %get-tuple-element.42), channel_id=1, source_target_pairs={{0,32},{32,0},{64,96},{96,64},{1,33},{33,1},{65,97},{97,65},{2,34}... | collective-permute-start | bytes 393224 | tf_op jit(solution)/shard_map/ppermute | solution.py:300
  39.8 2.5 %collective-permute-start.6 = (f32[128,256]{1,0:T(8,128)S(1)}, f32[128,256]{1,0:T(8,128)S(1)}, u32[]{:S(2)}, u32[]{:S(2)}) collective-permute-start(f32[128,256]{1,0:T(8,128)S(1)} %get-tuple-element.43), channel_id=1, source_target_pairs={{0,96},{32,64},{64,32},{96,0},{1,97},{33,65},{65,33},{97,1},{2,98}... | collective-permute-start | bytes 393224 | tf_op jit(solution)/shard_map/ppermute | solution.py:300
  42.3 1.3 collective-permute-done.4
  43.6 3.9 %collective-permute-start.5 = (f32[128,256]{1,0:T(8,128)S(1)}, f32[128,256]{1,0:T(8,128)S(1)}, u32[]{:S(2)}, u32[]{:S(2)}) collective-permute-start(f32[128,256]{1,0:T(8,128)S(1)} %add.54), channel_id=1, source_target_pairs={{0,96},{32,64},{64,32},{96,0},{1,97},{33,65},{65,33},{97,1},{2,98}... | collective-permute-start | bytes 393224 | tf_op jit(solution)/shard_map/ppermute | solution.py:300
  47.7 2.8 %collective-permute-done.5 = f32[128,256]{1,0:T(8,128)S(1)} collective-permute-done((f32[128,256]{1,0:T(8,128)S(1)}, f32[128,256]{1,0:T(8,128)S(1)}, u32[]{:S(2)}, u32[]{:S(2)}) %collective-permute-start.5) | collective-permute-done | bytes 131104 | tf_op jit(solution)/shard_map/ppermute | solution.py:300
  50.5 2.1 %collective-permute-done.7 = f32[128,256]{1,0:T(8,128)S(1)} collective-permute-done((f32[128,256]{1,0:T(8,128)S(1)}, f32[128,256]{1,0:T(8,128)S(1)}, u32[]{:S(2)}, u32[]{:S(2)}) %collective-permute-start.7) | collective-permute-done | bytes 131104 | tf_op jit(solution)/shard_map/ppermute | solution.py:300
  52.6 0.5 gram_and_cores.2
  53.3 1.7 %collective-permute-done.8 = f32[16,24,256]{2,1,0:T(8,128)S(1)} collective-permute-done((f32[16,24,256]{2,1,0:T(8,128)S(1)}, f32[16,24,256]{2,1,0:T(8,128)S(1)}, u32[]{:S(2)}, u32[]{:S(2)}) %collective-permute-start.8) | collective-permute-done | bytes 393248 | tf_op jit(solution)/shard_map/ppermute | solution.py:300
  55.0 0.8 add.58
  55.8 7.1 %all-to-all-start.2 = ((f32[16,24,256]{2,1,0:T(8,128)}), f32[16,24,256]{2,1,0:T(8,128)S(1)}, u32[]{:S(2)}, u32[]{:S(2)}) async-start(f32[16,24,256]{2,1,0:T(8,128)} %add.58), calls=%async_computation.2 | async-start | bytes 786432 | tf_op jit(solution)/shard_map/all_to_all | solution.py:295
  63.1 10.8 %collective-permute-done.9.q1 = f32[256,256]{1,0:T(8,128)S(1)} collective-permute-done((f32[256,256]{1,0:T(8,128)S(1)}, f32[256,256]{1,0:T(8,128)S(1)}, u32[]{:S(2)}, u32[]{:S(2)}) %collective-permute-start.9) | collective-permute-done | bytes 262176 | tf_op jit(solution)/shard_map/ppermute | solution.py:300
  74.0 0.8 owner_sum.2
  74.8 7.9 %all-to-all-start.3 = ((f32[16,24,256]{2,1,0:T(8,128)}), f32[16,24,256]{2,1,0:T(8,128)S(1)}, u32[]{:S(2)}, u32[]{:S(2)}) async-start(f32[16,24,256]{2,1,0:T(8,128)} %owner_sum.2), calls=%async_computation.3 | async-start | bytes 786432 | tf_op jit(solution)/shard_map/all_to_all | solution.py:295
  82.7 0.5 collective-permute-start.11
  83.3 0.3 collective-permute-start.13
  83.6 1.9 %collective-permute-start.12 = (f32[128,256]{1,0:T(8,128)S(1)}, f32[128,256]{1,0:T(8,128)S(1)}, u32[]{:S(2)}, u32[]{:S(2)}) collective-permute-start(f32[128,256]{1,0:T(8,128)S(1)} %get-tuple-element.72), channel_id=1, source_target_pairs={{0,16},{8,24},{16,0},{24,8},{1,17},{9,25},{17,1},{25,9},{2,18},{10... | collective-permute-start | bytes 393224 | tf_op jit(solution)/shard_map/ppermute | solution.py:300
  85.5 6.1 %collective-permute-done.14.f3 = f32[128,256]{1,0:T(8,128)S(1)} collective-permute-done((f32[128,256]{1,0:T(8,128)S(1)}, f32[128,256]{1,0:T(8,128)S(1)}, u32[]{:S(2)}, u32[]{:S(2)}) %collective-permute-start.14) | collective-permute-done | bytes 131104 | tf_op jit(solution)/shard_map/ppermute | solution.py:300
  91.6 3.0 %collective-permute-done.12.f1 = f32[128,256]{1,0:T(8,128)S(1)} collective-permute-done((f32[128,256]{1,0:T(8,128)S(1)}, f32[128,256]{1,0:T(8,128)S(1)}, u32[]{:S(2)}, u32[]{:S(2)}) %collective-permute-start.12) | collective-permute-done | bytes 131104 | tf_op jit(solution)/shard_map/ppermute | solution.py:300
  94.9 1.7 %collective-permute-done.15.other_ref = f32[16,24,256]{2,1,0:T(8,128)S(1)} collective-permute-done((f32[16,24,256]{2,1,0:T(8,128)S(1)}, f32[16,24,256]{2,1,0:T(8,128)S(1)}, u32[]{:S(2)}, u32[]{:S(2)}) %collective-permute-start.15) | collective-permute-done | bytes 393248 | tf_op jit(solution)/shard_map/ppermute | solution.py:300
  96.6 7.3 %turn_over.1 = (f32[256,256]{1,0:T(8,128)S(1)}, f32[8,16,256]{2,1,0:T(8,128)}, f32[128,256]{1,0:T(8,128)S(1)}, f32[128,256]{1,0:T(8,128)S(1)}) custom-call(s32[1]{0:T(128)} %bitcast.quarter_ref, f32[16,24,256]{2,1,0:T(8,128)S(1)} %all-to-all-done.3.mine_ref, f32[16,24,256]{2,1,0:T(8,128)S(1)} %collective-permute-done.15.other_ref, ...), custom_call_target="tpu_custom_call" | custom-call | tf_op jit(solution)/shard_map/turn_over/pallas_call | solution.py:154
  103.9 1.6 %collective-permute-start.18 = (f32[128,256]{1,0:T(8,128)S(1)}, f32[128,256]{1,0:T(8,128)S(1)}, u32[]{:S(2)}, u32[]{:S(2)}) collective-permute-start(f32[128,256]{1,0:T(8,128)S(1)} %get-tuple-element.54), channel_id=1, source_target_pairs={{0,96},{32,64},{64,32},{96,0},{1,97},{33,65},{65,33},{97,1},{2,98}... | collective-permute-start | bytes 393224 | tf_op jit(solution)/shard_map/ppermute | solution.py:300
  105.5 3.9 %collective-permute-done.16 = f32[128,256]{1,0:T(8,128)S(1)} collective-permute-done((f32[128,256]{1,0:T(8,128)S(1)}, f32[128,256]{1,0:T(8,128)S(1)}, u32[]{:S(2)}, u32[]{:S(2)}) %collective-permute-start.16) | collective-permute-done | bytes 131104 | tf_op jit(solution)/shard_map/ppermute | solution.py:300
  109.5 1.3 collective-permute-start.17
  110.8 0.5 collective-permute-start.19
  111.3 4.4 %collective-permute-done.17 = f32[128,256]{1,0:T(8,128)S(1)} collective-permute-done((f32[128,256]{1,0:T(8,128)S(1)}, f32[128,256]{1,0:T(8,128)S(1)}, u32[]{:S(2)}, u32[]{:S(2)}) %collective-permute-start.17) | collective-permute-done | bytes 131104 | tf_op jit(solution)/shard_map/ppermute | solution.py:300
  115.9 0.5 gram_and_cores.3
  116.5 1.6 left_basis.1
  118.2 0.8 add.63
  119.0 6.6 %all-to-all-start.4 = ((f32[16,24,256]{2,1,0:T(8,128)}), f32[16,24,256]{2,1,0:T(8,128)S(1)}, u32[]{:S(2)}, u32[]{:S(2)}) async-start(f32[16,24,256]{2,1,0:T(8,128)} %add.63), calls=%async_computation.4 | async-start | bytes 786432 | tf_op jit(solution)/shard_map/all_to_all | solution.py:295
  125.8 11.1 %collective-permute-done.21.q1 = f32[256,256]{1,0:T(8,128)S(1)} collective-permute-done((f32[256,256]{1,0:T(8,128)S(1)}, f32[256,256]{1,0:T(8,128)S(1)}, u32[]{:S(2)}, u32[]{:S(2)}) %collective-permute-start.21) | collective-permute-done | bytes 262176 | tf_op jit(solution)/shard_map/ppermute | solution.py:300
  136.9 0.8 owner_sum.3
  137.7 7.8 %all-to-all-start.5 = ((f32[16,24,256]{2,1,0:T(8,128)}), f32[16,24,256]{2,1,0:T(8,128)S(1)}, u32[]{:S(2)}, u32[]{:S(2)}) async-start(f32[16,24,256]{2,1,0:T(8,128)} %owner_sum.3), calls=%async_computation.5 | async-start | bytes 786432 | tf_op jit(solution)/shard_map/all_to_all | solution.py:295
  145.5 0.5 collective-permute-start.23
  146.0 1.0 collective-permute-done.22.q2
  147.1 0.4 collective-permute-done.23.q3
  147.4 6.8 %all-to-all-done.5.mine_ref = f32[16,24,256]{2,1,0:T(8,128)S(1)} async-done(((f32[16,24,256]{2,1,0:T(8,128)}), f32[16,24,256]{2,1,0:T(8,128)S(1)}, u32[]{:S(2)}, u32[]{:S(2)}) %all-to-all-start.5) | async-done | bytes 393248 | tf_op jit(solution)/shard_map/all_to_all | solution.py:295
  154.2 1.7 %collective-permute-done.24.other_ref = f32[16,24,256]{2,1,0:T(8,128)S(1)} collective-permute-done((f32[16,24,256]{2,1,0:T(8,128)S(1)}, f32[16,24,256]{2,1,0:T(8,128)S(1)}, u32[]{:S(2)}, u32[]{:S(2)}) %collective-permute-start.24) | collective-permute-done | bytes 393248 | tf_op jit(solution)/shard_map/ppermute | solution.py:300
  155.9 7.3 %finish.1 = (f32[1024,256]{1,0:T(8,128)}, f32[8,16,256]{2,1,0:T(8,128)}) custom-call(s32[1]{0:T(128)} %bitcast.quarter_ref, f32[16,24,256]{2,1,0:T(8,128)S(1)} %all-to-all-done.5.mine_ref, f32[16,24,256]{2,1,0:T(8,128)S(1)} %collective-permute-done.24.other_ref, f32[256,256]{1,0:T(8,128)S(1)} %pad_maximum_fusion.1.q0, ...), custom_call_target="tpu_custom_call" | custom-call | tf_op jit(solution)/shard_map/finish/pallas_call | solution.py:154
  (41 shorter events, 1.6 us)
Async XLA Ops:
  18.7 4.9 %copy-start = (f32[8,16,1024]{2,1,0:T(8,128)S(1)}, f32[8,16,1024]{2,1,0:T(8,128)}, u32[]{:S(2)}) copy-start(f32[8,16,1024]{2,1,0:T(8,128)} %param.4) | copy-start | bytes 1572868
  18.8 16.7 %all-to-all-start.1 = ((f32[16,32,256]{2,1,0:T(8,128)}), f32[16,32,256]{2,1,0:T(8,128)S(1)}, u32[]{:S(2)}, u32[]{:S(2)}) async-start(f32[16,32,256]{2,1,0:T(8,128)} %owner_coefficients.1), calls=%async_computation.1 | async-start | bytes 1048576 | tf_op jit(solution)/shard_map/all_to_all | solution.py:295
  23.7 9.3 %collective-permute-start.2 = (f32[128,256]{1,0:T(8,128)S(1)}, f32[128,256]{1,0:T(8,128)S(1)}, u32[]{:S(2)}, u32[]{:S(2)}) collective-permute-start(f32[128,256]{1,0:T(8,128)S(1)} %get-tuple-element.74), channel_id=1, source_target_pairs={{0,24},{8,16},{16,8},{24,0},{1,25},{9,17},{17,9},{25,1},{2,26},{10... | collective-permute-start | bytes 393224 | tf_op jit(solution)/shard_map/ppermute | solution.py:300
  23.8 9.2 %collective-permute-start.1 = (f32[128,256]{1,0:T(8,128)S(1)}, f32[128,256]{1,0:T(8,128)S(1)}, u32[]{:S(2)}, u32[]{:S(2)}) collective-permute-start(f32[128,256]{1,0:T(8,128)S(1)} %get-tuple-element.75), channel_id=1, source_target_pairs={{0,8},{8,0},{16,24},{24,16},{1,9},{9,1},{17,25},{25,17},{2,10},{10... | collective-permute-start | bytes 393224 | tf_op jit(solution)/shard_map/ppermute | solution.py:300
  24.1 11.3 %collective-permute-start = (f32[128,256]{1,0:T(8,128)S(1)}, f32[128,256]{1,0:T(8,128)S(1)}, u32[]{:S(2)}, u32[]{:S(2)}) collective-permute-start(f32[128,256]{1,0:T(8,128)S(1)} %get-tuple-element.76), channel_id=1, source_target_pairs={{0,16},{8,24},{16,0},{24,8},{1,17},{9,25},{17,1},{25,9},{2,18},{10... | collective-permute-start | bytes 393224 | tf_op jit(solution)/shard_map/ppermute | solution.py:300
  35.4 1.9 %collective-permute-start.3 = (f32[16,32,256]{2,1,0:T(8,128)S(1)}, f32[16,32,256]{2,1,0:T(8,128)S(1)}, u32[]{:S(2)}, u32[]{:S(2)}) collective-permute-start(f32[16,32,256]{2,1,0:T(8,128)S(1)} %all-to-all-done.1.mine_ref.pair_ref), channel_id=1, source_target_pairs={{0,8},{8,0},{1,9},{9,1},{2,10},{10,2},{3,11},{11,3},{4,12},{12,4},... | collective-permute-start | bytes 1572872 | tf_op jit(solution)/shard_map/ppermute | solution.py:300
  37.8 5.8 %collective-permute-start.4 = (f32[128,256]{1,0:T(8,128)S(1)}, f32[128,256]{1,0:T(8,128)S(1)}, u32[]{:S(2)}, u32[]{:S(2)}) collective-permute-start(f32[128,256]{1,0:T(8,128)S(1)} %get-tuple-element.42), channel_id=1, source_target_pairs={{0,32},{32,0},{64,96},{96,64},{1,33},{33,1},{65,97},{97,65},{2,34}... | collective-permute-start | bytes 393224 | tf_op jit(solution)/shard_map/ppermute | solution.py:300
  39.8 7.8 %collective-permute-start.6 = (f32[128,256]{1,0:T(8,128)S(1)}, f32[128,256]{1,0:T(8,128)S(1)}, u32[]{:S(2)}, u32[]{:S(2)}) collective-permute-start(f32[128,256]{1,0:T(8,128)S(1)} %get-tuple-element.43), channel_id=1, source_target_pairs={{0,96},{32,64},{64,32},{96,0},{1,97},{33,65},{65,33},{97,1},{2,98}... | collective-permute-start | bytes 393224 | tf_op jit(solution)/shard_map/ppermute | solution.py:300
  43.6 6.9 %collective-permute-start.5 = (f32[128,256]{1,0:T(8,128)S(1)}, f32[128,256]{1,0:T(8,128)S(1)}, u32[]{:S(2)}, u32[]{:S(2)}) collective-permute-start(f32[128,256]{1,0:T(8,128)S(1)} %add.54), channel_id=1, source_target_pairs={{0,96},{32,64},{64,32},{96,0},{1,97},{33,65},{65,33},{97,1},{2,98}... | collective-permute-start | bytes 393224 | tf_op jit(solution)/shard_map/ppermute | solution.py:300
  47.6 5.0 %collective-permute-start.7 = (f32[128,256]{1,0:T(8,128)S(1)}, f32[128,256]{1,0:T(8,128)S(1)}, u32[]{:S(2)}, u32[]{:S(2)}) collective-permute-start(f32[128,256]{1,0:T(8,128)S(1)} %add.56), channel_id=1, source_target_pairs={{0,32},{32,0},{64,96},{96,64},{1,33},{33,1},{65,97},{97,65},{2,34}... | collective-permute-start | bytes 393224 | tf_op jit(solution)/shard_map/ppermute | solution.py:300
  53.2 1.8 %collective-permute-start.8 = (f32[16,24,256]{2,1,0:T(8,128)S(1)}, f32[16,24,256]{2,1,0:T(8,128)S(1)}, u32[]{:S(2)}, u32[]{:S(2)}) collective-permute-start(f32[16,24,256]{2,1,0:T(8,128)S(1)} %get-tuple-element.45), channel_id=1, source_target_pairs={{0,8},{8,0},{1,9},{9,1},{2,10},{10,2},{3,11},{11,3},{4,12},{12,4},... | collective-permute-start | bytes 1179656 | tf_op jit(solution)/shard_map/ppermute | solution.py:300
  55.8 18.2 %all-to-all-start.2 = ((f32[16,24,256]{2,1,0:T(8,128)}), f32[16,24,256]{2,1,0:T(8,128)S(1)}, u32[]{:S(2)}, u32[]{:S(2)}) async-start(f32[16,24,256]{2,1,0:T(8,128)} %add.58), calls=%async_computation.2 | async-start | bytes 786432 | tf_op jit(solution)/shard_map/all_to_all | solution.py:295
  62.9 11.0 %collective-permute-start.9 = (f32[256,256]{1,0:T(8,128)S(1)}, f32[256,256]{1,0:T(8,128)S(1)}, u32[]{:S(2)}, u32[]{:S(2)}) collective-permute-start(f32[256,256]{1,0:T(8,128)S(1)} %pad_maximum_fusion.q0), channel_id=1, source_target_pairs={{0,16},{16,0},{1,17},{17,1},{2,18},{18,2},{3,19},{19,3},{4,20},{20... | collective-permute-start | bytes 786440 | tf_op jit(solution)/shard_map/ppermute | solution.py:300
  74.8 8.5 %copy-start.1 = (f32[8,16,1024]{2,1,0:T(8,128)S(1)}, f32[8,16,1024]{2,1,0:T(8,128)}, u32[]{:S(2)}) copy-start(f32[8,16,1024]{2,1,0:T(8,128)} %param.5) | copy-start | bytes 1572868
  74.8 19.8 %all-to-all-start.3 = ((f32[16,24,256]{2,1,0:T(8,128)}), f32[16,24,256]{2,1,0:T(8,128)S(1)}, u32[]{:S(2)}, u32[]{:S(2)}) async-start(f32[16,24,256]{2,1,0:T(8,128)} %owner_sum.2), calls=%async_computation.3 | async-start | bytes 786432 | tf_op jit(solution)/shard_map/all_to_all | solution.py:295
  82.7 11.9 %collective-permute-start.10 = (f32[256,256]{1,0:T(8,128)S(1)}, f32[256,256]{1,0:T(8,128)S(1)}, u32[]{:S(2)}, u32[]{:S(2)}) collective-permute-start(f32[256,256]{1,0:T(8,128)S(1)} %pad_maximum_fusion.q0), channel_id=1, source_target_pairs={{0,8},{8,0},{1,9},{9,1},{2,10},{10,2},{3,11},{11,3},{4,12},{12,4},... | collective-permute-start | bytes 786440 | tf_op jit(solution)/shard_map/ppermute | solution.py:300
  82.7 11.9 %collective-permute-start.11 = (f32[256,256]{1,0:T(8,128)S(1)}, f32[256,256]{1,0:T(8,128)S(1)}, u32[]{:S(2)}, u32[]{:S(2)}) collective-permute-start(f32[256,256]{1,0:T(8,128)S(1)} %collective-permute-done.9.q1), channel_id=1, source_target_pairs={{0,8},{8,0},{1,9},{9,1},{2,10},{10,2},{3,11},{11,3},{4,12},{12,4},... | collective-permute-start | bytes 786440 | tf_op jit(solution)/shard_map/ppermute | solution.py:300
  83.3 8.3 %collective-permute-start.14 = (f32[128,256]{1,0:T(8,128)S(1)}, f32[128,256]{1,0:T(8,128)S(1)}, u32[]{:S(2)}, u32[]{:S(2)}) collective-permute-start(f32[128,256]{1,0:T(8,128)S(1)} %get-tuple-element.70), channel_id=1, source_target_pairs={{0,24},{8,16},{16,8},{24,0},{1,25},{9,17},{17,9},{25,1},{2,26},{10... | collective-permute-start | bytes 393224 | tf_op jit(solution)/shard_map/ppermute | solution.py:300
  83.3 8.2 %collective-permute-start.13 = (f32[128,256]{1,0:T(8,128)S(1)}, f32[128,256]{1,0:T(8,128)S(1)}, u32[]{:S(2)}, u32[]{:S(2)}) collective-permute-start(f32[128,256]{1,0:T(8,128)S(1)} %get-tuple-element.71), channel_id=1, source_target_pairs={{0,8},{8,0},{16,24},{24,16},{1,9},{9,1},{17,25},{25,17},{2,10},{10... | collective-permute-start | bytes 393224 | tf_op jit(solution)/shard_map/ppermute | solution.py:300
  83.6 10.9 %collective-permute-start.12 = (f32[128,256]{1,0:T(8,128)S(1)}, f32[128,256]{1,0:T(8,128)S(1)}, u32[]{:S(2)}, u32[]{:S(2)}) collective-permute-start(f32[128,256]{1,0:T(8,128)S(1)} %get-tuple-element.72), channel_id=1, source_target_pairs={{0,16},{8,24},{16,0},{24,8},{1,17},{9,25},{17,1},{25,9},{2,18},{10... | collective-permute-start | bytes 393224 | tf_op jit(solution)/shard_map/ppermute | solution.py:300
  94.6 2.0 %collective-permute-start.15 = (f32[16,24,256]{2,1,0:T(8,128)S(1)}, f32[16,24,256]{2,1,0:T(8,128)S(1)}, u32[]{:S(2)}, u32[]{:S(2)}) collective-permute-start(f32[16,24,256]{2,1,0:T(8,128)S(1)} %all-to-all-done.3.mine_ref), channel_id=1, source_target_pairs={{0,8},{8,0},{1,9},{9,1},{2,10},{10,2},{3,11},{11,3},{4,12},{12,4},... | collective-permute-start | bytes 1179656 | tf_op jit(solution)/shard_map/ppermute | solution.py:300
  103.9 5.5 %collective-permute-start.16 = (f32[128,256]{1,0:T(8,128)S(1)}, f32[128,256]{1,0:T(8,128)S(1)}, u32[]{:S(2)}, u32[]{:S(2)}) collective-permute-start(f32[128,256]{1,0:T(8,128)S(1)} %get-tuple-element.53), channel_id=1, source_target_pairs={{0,32},{32,0},{64,96},{96,64},{1,33},{33,1},{65,97},{97,65},{2,34}... | collective-permute-start | bytes 393224 | tf_op jit(solution)/shard_map/ppermute | solution.py:300
  103.9 6.9 %collective-permute-start.18 = (f32[128,256]{1,0:T(8,128)S(1)}, f32[128,256]{1,0:T(8,128)S(1)}, u32[]{:S(2)}, u32[]{:S(2)}) collective-permute-start(f32[128,256]{1,0:T(8,128)S(1)} %get-tuple-element.54), channel_id=1, source_target_pairs={{0,96},{32,64},{64,32},{96,0},{1,97},{33,65},{65,33},{97,1},{2,98}... | collective-permute-start | bytes 393224 | tf_op jit(solution)/shard_map/ppermute | solution.py:300
  109.5 6.3 %collective-permute-start.17 = (f32[128,256]{1,0:T(8,128)S(1)}, f32[128,256]{1,0:T(8,128)S(1)}, u32[]{:S(2)}, u32[]{:S(2)}) collective-permute-start(f32[128,256]{1,0:T(8,128)S(1)} %add.59), channel_id=1, source_target_pairs={{0,96},{32,64},{64,32},{96,0},{1,97},{33,65},{65,33},{97,1},{2,98}... | collective-permute-start | bytes 393224 | tf_op jit(solution)/shard_map/ppermute | solution.py:300
  110.8 5.0 %collective-permute-start.19 = (f32[128,256]{1,0:T(8,128)S(1)}, f32[128,256]{1,0:T(8,128)S(1)}, u32[]{:S(2)}, u32[]{:S(2)}) collective-permute-start(f32[128,256]{1,0:T(8,128)S(1)} %add.61), channel_id=1, source_target_pairs={{0,32},{32,0},{64,96},{96,64},{1,33},{33,1},{65,97},{97,65},{2,34}... | collective-permute-start | bytes 393224 | tf_op jit(solution)/shard_map/ppermute | solution.py:300
  116.4 1.8 %collective-permute-start.20 = (f32[16,24,256]{2,1,0:T(8,128)S(1)}, f32[16,24,256]{2,1,0:T(8,128)S(1)}, u32[]{:S(2)}, u32[]{:S(2)}) collective-permute-start(f32[16,24,256]{2,1,0:T(8,128)S(1)} %get-tuple-element.55), channel_id=1, source_target_pairs={{0,8},{8,0},{1,9},{9,1},{2,10},{10,2},{3,11},{11,3},{4,12},{12,4},... | collective-permute-start | bytes 1179656 | tf_op jit(solution)/shard_map/ppermute | solution.py:300
  119.0 17.9 %all-to-all-start.4 = ((f32[16,24,256]{2,1,0:T(8,128)}), f32[16,24,256]{2,1,0:T(8,128)S(1)}, u32[]{:S(2)}, u32[]{:S(2)}) async-start(f32[16,24,256]{2,1,0:T(8,128)} %add.63), calls=%async_computation.4 | async-start | bytes 786432 | tf_op jit(solution)/shard_map/all_to_all | solution.py:295
  125.6 11.3 %collective-permute-start.21 = (f32[256,256]{1,0:T(8,128)S(1)}, f32[256,256]{1,0:T(8,128)S(1)}, u32[]{:S(2)}, u32[]{:S(2)}) collective-permute-start(f32[256,256]{1,0:T(8,128)S(1)} %pad_maximum_fusion.1.q0), channel_id=1, source_target_pairs={{0,16},{16,0},{1,17},{17,1},{2,18},{18,2},{3,19},{19,3},{4,20},{20... | collective-permute-start | bytes 786440 | tf_op jit(solution)/shard_map/ppermute | solution.py:300
  137.7 16.5 %all-to-all-start.5 = ((f32[16,24,256]{2,1,0:T(8,128)}), f32[16,24,256]{2,1,0:T(8,128)S(1)}, u32[]{:S(2)}, u32[]{:S(2)}) async-start(f32[16,24,256]{2,1,0:T(8,128)} %owner_sum.3), calls=%async_computation.5 | async-start | bytes 786432 | tf_op jit(solution)/shard_map/all_to_all | solution.py:295
  145.5 1.5 collective-permute-start.22
  145.5 1.9 %collective-permute-start.23 = (f32[256,256]{1,0:T(8,128)S(1)}, f32[256,256]{1,0:T(8,128)S(1)}, u32[]{:S(2)}, u32[]{:S(2)}) collective-permute-start(f32[256,256]{1,0:T(8,128)S(1)} %collective-permute-done.21.q1), channel_id=1, source_target_pairs={{0,8},{8,0},{1,9},{9,1},{2,10},{10,2},{3,11},{11,3},{4,12},{12,4},... | collective-permute-start | bytes 786440 | tf_op jit(solution)/shard_map/ppermute | solution.py:300
  154.2 1.7 %collective-permute-start.24 = (f32[16,24,256]{2,1,0:T(8,128)S(1)}, f32[16,24,256]{2,1,0:T(8,128)S(1)}, u32[]{:S(2)}, u32[]{:S(2)}) collective-permute-start(f32[16,24,256]{2,1,0:T(8,128)S(1)} %all-to-all-done.5.mine_ref), channel_id=1, source_target_pairs={{0,8},{8,0},{1,9},{9,1},{2,10},{10,2},{3,11},{11,3},{4,12},{12,4},... | collective-permute-start | bytes 1179656 | tf_op jit(solution)/shard_map/ppermute | solution.py:300

commit v8 on v7

--- a/solution.py
+++ b/solution.py
@@ -14,8 +14,7 @@
 SUBLANES = 8
 PANEL = 32
 STEPS = 4
-ROW = ("y_lo", "row")
-QUARTER = ("y_lo", "core")
+ROW = ("z_lo", "row")
 STEPS_AWAY = (0, 2, 1, 3)
 
 
@@ -204,21 +203,20 @@
     return jnp.concatenate([ref[...] for ref in refs])
 
 
-def by_distance(quarter, ref):
+def by_distance(pair, ref):
     count = len(ref) // 2
-    half = quarter // 2
-    return [pl.ds(place * count, count) for place in (half, 1 - half)]
-
-
-def tenants(quarter, refs, first):
+    return [pl.ds(place * count, count) for place in (pair, 1 - pair)]
+
+
+def tenants(pair, refs, first):
     rows = pl.ds(first, RANK)
-    tiles = [ref[place, rows] for ref in refs for place in by_distance(quarter, ref)]
+    tiles = [ref[place, rows] for ref in refs for place in by_distance(pair, ref)]
     return jnp.concatenate([matrix(x) for x in tiles])
 
 
-def load_sum(quarter_ref, f0, f1, f2, f3, mine_ref, other_ref, *out_refs):
-    coeffs = tenants(quarter_ref[0], (mine_ref, other_ref), 0)
-    store_load(product(stacked((f0, f1, f2, f3)), coeffs, 0, 0), out_refs)
+def load_sum(place_ref, f0, f1, f2, mine_ref, other_ref, *out_refs):
+    coeffs = tenants(place_ref[1], (mine_ref, other_ref), 0)
+    store_load(product(stacked((f0, f1, f2)), coeffs, 0, 0), out_refs)
 
 
 def store_load(load, out_refs):
@@ -227,15 +225,14 @@
         ref[...] = load[i * count : (i + 1) * count]
 
 
-def gram_and_cores(quarter_ref, f0, f1, f2, f3, x_ref, y_ref, mine_ref, other_ref, gram_ref):
+def gram_and_cores(place_ref, f0, f1, f2, x_ref, y_ref, mine_ref, other_ref, gram_ref):
     basis = stacked((x_ref, y_ref))
-    cores = product(stacked((f0, f1, f2, f3)), basis)
+    cores = product(stacked((f0, f1, f2)), basis)
     gram_ref[...] = product(basis, basis, 0, 0)
-    quarter = quarter_ref[0]
-    core, half = quarter % 2, len(gram_ref) // 2
+    core, half = place_ref[0] % 2, len(gram_ref) // 2
     block = len(cores) // 4
     for i, (ref, which) in enumerate(((mine_ref, core), (other_ref, 1 - core))):
-        for j, place in enumerate(by_distance(quarter, ref)):
+        for j, place in enumerate(by_distance(place_ref[1], ref)):
             rows = cores[(2 * i + j) * block : (2 * i + j + 1) * block]
             ref[place, :RANK] = rows.reshape(-1, RANK, rows.shape[1])
         rows = gram_ref[pl.ds(which * half, half), :]
@@ -250,13 +247,13 @@
 
 
 def turn_over(
-    quarter_ref, mine_ref, other_ref, pair_ref, pair_other_ref, f0, f1, f2, f3,
+    place_ref, mine_ref, other_ref, pair_ref, pair_other_ref, f0, f1, f2,
     inverse_ref, left_ref, x_ref, y_ref, *scratch,
 ):
-    quarter = quarter_ref[0]
-    inverse_factor(quarter % 2, mine_ref, other_ref, inverse_ref, *scratch)
-    left = product(tenants(quarter, (mine_ref, other_ref), 0), inverse_ref[...], 1, 1)
-    right = tenants(quarter, (pair_ref, pair_other_ref), RANK)
+    pair = place_ref[1]
+    inverse_factor(place_ref[0] % 2, mine_ref, other_ref, inverse_ref, *scratch)
+    left = product(tenants(pair, (mine_ref, other_ref), 0), inverse_ref[...], 1, 1)
+    right = tenants(pair, (pair_ref, pair_other_ref), RANK)
     own = left[: len(left) // 4]
     left_ref[...] = own.reshape(left_ref.shape)
     half = len(left) // 2
@@ -265,7 +262,7 @@
     for part in (slice(0, half), slice(half, None)):
         weight = jnp.where(tenant[0] == tenant[1], product(left[part], left[part], 1, 1), 0.0)
         coeffs.append(product(weight, right[part]))
-    load = product(stacked((f0, f1, f2, f3)), jnp.concatenate(coeffs), 0, 0)
+    load = product(stacked((f0, f1, f2)), jnp.concatenate(coeffs), 0, 0)
     store_load(load, (x_ref, y_ref))
 
 
@@ -276,17 +273,17 @@
         out_ref[rows, :] = product(ref[...], inverse, 1, 1) * scale
 
 
-def left_basis(quarter_ref, inverse_ref, q0, q1, q2, q3, out_ref):
-    scaled_basis(quarter_ref[0], inverse_ref[...], (q0, q1, q2, q3), out_ref)
+def left_basis(place_ref, inverse_ref, q0, q1, q2, q3, out_ref):
+    scaled_basis(place_ref[0], inverse_ref[...], (q0, q1, q2, q3), out_ref)
 
 
 def finish(
-    quarter_ref, mine_ref, other_ref, q0, q1, q2, q3, out_ref, right_ref, inverse_ref, *scratch
+    place_ref, mine_ref, other_ref, q0, q1, q2, q3, out_ref, right_ref, inverse_ref, *scratch
 ):
-    quarter = quarter_ref[0]
+    quarter = place_ref[0]
     inverse_factor(quarter % 2, mine_ref, other_ref, inverse_ref, *scratch)
     inverse = inverse_ref[...]
-    own = matrix(mine_ref[by_distance(quarter, mine_ref)[0], :RANK])
+    own = matrix(mine_ref[by_distance(place_ref[1], mine_ref)[0], :RANK])
     right_ref[...] = product(own, inverse, 1, 1).reshape(right_ref.shape)
     scaled_basis(quarter, inverse, (q0, q1, q2, q3), out_ref)
 
@@ -304,62 +301,75 @@
     return lax.optimization_barrier((x, others))
 
 
-def row_total(tiles, parts, others):
-    basis = jnp.concatenate(parts)
-    tiles, across = together(exchanged(tiles, ROW), from_peer(basis, "y_lo", 1))
-    whole = exchanged(call(owner_sum, [tiles.shape], tiles), ROW)
-    quarters = (from_sibling(basis), from_sibling(across))
-    whole, (quarters, others) = together(whole, (quarters, others))
-    return whole, (basis, across, *quarters), others
-
-
-def plane_total(x, y):
-    for x_step, y_step in ((1, 3), (3, 1)):
-        x, y = x + from_peer(x, "z", x_step), y + from_peer(y, "z", y_step)
-    return x, y
-
-
 def from_sibling(x):
     return from_peer(x, "core", 1)
 
 
-def column_quarters(factors, quarter):
-    size = factors.shape[1] // 4
-
-    def columns(step):
-        return lax.dynamic_slice_in_dim(factors, (quarter ^ step) * size, size, 1)
-
-    moved = [from_peer(columns(step), QUARTER, step) for step in STEPS_AWAY[1:]]
-    return columns(0), *moved
-
-
-def with_quarter(count):
+def across(x):
+    return from_peer(x, "z_lo", 1)
+
+
+def plane_total(x, y):
+    orders = (((("z_hi", "z_lo"), 3), ("y_lo", 1)), (("y_lo", 1), (("z_hi", "z_lo"), 3)))
+    for x_step, y_step in zip(*orders):
+        x, y = x + from_peer(x, *x_step), y + from_peer(y, *y_step)
+    return x, y
+
+
+def column_half(factors, bit):
+    half = factors.shape[1] // 2
+    mine, its = (
+        lax.dynamic_slice_in_dim(factors, which * half, half, 1) for which in (bit, 1 - bit)
+    )
+    return mine, across(its)
+
+
+def column_quarter(halves, core):
+    size = halves[0].shape[1] // 2
+
+    def columns(which):
+        return [lax.dynamic_slice_in_dim(x, which * size, size, 1) for x in halves]
+
+    return *columns(core), from_sibling(jnp.concatenate(columns(1 - core)))
+
+
+def with_place(count):
     return [pl.BlockSpec(memory_space=m) for m in (pltpu.SMEM, *[pltpu.VMEM] * count)]
 
 
-def gram_total(quarter, factors, parts, rank, beside=(), others=()):
+def work(products, size):
+    return pl.CostEstimate(flops=6 * products * size**3, bytes_accessed=0, transcendentals=0)
+
+
+def gram_tiles(place, factors, parts, rank, beside):
     tiles = (lax.axis_size(ROW), RANK + rank // 2 // lax.axis_size(ROW), rank)
     mine, other = call(
         gram_and_cores,
         [tiles, tiles],
-        quarter,
+        place,
         *factors,
         *parts,
-        in_specs=with_quarter(6),
+        in_specs=with_place(5),
         scratch_shapes=[pltpu.VMEM((rank, rank), jnp.float32)],
     )
     other, beside = together(from_sibling(other), beside)
-    return *row_total(mine + other, parts, others), beside
+    return mine + other, beside
+
+
+def row_total(tiles):
+    tiles = exchanged(tiles, ROW)
+    return exchanged(call(owner_sum, [tiles.shape], tiles), ROW)
 
 
 def local(b_factors, a_factors, u_start, v_start):
     shape = (*b_factors.shape[:2], u_start.shape[1])
     width, rank = u_start.shape
-    place = lax.axis_index(QUARTER)
-    quarter = jnp.reshape(place, (1,)).astype(jnp.int32)
+    pair_index, core = lax.axis_index("z_lo"), lax.axis_index("core")
+    bit = pair_index ^ lax.axis_index("z_hi")
+    place = jnp.stack([2 * bit + core, pair_index]).astype(jnp.int32)
     b = b_factors.reshape(-1, width)
     a = a_factors.reshape(-1, width)
-    b_quarters, a_quarters = column_quarters(b, place), column_quarters(a, place)
+    b_half, a_half = column_half(b, bit), column_half(a, bit)
 
     partial = call(
         projections,
@@ -372,51 +382,61 @@
         ],
     )
     copies = (lax.axis_size(ROW), 2 * RANK, rank)
-    pair = exchanged(call(owner_coefficients, [copies], exchanged(partial, "row")), ROW)
-    pair, b_quarters = together(pair, b_quarters)
+    tiles, (b_half, a_half) = together(exchanged(partial, "row"), (b_half, a_half))
+    b_quarter, a_quarter = column_quarter(b_half, core), column_quarter(a_half, core)
+    pair = exchanged(call(owner_coefficients, [copies], tiles), ROW)
+    pair, (b_quarter, a_quarter) = together(pair, (b_quarter, a_quarter))
     pair_other = from_sibling(pair)
 
     part = (width // 8, rank)
     parts = call(
-        load_sum, [part, part], quarter, *b_quarters, pair, pair_other, in_specs=with_quarter(6)
+        load_sum, [part, part], place, *b_quarter, pair, pair_other, in_specs=with_place(5)
     )
     parts = plane_total(*parts)
-    mine, basis, a_quarters, _ = gram_total(
-        quarter, b_quarters, parts, rank, others=a_quarters
-    )
+    basis = jnp.concatenate(parts)
+    tiles, _ = gram_tiles(place, b_quarter, parts, rank, ())
+    mine = row_total(tiles)
     inverse, left, *parts = call(
         turn_over,
         [(rank, rank), shape, part, part],
-        quarter,
+        place,
         mine,
         from_sibling(mine),
         pair,
         pair_other,
-        *a_quarters,
-        in_specs=with_quarter(8),
+        *a_quarter,
+        in_specs=with_place(7),
         scratch_shapes=factor_scratch(rank),
-    )
+        cost_estimate=work(64, rank),
+    )
+    parts, moved = together(parts, across(basis))
+    parts = plane_total(*parts)
     u_scaled = call(
         left_basis,
         [(width, rank)],
-        quarter,
+        place,
         inverse,
-        *basis,
-        in_specs=with_quarter(5),
-        cost_estimate=pl.CostEstimate(
-            flops=6 * width * rank * rank, bytes_accessed=8 * width * rank, transcendentals=0
-        ),
-    )
-    parts = plane_total(*parts)
-    mine, basis, _, u_scaled = gram_total(quarter, a_quarters, parts, rank, u_scaled)
+        basis,
+        moved,
+        from_sibling(basis),
+        from_sibling(moved),
+        in_specs=with_place(5),
+        cost_estimate=work(4, rank),
+    )
+    basis = jnp.concatenate(parts)
+    tiles, (u_scaled, moved) = gram_tiles(place, a_quarter, parts, rank, (u_scaled, across(basis)))
+    mine = row_total(tiles)
+    mine, siblings = together(mine, (from_sibling(basis), from_sibling(moved)))
     v_scaled, right = call(
         finish,
         [(width, rank), shape],
-        quarter,
+        place,
         mine,
         from_sibling(mine),
-        *basis,
-        in_specs=with_quarter(6),
+        basis,
+        moved,
+        *siblings,
+        in_specs=with_place(6),
         scratch_shapes=[pltpu.VMEM((rank, rank), jnp.float32), *factor_scratch(rank)],
     )
     return u_scaled, v_scaled, left, right
@@ -424,8 +444,10 @@
 
 def solution(mesh):
     count, rows = mesh.devices.shape
-    mesh = Mesh(mesh.devices.reshape(count // 4, 2, 2, rows), ("z", "y_lo", "core", "row"))
-    tenant = ("z", "y_lo", "core")
+    mesh = Mesh(
+        mesh.devices.reshape(count // 8, 2, 2, 2, rows), ("z_hi", "z_lo", "y_lo", "core", "row")
+    )
+    tenant = ("z_hi", "z_lo", "y_lo", "core")
     in_specs = (P(tenant, None, "row"), P(tenant, None, "row"), P("row", None), P("row", None))
     out_specs = (P("row", None), P("row", None), P(tenant, None, None), P(tenant, None, None))
     return jax.shard_map(local, mesh=mesh, in_specs=in_specs, out_specs=out_specs, check_vma=False)

time: 166 us -> 160 us (0.964)
  blocking collectives: 14.5 us -> 39.9 us
  waiting for transfers between devices: 70.5 us -> 51.1 us
  starting transfers between devices: 52.7 us -> 37.5 us
  Pallas kernels: 22.9 us -> 26.1 us
    ppermute x25 -> x23, waiting for transfers between devices: 63.7 us -> 26.5 us  [from_peer(): return lax.ppermute(x, axis, [(i, i ^ step) for i in range(count)])]
    all_to_all x1 -> x3, blocking collectives: 14.5 us -> 39.9 us  [exchanged(): return lax.all_to_all(tiles, axis, 0, 0, tiled=True)]
    all_to_all x5 -> x3, starting transfers between devices: 34.4 us -> 14.1 us  [exchanged(): return lax.all_to_all(tiles, axis, 0, 0, tiled=True)]
    all_to_all x5 -> x3, waiting for transfers between devices: 6.79 us -> 24.6 us  [exchanged(): return lax.all_to_all(tiles, axis, 0, 0, tiled=True)]
    ppermute x25 -> x23, starting transfers between devices: 18.3 us -> 23.4 us  [from_peer(): return lax.ppermute(x, axis, [(i, i ^ step) for i in range(count)])]
    pallas_call x10, Pallas kernels: 22.9 us -> 26.1 us  [call(): pl.pallas_call(kernel, out_shape=shapes if len(shapes) > 1 else shapes[0]...]
  transfers between devices with their start and end apart: 30 -> 26, of which waited for: 20 -> 21; matrix products, arithmetic and copies ran while one was open for 0% -> 0% of each run, Pallas kernels for 1% -> 8%
where the time goes in v8:
time: 160 us; the launch traced here: 157 us
  waiting for transfers between devices  51.1 us (32%)
  blocking collectives  39.9 us (25%)
  starting transfers between devices  37.5 us (23%)
  Pallas kernels  26.1 us (16%)
    all_to_all x3, blocking collectives, exchanged(): return lax.all_to_all(tiles, axis, 0, 0, tiled=True)  39.9 us
    ppermute x23, waiting for transfers between devices, from_peer(): return lax.ppermute(x, axis, [(i, i ^ step) for i in range(count)])  26.5 us
    pallas_call x10, Pallas kernels, call(): pl.pallas_call(kernel, out_shape=shapes if len(shapes) > 1 else shapes[0]...  26.1 us
    all_to_all x3, waiting for transfers between devices, exchanged(): return lax.all_to_all(tiles, axis, 0, 0, tiled=True)  24.6 us
    ppermute x23, starting transfers between devices, from_peer(): return lax.ppermute(x, axis, [(i, i ^ step) for i in range(count)])  23.4 us
    all_to_all x3, starting transfers between devices, exchanged(): return lax.all_to_all(tiles, axis, 0, 0, tiled=True)  14.1 us
  transfers between devices with their start and end apart: 26, of which 21 were waited for; matrix products, arithmetic and copies ran while one was open for 0% of the time, Pallas kernels for 8%

profile of v8, /device:TPU:8, one launch (start us, length us, event | category | flops | bytes accessed | tf_op | source)
XLA Modules:
  0.0 157.1 jit_solution(16632235447781254846)
XLA Ops:
  0.7 1.1 constant_dynamic-slice_fusion.10
  1.8 2.0 %collective-permute-start = (f32[128,512]{1,0:T(8,128)S(1)}, f32[128,512]{1,0:T(8,128)S(1)}, u32[]{:S(2)}, u32[]{:S(2)}) collective-permute-start(f32[128,512]{1,0:T(8,128)S(1)} %get-tuple-element.72), channel_id=1, source_target_pairs={{0,32},{32,0},{1,33},{33,1},{2,34},{34,2},{3,35},{35,3},{4,36},{36... | collective-permute-start | bytes 786440 | tf_op jit(solution)/shard_map/ppermute | solution.py:297
  4.0 3.2 %projections.1 = f32[8,32,256]{2,1,0:T(8,128)} custom-call(f32[128,1024]{1,0:T(8,128)} %bitcast.5, f32[128,1024]{1,0:T(8,128)} %bitcast.6, f32[1024,256]{1,0:T(8,128)} %u_hbm.1, f32[1024,256]{1,0:T(8,128)} %v_hbm.1), custom_call_target="tpu_custom_call" | custom-call | tf_op jit(solution)/shard_map/projections/pallas_call | solution.py:153
  7.2 6.0 %all-to-all-start = ((f32[8,32,256]{2,1,0:T(8,128)}), f32[8,32,256]{2,1,0:T(8,128)S(1)}, u32[]{:S(2)}, u32[]{:S(2)}) async-start(f32[8,32,256]{2,1,0:T(8,128)} %projections.1), calls=%async_computation | async-start | bytes 524288 | tf_op jit(solution)/shard_map/all_to_all | solution.py:292
  13.2 8.4 %all-to-all-done.tiles_ref = f32[8,32,256]{2,1,0:T(8,128)S(1)} async-done(((f32[8,32,256]{2,1,0:T(8,128)}), f32[8,32,256]{2,1,0:T(8,128)S(1)}, u32[]{:S(2)}, u32[]{:S(2)}) %all-to-all-start) | async-done | bytes 262176 | tf_op jit(solution)/shard_map/all_to_all | solution.py:292
  21.7 1.1 owner_coefficients.1
  22.8 4.5 %all-to-all-start.1 = ((f32[16,32,256]{2,1,0:T(8,128)}), f32[16,32,256]{2,1,0:T(8,128)S(1)}, u32[]{:S(2)}, u32[]{:S(2)}) async-start(f32[16,32,256]{2,1,0:T(8,128)} %owner_coefficients.1), calls=%async_computation.1 | async-start | bytes 1048576 | tf_op jit(solution)/shard_map/all_to_all | solution.py:292
  27.6 0.6 collective-permute-start.3
  28.1 0.9 collective-permute-done.2.f2
  29.0 0.4 collective-permute-done.3.f2
  29.4 8.4 %all-to-all-done.1.mine_ref.pair_ref = f32[16,32,256]{2,1,0:T(8,128)S(1)} async-done(((f32[16,32,256]{2,1,0:T(8,128)}), f32[16,32,256]{2,1,0:T(8,128)S(1)}, u32[]{:S(2)}, u32[]{:S(2)}) %all-to-all-start.1) | async-done | bytes 524320 | tf_op jit(solution)/shard_map/all_to_all | solution.py:292
  37.9 1.8 %collective-permute-done.4.other_ref.pair_other_ref = f32[16,32,256]{2,1,0:T(8,128)S(1)} collective-permute-done((f32[16,32,256]{2,1,0:T(8,128)S(1)}, f32[16,32,256]{2,1,0:T(8,128)S(1)}, u32[]{:S(2)}, u32[]{:S(2)}) %collective-permute-start.4) | collective-permute-done | bytes 524320 | tf_op jit(solution)/shard_map/ppermute | solution.py:297
  39.7 1.0 load_sum.1
  40.7 3.2 %collective-permute-start.5 = (f32[128,256]{1,0:T(8,128)S(1)}, f32[128,256]{1,0:T(8,128)S(1)}, u32[]{:S(2)}, u32[]{:S(2)}) collective-permute-start(f32[128,256]{1,0:T(8,128)S(1)} %get-tuple-element.49), channel_id=1, source_target_pairs={{0,96},{32,64},{64,32},{96,0},{1,97},{33,65},{65,33},{97,1},{2,98}... | collective-permute-start | bytes 393224 | tf_op jit(solution)/shard_map/ppermute | solution.py:297
  43.9 1.3 collective-permute-start.7
  45.3 2.4 %collective-permute-done.5 = f32[128,256]{1,0:T(8,128)S(1)} collective-permute-done((f32[128,256]{1,0:T(8,128)S(1)}, f32[128,256]{1,0:T(8,128)S(1)}, u32[]{:S(2)}, u32[]{:S(2)}) %collective-permute-start.5) | collective-permute-done | bytes 131104 | tf_op jit(solution)/shard_map/ppermute | solution.py:297
  47.7 1.4 collective-permute-start.6
  49.2 3.0 %collective-permute-start.8 = (f32[128,256]{1,0:T(8,128)S(1)}, f32[128,256]{1,0:T(8,128)S(1)}, u32[]{:S(2)}, u32[]{:S(2)}) collective-permute-start(f32[128,256]{1,0:T(8,128)S(1)} %add.60), channel_id=1, source_target_pairs={{0,96},{32,64},{64,32},{96,0},{1,97},{33,65},{65,33},{97,1},{2,98}... | collective-permute-start | bytes 393224 | tf_op jit(solution)/shard_map/ppermute | solution.py:297
  52.2 0.6 collective-permute-done.6
  52.8 2.7 %collective-permute-done.8 = f32[128,256]{1,0:T(8,128)S(1)} collective-permute-done((f32[128,256]{1,0:T(8,128)S(1)}, f32[128,256]{1,0:T(8,128)S(1)}, u32[]{:S(2)}, u32[]{:S(2)}) %collective-permute-start.8) | collective-permute-done | bytes 131104 | tf_op jit(solution)/shard_map/ppermute | solution.py:297
  55.5 1.1 gram_and_cores.2
  56.6 1.7 %collective-permute-done.9 = f32[16,24,256]{2,1,0:T(8,128)S(1)} collective-permute-done((f32[16,24,256]{2,1,0:T(8,128)S(1)}, f32[16,24,256]{2,1,0:T(8,128)S(1)}, u32[]{:S(2)}, u32[]{:S(2)}) %collective-permute-start.9) | collective-permute-done | bytes 393248 | tf_op jit(solution)/shard_map/ppermute | solution.py:297
  58.4 13.8 %all_to_all.30.tiles_ref = f32[16,24,256]{2,1,0:T(8,128)S(1)} all-to-all(f32[16,24,256]{2,1,0:T(8,128)S(1)} %add.62), channel_id=1, replica_groups=mesh['z_hi'=2,'z_lo'=2,'y_lo'=2,'core'=2,'row'=8] {'z_lo','row'}, dimensions={0} | all-to-all | bytes 786432 | tf_op jit(solution)/shard_map/all_to_all | solution.py:292
  72.2 12.9 %all_to_all.31.mine_ref = f32[16,24,256]{2,1,0:T(8,128)S(1)} all-to-all(f32[16,24,256]{2,1,0:T(8,128)S(1)} %owner_sum.2), channel_id=1, replica_groups=mesh['z_hi'=2,'z_lo'=2,'y_lo'=2,'core'=2,'row'=8] {'z_lo','row'}, dimensions={0} | all-to-all | bytes 786432 | tf_op jit(solution)/shard_map/all_to_all | solution.py:292
  85.2 1.2 collective-permute-start.11
  86.3 0.5 collective-permute-done.10.other_ref
  86.9 7.9 %turn_over.1 = (f32[256,256]{1,0:T(8,128)S(1)}, f32[8,16,256]{2,1,0:T(8,128)}, f32[128,256]{1,0:T(8,128)S(1)}, f32[128,256]{1,0:T(8,128)S(1)}) custom-call(s32[2]{0:T(128)S(1)} %pad_add_fusion.place_ref, f32[16,24,256]{2,1,0:T(8,128)S(1)} %all_to_all.31.mine_ref, f32[16,24,256]{2,1,0:T(8,128)S(1)} %collective-permute-done.10.other_ref, ...), custom_call_target="tpu_custom_call" | custom-call | flops 6442450944 | tf_op jit(solution)/shard_map/turn_over/pallas_call | solution.py:153
  94.7 3.3 %collective-permute-start.12 = (f32[128,256]{1,0:T(8,128)S(1)}, f32[128,256]{1,0:T(8,128)S(1)}, u32[]{:S(2)}, u32[]{:S(2)}) collective-permute-start(f32[128,256]{1,0:T(8,128)S(1)} %get-tuple-element.55), channel_id=1, source_target_pairs={{0,96},{32,64},{64,32},{96,0},{1,97},{33,65},{65,33},{97,1},{2,98}... | collective-permute-start | bytes 393224 | tf_op jit(solution)/shard_map/ppermute | solution.py:297
  98.1 1.3 collective-permute-start.14
  99.4 2.5 %collective-permute-done.12 = f32[128,256]{1,0:T(8,128)S(1)} collective-permute-done((f32[128,256]{1,0:T(8,128)S(1)}, f32[128,256]{1,0:T(8,128)S(1)}, u32[]{:S(2)}, u32[]{:S(2)}) %collective-permute-start.12) | collective-permute-done | bytes 131104 | tf_op jit(solution)/shard_map/ppermute | solution.py:297
  101.9 1.4 collective-permute-start.13
  103.4 3.0 %collective-permute-start.15 = (f32[128,256]{1,0:T(8,128)S(1)}, f32[128,256]{1,0:T(8,128)S(1)}, u32[]{:S(2)}, u32[]{:S(2)}) collective-permute-start(f32[128,256]{1,0:T(8,128)S(1)} %add.65), channel_id=1, source_target_pairs={{0,96},{32,64},{64,32},{96,0},{1,97},{33,65},{65,33},{97,1},{2,98}... | collective-permute-start | bytes 393224 | tf_op jit(solution)/shard_map/ppermute | solution.py:297
  106.3 0.6 collective-permute-done.13
  107.0 2.6 %collective-permute-done.15 = f32[128,256]{1,0:T(8,128)S(1)} collective-permute-done((f32[128,256]{1,0:T(8,128)S(1)}, f32[128,256]{1,0:T(8,128)S(1)}, u32[]{:S(2)}, u32[]{:S(2)}) %collective-permute-start.15) | collective-permute-done | bytes 131104 | tf_op jit(solution)/shard_map/ppermute | solution.py:297
  109.6 1.1 gram_and_cores.3
  110.8 0.5 collective-permute-start.17
  111.5 1.4 collective-permute-done.17.q2
  112.9 0.4 collective-permute-done.18.q3
  113.3 2.2 %left_basis.1 = f32[1024,256]{1,0:T(8,128)} custom-call(s32[2]{0:T(128)S(1)} %pad_add_fusion.place_ref, f32[256,256]{1,0:T(8,128)S(1)} %get-tuple-element.58.inverse_ref, f32[256,256]{1,0:T(8,128)S(1)} %pad_maximum_fusion.2.q0, f32[256,256]{1,0:T(8,128)S(1)} %collective-permute-done.11.q1, f32[256,256]{1,0:T(8,128)S(1)} %collective-permute-done.17.q2, ...), custom_call_target="tpu_custom_call" | custom-call | flops 402653184 | tf_op jit(solution)/shard_map/left_basis/pallas_call | solution.py:153
  115.4 4.7 %collective-permute-done.19.q1 = f32[256,256]{1,0:T(8,128)S(1)} collective-permute-done((f32[256,256]{1,0:T(8,128)S(1)}, f32[256,256]{1,0:T(8,128)S(1)}, u32[]{:S(2)}, u32[]{:S(2)}) %collective-permute-start.19) | collective-permute-done | bytes 262176 | tf_op jit(solution)/shard_map/ppermute | solution.py:297
  120.2 13.2 %all_to_all.32.tiles_ref = f32[16,24,256]{2,1,0:T(8,128)S(1)} all-to-all(f32[16,24,256]{2,1,0:T(8,128)S(1)} %add.67), channel_id=1, replica_groups=mesh['z_hi'=2,'z_lo'=2,'y_lo'=2,'core'=2,'row'=8] {'z_lo','row'}, dimensions={0} | all-to-all | bytes 786432 | tf_op jit(solution)/shard_map/all_to_all | solution.py:292
  133.4 0.8 owner_sum.3
  134.2 3.6 %all-to-all-start.5 = ((f32[16,24,256]{2,1,0:T(8,128)}), f32[16,24,256]{2,1,0:T(8,128)S(1)}, u32[]{:S(2)}, u32[]{:S(2)}) async-start(f32[16,24,256]{2,1,0:T(8,128)} %owner_sum.3), calls=%async_computation.5 | async-start | bytes 786432 | tf_op jit(solution)/shard_map/all_to_all | solution.py:292
  137.8 0.5 collective-permute-start.21
  138.3 1.0 collective-permute-done.20.q2
  139.7 7.8 %all-to-all-done.5.mine_ref = f32[16,24,256]{2,1,0:T(8,128)S(1)} async-done(((f32[16,24,256]{2,1,0:T(8,128)}), f32[16,24,256]{2,1,0:T(8,128)S(1)}, u32[]{:S(2)}, u32[]{:S(2)}) %all-to-all-start.5) | async-done | bytes 393248 | tf_op jit(solution)/shard_map/all_to_all | solution.py:292
  147.5 1.7 %collective-permute-done.22.other_ref = f32[16,24,256]{2,1,0:T(8,128)S(1)} collective-permute-done((f32[16,24,256]{2,1,0:T(8,128)S(1)}, f32[16,24,256]{2,1,0:T(8,128)S(1)}, u32[]{:S(2)}, u32[]{:S(2)}) %collective-permute-start.22) | collective-permute-done | bytes 393248 | tf_op jit(solution)/shard_map/ppermute | solution.py:297
  149.2 7.9 %finish.1 = (f32[1024,256]{1,0:T(8,128)}, f32[8,16,256]{2,1,0:T(8,128)}) custom-call(s32[2]{0:T(128)S(1)} %pad_add_fusion.place_ref, f32[16,24,256]{2,1,0:T(8,128)S(1)} %all-to-all-done.5.mine_ref, f32[16,24,256]{2,1,0:T(8,128)S(1)} %collective-permute-done.22.other_ref, f32[256,256]{1,0:T(8,128)S(1)} %pad_maximum_fusion.3.q0, ...), custom_call_target="tpu_custom_call" | custom-call | tf_op jit(solution)/shard_map/finish/pallas_call | solution.py:153
  (38 shorter events, 1.8 us)
Async XLA Ops:
  0.6 3.1 %copy-start = (f32[8,16,1024]{2,1,0:T(8,128)S(1)}, f32[8,16,1024]{2,1,0:T(8,128)}, u32[]{:S(2)}) copy-start(f32[8,16,1024]{2,1,0:T(8,128)} %param.5) | copy-start | bytes 1572868
  1.8 19.9 %collective-permute-start = (f32[128,512]{1,0:T(8,128)S(1)}, f32[128,512]{1,0:T(8,128)S(1)}, u32[]{:S(2)}, u32[]{:S(2)}) collective-permute-start(f32[128,512]{1,0:T(8,128)S(1)} %get-tuple-element.72), channel_id=1, source_target_pairs={{0,32},{32,0},{1,33},{33,1},{2,34},{34,2},{3,35},{35,3},{4,36},{36... | collective-permute-start | bytes 786440 | tf_op jit(solution)/shard_map/ppermute | solution.py:297
  3.8 17.9 %collective-permute-start.1 = (f32[128,512]{1,0:T(8,128)S(1)}, f32[128,512]{1,0:T(8,128)S(1)}, u32[]{:S(2)}, u32[]{:S(2)}) collective-permute-start(f32[128,512]{1,0:T(8,128)S(1)} %get-tuple-element.70), channel_id=1, source_target_pairs={{0,32},{32,0},{1,33},{33,1},{2,34},{34,2},{3,35},{35,3},{4,36},{36... | collective-permute-start | bytes 786440 | tf_op jit(solution)/shard_map/ppermute | solution.py:297
  7.2 14.5 %all-to-all-start = ((f32[8,32,256]{2,1,0:T(8,128)}), f32[8,32,256]{2,1,0:T(8,128)S(1)}, u32[]{:S(2)}, u32[]{:S(2)}) async-start(f32[8,32,256]{2,1,0:T(8,128)} %projections.1), calls=%async_computation | async-start | bytes 524288 | tf_op jit(solution)/shard_map/all_to_all | solution.py:292
  22.8 15.0 %all-to-all-start.1 = ((f32[16,32,256]{2,1,0:T(8,128)}), f32[16,32,256]{2,1,0:T(8,128)S(1)}, u32[]{:S(2)}, u32[]{:S(2)}) async-start(f32[16,32,256]{2,1,0:T(8,128)} %owner_coefficients.1), calls=%async_computation.1 | async-start | bytes 1048576 | tf_op jit(solution)/shard_map/all_to_all | solution.py:292
  27.4 1.6 %collective-permute-start.2 = (f32[256,256]{1,0:T(8,128)S(1)}, f32[256,256]{1,0:T(8,128)S(1)}, u32[]{:S(2)}, u32[]{:S(2)}) collective-permute-start(f32[256,256]{1,0:T(8,128)S(1)} %pad_maximum_fusion), channel_id=1, source_target_pairs={{0,8},{8,0},{1,9},{9,1},{2,10},{10,2},{3,11},{11,3},{4,12},{12,4},... | collective-permute-start | bytes 786440 | tf_op jit(solution)/shard_map/ppermute | solution.py:297
  27.6 1.8 %collective-permute-start.3 = (f32[256,256]{1,0:T(8,128)S(1)}, f32[256,256]{1,0:T(8,128)S(1)}, u32[]{:S(2)}, u32[]{:S(2)}) collective-permute-start(f32[256,256]{1,0:T(8,128)S(1)} %pad_maximum_fusion.1), channel_id=1, source_target_pairs={{0,8},{8,0},{1,9},{9,1},{2,10},{10,2},{3,11},{11,3},{4,12},{12,4},... | collective-permute-start | bytes 786440 | tf_op jit(solution)/shard_map/ppermute | solution.py:297
  37.8 1.9 %collective-permute-start.4 = (f32[16,32,256]{2,1,0:T(8,128)S(1)}, f32[16,32,256]{2,1,0:T(8,128)S(1)}, u32[]{:S(2)}, u32[]{:S(2)}) collective-permute-start(f32[16,32,256]{2,1,0:T(8,128)S(1)} %all-to-all-done.1.mine_ref.pair_ref), channel_id=1, source_target_pairs={{0,8},{8,0},{1,9},{9,1},{2,10},{10,2},{3,11},{11,3},{4,12},{12,4},... | collective-permute-start | bytes 1572872 | tf_op jit(solution)/shard_map/ppermute | solution.py:297
  40.7 7.0 %collective-permute-start.5 = (f32[128,256]{1,0:T(8,128)S(1)}, f32[128,256]{1,0:T(8,128)S(1)}, u32[]{:S(2)}, u32[]{:S(2)}) collective-permute-start(f32[128,256]{1,0:T(8,128)S(1)} %get-tuple-element.49), channel_id=1, source_target_pairs={{0,96},{32,64},{64,32},{96,0},{1,97},{33,65},{65,33},{97,1},{2,98}... | collective-permute-start | bytes 393224 | tf_op jit(solution)/shard_map/ppermute | solution.py:297
  43.9 5.3 %collective-permute-start.7 = (f32[128,256]{1,0:T(8,128)S(1)}, f32[128,256]{1,0:T(8,128)S(1)}, u32[]{:S(2)}, u32[]{:S(2)}) collective-permute-start(f32[128,256]{1,0:T(8,128)S(1)} %get-tuple-element.50), channel_id=1, source_target_pairs={{0,16},{16,0},{1,17},{17,1},{2,18},{18,2},{3,19},{19,3},{4,20},{20... | collective-permute-start | bytes 393224 | tf_op jit(solution)/shard_map/ppermute | solution.py:297
  47.7 5.0 %collective-permute-start.6 = (f32[128,256]{1,0:T(8,128)S(1)}, f32[128,256]{1,0:T(8,128)S(1)}, u32[]{:S(2)}, u32[]{:S(2)}) collective-permute-start(f32[128,256]{1,0:T(8,128)S(1)} %add.58), channel_id=1, source_target_pairs={{0,16},{16,0},{1,17},{17,1},{2,18},{18,2},{3,19},{19,3},{4,20},{20... | collective-permute-start | bytes 393224 | tf_op jit(solution)/shard_map/ppermute | solution.py:297
  49.2 6.3 %collective-permute-start.8 = (f32[128,256]{1,0:T(8,128)S(1)}, f32[128,256]{1,0:T(8,128)S(1)}, u32[]{:S(2)}, u32[]{:S(2)}) collective-permute-start(f32[128,256]{1,0:T(8,128)S(1)} %add.60), channel_id=1, source_target_pairs={{0,96},{32,64},{64,32},{96,0},{1,97},{33,65},{65,33},{97,1},{2,98}... | collective-permute-start | bytes 393224 | tf_op jit(solution)/shard_map/ppermute | solution.py:297
  56.5 1.8 %collective-permute-start.9 = (f32[16,24,256]{2,1,0:T(8,128)S(1)}, f32[16,24,256]{2,1,0:T(8,128)S(1)}, u32[]{:S(2)}, u32[]{:S(2)}) collective-permute-start(f32[16,24,256]{2,1,0:T(8,128)S(1)} %get-tuple-element.52), channel_id=1, source_target_pairs={{0,8},{8,0},{1,9},{9,1},{2,10},{10,2},{3,11},{11,3},{4,12},{12,4},... | collective-permute-start | bytes 1179656 | tf_op jit(solution)/shard_map/ppermute | solution.py:297
  85.1 1.7 %collective-permute-start.10 = (f32[16,24,256]{2,1,0:T(8,128)S(1)}, f32[16,24,256]{2,1,0:T(8,128)S(1)}, u32[]{:S(2)}, u32[]{:S(2)}) collective-permute-start(f32[16,24,256]{2,1,0:T(8,128)S(1)} %all_to_all.31.mine_ref), channel_id=1, source_target_pairs={{0,8},{8,0},{1,9},{9,1},{2,10},{10,2},{3,11},{11,3},{4,12},{12,4},... | collective-permute-start | bytes 1179656 | tf_op jit(solution)/shard_map/ppermute | solution.py:297
  85.2 9.6 %collective-permute-start.11 = (f32[256,256]{1,0:T(8,128)S(1)}, f32[256,256]{1,0:T(8,128)S(1)}, u32[]{:S(2)}, u32[]{:S(2)}) collective-permute-start(f32[256,256]{1,0:T(8,128)S(1)} %pad_maximum_fusion.2.q0), channel_id=1, source_target_pairs={{0,32},{32,0},{1,33},{33,1},{2,34},{34,2},{3,35},{35,3},{4,36},{36... | collective-permute-start | bytes 786440 | tf_op jit(solution)/shard_map/ppermute | solution.py:297
  94.7 7.1 %collective-permute-start.12 = (f32[128,256]{1,0:T(8,128)S(1)}, f32[128,256]{1,0:T(8,128)S(1)}, u32[]{:S(2)}, u32[]{:S(2)}) collective-permute-start(f32[128,256]{1,0:T(8,128)S(1)} %get-tuple-element.55), channel_id=1, source_target_pairs={{0,96},{32,64},{64,32},{96,0},{1,97},{33,65},{65,33},{97,1},{2,98}... | collective-permute-start | bytes 393224 | tf_op jit(solution)/shard_map/ppermute | solution.py:297
  98.1 5.3 %collective-permute-start.14 = (f32[128,256]{1,0:T(8,128)S(1)}, f32[128,256]{1,0:T(8,128)S(1)}, u32[]{:S(2)}, u32[]{:S(2)}) collective-permute-start(f32[128,256]{1,0:T(8,128)S(1)} %get-tuple-element.56), channel_id=1, source_target_pairs={{0,16},{16,0},{1,17},{17,1},{2,18},{18,2},{3,19},{19,3},{4,20},{20... | collective-permute-start | bytes 393224 | tf_op jit(solution)/shard_map/ppermute | solution.py:297
  101.9 5.1 %collective-permute-start.13 = (f32[128,256]{1,0:T(8,128)S(1)}, f32[128,256]{1,0:T(8,128)S(1)}, u32[]{:S(2)}, u32[]{:S(2)}) collective-permute-start(f32[128,256]{1,0:T(8,128)S(1)} %add.63), channel_id=1, source_target_pairs={{0,16},{16,0},{1,17},{17,1},{2,18},{18,2},{3,19},{19,3},{4,20},{20... | collective-permute-start | bytes 393224 | tf_op jit(solution)/shard_map/ppermute | solution.py:297
  103.4 6.3 %collective-permute-start.15 = (f32[128,256]{1,0:T(8,128)S(1)}, f32[128,256]{1,0:T(8,128)S(1)}, u32[]{:S(2)}, u32[]{:S(2)}) collective-permute-start(f32[128,256]{1,0:T(8,128)S(1)} %add.65), channel_id=1, source_target_pairs={{0,96},{32,64},{64,32},{96,0},{1,97},{33,65},{65,33},{97,1},{2,98}... | collective-permute-start | bytes 393224 | tf_op jit(solution)/shard_map/ppermute | solution.py:297
  110.7 9.4 %collective-permute-start.16 = (f32[16,24,256]{2,1,0:T(8,128)S(1)}, f32[16,24,256]{2,1,0:T(8,128)S(1)}, u32[]{:S(2)}, u32[]{:S(2)}) collective-permute-start(f32[16,24,256]{2,1,0:T(8,128)S(1)} %get-tuple-element.57), channel_id=1, source_target_pairs={{0,8},{8,0},{1,9},{9,1},{2,10},{10,2},{3,11},{11,3},{4,12},{12,4},... | collective-permute-start | bytes 1179656 | tf_op jit(solution)/shard_map/ppermute | solution.py:297
  110.8 2.1 %collective-permute-start.17 = (f32[256,256]{1,0:T(8,128)S(1)}, f32[256,256]{1,0:T(8,128)S(1)}, u32[]{:S(2)}, u32[]{:S(2)}) collective-permute-start(f32[256,256]{1,0:T(8,128)S(1)} %pad_maximum_fusion.2.q0), channel_id=1, source_target_pairs={{0,8},{8,0},{1,9},{9,1},{2,10},{10,2},{3,11},{11,3},{4,12},{12,4},... | collective-permute-start | bytes 786440 | tf_op jit(solution)/shard_map/ppermute | solution.py:297
  111.3 2.0 %collective-permute-start.18 = (f32[256,256]{1,0:T(8,128)S(1)}, f32[256,256]{1,0:T(8,128)S(1)}, u32[]{:S(2)}, u32[]{:S(2)}) collective-permute-start(f32[256,256]{1,0:T(8,128)S(1)} %collective-permute-done.11.q1), channel_id=1, source_target_pairs={{0,8},{8,0},{1,9},{9,1},{2,10},{10,2},{3,11},{11,3},{4,12},{12,4},... | collective-permute-start | bytes 786440 | tf_op jit(solution)/shard_map/ppermute | solution.py:297
  111.4 8.7 %collective-permute-start.19 = (f32[256,256]{1,0:T(8,128)S(1)}, f32[256,256]{1,0:T(8,128)S(1)}, u32[]{:S(2)}, u32[]{:S(2)}) collective-permute-start(f32[256,256]{1,0:T(8,128)S(1)} %pad_maximum_fusion.3.q0), channel_id=1, source_target_pairs={{0,32},{32,0},{1,33},{33,1},{2,34},{34,2},{3,35},{35,3},{4,36},{36... | collective-permute-start | bytes 786440 | tf_op jit(solution)/shard_map/ppermute | solution.py:297
  134.2 13.3 %all-to-all-start.5 = ((f32[16,24,256]{2,1,0:T(8,128)}), f32[16,24,256]{2,1,0:T(8,128)S(1)}, u32[]{:S(2)}, u32[]{:S(2)}) async-start(f32[16,24,256]{2,1,0:T(8,128)} %owner_sum.3), calls=%async_computation.5 | async-start | bytes 786432 | tf_op jit(solution)/shard_map/all_to_all | solution.py:292
  137.7 1.6 %collective-permute-start.20 = (f32[256,256]{1,0:T(8,128)S(1)}, f32[256,256]{1,0:T(8,128)S(1)}, u32[]{:S(2)}, u32[]{:S(2)}) collective-permute-start(f32[256,256]{1,0:T(8,128)S(1)} %pad_maximum_fusion.3.q0), channel_id=1, source_target_pairs={{0,8},{8,0},{1,9},{9,1},{2,10},{10,2},{3,11},{11,3},{4,12},{12,4},... | collective-permute-start | bytes 786440 | tf_op jit(solution)/shard_map/ppermute | solution.py:297
  137.8 1.9 %collective-permute-start.21 = (f32[256,256]{1,0:T(8,128)S(1)}, f32[256,256]{1,0:T(8,128)S(1)}, u32[]{:S(2)}, u32[]{:S(2)}) collective-permute-start(f32[256,256]{1,0:T(8,128)S(1)} %collective-permute-done.19.q1), channel_id=1, source_target_pairs={{0,8},{8,0},{1,9},{9,1},{2,10},{10,2},{3,11},{11,3},{4,12},{12,4},... | collective-permute-start | bytes 786440 | tf_op jit(solution)/shard_map/ppermute | solution.py:297
  147.5 1.7 %collective-permute-start.22 = (f32[16,24,256]{2,1,0:T(8,128)S(1)}, f32[16,24,256]{2,1,0:T(8,128)S(1)}, u32[]{:S(2)}, u32[]{:S(2)}) collective-permute-start(f32[16,24,256]{2,1,0:T(8,128)S(1)} %all-to-all-done.5.mine_ref), channel_id=1, source_target_pairs={{0,8},{8,0},{1,9},{9,1},{2,10},{10,2},{3,11},{11,3},{4,12},{12,4},... | collective-permute-start | bytes 1179656 | tf_op jit(solution)/shard_map/ppermute | solution.py:297

commit v9 on v8

--- a/solution.py
+++ b/solution.py
@@ -203,6 +203,18 @@
     return jnp.concatenate([ref[...] for ref in refs])
 
 
+def quarter_of(place_ref):
+    return place_ref[0] // 2
+
+
+def core_of(place_ref):
+    return place_ref[0] // 2 % 2
+
+
+def pair_of(place_ref):
+    return place_ref[0] % 2
+
+
 def by_distance(pair, ref):
     count = len(ref) // 2
     return [pl.ds(place * count, count) for place in (pair, 1 - pair)]
@@ -215,7 +227,7 @@
 
 
 def load_sum(place_ref, f0, f1, f2, mine_ref, other_ref, *out_refs):
-    coeffs = tenants(place_ref[1], (mine_ref, other_ref), 0)
+    coeffs = tenants(pair_of(place_ref), (mine_ref, other_ref), 0)
     store_load(product(stacked((f0, f1, f2)), coeffs, 0, 0), out_refs)
 
 
@@ -229,10 +241,10 @@
     basis = stacked((x_ref, y_ref))
     cores = product(stacked((f0, f1, f2)), basis)
     gram_ref[...] = product(basis, basis, 0, 0)
-    core, half = place_ref[0] % 2, len(gram_ref) // 2
+    core, half = core_of(place_ref), len(gram_ref) // 2
     block = len(cores) // 4
     for i, (ref, which) in enumerate(((mine_ref, core), (other_ref, 1 - core))):
-        for j, place in enumerate(by_distance(place_ref[1], ref)):
+        for j, place in enumerate(by_distance(pair_of(place_ref), ref)):
             rows = cores[(2 * i + j) * block : (2 * i + j + 1) * block]
             ref[place, :RANK] = rows.reshape(-1, RANK, rows.shape[1])
         rows = gram_ref[pl.ds(which * half, half), :]
@@ -250,8 +262,8 @@
     place_ref, mine_ref, other_ref, pair_ref, pair_other_ref, f0, f1, f2,
     inverse_ref, left_ref, x_ref, y_ref, *scratch,
 ):
-    pair = place_ref[1]
-    inverse_factor(place_ref[0] % 2, mine_ref, other_ref, inverse_ref, *scratch)
+    pair = pair_of(place_ref)
+    inverse_factor(core_of(place_ref), mine_ref, other_ref, inverse_ref, *scratch)
     left = product(tenants(pair, (mine_ref, other_ref), 0), inverse_ref[...], 1, 1)
     right = tenants(pair, (pair_ref, pair_other_ref), RANK)
     own = left[: len(left) // 4]
@@ -274,16 +286,16 @@
 
 
 def left_basis(place_ref, inverse_ref, q0, q1, q2, q3, out_ref):
-    scaled_basis(place_ref[0], inverse_ref[...], (q0, q1, q2, q3), out_ref)
+    scaled_basis(quarter_of(place_ref), inverse_ref[...], (q0, q1, q2, q3), out_ref)
 
 
 def finish(
     place_ref, mine_ref, other_ref, q0, q1, q2, q3, out_ref, right_ref, inverse_ref, *scratch
 ):
-    quarter = place_ref[0]
-    inverse_factor(quarter % 2, mine_ref, other_ref, inverse_ref, *scratch)
+    quarter = quarter_of(place_ref)
+    inverse_factor(core_of(place_ref), mine_ref, other_ref, inverse_ref, *scratch)
     inverse = inverse_ref[...]
-    own = matrix(mine_ref[by_distance(place_ref[1], mine_ref)[0], :RANK])
+    own = matrix(mine_ref[by_distance(pair_of(place_ref), mine_ref)[0], :RANK])
     right_ref[...] = product(own, inverse, 1, 1).reshape(right_ref.shape)
     scaled_basis(quarter, inverse, (q0, q1, q2, q3), out_ref)
 
@@ -309,11 +321,14 @@
     return from_peer(x, "z_lo", 1)
 
 
-def plane_total(x, y):
-    orders = (((("z_hi", "z_lo"), 3), ("y_lo", 1)), (("y_lo", 1), (("z_hi", "z_lo"), 3)))
-    for x_step, y_step in zip(*orders):
-        x, y = x + from_peer(x, *x_step), y + from_peer(y, *y_step)
-    return x, y
+def plane_total(x, y, besides):
+    z, y_lo = (("z_hi", "z_lo"), 3), ("y_lo", 1)
+    done = []
+    for x_step, y_step, beside in zip((z, y_lo), (y_lo, z), besides):
+        moved, beside = together((from_peer(x, *x_step), from_peer(y, *y_step)), beside)
+        x, y = x + moved[0], y + moved[1]
+        done.append(beside)
+    return (x, y), done
 
 
 def column_half(factors, bit):
@@ -366,10 +381,10 @@
     width, rank = u_start.shape
     pair_index, core = lax.axis_index("z_lo"), lax.axis_index("core")
     bit = pair_index ^ lax.axis_index("z_hi")
-    place = jnp.stack([2 * bit + core, pair_index]).astype(jnp.int32)
+    place = jnp.reshape(4 * bit + 2 * core + pair_index, (1,)).astype(jnp.int32)
     b = b_factors.reshape(-1, width)
     a = a_factors.reshape(-1, width)
-    b_half, a_half = column_half(b, bit), column_half(a, bit)
+    b_half = column_half(b, bit)
 
     partial = call(
         projections,
@@ -382,20 +397,21 @@
         ],
     )
     copies = (lax.axis_size(ROW), 2 * RANK, rank)
-    tiles, (b_half, a_half) = together(exchanged(partial, "row"), (b_half, a_half))
-    b_quarter, a_quarter = column_quarter(b_half, core), column_quarter(a_half, core)
+    tiles, b_half = together(exchanged(partial, "row"), b_half)
+    b_quarter = column_quarter(b_half, core)
     pair = exchanged(call(owner_coefficients, [copies], tiles), ROW)
-    pair, (b_quarter, a_quarter) = together(pair, (b_quarter, a_quarter))
+    pair, b_quarter = together(pair, b_quarter)
     pair_other = from_sibling(pair)
 
     part = (width // 8, rank)
     parts = call(
         load_sum, [part, part], place, *b_quarter, pair, pair_other, in_specs=with_place(5)
     )
-    parts = plane_total(*parts)
+    parts, (_, a_half) = plane_total(*parts, ((), column_half(a, bit)))
+    a_quarter = column_quarter(a_half, core)
     basis = jnp.concatenate(parts)
     tiles, _ = gram_tiles(place, b_quarter, parts, rank, ())
-    mine = row_total(tiles)
+    mine, a_quarter = together(row_total(tiles), a_quarter)
     inverse, left, *parts = call(
         turn_over,
         [(rank, rank), shape, part, part],
@@ -410,7 +426,6 @@
         cost_estimate=work(64, rank),
     )
     parts, moved = together(parts, across(basis))
-    parts = plane_total(*parts)
     u_scaled = call(
         left_basis,
         [(width, rank)],
@@ -423,8 +438,9 @@
         in_specs=with_place(5),
         cost_estimate=work(4, rank),
     )
+    parts, (u_scaled, _) = plane_total(*parts, (u_scaled, ()))
     basis = jnp.concatenate(parts)
-    tiles, (u_scaled, moved) = gram_tiles(place, a_quarter, parts, rank, (u_scaled, across(basis)))
+    tiles, moved = gram_tiles(place, a_quarter, parts, rank, across(basis))
     mine = row_total(tiles)
     mine, siblings = together(mine, (from_sibling(basis), from_sibling(moved)))
     v_scaled, right = call(

time: 160 us -> 158 us (0.988)
  blocking collectives: 39.9 us -> 13.2 us
  waiting for transfers between devices: 51.1 us -> 76.9 us
  Pallas kernels: 26.1 us -> 23.6 us
    all_to_all x3 -> x1, blocking collectives: 39.9 us -> 13.2 us  [exchanged(): return lax.all_to_all(tiles, axis, 0, 0, tiled=True)]
    all_to_all x3 -> x5, waiting for transfers between devices: 24.6 us -> 44.1 us  [exchanged(): return lax.all_to_all(tiles, axis, 0, 0, tiled=True)]
    ppermute x23, waiting for transfers between devices: 26.5 us -> 32.7 us  [from_peer(): return lax.ppermute(x, axis, [(i, i ^ step) for i in range(count)])]
    all_to_all x3 -> x5, starting transfers between devices: 14.1 us -> 20.3 us  [exchanged(): return lax.all_to_all(tiles, axis, 0, 0, tiled=True)]
    ppermute x23, starting transfers between devices: 23.4 us -> 18.6 us  [from_peer(): return lax.ppermute(x, axis, [(i, i ^ step) for i in range(count)])]
    pallas_call x10, Pallas kernels: 26.1 us -> 23.6 us  [call(): pl.pallas_call(kernel, out_shape=shapes if len(shapes) > 1 else shapes[0]...]
  transfers between devices with their start and end apart: 26 -> 28, of which waited for: 21 -> 22; matrix products, arithmetic and copies ran while one was open for 0% -> 0% of each run, Pallas kernels for 8% -> 8%
where the time goes in v9:
time: 158 us; the launch traced here: 156 us
  waiting for transfers between devices  76.9 us (49%)
  starting transfers between devices  38.9 us (25%)
  Pallas kernels  23.6 us (15%)
  blocking collectives  13.2 us (8%)
    all_to_all x5, waiting for transfers between devices, exchanged(): return lax.all_to_all(tiles, axis, 0, 0, tiled=True)  44.1 us
    ppermute x23, waiting for transfers between devices, from_peer(): return lax.ppermute(x, axis, [(i, i ^ step) for i in range(count)])  32.7 us
    pallas_call x10, Pallas kernels, call(): pl.pallas_call(kernel, out_shape=shapes if len(shapes) > 1 else shapes[0]...  23.6 us
    all_to_all x5, starting transfers between devices, exchanged(): return lax.all_to_all(tiles, axis, 0, 0, tiled=True)  20.3 us
    ppermute x23, starting transfers between devices, from_peer(): return lax.ppermute(x, axis, [(i, i ^ step) for i in range(count)])  18.6 us
    all_to_all x1, blocking collectives, exchanged(): return lax.all_to_all(tiles, axis, 0, 0, tiled=True)  13.2 us
  transfers between devices with their start and end apart: 28, of which 22 were waited for; matrix products, arithmetic and copies ran while one was open for 0% of the time, Pallas kernels for 8%

profile of v9, /device:TPU:8, one launch (start us, length us, event | category | flops | bytes accessed | tf_op | source)
XLA Modules:
  0.0 155.8 jit_solution(1189198528324268333)
XLA Ops:
  0.6 1.1 constant_dynamic-slice_fusion.10
  1.7 2.0 %collective-permute-start = (f32[128,512]{1,0:T(8,128)S(1)}, f32[128,512]{1,0:T(8,128)S(1)}, u32[]{:S(2)}, u32[]{:S(2)}) collective-permute-start(f32[128,512]{1,0:T(8,128)S(1)} %get-tuple-element.90), channel_id=1, source_target_pairs={{0,32},{32,0},{1,33},{33,1},{2,34},{34,2},{3,35},{35,3},{4,36},{36... | collective-permute-start | bytes 786440 | tf_op jit(solution)/shard_map/ppermute | solution.py:309
  3.7 3.2 %projections.1 = f32[8,32,256]{2,1,0:T(8,128)} custom-call(f32[128,1024]{1,0:T(8,128)} %bitcast.4, f32[128,1024]{1,0:T(8,128)} %bitcast.5, f32[1024,256]{1,0:T(8,128)} %u_hbm.1, f32[1024,256]{1,0:T(8,128)} %v_hbm.1), custom_call_target="tpu_custom_call" | custom-call | tf_op jit(solution)/shard_map/projections/pallas_call | solution.py:153
  6.9 6.0 %all-to-all-start = ((f32[8,32,256]{2,1,0:T(8,128)}), f32[8,32,256]{2,1,0:T(8,128)S(1)}, u32[]{:S(2)}, u32[]{:S(2)}) async-start(f32[8,32,256]{2,1,0:T(8,128)} %projections.1), calls=%async_computation | async-start | bytes 524288 | tf_op jit(solution)/shard_map/all_to_all | solution.py:304
  12.9 8.4 %all-to-all-done.tiles_ref = f32[8,32,256]{2,1,0:T(8,128)S(1)} async-done(((f32[8,32,256]{2,1,0:T(8,128)}), f32[8,32,256]{2,1,0:T(8,128)S(1)}, u32[]{:S(2)}, u32[]{:S(2)}) %all-to-all-start) | async-done | bytes 262176 | tf_op jit(solution)/shard_map/all_to_all | solution.py:304
  21.4 1.1 owner_coefficients.1
  22.5 3.6 %all-to-all-start.1 = ((f32[16,32,256]{2,1,0:T(8,128)}), f32[16,32,256]{2,1,0:T(8,128)S(1)}, u32[]{:S(2)}, u32[]{:S(2)}) async-start(f32[16,32,256]{2,1,0:T(8,128)} %owner_coefficients.1), calls=%async_computation.1 | async-start | bytes 1048576 | tf_op jit(solution)/shard_map/all_to_all | solution.py:304
  26.2 1.5 collective-permute-done.1.f2
  27.8 8.7 %all-to-all-done.1.mine_ref.pair_ref = f32[16,32,256]{2,1,0:T(8,128)S(1)} async-done(((f32[16,32,256]{2,1,0:T(8,128)}), f32[16,32,256]{2,1,0:T(8,128)S(1)}, u32[]{:S(2)}, u32[]{:S(2)}) %all-to-all-start.1) | async-done | bytes 524320 | tf_op jit(solution)/shard_map/all_to_all | solution.py:304
  36.5 1.9 %collective-permute-done.2.other_ref.pair_other_ref = f32[16,32,256]{2,1,0:T(8,128)S(1)} collective-permute-done((f32[16,32,256]{2,1,0:T(8,128)S(1)}, f32[16,32,256]{2,1,0:T(8,128)S(1)}, u32[]{:S(2)}, u32[]{:S(2)}) %collective-permute-start.2) | collective-permute-done | bytes 524320 | tf_op jit(solution)/shard_map/ppermute | solution.py:309
  38.8 3.2 %collective-permute-start.3 = (f32[128,256]{1,0:T(8,128)S(1)}, f32[128,256]{1,0:T(8,128)S(1)}, u32[]{:S(2)}, u32[]{:S(2)}) collective-permute-start(f32[128,256]{1,0:T(8,128)S(1)} %get-tuple-element.53), channel_id=1, source_target_pairs={{0,96},{32,64},{64,32},{96,0},{1,97},{33,65},{65,33},{97,1},{2,98}... | collective-permute-start | bytes 393224 | tf_op jit(solution)/shard_map/ppermute | solution.py:309
  42.1 1.3 collective-permute-start.4
  43.9 1.9 %collective-permute-done.3 = f32[128,256]{1,0:T(8,128)S(1)} collective-permute-done((f32[128,256]{1,0:T(8,128)S(1)}, f32[128,256]{1,0:T(8,128)S(1)}, u32[]{:S(2)}, u32[]{:S(2)}) %collective-permute-start.3) | collective-permute-done | bytes 131104 | tf_op jit(solution)/shard_map/ppermute | solution.py:309
  45.9 1.5 collective-permute-done.4
  47.4 1.6 %collective-permute-start.6 = (f32[128,256]{1,0:T(8,128)S(1)}, f32[128,256]{1,0:T(8,128)S(1)}, u32[]{:S(2)}, u32[]{:S(2)}) collective-permute-start(f32[128,256]{1,0:T(8,128)S(1)} %add.63), channel_id=1, source_target_pairs={{0,96},{32,64},{64,32},{96,0},{1,97},{33,65},{65,33},{97,1},{2,98}... | collective-permute-start | bytes 393224 | tf_op jit(solution)/shard_map/ppermute | solution.py:309
  48.9 1.3 collective-permute-start.5
  50.3 1.0 collective-permute-done.7
  51.3 2.3 %collective-permute-done.6 = f32[128,256]{1,0:T(8,128)S(1)} collective-permute-done((f32[128,256]{1,0:T(8,128)S(1)}, f32[128,256]{1,0:T(8,128)S(1)}, u32[]{:S(2)}, u32[]{:S(2)}) %collective-permute-start.6) | collective-permute-done | bytes 131104 | tf_op jit(solution)/shard_map/ppermute | solution.py:309
  54.0 0.5 gram_and_cores.2
  54.6 1.7 %collective-permute-done.8 = f32[16,24,256]{2,1,0:T(8,128)S(1)} collective-permute-done((f32[16,24,256]{2,1,0:T(8,128)S(1)}, f32[16,24,256]{2,1,0:T(8,128)S(1)}, u32[]{:S(2)}, u32[]{:S(2)}) %collective-permute-start.8) | collective-permute-done | bytes 393248 | tf_op jit(solution)/shard_map/ppermute | solution.py:309
  56.3 0.8 add.66
  57.1 3.6 %all-to-all-start.2 = ((f32[16,24,256]{2,1,0:T(8,128)}), f32[16,24,256]{2,1,0:T(8,128)S(1)}, u32[]{:S(2)}, u32[]{:S(2)}) async-start(f32[16,24,256]{2,1,0:T(8,128)} %add.66), calls=%async_computation.2 | async-start | bytes 786432 | tf_op jit(solution)/shard_map/all_to_all | solution.py:304
  60.7 11.1 %all-to-all-done.2.tiles_ref = f32[16,24,256]{2,1,0:T(8,128)S(1)} async-done(((f32[16,24,256]{2,1,0:T(8,128)}), f32[16,24,256]{2,1,0:T(8,128)S(1)}, u32[]{:S(2)}, u32[]{:S(2)}) %all-to-all-start.2) | async-done | bytes 393248 | tf_op jit(solution)/shard_map/all_to_all | solution.py:304
  71.8 0.8 owner_sum.2
  72.6 3.6 %all-to-all-start.3 = ((f32[16,24,256]{2,1,0:T(8,128)}), f32[16,24,256]{2,1,0:T(8,128)S(1)}, u32[]{:S(2)}, u32[]{:S(2)}) async-start(f32[16,24,256]{2,1,0:T(8,128)} %owner_sum.2), calls=%async_computation.3 | async-start | bytes 786432 | tf_op jit(solution)/shard_map/all_to_all | solution.py:304
  76.3 1.5 collective-permute-done.9.f2
  77.8 8.1 %all-to-all-done.3.mine_ref = f32[16,24,256]{2,1,0:T(8,128)S(1)} async-done(((f32[16,24,256]{2,1,0:T(8,128)}), f32[16,24,256]{2,1,0:T(8,128)S(1)}, u32[]{:S(2)}, u32[]{:S(2)}) %all-to-all-start.3) | async-done | bytes 393248 | tf_op jit(solution)/shard_map/all_to_all | solution.py:304
  85.9 0.6 collective-permute-start.14
  86.5 1.1 collective-permute-start.11
  87.6 7.3 %turn_over.1 = (f32[256,256]{1,0:T(8,128)S(1)}, f32[8,16,256]{2,1,0:T(8,128)}, f32[128,256]{1,0:T(8,128)S(1)}, f32[128,256]{1,0:T(8,128)S(1)}) custom-call(s32[1]{0:T(128)} %bitcast.place_ref, f32[16,24,256]{2,1,0:T(8,128)S(1)} %all-to-all-done.3.mine_ref, f32[16,24,256]{2,1,0:T(8,128)S(1)} %collective-permute-done.10.other_ref, ...), custom_call_target="tpu_custom_call" | custom-call | flops 6442450944 | tf_op jit(solution)/shard_map/turn_over/pallas_call | solution.py:153
  95.1 1.3 collective-permute-start.12
  96.4 1.3 collective-permute-start.13
  97.8 1.6 %left_basis.1 = f32[1024,256]{1,0:T(8,128)} custom-call(s32[1]{0:T(128)} %bitcast.place_ref, f32[256,256]{1,0:T(8,128)S(1)} %get-tuple-element.71.inverse_ref, f32[256,256]{1,0:T(8,128)S(1)} %pad_maximum_fusion.2.q0, f32[256,256]{1,0:T(8,128)S(1)} %collective-permute-done.11.q1, f32[256,256]{1,0:T(8,128)S(1)} %collective-permute-done.14.q2, ...), custom_call_target="tpu_custom_call" | custom-call | flops 402653184 | tf_op jit(solution)/shard_map/left_basis/pallas_call | solution.py:153
  99.4 2.7 %collective-permute-done.12 = f32[128,256]{1,0:T(8,128)S(1)} collective-permute-done((f32[128,256]{1,0:T(8,128)S(1)}, f32[128,256]{1,0:T(8,128)S(1)}, u32[]{:S(2)}, u32[]{:S(2)}) %collective-permute-start.12) | collective-permute-done | bytes 131104 | tf_op jit(solution)/shard_map/ppermute | solution.py:309
  102.2 1.4 collective-permute-start.16
  103.6 1.7 %collective-permute-start.17 = (f32[128,256]{1,0:T(8,128)S(1)}, f32[128,256]{1,0:T(8,128)S(1)}, u32[]{:S(2)}, u32[]{:S(2)}) collective-permute-start(f32[128,256]{1,0:T(8,128)S(1)} %add.68), channel_id=1, source_target_pairs={{0,96},{32,64},{64,32},{96,0},{1,97},{33,65},{65,33},{97,1},{2,98}... | collective-permute-start | bytes 393224 | tf_op jit(solution)/shard_map/ppermute | solution.py:309
  105.4 1.9 %collective-permute-done.16 = f32[128,256]{1,0:T(8,128)S(1)} collective-permute-done((f32[128,256]{1,0:T(8,128)S(1)}, f32[128,256]{1,0:T(8,128)S(1)}, u32[]{:S(2)}, u32[]{:S(2)}) %collective-permute-start.16) | collective-permute-done | bytes 131104 | tf_op jit(solution)/shard_map/ppermute | solution.py:309
  107.3 2.5 %collective-permute-done.17 = f32[128,256]{1,0:T(8,128)S(1)} collective-permute-done((f32[128,256]{1,0:T(8,128)S(1)}, f32[128,256]{1,0:T(8,128)S(1)}, u32[]{:S(2)}, u32[]{:S(2)}) %collective-permute-start.17) | collective-permute-done | bytes 131104 | tf_op jit(solution)/shard_map/ppermute | solution.py:309
  109.9 0.5 gram_and_cores.3
  110.6 8.7 %collective-permute-done.19.q1 = f32[256,256]{1,0:T(8,128)S(1)} collective-permute-done((f32[256,256]{1,0:T(8,128)S(1)}, f32[256,256]{1,0:T(8,128)S(1)}, u32[]{:S(2)}, u32[]{:S(2)}) %collective-permute-start.19) | collective-permute-done | bytes 262176 | tf_op jit(solution)/shard_map/ppermute | solution.py:309
  119.4 13.2 %all_to_all.30.tiles_ref = f32[16,24,256]{2,1,0:T(8,128)S(1)} all-to-all(f32[16,24,256]{2,1,0:T(8,128)S(1)} %add.71), channel_id=1, replica_groups=mesh['z_hi'=2,'z_lo'=2,'y_lo'=2,'core'=2,'row'=8] {'z_lo','row'}, dimensions={0} | all-to-all | bytes 786432 | tf_op jit(solution)/shard_map/all_to_all | solution.py:304
  132.6 0.8 owner_sum.3
  133.4 3.6 %all-to-all-start.5 = ((f32[16,24,256]{2,1,0:T(8,128)}), f32[16,24,256]{2,1,0:T(8,128)S(1)}, u32[]{:S(2)}, u32[]{:S(2)}) async-start(f32[16,24,256]{2,1,0:T(8,128)} %owner_sum.3), calls=%async_computation.5 | async-start | bytes 786432 | tf_op jit(solution)/shard_map/all_to_all | solution.py:304
  137.0 0.5 collective-permute-start.21
  137.5 1.0 collective-permute-done.20.q2
  138.9 7.8 %all-to-all-done.5.mine_ref = f32[16,24,256]{2,1,0:T(8,128)S(1)} async-done(((f32[16,24,256]{2,1,0:T(8,128)}), f32[16,24,256]{2,1,0:T(8,128)S(1)}, u32[]{:S(2)}, u32[]{:S(2)}) %all-to-all-start.5) | async-done | bytes 393248 | tf_op jit(solution)/shard_map/all_to_all | solution.py:304
  146.7 1.7 %collective-permute-done.22.other_ref = f32[16,24,256]{2,1,0:T(8,128)S(1)} collective-permute-done((f32[16,24,256]{2,1,0:T(8,128)S(1)}, f32[16,24,256]{2,1,0:T(8,128)S(1)}, u32[]{:S(2)}, u32[]{:S(2)}) %collective-permute-start.22) | collective-permute-done | bytes 393248 | tf_op jit(solution)/shard_map/ppermute | solution.py:309
  148.4 7.3 %finish.1 = (f32[1024,256]{1,0:T(8,128)}, f32[8,16,256]{2,1,0:T(8,128)}) custom-call(s32[1]{0:T(128)} %bitcast.place_ref, f32[16,24,256]{2,1,0:T(8,128)S(1)} %all-to-all-done.5.mine_ref, f32[16,24,256]{2,1,0:T(8,128)S(1)} %collective-permute-done.22.other_ref, f32[256,256]{1,0:T(8,128)S(1)} %pad_maximum_fusion.3.q0, ...), custom_call_target="tpu_custom_call" | custom-call | tf_op jit(solution)/shard_map/finish/pallas_call | solution.py:153
  (40 shorter events, 2.7 us)
Async XLA Ops:
  1.7 19.7 %collective-permute-start = (f32[128,512]{1,0:T(8,128)S(1)}, f32[128,512]{1,0:T(8,128)S(1)}, u32[]{:S(2)}, u32[]{:S(2)}) collective-permute-start(f32[128,512]{1,0:T(8,128)S(1)} %get-tuple-element.90), channel_id=1, source_target_pairs={{0,32},{32,0},{1,33},{33,1},{2,34},{34,2},{3,35},{35,3},{4,36},{36... | collective-permute-start | bytes 786440 | tf_op jit(solution)/shard_map/ppermute | solution.py:309
  6.9 14.5 %all-to-all-start = ((f32[8,32,256]{2,1,0:T(8,128)}), f32[8,32,256]{2,1,0:T(8,128)S(1)}, u32[]{:S(2)}, u32[]{:S(2)}) async-start(f32[8,32,256]{2,1,0:T(8,128)} %projections.1), calls=%async_computation | async-start | bytes 524288 | tf_op jit(solution)/shard_map/all_to_all | solution.py:304
  22.5 14.0 %all-to-all-start.1 = ((f32[16,32,256]{2,1,0:T(8,128)}), f32[16,32,256]{2,1,0:T(8,128)S(1)}, u32[]{:S(2)}, u32[]{:S(2)}) async-start(f32[16,32,256]{2,1,0:T(8,128)} %owner_coefficients.1), calls=%async_computation.1 | async-start | bytes 1048576 | tf_op jit(solution)/shard_map/all_to_all | solution.py:304
  26.1 1.6 %collective-permute-start.1 = (f32[256,256]{1,0:T(8,128)S(1)}, f32[256,256]{1,0:T(8,128)S(1)}, u32[]{:S(2)}, u32[]{:S(2)}) collective-permute-start(f32[256,256]{1,0:T(8,128)S(1)} %pad_maximum_fusion), channel_id=1, source_target_pairs={{0,8},{8,0},{1,9},{9,1},{2,10},{10,2},{3,11},{11,3},{4,12},{12,4},... | collective-permute-start | bytes 786440 | tf_op jit(solution)/shard_map/ppermute | solution.py:309
  36.5 1.9 %collective-permute-start.2 = (f32[16,32,256]{2,1,0:T(8,128)S(1)}, f32[16,32,256]{2,1,0:T(8,128)S(1)}, u32[]{:S(2)}, u32[]{:S(2)}) collective-permute-start(f32[16,32,256]{2,1,0:T(8,128)S(1)} %all-to-all-done.1.mine_ref.pair_ref), channel_id=1, source_target_pairs={{0,8},{8,0},{1,9},{9,1},{2,10},{10,2},{3,11},{11,3},{4,12},{12,4},... | collective-permute-start | bytes 1572872 | tf_op jit(solution)/shard_map/ppermute | solution.py:309
  38.4 5.0 %copy-start = (f32[8,16,1024]{2,1,0:T(8,128)S(1)}, f32[8,16,1024]{2,1,0:T(8,128)}, u32[]{:S(2)}) copy-start(f32[8,16,1024]{2,1,0:T(8,128)} %param.5) | copy-start | bytes 1572868
  38.8 7.0 %collective-permute-start.3 = (f32[128,256]{1,0:T(8,128)S(1)}, f32[128,256]{1,0:T(8,128)S(1)}, u32[]{:S(2)}, u32[]{:S(2)}) collective-permute-start(f32[128,256]{1,0:T(8,128)S(1)} %get-tuple-element.53), channel_id=1, source_target_pairs={{0,96},{32,64},{64,32},{96,0},{1,97},{33,65},{65,33},{97,1},{2,98}... | collective-permute-start | bytes 393224 | tf_op jit(solution)/shard_map/ppermute | solution.py:309
  42.1 5.3 %collective-permute-start.4 = (f32[128,256]{1,0:T(8,128)S(1)}, f32[128,256]{1,0:T(8,128)S(1)}, u32[]{:S(2)}, u32[]{:S(2)}) collective-permute-start(f32[128,256]{1,0:T(8,128)S(1)} %get-tuple-element.54), channel_id=1, source_target_pairs={{0,16},{16,0},{1,17},{17,1},{2,18},{18,2},{3,19},{19,3},{4,20},{20... | collective-permute-start | bytes 393224 | tf_op jit(solution)/shard_map/ppermute | solution.py:309
  43.5 7.9 %collective-permute-start.7 = (f32[128,512]{1,0:T(8,128)S(1)}, f32[128,512]{1,0:T(8,128)S(1)}, u32[]{:S(2)}, u32[]{:S(2)}) collective-permute-start(f32[128,512]{1,0:T(8,128)S(1)} %get-tuple-element.88), channel_id=1, source_target_pairs={{0,32},{32,0},{1,33},{33,1},{2,34},{34,2},{3,35},{35,3},{4,36},{36... | collective-permute-start | bytes 786440 | tf_op jit(solution)/shard_map/ppermute | solution.py:309
  47.4 6.3 %collective-permute-start.6 = (f32[128,256]{1,0:T(8,128)S(1)}, f32[128,256]{1,0:T(8,128)S(1)}, u32[]{:S(2)}, u32[]{:S(2)}) collective-permute-start(f32[128,256]{1,0:T(8,128)S(1)} %add.63), channel_id=1, source_target_pairs={{0,96},{32,64},{64,32},{96,0},{1,97},{33,65},{65,33},{97,1},{2,98}... | collective-permute-start | bytes 393224 | tf_op jit(solution)/shard_map/ppermute | solution.py:309
  48.9 5.0 %collective-permute-start.5 = (f32[128,256]{1,0:T(8,128)S(1)}, f32[128,256]{1,0:T(8,128)S(1)}, u32[]{:S(2)}, u32[]{:S(2)}) collective-permute-start(f32[128,256]{1,0:T(8,128)S(1)} %add.62), channel_id=1, source_target_pairs={{0,16},{16,0},{1,17},{17,1},{2,18},{18,2},{3,19},{19,3},{4,20},{20... | collective-permute-start | bytes 393224 | tf_op jit(solution)/shard_map/ppermute | solution.py:309
  54.5 1.8 %collective-permute-start.8 = (f32[16,24,256]{2,1,0:T(8,128)S(1)}, f32[16,24,256]{2,1,0:T(8,128)S(1)}, u32[]{:S(2)}, u32[]{:S(2)}) collective-permute-start(f32[16,24,256]{2,1,0:T(8,128)S(1)} %get-tuple-element.60), channel_id=1, source_target_pairs={{0,8},{8,0},{1,9},{9,1},{2,10},{10,2},{3,11},{11,3},{4,12},{12,4},... | collective-permute-start | bytes 1179656 | tf_op jit(solution)/shard_map/ppermute | solution.py:309
  57.1 14.7 %all-to-all-start.2 = ((f32[16,24,256]{2,1,0:T(8,128)}), f32[16,24,256]{2,1,0:T(8,128)S(1)}, u32[]{:S(2)}, u32[]{:S(2)}) async-start(f32[16,24,256]{2,1,0:T(8,128)} %add.66), calls=%async_computation.2 | async-start | bytes 786432 | tf_op jit(solution)/shard_map/all_to_all | solution.py:304
  72.6 13.3 %all-to-all-start.3 = ((f32[16,24,256]{2,1,0:T(8,128)}), f32[16,24,256]{2,1,0:T(8,128)S(1)}, u32[]{:S(2)}, u32[]{:S(2)}) async-start(f32[16,24,256]{2,1,0:T(8,128)} %owner_sum.2), calls=%async_computation.3 | async-start | bytes 786432 | tf_op jit(solution)/shard_map/all_to_all | solution.py:304
  76.2 1.6 %collective-permute-start.9 = (f32[256,256]{1,0:T(8,128)S(1)}, f32[256,256]{1,0:T(8,128)S(1)}, u32[]{:S(2)}, u32[]{:S(2)}) collective-permute-start(f32[256,256]{1,0:T(8,128)S(1)} %pad_maximum_fusion.1), channel_id=1, source_target_pairs={{0,8},{8,0},{1,9},{9,1},{2,10},{10,2},{3,11},{11,3},{4,12},{12,4},... | collective-permute-start | bytes 786440 | tf_op jit(solution)/shard_map/ppermute | solution.py:309
  85.9 1.7 %collective-permute-start.10 = (f32[16,24,256]{2,1,0:T(8,128)S(1)}, f32[16,24,256]{2,1,0:T(8,128)S(1)}, u32[]{:S(2)}, u32[]{:S(2)}) collective-permute-start(f32[16,24,256]{2,1,0:T(8,128)S(1)} %all-to-all-done.3.mine_ref), channel_id=1, source_target_pairs={{0,8},{8,0},{1,9},{9,1},{2,10},{10,2},{3,11},{11,3},{4,12},{12,4},... | collective-permute-start | bytes 1179656 | tf_op jit(solution)/shard_map/ppermute | solution.py:309
  85.9 11.8 %collective-permute-start.14 = (f32[256,256]{1,0:T(8,128)S(1)}, f32[256,256]{1,0:T(8,128)S(1)}, u32[]{:S(2)}, u32[]{:S(2)}) collective-permute-start(f32[256,256]{1,0:T(8,128)S(1)} %pad_maximum_fusion.2.q0), channel_id=1, source_target_pairs={{0,8},{8,0},{1,9},{9,1},{2,10},{10,2},{3,11},{11,3},{4,12},{12,4},... | collective-permute-start | bytes 786440 | tf_op jit(solution)/shard_map/ppermute | solution.py:309
  86.5 8.5 %collective-permute-start.11 = (f32[256,256]{1,0:T(8,128)S(1)}, f32[256,256]{1,0:T(8,128)S(1)}, u32[]{:S(2)}, u32[]{:S(2)}) collective-permute-start(f32[256,256]{1,0:T(8,128)S(1)} %pad_maximum_fusion.2.q0), channel_id=1, source_target_pairs={{0,32},{32,0},{1,33},{33,1},{2,34},{34,2},{3,35},{35,3},{4,36},{36... | collective-permute-start | bytes 786440 | tf_op jit(solution)/shard_map/ppermute | solution.py:309
  95.0 2.8 %collective-permute-start.15 = (f32[256,256]{1,0:T(8,128)S(1)}, f32[256,256]{1,0:T(8,128)S(1)}, u32[]{:S(2)}, u32[]{:S(2)}) collective-permute-start(f32[256,256]{1,0:T(8,128)S(1)} %collective-permute-done.11.q1), channel_id=1, source_target_pairs={{0,8},{8,0},{1,9},{9,1},{2,10},{10,2},{3,11},{11,3},{4,12},{12,4},... | collective-permute-start | bytes 786440 | tf_op jit(solution)/shard_map/ppermute | solution.py:309
  95.1 7.0 %collective-permute-start.12 = (f32[128,256]{1,0:T(8,128)S(1)}, f32[128,256]{1,0:T(8,128)S(1)}, u32[]{:S(2)}, u32[]{:S(2)}) collective-permute-start(f32[128,256]{1,0:T(8,128)S(1)} %get-tuple-element.69), channel_id=1, source_target_pairs={{0,96},{32,64},{64,32},{96,0},{1,97},{33,65},{65,33},{97,1},{2,98}... | collective-permute-start | bytes 393224 | tf_op jit(solution)/shard_map/ppermute | solution.py:309
  96.4 5.7 %collective-permute-start.13 = (f32[128,256]{1,0:T(8,128)S(1)}, f32[128,256]{1,0:T(8,128)S(1)}, u32[]{:S(2)}, u32[]{:S(2)}) collective-permute-start(f32[128,256]{1,0:T(8,128)S(1)} %get-tuple-element.70), channel_id=1, source_target_pairs={{0,16},{16,0},{1,17},{17,1},{2,18},{18,2},{3,19},{19,3},{4,20},{20... | collective-permute-start | bytes 393224 | tf_op jit(solution)/shard_map/ppermute | solution.py:309
  102.2 5.1 %collective-permute-start.16 = (f32[128,256]{1,0:T(8,128)S(1)}, f32[128,256]{1,0:T(8,128)S(1)}, u32[]{:S(2)}, u32[]{:S(2)}) collective-permute-start(f32[128,256]{1,0:T(8,128)S(1)} %add.67), channel_id=1, source_target_pairs={{0,16},{16,0},{1,17},{17,1},{2,18},{18,2},{3,19},{19,3},{4,20},{20... | collective-permute-start | bytes 393224 | tf_op jit(solution)/shard_map/ppermute | solution.py:309
  103.6 6.2 %collective-permute-start.17 = (f32[128,256]{1,0:T(8,128)S(1)}, f32[128,256]{1,0:T(8,128)S(1)}, u32[]{:S(2)}, u32[]{:S(2)}) collective-permute-start(f32[128,256]{1,0:T(8,128)S(1)} %add.68), channel_id=1, source_target_pairs={{0,96},{32,64},{64,32},{96,0},{1,97},{33,65},{65,33},{97,1},{2,98}... | collective-permute-start | bytes 393224 | tf_op jit(solution)/shard_map/ppermute | solution.py:309
  110.4 8.9 %collective-permute-start.18 = (f32[16,24,256]{2,1,0:T(8,128)S(1)}, f32[16,24,256]{2,1,0:T(8,128)S(1)}, u32[]{:S(2)}, u32[]{:S(2)}) collective-permute-start(f32[16,24,256]{2,1,0:T(8,128)S(1)} %get-tuple-element.79), channel_id=1, source_target_pairs={{0,8},{8,0},{1,9},{9,1},{2,10},{10,2},{3,11},{11,3},{4,12},{12,4},... | collective-permute-start | bytes 1179656 | tf_op jit(solution)/shard_map/ppermute | solution.py:309
  110.5 8.8 %collective-permute-start.19 = (f32[256,256]{1,0:T(8,128)S(1)}, f32[256,256]{1,0:T(8,128)S(1)}, u32[]{:S(2)}, u32[]{:S(2)}) collective-permute-start(f32[256,256]{1,0:T(8,128)S(1)} %pad_maximum_fusion.3.q0), channel_id=1, source_target_pairs={{0,32},{32,0},{1,33},{33,1},{2,34},{34,2},{3,35},{35,3},{4,36},{36... | collective-permute-start | bytes 786440 | tf_op jit(solution)/shard_map/ppermute | solution.py:309
  133.4 13.3 %all-to-all-start.5 = ((f32[16,24,256]{2,1,0:T(8,128)}), f32[16,24,256]{2,1,0:T(8,128)S(1)}, u32[]{:S(2)}, u32[]{:S(2)}) async-start(f32[16,24,256]{2,1,0:T(8,128)} %owner_sum.3), calls=%async_computation.5 | async-start | bytes 786432 | tf_op jit(solution)/shard_map/all_to_all | solution.py:304
  136.9 1.6 %collective-permute-start.20 = (f32[256,256]{1,0:T(8,128)S(1)}, f32[256,256]{1,0:T(8,128)S(1)}, u32[]{:S(2)}, u32[]{:S(2)}) collective-permute-start(f32[256,256]{1,0:T(8,128)S(1)} %pad_maximum_fusion.3.q0), channel_id=1, source_target_pairs={{0,8},{8,0},{1,9},{9,1},{2,10},{10,2},{3,11},{11,3},{4,12},{12,4},... | collective-permute-start | bytes 786440 | tf_op jit(solution)/shard_map/ppermute | solution.py:309
  137.0 1.9 %collective-permute-start.21 = (f32[256,256]{1,0:T(8,128)S(1)}, f32[256,256]{1,0:T(8,128)S(1)}, u32[]{:S(2)}, u32[]{:S(2)}) collective-permute-start(f32[256,256]{1,0:T(8,128)S(1)} %collective-permute-done.19.q1), channel_id=1, source_target_pairs={{0,8},{8,0},{1,9},{9,1},{2,10},{10,2},{3,11},{11,3},{4,12},{12,4},... | collective-permute-start | bytes 786440 | tf_op jit(solution)/shard_map/ppermute | solution.py:309
  146.7 1.7 %collective-permute-start.22 = (f32[16,24,256]{2,1,0:T(8,128)S(1)}, f32[16,24,256]{2,1,0:T(8,128)S(1)}, u32[]{:S(2)}, u32[]{:S(2)}) collective-permute-start(f32[16,24,256]{2,1,0:T(8,128)S(1)} %all-to-all-done.5.mine_ref), channel_id=1, source_target_pairs={{0,8},{8,0},{1,9},{9,1},{2,10},{10,2},{3,11},{11,3},{4,12},{12,4},... | collective-permute-start | bytes 1179656 | tf_op jit(solution)/shard_map/ppermute | solution.py:309

commit v10 on v9

--- a/solution.py
+++ b/solution.py
@@ -14,7 +14,7 @@
 SUBLANES = 8
 PANEL = 32
 STEPS = 4
-ROW = ("z_lo", "row")
+ROW = ("y_lo", "row")
 STEPS_AWAY = (0, 2, 1, 3)
 
 
@@ -204,15 +204,15 @@
 
 
 def quarter_of(place_ref):
+    return place_ref[0]
+
+
+def core_of(place_ref):
+    return place_ref[0] % 2
+
+
+def pair_of(place_ref):
     return place_ref[0] // 2
-
-
-def core_of(place_ref):
-    return place_ref[0] // 2 % 2
-
-
-def pair_of(place_ref):
-    return place_ref[0] % 2
 
 
 def by_distance(pair, ref):
@@ -318,14 +318,13 @@
 
 
 def across(x):
-    return from_peer(x, "z_lo", 1)
+    return from_peer(x, "y_lo", 1)
 
 
 def plane_total(x, y, besides):
-    z, y_lo = (("z_hi", "z_lo"), 3), ("y_lo", 1)
     done = []
-    for x_step, y_step, beside in zip((z, y_lo), (y_lo, z), besides):
-        moved, beside = together((from_peer(x, *x_step), from_peer(y, *y_step)), beside)
+    for x_step, y_step, beside in zip((1, 3), (3, 1), besides):
+        moved, beside = together((from_peer(x, "z", x_step), from_peer(y, "z", y_step)), beside)
         x, y = x + moved[0], y + moved[1]
         done.append(beside)
     return (x, y), done
@@ -379,9 +378,8 @@
 def local(b_factors, a_factors, u_start, v_start):
     shape = (*b_factors.shape[:2], u_start.shape[1])
     width, rank = u_start.shape
-    pair_index, core = lax.axis_index("z_lo"), lax.axis_index("core")
-    bit = pair_index ^ lax.axis_index("z_hi")
-    place = jnp.reshape(4 * bit + 2 * core + pair_index, (1,)).astype(jnp.int32)
+    bit, core = lax.axis_index("y_lo"), lax.axis_index("core")
+    place = jnp.reshape(2 * bit + core, (1,)).astype(jnp.int32)
     b = b_factors.reshape(-1, width)
     a = a_factors.reshape(-1, width)
     b_half = column_half(b, bit)
@@ -460,10 +458,8 @@
 
 def solution(mesh):
     count, rows = mesh.devices.shape
-    mesh = Mesh(
-        mesh.devices.reshape(count // 8, 2, 2, 2, rows), ("z_hi", "z_lo", "y_lo", "core", "row")
-    )
-    tenant = ("z_hi", "z_lo", "y_lo", "core")
+    mesh = Mesh(mesh.devices.reshape(count // 4, 2, 2, rows), ("z", "y_lo", "core", "row"))
+    tenant = ("z", "y_lo", "core")
     in_specs = (P(tenant, None, "row"), P(tenant, None, "row"), P("row", None), P("row", None))
     out_specs = (P("row", None), P("row", None), P(tenant, None, None), P(tenant, None, None))
     return jax.shard_map(local, mesh=mesh, in_specs=in_specs, out_specs=out_specs, check_vma=False)

time: 158 us -> 157 us (level)
  waiting for transfers between devices: 76.9 us -> 68.6 us
  starting transfers between devices: 38.9 us -> 45.2 us
    all_to_all x5, waiting for transfers between devices: 44.1 us -> 37.4 us  [exchanged(): return lax.all_to_all(tiles, axis, 0, 0, tiled=True)]
    all_to_all x5, starting transfers between devices: 20.3 us -> 26.2 us  [exchanged(): return lax.all_to_all(tiles, axis, 0, 0, tiled=True)]
  transfers between devices with their start and end apart: 28 -> 28, of which waited for: 22 -> 21; matrix products, arithmetic and copies ran while one was open for 0% -> 0% of each run, Pallas kernels for 8% -> 8%
where the time goes in v10:
time: 157 us; the launch traced here: 154 us
  waiting for transfers between devices  68.6 us (44%)
  starting transfers between devices  45.2 us (29%)
  Pallas kernels  23.6 us (15%)
  blocking collectives  13.2 us (8%)
    all_to_all x5, waiting for transfers between devices, exchanged(): return lax.all_to_all(tiles, axis, 0, 0, tiled=True)  37.4 us
    ppermute x23, waiting for transfers between devices, from_peer(): return lax.ppermute(x, axis, [(i, i ^ step) for i in range(count)])  31.2 us
    all_to_all x5, starting transfers between devices, exchanged(): return lax.all_to_all(tiles, axis, 0, 0, tiled=True)  26.2 us
    pallas_call x10, Pallas kernels, call(): pl.pallas_call(kernel, out_shape=shapes if len(shapes) > 1 else shapes[0]...  23.6 us
    ppermute x23, starting transfers between devices, from_peer(): return lax.ppermute(x, axis, [(i, i ^ step) for i in range(count)])  19 us
    all_to_all x1, blocking collectives, exchanged(): return lax.all_to_all(tiles, axis, 0, 0, tiled=True)  13.2 us
  transfers between devices with their start and end apart: 28, of which 21 were waited for; matrix products, arithmetic and copies ran while one was open for 0% of the time, Pallas kernels for 8%

profile of v10, /device:TPU:8, one launch (start us, length us, event | category | flops | bytes accessed | tf_op | source)
XLA Modules:
  0.0 153.7 jit_solution(14791024660844106631)
XLA Ops:
  0.6 1.1 constant_dynamic-slice_fusion.10
  2.2 3.2 %projections.1 = f32[8,32,256]{2,1,0:T(8,128)} custom-call(f32[128,1024]{1,0:T(8,128)} %bitcast.4, f32[128,1024]{1,0:T(8,128)} %bitcast.5, f32[1024,256]{1,0:T(8,128)} %u_hbm.1, f32[1024,256]{1,0:T(8,128)} %v_hbm.1), custom_call_target="tpu_custom_call" | custom-call | tf_op jit(solution)/shard_map/projections/pallas_call | solution.py:153
  5.3 6.4 %all-to-all-start = ((f32[8,32,256]{2,1,0:T(8,128)}), f32[8,32,256]{2,1,0:T(8,128)S(1)}, u32[]{:S(2)}, u32[]{:S(2)}) async-start(f32[8,32,256]{2,1,0:T(8,128)} %projections.1), calls=%async_computation | async-start | bytes 524288 | tf_op jit(solution)/shard_map/all_to_all | solution.py:304
  11.7 8.4 %all-to-all-done.tiles_ref = f32[8,32,256]{2,1,0:T(8,128)S(1)} async-done(((f32[8,32,256]{2,1,0:T(8,128)}), f32[8,32,256]{2,1,0:T(8,128)S(1)}, u32[]{:S(2)}, u32[]{:S(2)}) %all-to-all-start) | async-done | bytes 262176 | tf_op jit(solution)/shard_map/all_to_all | solution.py:304
  20.2 1.1 owner_coefficients.1
  21.3 5.3 %all-to-all-start.1 = ((f32[16,32,256]{2,1,0:T(8,128)}), f32[16,32,256]{2,1,0:T(8,128)S(1)}, u32[]{:S(2)}, u32[]{:S(2)}) async-start(f32[16,32,256]{2,1,0:T(8,128)} %owner_coefficients.1), calls=%async_computation.1 | async-start | bytes 1048576 | tf_op jit(solution)/shard_map/all_to_all | solution.py:304
  26.7 1.5 collective-permute-done.1.f2
  28.3 7.0 %all-to-all-done.1.mine_ref.pair_ref = f32[16,32,256]{2,1,0:T(8,128)S(1)} async-done(((f32[16,32,256]{2,1,0:T(8,128)}), f32[16,32,256]{2,1,0:T(8,128)S(1)}, u32[]{:S(2)}, u32[]{:S(2)}) %all-to-all-start.1) | async-done | bytes 524320 | tf_op jit(solution)/shard_map/all_to_all | solution.py:304
  35.3 1.9 %collective-permute-done.2.other_ref.pair_other_ref = f32[16,32,256]{2,1,0:T(8,128)S(1)} collective-permute-done((f32[16,32,256]{2,1,0:T(8,128)S(1)}, f32[16,32,256]{2,1,0:T(8,128)S(1)}, u32[]{:S(2)}, u32[]{:S(2)}) %collective-permute-start.2) | collective-permute-done | bytes 524320 | tf_op jit(solution)/shard_map/ppermute | solution.py:309
  37.6 2.0 %collective-permute-start.3 = (f32[128,256]{1,0:T(8,128)S(1)}, f32[128,256]{1,0:T(8,128)S(1)}, u32[]{:S(2)}, u32[]{:S(2)}) collective-permute-start(f32[128,256]{1,0:T(8,128)S(1)} %get-tuple-element.53), channel_id=1, source_target_pairs={{0,32},{32,0},{64,96},{96,64},{1,33},{33,1},{65,97},{97,65},{2,34}... | collective-permute-start | bytes 393224 | tf_op jit(solution)/shard_map/ppermute | solution.py:309
  39.6 2.5 %collective-permute-start.4 = (f32[128,256]{1,0:T(8,128)S(1)}, f32[128,256]{1,0:T(8,128)S(1)}, u32[]{:S(2)}, u32[]{:S(2)}) collective-permute-start(f32[128,256]{1,0:T(8,128)S(1)} %get-tuple-element.54), channel_id=1, source_target_pairs={{0,96},{32,64},{64,32},{96,0},{1,97},{33,65},{65,33},{97,1},{2,98}... | collective-permute-start | bytes 393224 | tf_op jit(solution)/shard_map/ppermute | solution.py:309
  42.2 1.5 collective-permute-start.7
  43.7 2.4 %collective-permute-done.4 = f32[128,256]{1,0:T(8,128)S(1)} collective-permute-done((f32[128,256]{1,0:T(8,128)S(1)}, f32[128,256]{1,0:T(8,128)S(1)}, u32[]{:S(2)}, u32[]{:S(2)}) %collective-permute-start.4) | collective-permute-done | bytes 131104 | tf_op jit(solution)/shard_map/ppermute | solution.py:309
  46.1 0.7 collective-permute-start.6
  46.8 2.3 %collective-permute-start.5 = (f32[128,256]{1,0:T(8,128)S(1)}, f32[128,256]{1,0:T(8,128)S(1)}, u32[]{:S(2)}, u32[]{:S(2)}) collective-permute-start(f32[128,256]{1,0:T(8,128)S(1)} %add.58), channel_id=1, source_target_pairs={{0,96},{32,64},{64,32},{96,0},{1,97},{33,65},{65,33},{97,1},{2,98}... | collective-permute-start | bytes 393224 | tf_op jit(solution)/shard_map/ppermute | solution.py:309
  49.2 0.9 collective-permute-done.7
  50.1 1.1 collective-permute-done.6
  51.2 1.8 %collective-permute-done.5 = f32[128,256]{1,0:T(8,128)S(1)} collective-permute-done((f32[128,256]{1,0:T(8,128)S(1)}, f32[128,256]{1,0:T(8,128)S(1)}, u32[]{:S(2)}, u32[]{:S(2)}) %collective-permute-start.5) | collective-permute-done | bytes 131104 | tf_op jit(solution)/shard_map/ppermute | solution.py:309
  53.0 0.5 gram_and_cores.2
  53.7 1.7 %collective-permute-done.8 = f32[16,24,256]{2,1,0:T(8,128)S(1)} collective-permute-done((f32[16,24,256]{2,1,0:T(8,128)S(1)}, f32[16,24,256]{2,1,0:T(8,128)S(1)}, u32[]{:S(2)}, u32[]{:S(2)}) %collective-permute-start.8) | collective-permute-done | bytes 393248 | tf_op jit(solution)/shard_map/ppermute | solution.py:309
  55.4 0.8 add.62
  56.2 4.9 %all-to-all-start.2 = ((f32[16,24,256]{2,1,0:T(8,128)}), f32[16,24,256]{2,1,0:T(8,128)S(1)}, u32[]{:S(2)}, u32[]{:S(2)}) async-start(f32[16,24,256]{2,1,0:T(8,128)} %add.62), calls=%async_computation.2 | async-start | bytes 786432 | tf_op jit(solution)/shard_map/all_to_all | solution.py:304
  61.1 9.2 %all-to-all-done.2.tiles_ref = f32[16,24,256]{2,1,0:T(8,128)S(1)} async-done(((f32[16,24,256]{2,1,0:T(8,128)}), f32[16,24,256]{2,1,0:T(8,128)S(1)}, u32[]{:S(2)}, u32[]{:S(2)}) %all-to-all-start.2) | async-done | bytes 393248 | tf_op jit(solution)/shard_map/all_to_all | solution.py:304
  70.3 0.8 owner_sum.2
  71.1 4.8 %all-to-all-start.3 = ((f32[16,24,256]{2,1,0:T(8,128)}), f32[16,24,256]{2,1,0:T(8,128)S(1)}, u32[]{:S(2)}, u32[]{:S(2)}) async-start(f32[16,24,256]{2,1,0:T(8,128)} %owner_sum.2), calls=%async_computation.3 | async-start | bytes 786432 | tf_op jit(solution)/shard_map/all_to_all | solution.py:304
  76.0 1.5 collective-permute-done.9.f2
  77.6 6.6 %all-to-all-done.3.mine_ref = f32[16,24,256]{2,1,0:T(8,128)S(1)} async-done(((f32[16,24,256]{2,1,0:T(8,128)}), f32[16,24,256]{2,1,0:T(8,128)S(1)}, u32[]{:S(2)}, u32[]{:S(2)}) %all-to-all-start.3) | async-done | bytes 393248 | tf_op jit(solution)/shard_map/all_to_all | solution.py:304
  84.2 0.6 collective-permute-start.14
  84.7 1.5 collective-permute-start.11
  86.2 7.3 %turn_over.1 = (f32[256,256]{1,0:T(8,128)S(1)}, f32[8,16,256]{2,1,0:T(8,128)}, f32[128,256]{1,0:T(8,128)S(1)}, f32[128,256]{1,0:T(8,128)S(1)}) custom-call(s32[1]{0:T(128)} %bitcast.place_ref, f32[16,24,256]{2,1,0:T(8,128)S(1)} %all-to-all-done.3.mine_ref, f32[16,24,256]{2,1,0:T(8,128)S(1)} %collective-permute-done.10.other_ref, ...), custom_call_target="tpu_custom_call" | custom-call | flops 6442450944 | tf_op jit(solution)/shard_map/turn_over/pallas_call | solution.py:153
  93.8 2.5 %collective-permute-start.13 = (f32[128,256]{1,0:T(8,128)S(1)}, f32[128,256]{1,0:T(8,128)S(1)}, u32[]{:S(2)}, u32[]{:S(2)}) collective-permute-start(f32[128,256]{1,0:T(8,128)S(1)} %get-tuple-element.70), channel_id=1, source_target_pairs={{0,96},{32,64},{64,32},{96,0},{1,97},{33,65},{65,33},{97,1},{2,98}... | collective-permute-start | bytes 393224 | tf_op jit(solution)/shard_map/ppermute | solution.py:309
  96.3 1.6 %left_basis.1 = f32[1024,256]{1,0:T(8,128)} custom-call(s32[1]{0:T(128)} %bitcast.place_ref, f32[256,256]{1,0:T(8,128)S(1)} %get-tuple-element.71.inverse_ref, f32[256,256]{1,0:T(8,128)S(1)} %pad_maximum_fusion.2.q0, f32[256,256]{1,0:T(8,128)S(1)} %collective-permute-done.11.q1, f32[256,256]{1,0:T(8,128)S(1)} %collective-permute-done.14.q2, ...), custom_call_target="tpu_custom_call" | custom-call | flops 402653184 | tf_op jit(solution)/shard_map/left_basis/pallas_call | solution.py:153
  98.0 1.5 collective-permute-done.12
  99.4 1.2 collective-permute-done.13
  100.7 2.5 %collective-permute-start.16 = (f32[128,256]{1,0:T(8,128)S(1)}, f32[128,256]{1,0:T(8,128)S(1)}, u32[]{:S(2)}, u32[]{:S(2)}) collective-permute-start(f32[128,256]{1,0:T(8,128)S(1)} %add.63), channel_id=1, source_target_pairs={{0,96},{32,64},{64,32},{96,0},{1,97},{33,65},{65,33},{97,1},{2,98}... | collective-permute-start | bytes 393224 | tf_op jit(solution)/shard_map/ppermute | solution.py:309
  103.2 3.7 %collective-permute-done.16 = f32[128,256]{1,0:T(8,128)S(1)} collective-permute-done((f32[128,256]{1,0:T(8,128)S(1)}, f32[128,256]{1,0:T(8,128)S(1)}, u32[]{:S(2)}, u32[]{:S(2)}) %collective-permute-start.16) | collective-permute-done | bytes 131104 | tf_op jit(solution)/shard_map/ppermute | solution.py:309
  107.0 1.3 collective-permute-done.17
  108.3 0.5 gram_and_cores.3
  108.9 1.3 collective-permute-start.19
  110.2 7.5 %collective-permute-done.19.q1 = f32[256,256]{1,0:T(8,128)S(1)} collective-permute-done((f32[256,256]{1,0:T(8,128)S(1)}, f32[256,256]{1,0:T(8,128)S(1)}, u32[]{:S(2)}, u32[]{:S(2)}) %collective-permute-start.19) | collective-permute-done | bytes 262176 | tf_op jit(solution)/shard_map/ppermute | solution.py:309
  117.7 13.2 %all_to_all.30.tiles_ref = f32[16,24,256]{2,1,0:T(8,128)S(1)} all-to-all(f32[16,24,256]{2,1,0:T(8,128)S(1)} %add.67), channel_id=1, replica_groups=mesh['z'=4,'y_lo'=2,'core'=2,'row'=8] {'y_lo','row'}, dimensions={0} | all-to-all | bytes 786432 | tf_op jit(solution)/shard_map/all_to_all | solution.py:304
  131.0 0.8 owner_sum.3
  131.8 4.8 %all-to-all-start.5 = ((f32[16,24,256]{2,1,0:T(8,128)}), f32[16,24,256]{2,1,0:T(8,128)S(1)}, u32[]{:S(2)}, u32[]{:S(2)}) async-start(f32[16,24,256]{2,1,0:T(8,128)} %owner_sum.3), calls=%async_computation.5 | async-start | bytes 786432 | tf_op jit(solution)/shard_map/all_to_all | solution.py:304
  136.6 0.5 collective-permute-start.21
  137.1 1.0 collective-permute-done.20.q2
  138.5 6.2 %all-to-all-done.5.mine_ref = f32[16,24,256]{2,1,0:T(8,128)S(1)} async-done(((f32[16,24,256]{2,1,0:T(8,128)}), f32[16,24,256]{2,1,0:T(8,128)S(1)}, u32[]{:S(2)}, u32[]{:S(2)}) %all-to-all-start.5) | async-done | bytes 393248 | tf_op jit(solution)/shard_map/all_to_all | solution.py:304
  144.7 1.7 %collective-permute-done.22.other_ref = f32[16,24,256]{2,1,0:T(8,128)S(1)} collective-permute-done((f32[16,24,256]{2,1,0:T(8,128)S(1)}, f32[16,24,256]{2,1,0:T(8,128)S(1)}, u32[]{:S(2)}, u32[]{:S(2)}) %collective-permute-start.22) | collective-permute-done | bytes 393248 | tf_op jit(solution)/shard_map/ppermute | solution.py:309
  146.4 7.3 %finish.1 = (f32[1024,256]{1,0:T(8,128)}, f32[8,16,256]{2,1,0:T(8,128)}) custom-call(s32[1]{0:T(128)} %bitcast.place_ref, f32[16,24,256]{2,1,0:T(8,128)S(1)} %all-to-all-done.5.mine_ref, f32[16,24,256]{2,1,0:T(8,128)S(1)} %collective-permute-done.22.other_ref, f32[256,256]{1,0:T(8,128)S(1)} %pad_maximum_fusion.3.q0, ...), custom_call_target="tpu_custom_call" | custom-call | tf_op jit(solution)/shard_map/finish/pallas_call | solution.py:153
  (40 shorter events, 2.3 us)
Async XLA Ops:
  1.7 18.5 %collective-permute-start = (f32[128,512]{1,0:T(8,128)S(1)}, f32[128,512]{1,0:T(8,128)S(1)}, u32[]{:S(2)}, u32[]{:S(2)}) collective-permute-start(f32[128,512]{1,0:T(8,128)S(1)} %get-tuple-element.90), channel_id=1, source_target_pairs={{0,16},{16,0},{1,17},{17,1},{2,18},{18,2},{3,19},{19,3},{4,20},{20... | collective-permute-start | bytes 786440 | tf_op jit(solution)/shard_map/ppermute | solution.py:309
  5.3 14.9 %all-to-all-start = ((f32[8,32,256]{2,1,0:T(8,128)}), f32[8,32,256]{2,1,0:T(8,128)S(1)}, u32[]{:S(2)}, u32[]{:S(2)}) async-start(f32[8,32,256]{2,1,0:T(8,128)} %projections.1), calls=%async_computation | async-start | bytes 524288 | tf_op jit(solution)/shard_map/all_to_all | solution.py:304
  21.3 14.0 %all-to-all-start.1 = ((f32[16,32,256]{2,1,0:T(8,128)}), f32[16,32,256]{2,1,0:T(8,128)S(1)}, u32[]{:S(2)}, u32[]{:S(2)}) async-start(f32[16,32,256]{2,1,0:T(8,128)} %owner_coefficients.1), calls=%async_computation.1 | async-start | bytes 1048576 | tf_op jit(solution)/shard_map/all_to_all | solution.py:304
  26.7 1.6 %collective-permute-start.1 = (f32[256,256]{1,0:T(8,128)S(1)}, f32[256,256]{1,0:T(8,128)S(1)}, u32[]{:S(2)}, u32[]{:S(2)}) collective-permute-start(f32[256,256]{1,0:T(8,128)S(1)} %pad_maximum_fusion), channel_id=1, source_target_pairs={{0,8},{8,0},{1,9},{9,1},{2,10},{10,2},{3,11},{11,3},{4,12},{12,4},... | collective-permute-start | bytes 786440 | tf_op jit(solution)/shard_map/ppermute | solution.py:309
  35.3 1.9 %collective-permute-start.2 = (f32[16,32,256]{2,1,0:T(8,128)S(1)}, f32[16,32,256]{2,1,0:T(8,128)S(1)}, u32[]{:S(2)}, u32[]{:S(2)}) collective-permute-start(f32[16,32,256]{2,1,0:T(8,128)S(1)} %all-to-all-done.1.mine_ref.pair_ref), channel_id=1, source_target_pairs={{0,8},{8,0},{1,9},{9,1},{2,10},{10,2},{3,11},{11,3},{4,12},{12,4},... | collective-permute-start | bytes 1572872 | tf_op jit(solution)/shard_map/ppermute | solution.py:309
  37.2 5.0 %copy-start = (f32[8,16,1024]{2,1,0:T(8,128)S(1)}, f32[8,16,1024]{2,1,0:T(8,128)}, u32[]{:S(2)}) copy-start(f32[8,16,1024]{2,1,0:T(8,128)} %param.5) | copy-start | bytes 1572868
  37.6 6.1 %collective-permute-start.3 = (f32[128,256]{1,0:T(8,128)S(1)}, f32[128,256]{1,0:T(8,128)S(1)}, u32[]{:S(2)}, u32[]{:S(2)}) collective-permute-start(f32[128,256]{1,0:T(8,128)S(1)} %get-tuple-element.53), channel_id=1, source_target_pairs={{0,32},{32,0},{64,96},{96,64},{1,33},{33,1},{65,97},{97,65},{2,34}... | collective-permute-start | bytes 393224 | tf_op jit(solution)/shard_map/ppermute | solution.py:309
  39.6 6.5 %collective-permute-start.4 = (f32[128,256]{1,0:T(8,128)S(1)}, f32[128,256]{1,0:T(8,128)S(1)}, u32[]{:S(2)}, u32[]{:S(2)}) collective-permute-start(f32[128,256]{1,0:T(8,128)S(1)} %get-tuple-element.54), channel_id=1, source_target_pairs={{0,96},{32,64},{64,32},{96,0},{1,97},{33,65},{65,33},{97,1},{2,98}... | collective-permute-start | bytes 393224 | tf_op jit(solution)/shard_map/ppermute | solution.py:309
  42.2 7.9 %collective-permute-start.7 = (f32[128,512]{1,0:T(8,128)S(1)}, f32[128,512]{1,0:T(8,128)S(1)}, u32[]{:S(2)}, u32[]{:S(2)}) collective-permute-start(f32[128,512]{1,0:T(8,128)S(1)} %get-tuple-element.88), channel_id=1, source_target_pairs={{0,16},{16,0},{1,17},{17,1},{2,18},{18,2},{3,19},{19,3},{4,20},{20... | collective-permute-start | bytes 786440 | tf_op jit(solution)/shard_map/ppermute | solution.py:309
  46.1 5.0 %collective-permute-start.6 = (f32[128,256]{1,0:T(8,128)S(1)}, f32[128,256]{1,0:T(8,128)S(1)}, u32[]{:S(2)}, u32[]{:S(2)}) collective-permute-start(f32[128,256]{1,0:T(8,128)S(1)} %add.59), channel_id=1, source_target_pairs={{0,32},{32,0},{64,96},{96,64},{1,33},{33,1},{65,97},{97,65},{2,34}... | collective-permute-start | bytes 393224 | tf_op jit(solution)/shard_map/ppermute | solution.py:309
  46.8 6.2 %collective-permute-start.5 = (f32[128,256]{1,0:T(8,128)S(1)}, f32[128,256]{1,0:T(8,128)S(1)}, u32[]{:S(2)}, u32[]{:S(2)}) collective-permute-start(f32[128,256]{1,0:T(8,128)S(1)} %add.58), channel_id=1, source_target_pairs={{0,96},{32,64},{64,32},{96,0},{1,97},{33,65},{65,33},{97,1},{2,98}... | collective-permute-start | bytes 393224 | tf_op jit(solution)/shard_map/ppermute | solution.py:309
  53.6 1.8 %collective-permute-start.8 = (f32[16,24,256]{2,1,0:T(8,128)S(1)}, f32[16,24,256]{2,1,0:T(8,128)S(1)}, u32[]{:S(2)}, u32[]{:S(2)}) collective-permute-start(f32[16,24,256]{2,1,0:T(8,128)S(1)} %get-tuple-element.60), channel_id=1, source_target_pairs={{0,8},{8,0},{1,9},{9,1},{2,10},{10,2},{3,11},{11,3},{4,12},{12,4},... | collective-permute-start | bytes 1179656 | tf_op jit(solution)/shard_map/ppermute | solution.py:309
  56.2 14.2 %all-to-all-start.2 = ((f32[16,24,256]{2,1,0:T(8,128)}), f32[16,24,256]{2,1,0:T(8,128)S(1)}, u32[]{:S(2)}, u32[]{:S(2)}) async-start(f32[16,24,256]{2,1,0:T(8,128)} %add.62), calls=%async_computation.2 | async-start | bytes 786432 | tf_op jit(solution)/shard_map/all_to_all | solution.py:304
  71.1 13.0 %all-to-all-start.3 = ((f32[16,24,256]{2,1,0:T(8,128)}), f32[16,24,256]{2,1,0:T(8,128)S(1)}, u32[]{:S(2)}, u32[]{:S(2)}) async-start(f32[16,24,256]{2,1,0:T(8,128)} %owner_sum.2), calls=%async_computation.3 | async-start | bytes 786432 | tf_op jit(solution)/shard_map/all_to_all | solution.py:304
  75.9 1.6 %collective-permute-start.9 = (f32[256,256]{1,0:T(8,128)S(1)}, f32[256,256]{1,0:T(8,128)S(1)}, u32[]{:S(2)}, u32[]{:S(2)}) collective-permute-start(f32[256,256]{1,0:T(8,128)S(1)} %pad_maximum_fusion.1), channel_id=1, source_target_pairs={{0,8},{8,0},{1,9},{9,1},{2,10},{10,2},{3,11},{11,3},{4,12},{12,4},... | collective-permute-start | bytes 786440 | tf_op jit(solution)/shard_map/ppermute | solution.py:309
  84.1 2.1 %collective-permute-start.10 = (f32[16,24,256]{2,1,0:T(8,128)S(1)}, f32[16,24,256]{2,1,0:T(8,128)S(1)}, u32[]{:S(2)}, u32[]{:S(2)}) collective-permute-start(f32[16,24,256]{2,1,0:T(8,128)S(1)} %all-to-all-done.3.mine_ref), channel_id=1, source_target_pairs={{0,8},{8,0},{1,9},{9,1},{2,10},{10,2},{3,11},{11,3},{4,12},{12,4},... | collective-permute-start | bytes 1179656 | tf_op jit(solution)/shard_map/ppermute | solution.py:309
  84.2 12.2 %collective-permute-start.14 = (f32[256,256]{1,0:T(8,128)S(1)}, f32[256,256]{1,0:T(8,128)S(1)}, u32[]{:S(2)}, u32[]{:S(2)}) collective-permute-start(f32[256,256]{1,0:T(8,128)S(1)} %pad_maximum_fusion.2.q0), channel_id=1, source_target_pairs={{0,8},{8,0},{1,9},{9,1},{2,10},{10,2},{3,11},{11,3},{4,12},{12,4},... | collective-permute-start | bytes 786440 | tf_op jit(solution)/shard_map/ppermute | solution.py:309
  84.7 8.8 %collective-permute-start.11 = (f32[256,256]{1,0:T(8,128)S(1)}, f32[256,256]{1,0:T(8,128)S(1)}, u32[]{:S(2)}, u32[]{:S(2)}) collective-permute-start(f32[256,256]{1,0:T(8,128)S(1)} %pad_maximum_fusion.2.q0), channel_id=1, source_target_pairs={{0,16},{16,0},{1,17},{17,1},{2,18},{18,2},{3,19},{19,3},{4,20},{20... | collective-permute-start | bytes 786440 | tf_op jit(solution)/shard_map/ppermute | solution.py:309
  93.5 2.8 %collective-permute-start.15 = (f32[256,256]{1,0:T(8,128)S(1)}, f32[256,256]{1,0:T(8,128)S(1)}, u32[]{:S(2)}, u32[]{:S(2)}) collective-permute-start(f32[256,256]{1,0:T(8,128)S(1)} %collective-permute-done.11.q1), channel_id=1, source_target_pairs={{0,8},{8,0},{1,9},{9,1},{2,10},{10,2},{3,11},{11,3},{4,12},{12,4},... | collective-permute-start | bytes 786440 | tf_op jit(solution)/shard_map/ppermute | solution.py:309
  93.5 5.9 %collective-permute-start.12 = (f32[128,256]{1,0:T(8,128)S(1)}, f32[128,256]{1,0:T(8,128)S(1)}, u32[]{:S(2)}, u32[]{:S(2)}) collective-permute-start(f32[128,256]{1,0:T(8,128)S(1)} %get-tuple-element.69), channel_id=1, source_target_pairs={{0,32},{32,0},{64,96},{96,64},{1,33},{33,1},{65,97},{97,65},{2,34}... | collective-permute-start | bytes 393224 | tf_op jit(solution)/shard_map/ppermute | solution.py:309
  93.8 6.8 %collective-permute-start.13 = (f32[128,256]{1,0:T(8,128)S(1)}, f32[128,256]{1,0:T(8,128)S(1)}, u32[]{:S(2)}, u32[]{:S(2)}) collective-permute-start(f32[128,256]{1,0:T(8,128)S(1)} %get-tuple-element.70), channel_id=1, source_target_pairs={{0,96},{32,64},{64,32},{96,0},{1,97},{33,65},{65,33},{97,1},{2,98}... | collective-permute-start | bytes 393224 | tf_op jit(solution)/shard_map/ppermute | solution.py:309
  100.7 6.3 %collective-permute-start.16 = (f32[128,256]{1,0:T(8,128)S(1)}, f32[128,256]{1,0:T(8,128)S(1)}, u32[]{:S(2)}, u32[]{:S(2)}) collective-permute-start(f32[128,256]{1,0:T(8,128)S(1)} %add.63), channel_id=1, source_target_pairs={{0,96},{32,64},{64,32},{96,0},{1,97},{33,65},{65,33},{97,1},{2,98}... | collective-permute-start | bytes 393224 | tf_op jit(solution)/shard_map/ppermute | solution.py:309
  103.2 5.0 %collective-permute-start.17 = (f32[128,256]{1,0:T(8,128)S(1)}, f32[128,256]{1,0:T(8,128)S(1)}, u32[]{:S(2)}, u32[]{:S(2)}) collective-permute-start(f32[128,256]{1,0:T(8,128)S(1)} %add.64), channel_id=1, source_target_pairs={{0,32},{32,0},{64,96},{96,64},{1,33},{33,1},{65,97},{97,65},{2,34}... | collective-permute-start | bytes 393224 | tf_op jit(solution)/shard_map/ppermute | solution.py:309
  108.8 8.9 %collective-permute-start.18 = (f32[16,24,256]{2,1,0:T(8,128)S(1)}, f32[16,24,256]{2,1,0:T(8,128)S(1)}, u32[]{:S(2)}, u32[]{:S(2)}) collective-permute-start(f32[16,24,256]{2,1,0:T(8,128)S(1)} %get-tuple-element.79), channel_id=1, source_target_pairs={{0,8},{8,0},{1,9},{9,1},{2,10},{10,2},{3,11},{11,3},{4,12},{12,4},... | collective-permute-start | bytes 1179656 | tf_op jit(solution)/shard_map/ppermute | solution.py:309
  108.9 8.8 %collective-permute-start.19 = (f32[256,256]{1,0:T(8,128)S(1)}, f32[256,256]{1,0:T(8,128)S(1)}, u32[]{:S(2)}, u32[]{:S(2)}) collective-permute-start(f32[256,256]{1,0:T(8,128)S(1)} %pad_maximum_fusion.3.q0), channel_id=1, source_target_pairs={{0,16},{16,0},{1,17},{17,1},{2,18},{18,2},{3,19},{19,3},{4,20},{20... | collective-permute-start | bytes 786440 | tf_op jit(solution)/shard_map/ppermute | solution.py:309
  131.8 12.9 %all-to-all-start.5 = ((f32[16,24,256]{2,1,0:T(8,128)}), f32[16,24,256]{2,1,0:T(8,128)S(1)}, u32[]{:S(2)}, u32[]{:S(2)}) async-start(f32[16,24,256]{2,1,0:T(8,128)} %owner_sum.3), calls=%async_computation.5 | async-start | bytes 786432 | tf_op jit(solution)/shard_map/all_to_all | solution.py:304
  136.6 1.5 collective-permute-start.20
  136.6 1.9 %collective-permute-start.21 = (f32[256,256]{1,0:T(8,128)S(1)}, f32[256,256]{1,0:T(8,128)S(1)}, u32[]{:S(2)}, u32[]{:S(2)}) collective-permute-start(f32[256,256]{1,0:T(8,128)S(1)} %collective-permute-done.19.q1), channel_id=1, source_target_pairs={{0,8},{8,0},{1,9},{9,1},{2,10},{10,2},{3,11},{11,3},{4,12},{12,4},... | collective-permute-start | bytes 786440 | tf_op jit(solution)/shard_map/ppermute | solution.py:309
  144.7 1.7 %collective-permute-start.22 = (f32[16,24,256]{2,1,0:T(8,128)S(1)}, f32[16,24,256]{2,1,0:T(8,128)S(1)}, u32[]{:S(2)}, u32[]{:S(2)}) collective-permute-start(f32[16,24,256]{2,1,0:T(8,128)S(1)} %all-to-all-done.5.mine_ref), channel_id=1, source_target_pairs={{0,8},{8,0},{1,9},{9,1},{2,10},{10,2},{3,11},{11,3},{4,12},{12,4},... | collective-permute-start | bytes 1179656 | tf_op jit(solution)/shard_map/ppermute | solution.py:309

commit v11 on v10

--- a/solution.py
+++ b/solution.py
@@ -285,19 +285,14 @@
         out_ref[rows, :] = product(ref[...], inverse, 1, 1) * scale
 
 
-def left_basis(place_ref, inverse_ref, q0, q1, q2, q3, out_ref):
+def whole_basis(place_ref, inverse_ref, q0, q1, q2, q3, out_ref):
     scaled_basis(quarter_of(place_ref), inverse_ref[...], (q0, q1, q2, q3), out_ref)
 
 
-def finish(
-    place_ref, mine_ref, other_ref, q0, q1, q2, q3, out_ref, right_ref, inverse_ref, *scratch
-):
-    quarter = quarter_of(place_ref)
+def right_cores(place_ref, mine_ref, other_ref, inverse_ref, right_ref, *scratch):
     inverse_factor(core_of(place_ref), mine_ref, other_ref, inverse_ref, *scratch)
-    inverse = inverse_ref[...]
     own = matrix(mine_ref[by_distance(pair_of(place_ref), mine_ref)[0], :RANK])
-    right_ref[...] = product(own, inverse, 1, 1).reshape(right_ref.shape)
-    scaled_basis(quarter, inverse, (q0, q1, q2, q3), out_ref)
+    right_ref[...] = product(own, inverse_ref[...], 1, 1).reshape(right_ref.shape)
 
 
 def exchanged(tiles, axis):
@@ -353,6 +348,19 @@
 
 def work(products, size):
     return pl.CostEstimate(flops=6 * products * size**3, bytes_accessed=0, transcendentals=0)
+
+
+def basis_rows(place, inverse, quarters):
+    rank = inverse.shape[0]
+    return call(
+        whole_basis,
+        [(4 * len(quarters[0]), rank)],
+        place,
+        inverse,
+        *quarters,
+        in_specs=with_place(5),
+        cost_estimate=work(4, rank),
+    )
 
 
 def gram_tiles(place, factors, parts, rank, beside):
@@ -424,35 +432,24 @@
         cost_estimate=work(64, rank),
     )
     parts, moved = together(parts, across(basis))
-    u_scaled = call(
-        left_basis,
-        [(width, rank)],
-        place,
-        inverse,
-        basis,
-        moved,
-        from_sibling(basis),
-        from_sibling(moved),
-        in_specs=with_place(5),
-        cost_estimate=work(4, rank),
-    )
+    quarters = (basis, moved, from_sibling(basis), from_sibling(moved))
+    u_scaled = basis_rows(place, inverse, quarters)
     parts, (u_scaled, _) = plane_total(*parts, (u_scaled, ()))
     basis = jnp.concatenate(parts)
-    tiles, moved = gram_tiles(place, a_quarter, parts, rank, across(basis))
+    tiles, _ = gram_tiles(place, a_quarter, parts, rank, ())
     mine = row_total(tiles)
-    mine, siblings = together(mine, (from_sibling(basis), from_sibling(moved)))
-    v_scaled, right = call(
-        finish,
-        [(width, rank), shape],
+    inverse, right = call(
+        right_cores,
+        [(rank, rank), shape],
         place,
         mine,
         from_sibling(mine),
-        basis,
-        moved,
-        *siblings,
-        in_specs=with_place(6),
-        scratch_shapes=[pltpu.VMEM((rank, rank), jnp.float32), *factor_scratch(rank)],
-    )
+        in_specs=with_place(2),
+        scratch_shapes=factor_scratch(rank),
+    )
+    moved = across(basis)
+    quarters = (basis, moved, from_sibling(basis), from_sibling(moved))
+    v_scaled = basis_rows(place, inverse, quarters)
     return u_scaled, v_scaled, left, right
 
 

time: 157 us -> 150 us (0.955)
  starting transfers between devices: 45.2 us -> 40.9 us
  waiting for transfers between devices: 68.6 us -> 65.6 us
    ppermute x23, waiting for transfers between devices: 31.2 us -> 26.5 us  [from_peer(): return lax.ppermute(x, axis, [(i, i ^ step) for i in range(count)])]
    ppermute x23, starting transfers between devices: 19 us -> 14.7 us  [from_peer(): return lax.ppermute(x, axis, [(i, i ^ step) for i in range(count)])]
    all_to_all x5, waiting for transfers between devices: 37.4 us -> 39.1 us  [exchanged(): return lax.all_to_all(tiles, axis, 0, 0, tiled=True)]
    pallas_call x10 -> x11, Pallas kernels: 23.6 us -> 24.4 us  [call(): pl.pallas_call(kernel, out_shape=shapes if len(shapes) > 1 else shapes[0]...]
  transfers between devices with their start and end apart: 28 -> 28, of which waited for: 21 -> 19; matrix products, arithmetic and copies ran while one was open for 0% -> 0% of each run, Pallas kernels for 8% -> 13%
where the time goes in v11:
time: 150 us; the launch traced here: 148 us
  waiting for transfers between devices  65.6 us (44%)
  starting transfers between devices  40.9 us (27%)
  Pallas kernels  24.4 us (16%)
  blocking collectives  13.6 us (9%)
    all_to_all x5, waiting for transfers between devices, exchanged(): return lax.all_to_all(tiles, axis, 0, 0, tiled=True)  39.1 us
    ppermute x23, waiting for transfers between devices, from_peer(): return lax.ppermute(x, axis, [(i, i ^ step) for i in range(count)])  26.5 us
    all_to_all x5, starting transfers between devices, exchanged(): return lax.all_to_all(tiles, axis, 0, 0, tiled=True)  26.2 us
    pallas_call x11, Pallas kernels, call(): pl.pallas_call(kernel, out_shape=shapes if len(shapes) > 1 else shapes[0]...  24.4 us
    ppermute x23, starting transfers between devices, from_peer(): return lax.ppermute(x, axis, [(i, i ^ step) for i in range(count)])  14.7 us
    all_to_all x1, blocking collectives, exchanged(): return lax.all_to_all(tiles, axis, 0, 0, tiled=True)  13.6 us
  transfers between devices with their start and end apart: 28, of which 19 were waited for; matrix products, arithmetic and copies ran while one was open for 0% of the time, Pallas kernels for 13%

profile of v11, /device:TPU:8, one launch (start us, length us, event | category | flops | bytes accessed | tf_op | source)
XLA Modules:
  0.0 147.7 jit_solution(16542770592378333139)
XLA Ops:
  0.6 1.1 constant_dynamic-slice_fusion.10
  1.7 0.4 collective-permute-start
  2.2 3.2 %projections.1 = f32[8,32,256]{2,1,0:T(8,128)} custom-call(f32[128,1024]{1,0:T(8,128)} %bitcast.4, f32[128,1024]{1,0:T(8,128)} %bitcast.5, f32[1024,256]{1,0:T(8,128)} %u_hbm.1, f32[1024,256]{1,0:T(8,128)} %v_hbm.1), custom_call_target="tpu_custom_call" | custom-call | tf_op jit(solution)/shard_map/projections/pallas_call | solution.py:153
  5.3 6.4 %all-to-all-start = ((f32[8,32,256]{2,1,0:T(8,128)}), f32[8,32,256]{2,1,0:T(8,128)S(1)}, u32[]{:S(2)}, u32[]{:S(2)}) async-start(f32[8,32,256]{2,1,0:T(8,128)} %projections.1), calls=%async_computation | async-start | bytes 524288 | tf_op jit(solution)/shard_map/all_to_all | solution.py:299
  11.8 8.4 %all-to-all-done.tiles_ref = f32[8,32,256]{2,1,0:T(8,128)S(1)} async-done(((f32[8,32,256]{2,1,0:T(8,128)}), f32[8,32,256]{2,1,0:T(8,128)S(1)}, u32[]{:S(2)}, u32[]{:S(2)}) %all-to-all-start) | async-done | bytes 262176 | tf_op jit(solution)/shard_map/all_to_all | solution.py:299
  20.2 1.1 owner_coefficients.1
  21.3 5.3 %all-to-all-start.1 = ((f32[16,32,256]{2,1,0:T(8,128)}), f32[16,32,256]{2,1,0:T(8,128)S(1)}, u32[]{:S(2)}, u32[]{:S(2)}) async-start(f32[16,32,256]{2,1,0:T(8,128)} %owner_coefficients.1), calls=%async_computation.1 | async-start | bytes 1048576 | tf_op jit(solution)/shard_map/all_to_all | solution.py:299
  26.7 1.5 %collective-permute-done.1.f2 = f32[256,256]{1,0:T(8,128)S(1)} collective-permute-done((f32[256,256]{1,0:T(8,128)S(1)}, f32[256,256]{1,0:T(8,128)S(1)}, u32[]{:S(2)}, u32[]{:S(2)}) %collective-permute-start.1) | collective-permute-done | bytes 262176 | tf_op jit(solution)/shard_map/ppermute | solution.py:304
  28.3 7.0 %all-to-all-done.1.mine_ref.pair_ref = f32[16,32,256]{2,1,0:T(8,128)S(1)} async-done(((f32[16,32,256]{2,1,0:T(8,128)}), f32[16,32,256]{2,1,0:T(8,128)S(1)}, u32[]{:S(2)}, u32[]{:S(2)}) %all-to-all-start.1) | async-done | bytes 524320 | tf_op jit(solution)/shard_map/all_to_all | solution.py:299
  35.3 1.9 %collective-permute-done.2.other_ref.pair_other_ref = f32[16,32,256]{2,1,0:T(8,128)S(1)} collective-permute-done((f32[16,32,256]{2,1,0:T(8,128)S(1)}, f32[16,32,256]{2,1,0:T(8,128)S(1)}, u32[]{:S(2)}, u32[]{:S(2)}) %collective-permute-start.2) | collective-permute-done | bytes 524320 | tf_op jit(solution)/shard_map/ppermute | solution.py:304
  37.2 0.4 load_sum.1
  37.6 2.0 %collective-permute-start.3 = (f32[128,256]{1,0:T(8,128)S(1)}, f32[128,256]{1,0:T(8,128)S(1)}, u32[]{:S(2)}, u32[]{:S(2)}) collective-permute-start(f32[128,256]{1,0:T(8,128)S(1)} %get-tuple-element.48), channel_id=1, source_target_pairs={{0,32},{32,0},{64,96},{96,64},{1,33},{33,1},{65,97},{97,65},{2,34}... | collective-permute-start | bytes 393224 | tf_op jit(solution)/shard_map/ppermute | solution.py:304
  39.6 2.5 %collective-permute-start.4 = (f32[128,256]{1,0:T(8,128)S(1)}, f32[128,256]{1,0:T(8,128)S(1)}, u32[]{:S(2)}, u32[]{:S(2)}) collective-permute-start(f32[128,256]{1,0:T(8,128)S(1)} %get-tuple-element.49), channel_id=1, source_target_pairs={{0,96},{32,64},{64,32},{96,0},{1,97},{33,65},{65,33},{97,1},{2,98}... | collective-permute-start | bytes 393224 | tf_op jit(solution)/shard_map/ppermute | solution.py:304
  42.2 1.5 %collective-permute-start.7 = (f32[128,512]{1,0:T(8,128)S(1)}, f32[128,512]{1,0:T(8,128)S(1)}, u32[]{:S(2)}, u32[]{:S(2)}) collective-permute-start(f32[128,512]{1,0:T(8,128)S(1)} %get-tuple-element.78), channel_id=1, source_target_pairs={{0,16},{16,0},{1,17},{17,1},{2,18},{18,2},{3,19},{19,3},{4,20},{20... | collective-permute-start | bytes 786440 | tf_op jit(solution)/shard_map/ppermute | solution.py:304
  43.7 2.4 %collective-permute-done.4 = f32[128,256]{1,0:T(8,128)S(1)} collective-permute-done((f32[128,256]{1,0:T(8,128)S(1)}, f32[128,256]{1,0:T(8,128)S(1)}, u32[]{:S(2)}, u32[]{:S(2)}) %collective-permute-start.4) | collective-permute-done | bytes 131104 | tf_op jit(solution)/shard_map/ppermute | solution.py:304
  46.1 2.6 %collective-permute-start.5 = (f32[128,256]{1,0:T(8,128)S(1)}, f32[128,256]{1,0:T(8,128)S(1)}, u32[]{:S(2)}, u32[]{:S(2)}) collective-permute-start(f32[128,256]{1,0:T(8,128)S(1)} %add.58), channel_id=1, source_target_pairs={{0,96},{32,64},{64,32},{96,0},{1,97},{33,65},{65,33},{97,1},{2,98}... | collective-permute-start | bytes 393224 | tf_op jit(solution)/shard_map/ppermute | solution.py:304
  48.8 1.2 collective-permute-done.7
  50.1 2.3 %collective-permute-done.5 = f32[128,256]{1,0:T(8,128)S(1)} collective-permute-done((f32[128,256]{1,0:T(8,128)S(1)}, f32[128,256]{1,0:T(8,128)S(1)}, u32[]{:S(2)}, u32[]{:S(2)}) %collective-permute-start.5) | collective-permute-done | bytes 131104 | tf_op jit(solution)/shard_map/ppermute | solution.py:304
  52.4 1.4 collective-permute-done.6
  53.8 0.5 gram_and_cores.2
  54.5 1.7 %collective-permute-done.8 = f32[16,24,256]{2,1,0:T(8,128)S(1)} collective-permute-done((f32[16,24,256]{2,1,0:T(8,128)S(1)}, f32[16,24,256]{2,1,0:T(8,128)S(1)}, u32[]{:S(2)}, u32[]{:S(2)}) %collective-permute-start.8) | collective-permute-done | bytes 393248 | tf_op jit(solution)/shard_map/ppermute | solution.py:304
  56.2 0.8 add.62
  57.0 4.9 %all-to-all-start.2 = ((f32[16,24,256]{2,1,0:T(8,128)}), f32[16,24,256]{2,1,0:T(8,128)S(1)}, u32[]{:S(2)}, u32[]{:S(2)}) async-start(f32[16,24,256]{2,1,0:T(8,128)} %add.62), calls=%async_computation.2 | async-start | bytes 786432 | tf_op jit(solution)/shard_map/all_to_all | solution.py:299
  61.9 9.2 %all-to-all-done.2.tiles_ref = f32[16,24,256]{2,1,0:T(8,128)S(1)} async-done(((f32[16,24,256]{2,1,0:T(8,128)}), f32[16,24,256]{2,1,0:T(8,128)S(1)}, u32[]{:S(2)}, u32[]{:S(2)}) %all-to-all-start.2) | async-done | bytes 393248 | tf_op jit(solution)/shard_map/all_to_all | solution.py:299
  71.1 0.8 owner_sum.2
  71.9 4.8 %all-to-all-start.3 = ((f32[16,24,256]{2,1,0:T(8,128)}), f32[16,24,256]{2,1,0:T(8,128)S(1)}, u32[]{:S(2)}, u32[]{:S(2)}) async-start(f32[16,24,256]{2,1,0:T(8,128)} %owner_sum.2), calls=%async_computation.3 | async-start | bytes 786432 | tf_op jit(solution)/shard_map/all_to_all | solution.py:299
  76.8 1.5 %collective-permute-done.9.f2 = f32[256,256]{1,0:T(8,128)S(1)} collective-permute-done((f32[256,256]{1,0:T(8,128)S(1)}, f32[256,256]{1,0:T(8,128)S(1)}, u32[]{:S(2)}, u32[]{:S(2)}) %collective-permute-start.9) | collective-permute-done | bytes 262176 | tf_op jit(solution)/shard_map/ppermute | solution.py:304
  78.4 6.6 %all-to-all-done.3.mine_ref = f32[16,24,256]{2,1,0:T(8,128)S(1)} async-done(((f32[16,24,256]{2,1,0:T(8,128)}), f32[16,24,256]{2,1,0:T(8,128)S(1)}, u32[]{:S(2)}, u32[]{:S(2)}) %all-to-all-start.3) | async-done | bytes 393248 | tf_op jit(solution)/shard_map/all_to_all | solution.py:299
  85.0 1.5 %collective-permute-start.11 = (f32[256,256]{1,0:T(8,128)S(1)}, f32[256,256]{1,0:T(8,128)S(1)}, u32[]{:S(2)}, u32[]{:S(2)}) collective-permute-start(f32[256,256]{1,0:T(8,128)S(1)} %pad_maximum_fusion.2.q0), channel_id=1, source_target_pairs={{0,16},{16,0},{1,17},{17,1},{2,18},{18,2},{3,19},{19,3},{4,20},{20... | collective-permute-start | bytes 786440 | tf_op jit(solution)/shard_map/ppermute | solution.py:304
  86.7 7.3 %turn_over.1 = (f32[256,256]{1,0:T(8,128)S(1)}, f32[8,16,256]{2,1,0:T(8,128)}, f32[128,256]{1,0:T(8,128)S(1)}, f32[128,256]{1,0:T(8,128)S(1)}) custom-call(s32[1]{0:T(128)} %bitcast.place_ref, f32[16,24,256]{2,1,0:T(8,128)S(1)} %all-to-all-done.3.mine_ref, f32[16,24,256]{2,1,0:T(8,128)S(1)} %collective-permute-done.10.other_ref, ...), custom_call_target="tpu_custom_call" | custom-call | flops 6442450944 | tf_op jit(solution)/shard_map/turn_over/pallas_call | solution.py:153
  94.0 0.3 collective-permute-start.15
  94.3 1.1 collective-permute-start.13
  95.6 1.6 %whole_basis.2 = f32[1024,256]{1,0:T(8,128)} custom-call(s32[1]{0:T(128)} %bitcast.place_ref, f32[256,256]{1,0:T(8,128)S(1)} %get-tuple-element.66.inverse_ref, f32[256,256]{1,0:T(8,128)S(1)} %pad_maximum_fusion.2.q0, f32[256,256]{1,0:T(8,128)S(1)} %collective-permute-done.11.q1, f32[256,256]{1,0:T(8,128)S(1)} %collective-permute-done.14.q2, ...), custom_call_target="tpu_custom_call" | custom-call | flops 402653184 | tf_op jit(solution)/shard_map/whole_basis/pallas_call | solution.py:153
  97.2 2.8 %collective-permute-done.12 = f32[128,256]{1,0:T(8,128)S(1)} collective-permute-done((f32[128,256]{1,0:T(8,128)S(1)}, f32[128,256]{1,0:T(8,128)S(1)}, u32[]{:S(2)}, u32[]{:S(2)}) %collective-permute-start.12) | collective-permute-done | bytes 131104 | tf_op jit(solution)/shard_map/ppermute | solution.py:304
  100.0 1.2 collective-permute-done.13
  101.2 1.2 collective-permute-start.16
  102.5 5.0 %collective-permute-done.16 = f32[128,256]{1,0:T(8,128)S(1)} collective-permute-done((f32[128,256]{1,0:T(8,128)S(1)}, f32[128,256]{1,0:T(8,128)S(1)}, u32[]{:S(2)}, u32[]{:S(2)}) %collective-permute-start.16) | collective-permute-done | bytes 131104 | tf_op jit(solution)/shard_map/ppermute | solution.py:304
  107.5 0.5 gram_and_cores.3
  108.1 1.7 %collective-permute-done.18 = f32[16,24,256]{2,1,0:T(8,128)S(1)} collective-permute-done((f32[16,24,256]{2,1,0:T(8,128)S(1)}, f32[16,24,256]{2,1,0:T(8,128)S(1)}, u32[]{:S(2)}, u32[]{:S(2)}) %collective-permute-start.18) | collective-permute-done | bytes 393248 | tf_op jit(solution)/shard_map/ppermute | solution.py:304
  109.9 13.6 %all_to_all.30.tiles_ref = f32[16,24,256]{2,1,0:T(8,128)S(1)} all-to-all(f32[16,24,256]{2,1,0:T(8,128)S(1)} %add.67), channel_id=1, replica_groups=mesh['z'=4,'y_lo'=2,'core'=2,'row'=8] {'y_lo','row'}, dimensions={0} | all-to-all | bytes 786432 | tf_op jit(solution)/shard_map/all_to_all | solution.py:299
  123.5 0.8 owner_sum.3
  124.3 4.8 %all-to-all-start.5 = ((f32[16,24,256]{2,1,0:T(8,128)}), f32[16,24,256]{2,1,0:T(8,128)S(1)}, u32[]{:S(2)}, u32[]{:S(2)}) async-start(f32[16,24,256]{2,1,0:T(8,128)} %owner_sum.3), calls=%async_computation.5 | async-start | bytes 786432 | tf_op jit(solution)/shard_map/all_to_all | solution.py:299
  129.2 0.3 collective-permute-start.20
  129.4 7.9 %all-to-all-done.5.mine_ref = f32[16,24,256]{2,1,0:T(8,128)S(1)} async-done(((f32[16,24,256]{2,1,0:T(8,128)}), f32[16,24,256]{2,1,0:T(8,128)S(1)}, u32[]{:S(2)}, u32[]{:S(2)}) %all-to-all-start.5) | async-done | bytes 393248 | tf_op jit(solution)/shard_map/all_to_all | solution.py:299
  137.3 0.5 collective-permute-start.21
  137.8 1.7 %collective-permute-done.20.q1 = f32[256,256]{1,0:T(8,128)S(1)} collective-permute-done((f32[256,256]{1,0:T(8,128)S(1)}, f32[256,256]{1,0:T(8,128)S(1)}, u32[]{:S(2)}, u32[]{:S(2)}) %collective-permute-start.20) | collective-permute-done | bytes 262176 | tf_op jit(solution)/shard_map/ppermute | solution.py:304
  139.5 6.5 %right_cores.1 = (f32[256,256]{1,0:T(8,128)S(1)}, f32[8,16,256]{2,1,0:T(8,128)}) custom-call(s32[1]{0:T(128)} %bitcast.place_ref, f32[16,24,256]{2,1,0:T(8,128)S(1)} %all-to-all-done.5.mine_ref, f32[16,24,256]{2,1,0:T(8,128)S(1)} %collective-permute-done.19.other_ref), custom_call_target="tpu_custom_call" | custom-call | tf_op jit(solution)/shard_map/right_cores/pallas_call | solution.py:153
  146.1 1.6 %whole_basis.3 = f32[1024,256]{1,0:T(8,128)} custom-call(s32[1]{0:T(128)} %bitcast.place_ref, f32[256,256]{1,0:T(8,128)S(1)} %get-tuple-element.75.inverse_ref, f32[256,256]{1,0:T(8,128)S(1)} %pad_maximum_fusion.3.q0, f32[256,256]{1,0:T(8,128)S(1)} %collective-permute-done.20.q1, f32[256,256]{1,0:T(8,128)S(1)} %collective-permute-done.21.q2, ...), custom_call_target="tpu_custom_call" | custom-call | flops 402653184 | tf_op jit(solution)/shard_map/whole_basis/pallas_call | solution.py:153
  (41 shorter events, 1.3 us)
Async XLA Ops:
  1.7 18.5 %collective-permute-start = (f32[128,512]{1,0:T(8,128)S(1)}, f32[128,512]{1,0:T(8,128)S(1)}, u32[]{:S(2)}, u32[]{:S(2)}) collective-permute-start(f32[128,512]{1,0:T(8,128)S(1)} %get-tuple-element.80), channel_id=1, source_target_pairs={{0,16},{16,0},{1,17},{17,1},{2,18},{18,2},{3,19},{19,3},{4,20},{20... | collective-permute-start | bytes 786440 | tf_op jit(solution)/shard_map/ppermute | solution.py:304
  5.3 14.9 %all-to-all-start = ((f32[8,32,256]{2,1,0:T(8,128)}), f32[8,32,256]{2,1,0:T(8,128)S(1)}, u32[]{:S(2)}, u32[]{:S(2)}) async-start(f32[8,32,256]{2,1,0:T(8,128)} %projections.1), calls=%async_computation | async-start | bytes 524288 | tf_op jit(solution)/shard_map/all_to_all | solution.py:299
  21.3 14.0 %all-to-all-start.1 = ((f32[16,32,256]{2,1,0:T(8,128)}), f32[16,32,256]{2,1,0:T(8,128)S(1)}, u32[]{:S(2)}, u32[]{:S(2)}) async-start(f32[16,32,256]{2,1,0:T(8,128)} %owner_coefficients.1), calls=%async_computation.1 | async-start | bytes 1048576 | tf_op jit(solution)/shard_map/all_to_all | solution.py:299
  26.7 1.6 %collective-permute-start.1 = (f32[256,256]{1,0:T(8,128)S(1)}, f32[256,256]{1,0:T(8,128)S(1)}, u32[]{:S(2)}, u32[]{:S(2)}) collective-permute-start(f32[256,256]{1,0:T(8,128)S(1)} %pad_maximum_fusion), channel_id=1, source_target_pairs={{0,8},{8,0},{1,9},{9,1},{2,10},{10,2},{3,11},{11,3},{4,12},{12,4},... | collective-permute-start | bytes 786440 | tf_op jit(solution)/shard_map/ppermute | solution.py:304
  35.3 1.9 %collective-permute-start.2 = (f32[16,32,256]{2,1,0:T(8,128)S(1)}, f32[16,32,256]{2,1,0:T(8,128)S(1)}, u32[]{:S(2)}, u32[]{:S(2)}) collective-permute-start(f32[16,32,256]{2,1,0:T(8,128)S(1)} %all-to-all-done.1.mine_ref.pair_ref), channel_id=1, source_target_pairs={{0,8},{8,0},{1,9},{9,1},{2,10},{10,2},{3,11},{11,3},{4,12},{12,4},... | collective-permute-start | bytes 1572872 | tf_op jit(solution)/shard_map/ppermute | solution.py:304
  37.2 5.0 %copy-start = (f32[8,16,1024]{2,1,0:T(8,128)S(1)}, f32[8,16,1024]{2,1,0:T(8,128)}, u32[]{:S(2)}) copy-start(f32[8,16,1024]{2,1,0:T(8,128)} %param.5) | copy-start | bytes 1572868
  37.6 6.1 %collective-permute-start.3 = (f32[128,256]{1,0:T(8,128)S(1)}, f32[128,256]{1,0:T(8,128)S(1)}, u32[]{:S(2)}, u32[]{:S(2)}) collective-permute-start(f32[128,256]{1,0:T(8,128)S(1)} %get-tuple-element.48), channel_id=1, source_target_pairs={{0,32},{32,0},{64,96},{96,64},{1,33},{33,1},{65,97},{97,65},{2,34}... | collective-permute-start | bytes 393224 | tf_op jit(solution)/shard_map/ppermute | solution.py:304
  39.6 6.5 %collective-permute-start.4 = (f32[128,256]{1,0:T(8,128)S(1)}, f32[128,256]{1,0:T(8,128)S(1)}, u32[]{:S(2)}, u32[]{:S(2)}) collective-permute-start(f32[128,256]{1,0:T(8,128)S(1)} %get-tuple-element.49), channel_id=1, source_target_pairs={{0,96},{32,64},{64,32},{96,0},{1,97},{33,65},{65,33},{97,1},{2,98}... | collective-permute-start | bytes 393224 | tf_op jit(solution)/shard_map/ppermute | solution.py:304
  42.2 7.9 %collective-permute-start.7 = (f32[128,512]{1,0:T(8,128)S(1)}, f32[128,512]{1,0:T(8,128)S(1)}, u32[]{:S(2)}, u32[]{:S(2)}) collective-permute-start(f32[128,512]{1,0:T(8,128)S(1)} %get-tuple-element.78), channel_id=1, source_target_pairs={{0,16},{16,0},{1,17},{17,1},{2,18},{18,2},{3,19},{19,3},{4,20},{20... | collective-permute-start | bytes 786440 | tf_op jit(solution)/shard_map/ppermute | solution.py:304
  46.1 6.3 %collective-permute-start.5 = (f32[128,256]{1,0:T(8,128)S(1)}, f32[128,256]{1,0:T(8,128)S(1)}, u32[]{:S(2)}, u32[]{:S(2)}) collective-permute-start(f32[128,256]{1,0:T(8,128)S(1)} %add.58), channel_id=1, source_target_pairs={{0,96},{32,64},{64,32},{96,0},{1,97},{33,65},{65,33},{97,1},{2,98}... | collective-permute-start | bytes 393224 | tf_op jit(solution)/shard_map/ppermute | solution.py:304
  48.7 5.0 %collective-permute-start.6 = (f32[128,256]{1,0:T(8,128)S(1)}, f32[128,256]{1,0:T(8,128)S(1)}, u32[]{:S(2)}, u32[]{:S(2)}) collective-permute-start(f32[128,256]{1,0:T(8,128)S(1)} %add.59), channel_id=1, source_target_pairs={{0,32},{32,0},{64,96},{96,64},{1,33},{33,1},{65,97},{97,65},{2,34}... | collective-permute-start | bytes 393224 | tf_op jit(solution)/shard_map/ppermute | solution.py:304
  54.4 1.8 %collective-permute-start.8 = (f32[16,24,256]{2,1,0:T(8,128)S(1)}, f32[16,24,256]{2,1,0:T(8,128)S(1)}, u32[]{:S(2)}, u32[]{:S(2)}) collective-permute-start(f32[16,24,256]{2,1,0:T(8,128)S(1)} %get-tuple-element.55), channel_id=1, source_target_pairs={{0,8},{8,0},{1,9},{9,1},{2,10},{10,2},{3,11},{11,3},{4,12},{12,4},... | collective-permute-start | bytes 1179656 | tf_op jit(solution)/shard_map/ppermute | solution.py:304
  57.0 14.2 %all-to-all-start.2 = ((f32[16,24,256]{2,1,0:T(8,128)}), f32[16,24,256]{2,1,0:T(8,128)S(1)}, u32[]{:S(2)}, u32[]{:S(2)}) async-start(f32[16,24,256]{2,1,0:T(8,128)} %add.62), calls=%async_computation.2 | async-start | bytes 786432 | tf_op jit(solution)/shard_map/all_to_all | solution.py:299
  71.9 13.0 %all-to-all-start.3 = ((f32[16,24,256]{2,1,0:T(8,128)}), f32[16,24,256]{2,1,0:T(8,128)S(1)}, u32[]{:S(2)}, u32[]{:S(2)}) async-start(f32[16,24,256]{2,1,0:T(8,128)} %owner_sum.2), calls=%async_computation.3 | async-start | bytes 786432 | tf_op jit(solution)/shard_map/all_to_all | solution.py:299
  76.7 1.6 %collective-permute-start.9 = (f32[256,256]{1,0:T(8,128)S(1)}, f32[256,256]{1,0:T(8,128)S(1)}, u32[]{:S(2)}, u32[]{:S(2)}) collective-permute-start(f32[256,256]{1,0:T(8,128)S(1)} %pad_maximum_fusion.1), channel_id=1, source_target_pairs={{0,8},{8,0},{1,9},{9,1},{2,10},{10,2},{3,11},{11,3},{4,12},{12,4},... | collective-permute-start | bytes 786440 | tf_op jit(solution)/shard_map/ppermute | solution.py:304
  84.9 1.8 %collective-permute-start.10 = (f32[16,24,256]{2,1,0:T(8,128)S(1)}, f32[16,24,256]{2,1,0:T(8,128)S(1)}, u32[]{:S(2)}, u32[]{:S(2)}) collective-permute-start(f32[16,24,256]{2,1,0:T(8,128)S(1)} %all-to-all-done.3.mine_ref), channel_id=1, source_target_pairs={{0,8},{8,0},{1,9},{9,1},{2,10},{10,2},{3,11},{11,3},{4,12},{12,4},... | collective-permute-start | bytes 1179656 | tf_op jit(solution)/shard_map/ppermute | solution.py:304
  85.0 9.1 %collective-permute-start.11 = (f32[256,256]{1,0:T(8,128)S(1)}, f32[256,256]{1,0:T(8,128)S(1)}, u32[]{:S(2)}, u32[]{:S(2)}) collective-permute-start(f32[256,256]{1,0:T(8,128)S(1)} %pad_maximum_fusion.2.q0), channel_id=1, source_target_pairs={{0,16},{16,0},{1,17},{17,1},{2,18},{18,2},{3,19},{19,3},{4,20},{20... | collective-permute-start | bytes 786440 | tf_op jit(solution)/shard_map/ppermute | solution.py:304
  86.5 9.0 %collective-permute-start.14 = (f32[256,256]{1,0:T(8,128)S(1)}, f32[256,256]{1,0:T(8,128)S(1)}, u32[]{:S(2)}, u32[]{:S(2)}) collective-permute-start(f32[256,256]{1,0:T(8,128)S(1)} %pad_maximum_fusion.2.q0), channel_id=1, source_target_pairs={{0,8},{8,0},{1,9},{9,1},{2,10},{10,2},{3,11},{11,3},{4,12},{12,4},... | collective-permute-start | bytes 786440 | tf_op jit(solution)/shard_map/ppermute | solution.py:304
  94.0 1.5 %collective-permute-start.15 = (f32[256,256]{1,0:T(8,128)S(1)}, f32[256,256]{1,0:T(8,128)S(1)}, u32[]{:S(2)}, u32[]{:S(2)}) collective-permute-start(f32[256,256]{1,0:T(8,128)S(1)} %collective-permute-done.11.q1), channel_id=1, source_target_pairs={{0,8},{8,0},{1,9},{9,1},{2,10},{10,2},{3,11},{11,3},{4,12},{12,4},... | collective-permute-start | bytes 786440 | tf_op jit(solution)/shard_map/ppermute | solution.py:304
  94.3 5.6 %collective-permute-start.12 = (f32[128,256]{1,0:T(8,128)S(1)}, f32[128,256]{1,0:T(8,128)S(1)}, u32[]{:S(2)}, u32[]{:S(2)}) collective-permute-start(f32[128,256]{1,0:T(8,128)S(1)} %get-tuple-element.64), channel_id=1, source_target_pairs={{0,32},{32,0},{64,96},{96,64},{1,33},{33,1},{65,97},{97,65},{2,34}... | collective-permute-start | bytes 393224 | tf_op jit(solution)/shard_map/ppermute | solution.py:304
  94.3 6.8 %collective-permute-start.13 = (f32[128,256]{1,0:T(8,128)S(1)}, f32[128,256]{1,0:T(8,128)S(1)}, u32[]{:S(2)}, u32[]{:S(2)}) collective-permute-start(f32[128,256]{1,0:T(8,128)S(1)} %get-tuple-element.65), channel_id=1, source_target_pairs={{0,96},{32,64},{64,32},{96,0},{1,97},{33,65},{65,33},{97,1},{2,98}... | collective-permute-start | bytes 393224 | tf_op jit(solution)/shard_map/ppermute | solution.py:304
  101.2 6.3 %collective-permute-start.16 = (f32[128,256]{1,0:T(8,128)S(1)}, f32[128,256]{1,0:T(8,128)S(1)}, u32[]{:S(2)}, u32[]{:S(2)}) collective-permute-start(f32[128,256]{1,0:T(8,128)S(1)} %add.63), channel_id=1, source_target_pairs={{0,96},{32,64},{64,32},{96,0},{1,97},{33,65},{65,33},{97,1},{2,98}... | collective-permute-start | bytes 393224 | tf_op jit(solution)/shard_map/ppermute | solution.py:304
  102.4 5.0 %collective-permute-start.17 = (f32[128,256]{1,0:T(8,128)S(1)}, f32[128,256]{1,0:T(8,128)S(1)}, u32[]{:S(2)}, u32[]{:S(2)}) collective-permute-start(f32[128,256]{1,0:T(8,128)S(1)} %add.64), channel_id=1, source_target_pairs={{0,32},{32,0},{64,96},{96,64},{1,33},{33,1},{65,97},{97,65},{2,34}... | collective-permute-start | bytes 393224 | tf_op jit(solution)/shard_map/ppermute | solution.py:304
  108.0 1.8 %collective-permute-start.18 = (f32[16,24,256]{2,1,0:T(8,128)S(1)}, f32[16,24,256]{2,1,0:T(8,128)S(1)}, u32[]{:S(2)}, u32[]{:S(2)}) collective-permute-start(f32[16,24,256]{2,1,0:T(8,128)S(1)} %get-tuple-element.74), channel_id=1, source_target_pairs={{0,8},{8,0},{1,9},{9,1},{2,10},{10,2},{3,11},{11,3},{4,12},{12,4},... | collective-permute-start | bytes 1179656 | tf_op jit(solution)/shard_map/ppermute | solution.py:304
  124.3 13.0 %all-to-all-start.5 = ((f32[16,24,256]{2,1,0:T(8,128)}), f32[16,24,256]{2,1,0:T(8,128)S(1)}, u32[]{:S(2)}, u32[]{:S(2)}) async-start(f32[16,24,256]{2,1,0:T(8,128)} %owner_sum.3), calls=%async_computation.5 | async-start | bytes 786432 | tf_op jit(solution)/shard_map/all_to_all | solution.py:299
  129.2 10.4 %collective-permute-start.20 = (f32[256,256]{1,0:T(8,128)S(1)}, f32[256,256]{1,0:T(8,128)S(1)}, u32[]{:S(2)}, u32[]{:S(2)}) collective-permute-start(f32[256,256]{1,0:T(8,128)S(1)} %pad_maximum_fusion.3.q0), channel_id=1, source_target_pairs={{0,16},{16,0},{1,17},{17,1},{2,18},{18,2},{3,19},{19,3},{4,20},{20... | collective-permute-start | bytes 786440 | tf_op jit(solution)/shard_map/ppermute | solution.py:304
  137.3 2.2 %collective-permute-start.19 = (f32[16,24,256]{2,1,0:T(8,128)S(1)}, f32[16,24,256]{2,1,0:T(8,128)S(1)}, u32[]{:S(2)}, u32[]{:S(2)}) collective-permute-start(f32[16,24,256]{2,1,0:T(8,128)S(1)} %all-to-all-done.5.mine_ref), channel_id=1, source_target_pairs={{0,8},{8,0},{1,9},{9,1},{2,10},{10,2},{3,11},{11,3},{4,12},{12,4},... | collective-permute-start | bytes 1179656 | tf_op jit(solution)/shard_map/ppermute | solution.py:304
  137.3 8.8 %collective-permute-start.21 = (f32[256,256]{1,0:T(8,128)S(1)}, f32[256,256]{1,0:T(8,128)S(1)}, u32[]{:S(2)}, u32[]{:S(2)}) collective-permute-start(f32[256,256]{1,0:T(8,128)S(1)} %pad_maximum_fusion.3.q0), channel_id=1, source_target_pairs={{0,8},{8,0},{1,9},{9,1},{2,10},{10,2},{3,11},{11,3},{4,12},{12,4},... | collective-permute-start | bytes 786440 | tf_op jit(solution)/shard_map/ppermute | solution.py:304
  139.5 6.6 %collective-permute-start.22 = (f32[256,256]{1,0:T(8,128)S(1)}, f32[256,256]{1,0:T(8,128)S(1)}, u32[]{:S(2)}, u32[]{:S(2)}) collective-permute-start(f32[256,256]{1,0:T(8,128)S(1)} %collective-permute-done.20.q1), channel_id=1, source_target_pairs={{0,8},{8,0},{1,9},{9,1},{2,10},{10,2},{3,11},{11,3},{4,12},{12,4},... | collective-permute-start | bytes 786440 | tf_op jit(solution)/shard_map/ppermute | solution.py:304

commit v12 on v11

--- a/solution.py
+++ b/solution.py
@@ -378,9 +378,9 @@
     return mine + other, beside
 
 
-def row_total(tiles):
-    tiles = exchanged(tiles, ROW)
-    return exchanged(call(owner_sum, [tiles.shape], tiles), ROW)
+def row_total(tiles, beside=()):
+    tiles, beside = together(exchanged(tiles, ROW), beside)
+    return exchanged(call(owner_sum, [tiles.shape], tiles), ROW), beside
 
 
 def local(b_factors, a_factors, u_start, v_start):
@@ -403,10 +403,8 @@
         ],
     )
     copies = (lax.axis_size(ROW), 2 * RANK, rank)
-    tiles, b_half = together(exchanged(partial, "row"), b_half)
     b_quarter = column_quarter(b_half, core)
-    pair = exchanged(call(owner_coefficients, [copies], tiles), ROW)
-    pair, b_quarter = together(pair, b_quarter)
+    pair = exchanged(call(owner_coefficients, [copies], exchanged(partial, "row")), ROW)
     pair_other = from_sibling(pair)
 
     part = (width // 8, rank)
@@ -414,10 +412,10 @@
         load_sum, [part, part], place, *b_quarter, pair, pair_other, in_specs=with_place(5)
     )
     parts, (_, a_half) = plane_total(*parts, ((), column_half(a, bit)))
-    a_quarter = column_quarter(a_half, core)
     basis = jnp.concatenate(parts)
     tiles, _ = gram_tiles(place, b_quarter, parts, rank, ())
-    mine, a_quarter = together(row_total(tiles), a_quarter)
+    mine, a_half = row_total(tiles, a_half)
+    mine, a_quarter = together(mine, column_quarter(a_half, core))
     inverse, left, *parts = call(
         turn_over,
         [(rank, rank), shape, part, part],
@@ -437,7 +435,7 @@
     parts, (u_scaled, _) = plane_total(*parts, (u_scaled, ()))
     basis = jnp.concatenate(parts)
     tiles, _ = gram_tiles(place, a_quarter, parts, rank, ())
-    mine = row_total(tiles)
+    mine, _ = row_total(tiles)
     inverse, right = call(
         right_cores,
         [(rank, rank), shape],

time: 150 us -> 151 us (level)
  blocking collectives: 13.6 us -> 44.6 us
  waiting for transfers between devices: 65.6 us -> 50 us
  starting transfers between devices: 40.9 us -> 28.7 us
    all_to_all x1 -> x3, blocking collectives: 13.6 us -> 44.6 us  [exchanged(): return lax.all_to_all(tiles, axis, 0, 0, tiled=True)]
    all_to_all x5 -> x3, waiting for transfers between devices: 39.1 us -> 22.9 us  [exchanged(): return lax.all_to_all(tiles, axis, 0, 0, tiled=True)]
    all_to_all x5 -> x3, starting transfers between devices: 26.2 us -> 14.6 us  [exchanged(): return lax.all_to_all(tiles, axis, 0, 0, tiled=True)]
  transfers between devices with their start and end apart: 28 -> 26, of which waited for: 19 -> 18; matrix products, arithmetic and copies ran while one was open for 0% -> 0% of each run, Pallas kernels for 13% -> 10%
where the time goes in v12:
time: 151 us; the launch traced here: 148 us
  waiting for transfers between devices  50 us (33%)
  blocking collectives  44.6 us (30%)
  starting transfers between devices  28.7 us (19%)
  Pallas kernels  23.7 us (16%)
    all_to_all x3, blocking collectives, exchanged(): return lax.all_to_all(tiles, axis, 0, 0, tiled=True)  44.6 us
    ppermute x23, waiting for transfers between devices, from_peer(): return lax.ppermute(x, axis, [(i, i ^ step) for i in range(count)])  27 us
    pallas_call x11, Pallas kernels, call(): pl.pallas_call(kernel, out_shape=shapes if len(shapes) > 1 else shapes[0]...  23.7 us
    all_to_all x3, waiting for transfers between devices, exchanged(): return lax.all_to_all(tiles, axis, 0, 0, tiled=True)  22.9 us
    all_to_all x3, starting transfers between devices, exchanged(): return lax.all_to_all(tiles, axis, 0, 0, tiled=True)  14.6 us
    ppermute x23, starting transfers between devices, from_peer(): return lax.ppermute(x, axis, [(i, i ^ step) for i in range(count)])  14.1 us
  transfers between devices with their start and end apart: 26, of which 18 were waited for; matrix products, arithmetic and copies ran while one was open for 0% of the time, Pallas kernels for 10%

profile of v12, /device:TPU:8, one launch (start us, length us, event | category | flops | bytes accessed | tf_op | source)
XLA Modules:
  0.0 148.4 jit_solution(13894421791574855414)
XLA Ops:
  0.6 2.5 %projections.1 = f32[8,32,256]{2,1,0:T(8,128)S(1)} custom-call(f32[128,1024]{1,0:T(8,128)} %bitcast.3, f32[128,1024]{1,0:T(8,128)} %bitcast.6, f32[1024,256]{1,0:T(8,128)} %u_hbm.1, f32[1024,256]{1,0:T(8,128)} %v_hbm.1), custom_call_target="tpu_custom_call" | custom-call | tf_op jit(solution)/shard_map/projections/pallas_call | solution.py:153
  3.1 14.5 %all_to_all.30.tiles_ref = f32[8,32,256]{2,1,0:T(8,128)S(1)} all-to-all(f32[8,32,256]{2,1,0:T(8,128)S(1)} %projections.1), channel_id=1, replica_groups=mesh['z'=4,'y_lo'=2,'core'=2,'row'=8] {'row'}, dimensions={0} | all-to-all | bytes 524288 | tf_op jit(solution)/shard_map/all_to_all | solution.py:299
  17.7 1.1 owner_coefficients.1
  18.8 4.9 %all-to-all-start.1 = ((f32[16,32,256]{2,1,0:T(8,128)}), f32[16,32,256]{2,1,0:T(8,128)S(1)}, u32[]{:S(2)}, u32[]{:S(2)}) async-start(f32[16,32,256]{2,1,0:T(8,128)} %owner_coefficients.1), calls=%async_computation.1 | async-start | bytes 1048576 | tf_op jit(solution)/shard_map/all_to_all | solution.py:299
  23.7 0.3 collective-permute-start
  23.9 8.7 %all-to-all-done.1.mine_ref.pair_ref = f32[16,32,256]{2,1,0:T(8,128)S(1)} async-done(((f32[16,32,256]{2,1,0:T(8,128)}), f32[16,32,256]{2,1,0:T(8,128)S(1)}, u32[]{:S(2)}, u32[]{:S(2)}) %all-to-all-start.1) | async-done | bytes 524320 | tf_op jit(solution)/shard_map/all_to_all | solution.py:299
  32.6 0.1 constant_dynamic-slice_fusion.7
  32.8 2.1 %collective-permute-done = f32[128,512]{1,0:T(8,128)S(1)} collective-permute-done((f32[128,512]{1,0:T(8,128)S(1)}, f32[128,512]{1,0:T(8,128)S(1)}, u32[]{:S(2)}, u32[]{:S(2)}) %collective-permute-start) | collective-permute-done | bytes 262176 | tf_op jit(solution)/shard_map/ppermute | solution.py:304
  35.0 1.5 %collective-permute-done.1.f2 = f32[256,256]{1,0:T(8,128)S(1)} collective-permute-done((f32[256,256]{1,0:T(8,128)S(1)}, f32[256,256]{1,0:T(8,128)S(1)}, u32[]{:S(2)}, u32[]{:S(2)}) %collective-permute-start.1) | collective-permute-done | bytes 262176 | tf_op jit(solution)/shard_map/ppermute | solution.py:304
  36.5 0.4 load_sum.1
  37.0 2.0 %collective-permute-start.3 = (f32[128,256]{1,0:T(8,128)S(1)}, f32[128,256]{1,0:T(8,128)S(1)}, u32[]{:S(2)}, u32[]{:S(2)}) collective-permute-start(f32[128,256]{1,0:T(8,128)S(1)} %get-tuple-element.37), channel_id=1, source_target_pairs={{0,32},{32,0},{64,96},{96,64},{1,33},{33,1},{65,97},{97,65},{2,34}... | collective-permute-start | bytes 393224 | tf_op jit(solution)/shard_map/ppermute | solution.py:304
  39.0 2.5 %collective-permute-start.4 = (f32[128,256]{1,0:T(8,128)S(1)}, f32[128,256]{1,0:T(8,128)S(1)}, u32[]{:S(2)}, u32[]{:S(2)}) collective-permute-start(f32[128,256]{1,0:T(8,128)S(1)} %get-tuple-element.38), channel_id=1, source_target_pairs={{0,96},{32,64},{64,32},{96,0},{1,97},{33,65},{65,33},{97,1},{2,98}... | collective-permute-start | bytes 393224 | tf_op jit(solution)/shard_map/ppermute | solution.py:304
  41.5 1.1 collective-permute-start.7
  42.8 2.7 %collective-permute-done.4 = f32[128,256]{1,0:T(8,128)S(1)} collective-permute-done((f32[128,256]{1,0:T(8,128)S(1)}, f32[128,256]{1,0:T(8,128)S(1)}, u32[]{:S(2)}, u32[]{:S(2)}) %collective-permute-start.4) | collective-permute-done | bytes 131104 | tf_op jit(solution)/shard_map/ppermute | solution.py:304
  45.5 2.6 %collective-permute-start.5 = (f32[128,256]{1,0:T(8,128)S(1)}, f32[128,256]{1,0:T(8,128)S(1)}, u32[]{:S(2)}, u32[]{:S(2)}) collective-permute-start(f32[128,256]{1,0:T(8,128)S(1)} %add.62), channel_id=1, source_target_pairs={{0,96},{32,64},{64,32},{96,0},{1,97},{33,65},{65,33},{97,1},{2,98}... | collective-permute-start | bytes 393224 | tf_op jit(solution)/shard_map/ppermute | solution.py:304
  48.1 0.1 collective-permute-start.6
  48.2 1.2 collective-permute-done.7
  49.4 2.3 %collective-permute-done.5 = f32[128,256]{1,0:T(8,128)S(1)} collective-permute-done((f32[128,256]{1,0:T(8,128)S(1)}, f32[128,256]{1,0:T(8,128)S(1)}, u32[]{:S(2)}, u32[]{:S(2)}) %collective-permute-start.5) | collective-permute-done | bytes 131104 | tf_op jit(solution)/shard_map/ppermute | solution.py:304
  51.7 1.4 collective-permute-done.6
  53.2 0.5 gram_and_cores.2
  53.8 1.7 %collective-permute-done.8 = f32[16,24,256]{2,1,0:T(8,128)S(1)} collective-permute-done((f32[16,24,256]{2,1,0:T(8,128)S(1)}, f32[16,24,256]{2,1,0:T(8,128)S(1)}, u32[]{:S(2)}, u32[]{:S(2)}) %collective-permute-start.8) | collective-permute-done | bytes 393248 | tf_op jit(solution)/shard_map/ppermute | solution.py:304
  55.6 16.3 %all_to_all.31.tiles_ref = f32[16,24,256]{2,1,0:T(8,128)S(1)} all-to-all(f32[16,24,256]{2,1,0:T(8,128)S(1)} %add.66), channel_id=1, replica_groups=mesh['z'=4,'y_lo'=2,'core'=2,'row'=8] {'y_lo','row'}, dimensions={0} | all-to-all | bytes 786432 | tf_op jit(solution)/shard_map/all_to_all | solution.py:299
  71.9 0.8 owner_sum.2
  72.7 4.8 %all-to-all-start.3 = ((f32[16,24,256]{2,1,0:T(8,128)}), f32[16,24,256]{2,1,0:T(8,128)S(1)}, u32[]{:S(2)}, u32[]{:S(2)}) async-start(f32[16,24,256]{2,1,0:T(8,128)} %owner_sum.2), calls=%async_computation.3 | async-start | bytes 786432 | tf_op jit(solution)/shard_map/all_to_all | solution.py:299
  77.7 1.5 %collective-permute-done.9.f2 = f32[256,256]{1,0:T(8,128)S(1)} collective-permute-done((f32[256,256]{1,0:T(8,128)S(1)}, f32[256,256]{1,0:T(8,128)S(1)}, u32[]{:S(2)}, u32[]{:S(2)}) %collective-permute-start.9) | collective-permute-done | bytes 262176 | tf_op jit(solution)/shard_map/ppermute | solution.py:304
  79.2 6.4 %all-to-all-done.3.mine_ref = f32[16,24,256]{2,1,0:T(8,128)S(1)} async-done(((f32[16,24,256]{2,1,0:T(8,128)}), f32[16,24,256]{2,1,0:T(8,128)S(1)}, u32[]{:S(2)}, u32[]{:S(2)}) %all-to-all-start.3) | async-done | bytes 393248 | tf_op jit(solution)/shard_map/all_to_all | solution.py:299
  85.6 1.5 %collective-permute-start.11 = (f32[256,256]{1,0:T(8,128)S(1)}, f32[256,256]{1,0:T(8,128)S(1)}, u32[]{:S(2)}, u32[]{:S(2)}) collective-permute-start(f32[256,256]{1,0:T(8,128)S(1)} %pad_maximum_fusion.2.q0), channel_id=1, source_target_pairs={{0,16},{16,0},{1,17},{17,1},{2,18},{18,2},{3,19},{19,3},{4,20},{20... | collective-permute-start | bytes 786440 | tf_op jit(solution)/shard_map/ppermute | solution.py:304
  87.1 0.2 collective-permute-start.14
  87.4 7.3 %turn_over.1 = (f32[256,256]{1,0:T(8,128)S(1)}, f32[8,16,256]{2,1,0:T(8,128)}, f32[128,256]{1,0:T(8,128)S(1)}, f32[128,256]{1,0:T(8,128)S(1)}) custom-call(s32[1]{0:T(128)} %bitcast.place_ref, f32[16,24,256]{2,1,0:T(8,128)S(1)} %all-to-all-done.3.mine_ref, f32[16,24,256]{2,1,0:T(8,128)S(1)} %collective-permute-done.10.other_ref, ...), custom_call_target="tpu_custom_call" | custom-call | flops 6442450944 | tf_op jit(solution)/shard_map/turn_over/pallas_call | solution.py:153
  94.7 0.3 collective-permute-start.15
  95.0 1.1 collective-permute-start.13
  96.1 0.1 collective-permute-done.15.q3
  96.2 1.6 %whole_basis.2 = f32[1024,256]{1,0:T(8,128)} custom-call(s32[1]{0:T(128)} %bitcast.place_ref, f32[256,256]{1,0:T(8,128)S(1)} %get-tuple-element.58.inverse_ref, f32[256,256]{1,0:T(8,128)S(1)} %pad_maximum_fusion.2.q0, f32[256,256]{1,0:T(8,128)S(1)} %collective-permute-done.11.q1, f32[256,256]{1,0:T(8,128)S(1)} %collective-permute-done.14.q2, ...), custom_call_target="tpu_custom_call" | custom-call | flops 402653184 | tf_op jit(solution)/shard_map/whole_basis/pallas_call | solution.py:153
  97.8 2.7 %collective-permute-done.12 = f32[128,256]{1,0:T(8,128)S(1)} collective-permute-done((f32[128,256]{1,0:T(8,128)S(1)}, f32[128,256]{1,0:T(8,128)S(1)}, u32[]{:S(2)}, u32[]{:S(2)}) %collective-permute-start.12) | collective-permute-done | bytes 131104 | tf_op jit(solution)/shard_map/ppermute | solution.py:304
  100.6 1.2 collective-permute-done.13
  101.8 1.2 collective-permute-start.16
  103.1 5.0 %collective-permute-done.16 = f32[128,256]{1,0:T(8,128)S(1)} collective-permute-done((f32[128,256]{1,0:T(8,128)S(1)}, f32[128,256]{1,0:T(8,128)S(1)}, u32[]{:S(2)}, u32[]{:S(2)}) %collective-permute-start.16) | collective-permute-done | bytes 131104 | tf_op jit(solution)/shard_map/ppermute | solution.py:304
  108.1 0.5 gram_and_cores.3
  108.8 1.7 %collective-permute-done.18 = f32[16,24,256]{2,1,0:T(8,128)S(1)} collective-permute-done((f32[16,24,256]{2,1,0:T(8,128)S(1)}, f32[16,24,256]{2,1,0:T(8,128)S(1)}, u32[]{:S(2)}, u32[]{:S(2)}) %collective-permute-start.18) | collective-permute-done | bytes 393248 | tf_op jit(solution)/shard_map/ppermute | solution.py:304
  110.5 13.7 %all_to_all.32.tiles_ref = f32[16,24,256]{2,1,0:T(8,128)S(1)} all-to-all(f32[16,24,256]{2,1,0:T(8,128)S(1)} %add.71), channel_id=1, replica_groups=mesh['z'=4,'y_lo'=2,'core'=2,'row'=8] {'y_lo','row'}, dimensions={0} | all-to-all | bytes 786432 | tf_op jit(solution)/shard_map/all_to_all | solution.py:299
  124.2 0.8 owner_sum.3
  125.0 4.8 %all-to-all-start.5 = ((f32[16,24,256]{2,1,0:T(8,128)}), f32[16,24,256]{2,1,0:T(8,128)S(1)}, u32[]{:S(2)}, u32[]{:S(2)}) async-start(f32[16,24,256]{2,1,0:T(8,128)} %owner_sum.3), calls=%async_computation.5 | async-start | bytes 786432 | tf_op jit(solution)/shard_map/all_to_all | solution.py:299
  129.9 0.3 collective-permute-start.20
  130.1 7.9 %all-to-all-done.5.mine_ref = f32[16,24,256]{2,1,0:T(8,128)S(1)} async-done(((f32[16,24,256]{2,1,0:T(8,128)}), f32[16,24,256]{2,1,0:T(8,128)S(1)}, u32[]{:S(2)}, u32[]{:S(2)}) %all-to-all-start.5) | async-done | bytes 393248 | tf_op jit(solution)/shard_map/all_to_all | solution.py:299
  138.0 0.5 collective-permute-start.21
  138.5 1.7 %collective-permute-done.20.q1 = f32[256,256]{1,0:T(8,128)S(1)} collective-permute-done((f32[256,256]{1,0:T(8,128)S(1)}, f32[256,256]{1,0:T(8,128)S(1)}, u32[]{:S(2)}, u32[]{:S(2)}) %collective-permute-start.20) | collective-permute-done | bytes 262176 | tf_op jit(solution)/shard_map/ppermute | solution.py:304
  140.2 6.5 %right_cores.1 = (f32[256,256]{1,0:T(8,128)S(1)}, f32[8,16,256]{2,1,0:T(8,128)}) custom-call(s32[1]{0:T(128)} %bitcast.place_ref, f32[16,24,256]{2,1,0:T(8,128)S(1)} %all-to-all-done.5.mine_ref, f32[16,24,256]{2,1,0:T(8,128)S(1)} %collective-permute-done.19.other_ref), custom_call_target="tpu_custom_call" | custom-call | tf_op jit(solution)/shard_map/right_cores/pallas_call | solution.py:153
  146.8 1.6 %whole_basis.3 = f32[1024,256]{1,0:T(8,128)} custom-call(s32[1]{0:T(128)} %bitcast.place_ref, f32[256,256]{1,0:T(8,128)S(1)} %get-tuple-element.67.inverse_ref, f32[256,256]{1,0:T(8,128)S(1)} %pad_maximum_fusion.3.q0, f32[256,256]{1,0:T(8,128)S(1)} %collective-permute-done.20.q1, f32[256,256]{1,0:T(8,128)S(1)} %collective-permute-done.21.q2, ...), custom_call_target="tpu_custom_call" | custom-call | flops 402653184 | tf_op jit(solution)/shard_map/whole_basis/pallas_call | solution.py:153
  (41 shorter events, 1.0 us)
Async XLA Ops:
  18.7 4.9 %copy-start = (f32[8,16,1024]{2,1,0:T(8,128)S(1)}, f32[8,16,1024]{2,1,0:T(8,128)}, u32[]{:S(2)}) copy-start(f32[8,16,1024]{2,1,0:T(8,128)} %param.4) | copy-start | bytes 1572868
  18.8 13.9 %all-to-all-start.1 = ((f32[16,32,256]{2,1,0:T(8,128)}), f32[16,32,256]{2,1,0:T(8,128)S(1)}, u32[]{:S(2)}, u32[]{:S(2)}) async-start(f32[16,32,256]{2,1,0:T(8,128)} %owner_coefficients.1), calls=%async_computation.1 | async-start | bytes 1048576 | tf_op jit(solution)/shard_map/all_to_all | solution.py:299
  23.7 11.2 %collective-permute-start = (f32[128,512]{1,0:T(8,128)S(1)}, f32[128,512]{1,0:T(8,128)S(1)}, u32[]{:S(2)}, u32[]{:S(2)}) collective-permute-start(f32[128,512]{1,0:T(8,128)S(1)} %constant_dynamic-slice_fusion.9), channel_id=1, source_target_pairs={{0,16},{16,0},{1,17},{17,1},{2,18},{18,2},{3,19},{19,3},{4,20},{20... | collective-permute-start | bytes 786440 | tf_op jit(solution)/shard_map/ppermute | solution.py:304
  32.6 3.9 %collective-permute-start.2 = (f32[16,32,256]{2,1,0:T(8,128)S(1)}, f32[16,32,256]{2,1,0:T(8,128)S(1)}, u32[]{:S(2)}, u32[]{:S(2)}) collective-permute-start(f32[16,32,256]{2,1,0:T(8,128)S(1)} %all-to-all-done.1.mine_ref.pair_ref), channel_id=1, source_target_pairs={{0,8},{8,0},{1,9},{9,1},{2,10},{10,2},{3,11},{11,3},{4,12},{12,4},... | collective-permute-start | bytes 1572872 | tf_op jit(solution)/shard_map/ppermute | solution.py:304
  34.9 1.6 %collective-permute-start.1 = (f32[256,256]{1,0:T(8,128)S(1)}, f32[256,256]{1,0:T(8,128)S(1)}, u32[]{:S(2)}, u32[]{:S(2)}) collective-permute-start(f32[256,256]{1,0:T(8,128)S(1)} %pad_maximum_fusion), channel_id=1, source_target_pairs={{0,8},{8,0},{1,9},{9,1},{2,10},{10,2},{3,11},{11,3},{4,12},{12,4},... | collective-permute-start | bytes 786440 | tf_op jit(solution)/shard_map/ppermute | solution.py:304
  36.5 5.0 %copy-start.1 = (f32[8,16,1024]{2,1,0:T(8,128)S(1)}, f32[8,16,1024]{2,1,0:T(8,128)}, u32[]{:S(2)}) copy-start(f32[8,16,1024]{2,1,0:T(8,128)} %param.5) | copy-start | bytes 1572868
  37.0 5.8 %collective-permute-start.3 = (f32[128,256]{1,0:T(8,128)S(1)}, f32[128,256]{1,0:T(8,128)S(1)}, u32[]{:S(2)}, u32[]{:S(2)}) collective-permute-start(f32[128,256]{1,0:T(8,128)S(1)} %get-tuple-element.37), channel_id=1, source_target_pairs={{0,32},{32,0},{64,96},{96,64},{1,33},{33,1},{65,97},{97,65},{2,34}... | collective-permute-start | bytes 393224 | tf_op jit(solution)/shard_map/ppermute | solution.py:304
  39.0 6.5 %collective-permute-start.4 = (f32[128,256]{1,0:T(8,128)S(1)}, f32[128,256]{1,0:T(8,128)S(1)}, u32[]{:S(2)}, u32[]{:S(2)}) collective-permute-start(f32[128,256]{1,0:T(8,128)S(1)} %get-tuple-element.38), channel_id=1, source_target_pairs={{0,96},{32,64},{64,32},{96,0},{1,97},{33,65},{65,33},{97,1},{2,98}... | collective-permute-start | bytes 393224 | tf_op jit(solution)/shard_map/ppermute | solution.py:304
  41.5 7.9 %collective-permute-start.7 = (f32[128,512]{1,0:T(8,128)S(1)}, f32[128,512]{1,0:T(8,128)S(1)}, u32[]{:S(2)}, u32[]{:S(2)}) collective-permute-start(f32[128,512]{1,0:T(8,128)S(1)} %get-tuple-element.70), channel_id=1, source_target_pairs={{0,16},{16,0},{1,17},{17,1},{2,18},{18,2},{3,19},{19,3},{4,20},{20... | collective-permute-start | bytes 786440 | tf_op jit(solution)/shard_map/ppermute | solution.py:304
  45.5 6.3 %collective-permute-start.5 = (f32[128,256]{1,0:T(8,128)S(1)}, f32[128,256]{1,0:T(8,128)S(1)}, u32[]{:S(2)}, u32[]{:S(2)}) collective-permute-start(f32[128,256]{1,0:T(8,128)S(1)} %add.62), channel_id=1, source_target_pairs={{0,96},{32,64},{64,32},{96,0},{1,97},{33,65},{65,33},{97,1},{2,98}... | collective-permute-start | bytes 393224 | tf_op jit(solution)/shard_map/ppermute | solution.py:304
  48.1 5.0 %collective-permute-start.6 = (f32[128,256]{1,0:T(8,128)S(1)}, f32[128,256]{1,0:T(8,128)S(1)}, u32[]{:S(2)}, u32[]{:S(2)}) collective-permute-start(f32[128,256]{1,0:T(8,128)S(1)} %add.63), channel_id=1, source_target_pairs={{0,32},{32,0},{64,96},{96,64},{1,33},{33,1},{65,97},{97,65},{2,34}... | collective-permute-start | bytes 393224 | tf_op jit(solution)/shard_map/ppermute | solution.py:304
  53.7 1.8 %collective-permute-start.8 = (f32[16,24,256]{2,1,0:T(8,128)S(1)}, f32[16,24,256]{2,1,0:T(8,128)S(1)}, u32[]{:S(2)}, u32[]{:S(2)}) collective-permute-start(f32[16,24,256]{2,1,0:T(8,128)S(1)} %get-tuple-element.44), channel_id=1, source_target_pairs={{0,8},{8,0},{1,9},{9,1},{2,10},{10,2},{3,11},{11,3},{4,12},{12,4},... | collective-permute-start | bytes 1179656 | tf_op jit(solution)/shard_map/ppermute | solution.py:304
  72.7 12.9 %all-to-all-start.3 = ((f32[16,24,256]{2,1,0:T(8,128)}), f32[16,24,256]{2,1,0:T(8,128)S(1)}, u32[]{:S(2)}, u32[]{:S(2)}) async-start(f32[16,24,256]{2,1,0:T(8,128)} %owner_sum.2), calls=%async_computation.3 | async-start | bytes 786432 | tf_op jit(solution)/shard_map/all_to_all | solution.py:299
  77.6 1.6 %collective-permute-start.9 = (f32[256,256]{1,0:T(8,128)S(1)}, f32[256,256]{1,0:T(8,128)S(1)}, u32[]{:S(2)}, u32[]{:S(2)}) collective-permute-start(f32[256,256]{1,0:T(8,128)S(1)} %pad_maximum_fusion.1), channel_id=1, source_target_pairs={{0,8},{8,0},{1,9},{9,1},{2,10},{10,2},{3,11},{11,3},{4,12},{12,4},... | collective-permute-start | bytes 786440 | tf_op jit(solution)/shard_map/ppermute | solution.py:304
  85.6 1.7 %collective-permute-start.10 = (f32[16,24,256]{2,1,0:T(8,128)S(1)}, f32[16,24,256]{2,1,0:T(8,128)S(1)}, u32[]{:S(2)}, u32[]{:S(2)}) collective-permute-start(f32[16,24,256]{2,1,0:T(8,128)S(1)} %all-to-all-done.3.mine_ref), channel_id=1, source_target_pairs={{0,8},{8,0},{1,9},{9,1},{2,10},{10,2},{3,11},{11,3},{4,12},{12,4},... | collective-permute-start | bytes 1179656 | tf_op jit(solution)/shard_map/ppermute | solution.py:304
  85.6 9.0 %collective-permute-start.11 = (f32[256,256]{1,0:T(8,128)S(1)}, f32[256,256]{1,0:T(8,128)S(1)}, u32[]{:S(2)}, u32[]{:S(2)}) collective-permute-start(f32[256,256]{1,0:T(8,128)S(1)} %pad_maximum_fusion.2.q0), channel_id=1, source_target_pairs={{0,16},{16,0},{1,17},{17,1},{2,18},{18,2},{3,19},{19,3},{4,20},{20... | collective-permute-start | bytes 786440 | tf_op jit(solution)/shard_map/ppermute | solution.py:304
  87.1 9.0 %collective-permute-start.14 = (f32[256,256]{1,0:T(8,128)S(1)}, f32[256,256]{1,0:T(8,128)S(1)}, u32[]{:S(2)}, u32[]{:S(2)}) collective-permute-start(f32[256,256]{1,0:T(8,128)S(1)} %pad_maximum_fusion.2.q0), channel_id=1, source_target_pairs={{0,8},{8,0},{1,9},{9,1},{2,10},{10,2},{3,11},{11,3},{4,12},{12,4},... | collective-permute-start | bytes 786440 | tf_op jit(solution)/shard_map/ppermute | solution.py:304
  94.7 1.5 %collective-permute-start.15 = (f32[256,256]{1,0:T(8,128)S(1)}, f32[256,256]{1,0:T(8,128)S(1)}, u32[]{:S(2)}, u32[]{:S(2)}) collective-permute-start(f32[256,256]{1,0:T(8,128)S(1)} %collective-permute-done.11.q1), channel_id=1, source_target_pairs={{0,8},{8,0},{1,9},{9,1},{2,10},{10,2},{3,11},{11,3},{4,12},{12,4},... | collective-permute-start | bytes 786440 | tf_op jit(solution)/shard_map/ppermute | solution.py:304
  95.0 5.6 %collective-permute-start.12 = (f32[128,256]{1,0:T(8,128)S(1)}, f32[128,256]{1,0:T(8,128)S(1)}, u32[]{:S(2)}, u32[]{:S(2)}) collective-permute-start(f32[128,256]{1,0:T(8,128)S(1)} %get-tuple-element.56), channel_id=1, source_target_pairs={{0,32},{32,0},{64,96},{96,64},{1,33},{33,1},{65,97},{97,65},{2,34}... | collective-permute-start | bytes 393224 | tf_op jit(solution)/shard_map/ppermute | solution.py:304
  95.0 6.8 %collective-permute-start.13 = (f32[128,256]{1,0:T(8,128)S(1)}, f32[128,256]{1,0:T(8,128)S(1)}, u32[]{:S(2)}, u32[]{:S(2)}) collective-permute-start(f32[128,256]{1,0:T(8,128)S(1)} %get-tuple-element.57), channel_id=1, source_target_pairs={{0,96},{32,64},{64,32},{96,0},{1,97},{33,65},{65,33},{97,1},{2,98}... | collective-permute-start | bytes 393224 | tf_op jit(solution)/shard_map/ppermute | solution.py:304
  101.8 6.3 %collective-permute-start.16 = (f32[128,256]{1,0:T(8,128)S(1)}, f32[128,256]{1,0:T(8,128)S(1)}, u32[]{:S(2)}, u32[]{:S(2)}) collective-permute-start(f32[128,256]{1,0:T(8,128)S(1)} %add.67), channel_id=1, source_target_pairs={{0,96},{32,64},{64,32},{96,0},{1,97},{33,65},{65,33},{97,1},{2,98}... | collective-permute-start | bytes 393224 | tf_op jit(solution)/shard_map/ppermute | solution.py:304
  103.0 5.0 %collective-permute-start.17 = (f32[128,256]{1,0:T(8,128)S(1)}, f32[128,256]{1,0:T(8,128)S(1)}, u32[]{:S(2)}, u32[]{:S(2)}) collective-permute-start(f32[128,256]{1,0:T(8,128)S(1)} %add.68), channel_id=1, source_target_pairs={{0,32},{32,0},{64,96},{96,64},{1,33},{33,1},{65,97},{97,65},{2,34}... | collective-permute-start | bytes 393224 | tf_op jit(solution)/shard_map/ppermute | solution.py:304
  108.7 1.8 %collective-permute-start.18 = (f32[16,24,256]{2,1,0:T(8,128)S(1)}, f32[16,24,256]{2,1,0:T(8,128)S(1)}, u32[]{:S(2)}, u32[]{:S(2)}) collective-permute-start(f32[16,24,256]{2,1,0:T(8,128)S(1)} %get-tuple-element.66), channel_id=1, source_target_pairs={{0,8},{8,0},{1,9},{9,1},{2,10},{10,2},{3,11},{11,3},{4,12},{12,4},... | collective-permute-start | bytes 1179656 | tf_op jit(solution)/shard_map/ppermute | solution.py:304
  125.0 13.0 %all-to-all-start.5 = ((f32[16,24,256]{2,1,0:T(8,128)}), f32[16,24,256]{2,1,0:T(8,128)S(1)}, u32[]{:S(2)}, u32[]{:S(2)}) async-start(f32[16,24,256]{2,1,0:T(8,128)} %owner_sum.3), calls=%async_computation.5 | async-start | bytes 786432 | tf_op jit(solution)/shard_map/all_to_all | solution.py:299
  129.9 10.4 %collective-permute-start.20 = (f32[256,256]{1,0:T(8,128)S(1)}, f32[256,256]{1,0:T(8,128)S(1)}, u32[]{:S(2)}, u32[]{:S(2)}) collective-permute-start(f32[256,256]{1,0:T(8,128)S(1)} %pad_maximum_fusion.3.q0), channel_id=1, source_target_pairs={{0,16},{16,0},{1,17},{17,1},{2,18},{18,2},{3,19},{19,3},{4,20},{20... | collective-permute-start | bytes 786440 | tf_op jit(solution)/shard_map/ppermute | solution.py:304
  138.0 2.2 %collective-permute-start.19 = (f32[16,24,256]{2,1,0:T(8,128)S(1)}, f32[16,24,256]{2,1,0:T(8,128)S(1)}, u32[]{:S(2)}, u32[]{:S(2)}) collective-permute-start(f32[16,24,256]{2,1,0:T(8,128)S(1)} %all-to-all-done.5.mine_ref), channel_id=1, source_target_pairs={{0,8},{8,0},{1,9},{9,1},{2,10},{10,2},{3,11},{11,3},{4,12},{12,4},... | collective-permute-start | bytes 1179656 | tf_op jit(solution)/shard_map/ppermute | solution.py:304
  138.0 8.8 %collective-permute-start.21 = (f32[256,256]{1,0:T(8,128)S(1)}, f32[256,256]{1,0:T(8,128)S(1)}, u32[]{:S(2)}, u32[]{:S(2)}) collective-permute-start(f32[256,256]{1,0:T(8,128)S(1)} %pad_maximum_fusion.3.q0), channel_id=1, source_target_pairs={{0,8},{8,0},{1,9},{9,1},{2,10},{10,2},{3,11},{11,3},{4,12},{12,4},... | collective-permute-start | bytes 786440 | tf_op jit(solution)/shard_map/ppermute | solution.py:304
  140.2 6.6 %collective-permute-start.22 = (f32[256,256]{1,0:T(8,128)S(1)}, f32[256,256]{1,0:T(8,128)S(1)}, u32[]{:S(2)}, u32[]{:S(2)}) collective-permute-start(f32[256,256]{1,0:T(8,128)S(1)} %collective-permute-done.20.q1), channel_id=1, source_target_pairs={{0,8},{8,0},{1,9},{9,1},{2,10},{10,2},{3,11},{11,3},{4,12},{12,4},... | collective-permute-start | bytes 786440 | tf_op jit(solution)/shard_map/ppermute | solution.py:304

commit v13 on v11

--- a/solution.py
+++ b/solution.py
@@ -434,9 +434,9 @@
     parts, moved = together(parts, across(basis))
     quarters = (basis, moved, from_sibling(basis), from_sibling(moved))
     u_scaled = basis_rows(place, inverse, quarters)
-    parts, (u_scaled, _) = plane_total(*parts, (u_scaled, ()))
+    parts, _ = plane_total(*parts, ((), ()))
     basis = jnp.concatenate(parts)
-    tiles, _ = gram_tiles(place, a_quarter, parts, rank, ())
+    tiles, u_scaled = gram_tiles(place, a_quarter, parts, rank, u_scaled)
     mine = row_total(tiles)
     inverse, right = call(
         right_cores,

time: 150 us -> 153 us (1.020)
  waiting for transfers between devices: 65.6 us -> 67.5 us
    ppermute x23, waiting for transfers between devices: 26.5 us -> 28.4 us  [from_peer(): return lax.ppermute(x, axis, [(i, i ^ step) for i in range(count)])]
  transfers between devices with their start and end apart: 28 -> 28, of which waited for: 19 -> 20; matrix products, arithmetic and copies ran while one was open for 0% -> 0% of each run, Pallas kernels for 13% -> 12%
where the time goes in v13:
time: 153 us; the launch traced here: 150 us
  waiting for transfers between devices  67.5 us (44%)
  starting transfers between devices  41.2 us (27%)
  Pallas kernels  24.4 us (16%)
  blocking collectives  13.6 us (9%)
    all_to_all x5, waiting for transfers between devices, exchanged(): return lax.all_to_all(tiles, axis, 0, 0, tiled=True)  39.1 us
    ppermute x23, waiting for transfers between devices, from_peer(): return lax.ppermute(x, axis, [(i, i ^ step) for i in range(count)])  28.4 us
    all_to_all x5, starting transfers between devices, exchanged(): return lax.all_to_all(tiles, axis, 0, 0, tiled=True)  26.2 us
    pallas_call x11, Pallas kernels, call(): pl.pallas_call(kernel, out_shape=shapes if len(shapes) > 1 else shapes[0]...  24.4 us
    ppermute x23, starting transfers between devices, from_peer(): return lax.ppermute(x, axis, [(i, i ^ step) for i in range(count)])  15 us
    all_to_all x1, blocking collectives, exchanged(): return lax.all_to_all(tiles, axis, 0, 0, tiled=True)  13.6 us
  transfers between devices with their start and end apart: 28, of which 20 were waited for; matrix products, arithmetic and copies ran while one was open for 0% of the time, Pallas kernels for 12%

profile of v13, /device:TPU:8, one launch (start us, length us, event | category | flops | bytes accessed | tf_op | source)
XLA Modules:
  0.0 149.9 jit_solution(7973955813883365365)
XLA Ops:
  0.6 1.1 constant_dynamic-slice_fusion.10
  1.7 0.4 collective-permute-start
  2.2 3.2 %projections.1 = f32[8,32,256]{2,1,0:T(8,128)} custom-call(f32[128,1024]{1,0:T(8,128)} %bitcast.4, f32[128,1024]{1,0:T(8,128)} %bitcast.5, f32[1024,256]{1,0:T(8,128)} %u_hbm.1, f32[1024,256]{1,0:T(8,128)} %v_hbm.1), custom_call_target="tpu_custom_call" | custom-call | tf_op jit(solution)/shard_map/projections/pallas_call | solution.py:153
  5.3 6.4 %all-to-all-start = ((f32[8,32,256]{2,1,0:T(8,128)}), f32[8,32,256]{2,1,0:T(8,128)S(1)}, u32[]{:S(2)}, u32[]{:S(2)}) async-start(f32[8,32,256]{2,1,0:T(8,128)} %projections.1), calls=%async_computation | async-start | bytes 524288 | tf_op jit(solution)/shard_map/all_to_all | solution.py:299
  11.8 8.4 %all-to-all-done.tiles_ref = f32[8,32,256]{2,1,0:T(8,128)S(1)} async-done(((f32[8,32,256]{2,1,0:T(8,128)}), f32[8,32,256]{2,1,0:T(8,128)S(1)}, u32[]{:S(2)}, u32[]{:S(2)}) %all-to-all-start) | async-done | bytes 262176 | tf_op jit(solution)/shard_map/all_to_all | solution.py:299
  20.2 1.1 owner_coefficients.1
  21.3 5.3 %all-to-all-start.1 = ((f32[16,32,256]{2,1,0:T(8,128)}), f32[16,32,256]{2,1,0:T(8,128)S(1)}, u32[]{:S(2)}, u32[]{:S(2)}) async-start(f32[16,32,256]{2,1,0:T(8,128)} %owner_coefficients.1), calls=%async_computation.1 | async-start | bytes 1048576 | tf_op jit(solution)/shard_map/all_to_all | solution.py:299
  26.7 1.5 %collective-permute-done.1.f2 = f32[256,256]{1,0:T(8,128)S(1)} collective-permute-done((f32[256,256]{1,0:T(8,128)S(1)}, f32[256,256]{1,0:T(8,128)S(1)}, u32[]{:S(2)}, u32[]{:S(2)}) %collective-permute-start.1) | collective-permute-done | bytes 262176 | tf_op jit(solution)/shard_map/ppermute | solution.py:304
  28.3 7.0 %all-to-all-done.1.mine_ref.pair_ref = f32[16,32,256]{2,1,0:T(8,128)S(1)} async-done(((f32[16,32,256]{2,1,0:T(8,128)}), f32[16,32,256]{2,1,0:T(8,128)S(1)}, u32[]{:S(2)}, u32[]{:S(2)}) %all-to-all-start.1) | async-done | bytes 524320 | tf_op jit(solution)/shard_map/all_to_all | solution.py:299
  35.3 1.9 %collective-permute-done.2.other_ref.pair_other_ref = f32[16,32,256]{2,1,0:T(8,128)S(1)} collective-permute-done((f32[16,32,256]{2,1,0:T(8,128)S(1)}, f32[16,32,256]{2,1,0:T(8,128)S(1)}, u32[]{:S(2)}, u32[]{:S(2)}) %collective-permute-start.2) | collective-permute-done | bytes 524320 | tf_op jit(solution)/shard_map/ppermute | solution.py:304
  37.2 0.4 load_sum.1
  37.6 2.0 %collective-permute-start.3 = (f32[128,256]{1,0:T(8,128)S(1)}, f32[128,256]{1,0:T(8,128)S(1)}, u32[]{:S(2)}, u32[]{:S(2)}) collective-permute-start(f32[128,256]{1,0:T(8,128)S(1)} %get-tuple-element.49), channel_id=1, source_target_pairs={{0,32},{32,0},{64,96},{96,64},{1,33},{33,1},{65,97},{97,65},{2,34}... | collective-permute-start | bytes 393224 | tf_op jit(solution)/shard_map/ppermute | solution.py:304
  39.6 2.5 %collective-permute-start.4 = (f32[128,256]{1,0:T(8,128)S(1)}, f32[128,256]{1,0:T(8,128)S(1)}, u32[]{:S(2)}, u32[]{:S(2)}) collective-permute-start(f32[128,256]{1,0:T(8,128)S(1)} %get-tuple-element.50), channel_id=1, source_target_pairs={{0,96},{32,64},{64,32},{96,0},{1,97},{33,65},{65,33},{97,1},{2,98}... | collective-permute-start | bytes 393224 | tf_op jit(solution)/shard_map/ppermute | solution.py:304
  42.2 1.5 collective-permute-start.7
  43.7 2.4 %collective-permute-done.4 = f32[128,256]{1,0:T(8,128)S(1)} collective-permute-done((f32[128,256]{1,0:T(8,128)S(1)}, f32[128,256]{1,0:T(8,128)S(1)}, u32[]{:S(2)}, u32[]{:S(2)}) %collective-permute-start.4) | collective-permute-done | bytes 131104 | tf_op jit(solution)/shard_map/ppermute | solution.py:304
  46.1 2.6 %collective-permute-start.5 = (f32[128,256]{1,0:T(8,128)S(1)}, f32[128,256]{1,0:T(8,128)S(1)}, u32[]{:S(2)}, u32[]{:S(2)}) collective-permute-start(f32[128,256]{1,0:T(8,128)S(1)} %add.58), channel_id=1, source_target_pairs={{0,96},{32,64},{64,32},{96,0},{1,97},{33,65},{65,33},{97,1},{2,98}... | collective-permute-start | bytes 393224 | tf_op jit(solution)/shard_map/ppermute | solution.py:304
  48.8 1.2 collective-permute-done.7
  50.1 2.3 %collective-permute-done.5 = f32[128,256]{1,0:T(8,128)S(1)} collective-permute-done((f32[128,256]{1,0:T(8,128)S(1)}, f32[128,256]{1,0:T(8,128)S(1)}, u32[]{:S(2)}, u32[]{:S(2)}) %collective-permute-start.5) | collective-permute-done | bytes 131104 | tf_op jit(solution)/shard_map/ppermute | solution.py:304
  52.4 1.4 collective-permute-done.6
  53.8 0.5 gram_and_cores.2
  54.5 1.7 %collective-permute-done.8 = f32[16,24,256]{2,1,0:T(8,128)S(1)} collective-permute-done((f32[16,24,256]{2,1,0:T(8,128)S(1)}, f32[16,24,256]{2,1,0:T(8,128)S(1)}, u32[]{:S(2)}, u32[]{:S(2)}) %collective-permute-start.8) | collective-permute-done | bytes 393248 | tf_op jit(solution)/shard_map/ppermute | solution.py:304
  56.2 0.8 add.62
  57.0 4.9 %all-to-all-start.2 = ((f32[16,24,256]{2,1,0:T(8,128)}), f32[16,24,256]{2,1,0:T(8,128)S(1)}, u32[]{:S(2)}, u32[]{:S(2)}) async-start(f32[16,24,256]{2,1,0:T(8,128)} %add.62), calls=%async_computation.2 | async-start | bytes 786432 | tf_op jit(solution)/shard_map/all_to_all | solution.py:299
  61.9 9.2 %all-to-all-done.2.tiles_ref = f32[16,24,256]{2,1,0:T(8,128)S(1)} async-done(((f32[16,24,256]{2,1,0:T(8,128)}), f32[16,24,256]{2,1,0:T(8,128)S(1)}, u32[]{:S(2)}, u32[]{:S(2)}) %all-to-all-start.2) | async-done | bytes 393248 | tf_op jit(solution)/shard_map/all_to_all | solution.py:299
  71.1 0.8 owner_sum.2
  71.9 4.8 %all-to-all-start.3 = ((f32[16,24,256]{2,1,0:T(8,128)}), f32[16,24,256]{2,1,0:T(8,128)S(1)}, u32[]{:S(2)}, u32[]{:S(2)}) async-start(f32[16,24,256]{2,1,0:T(8,128)} %owner_sum.2), calls=%async_computation.3 | async-start | bytes 786432 | tf_op jit(solution)/shard_map/all_to_all | solution.py:299
  76.8 1.5 %collective-permute-done.9.f2 = f32[256,256]{1,0:T(8,128)S(1)} collective-permute-done((f32[256,256]{1,0:T(8,128)S(1)}, f32[256,256]{1,0:T(8,128)S(1)}, u32[]{:S(2)}, u32[]{:S(2)}) %collective-permute-start.9) | collective-permute-done | bytes 262176 | tf_op jit(solution)/shard_map/ppermute | solution.py:304
  78.4 6.6 %all-to-all-done.3.mine_ref = f32[16,24,256]{2,1,0:T(8,128)S(1)} async-done(((f32[16,24,256]{2,1,0:T(8,128)}), f32[16,24,256]{2,1,0:T(8,128)S(1)}, u32[]{:S(2)}, u32[]{:S(2)}) %all-to-all-start.3) | async-done | bytes 393248 | tf_op jit(solution)/shard_map/all_to_all | solution.py:299
  85.0 1.5 %collective-permute-start.11 = (f32[256,256]{1,0:T(8,128)S(1)}, f32[256,256]{1,0:T(8,128)S(1)}, u32[]{:S(2)}, u32[]{:S(2)}) collective-permute-start(f32[256,256]{1,0:T(8,128)S(1)} %pad_maximum_fusion.2.q0), channel_id=1, source_target_pairs={{0,16},{16,0},{1,17},{17,1},{2,18},{18,2},{3,19},{19,3},{4,20},{20... | collective-permute-start | bytes 786440 | tf_op jit(solution)/shard_map/ppermute | solution.py:304
  86.6 7.3 %turn_over.1 = (f32[256,256]{1,0:T(8,128)S(1)}, f32[8,16,256]{2,1,0:T(8,128)}, f32[128,256]{1,0:T(8,128)S(1)}, f32[128,256]{1,0:T(8,128)S(1)}) custom-call(s32[1]{0:T(128)} %bitcast.place_ref, f32[16,24,256]{2,1,0:T(8,128)S(1)} %all-to-all-done.3.mine_ref, f32[16,24,256]{2,1,0:T(8,128)S(1)} %collective-permute-done.10.other_ref, ...), custom_call_target="tpu_custom_call" | custom-call | flops 6442450944 | tf_op jit(solution)/shard_map/turn_over/pallas_call | solution.py:153
  94.1 1.2 collective-permute-start.13
  95.3 4.3 %collective-permute-done.12 = f32[128,256]{1,0:T(8,128)S(1)} collective-permute-done((f32[128,256]{1,0:T(8,128)S(1)}, f32[128,256]{1,0:T(8,128)S(1)}, u32[]{:S(2)}, u32[]{:S(2)}) %collective-permute-start.12) | collective-permute-done | bytes 131104 | tf_op jit(solution)/shard_map/ppermute | solution.py:304
  99.7 1.3 collective-permute-done.13
  101.0 1.2 collective-permute-start.14
  102.3 5.0 %collective-permute-done.14 = f32[128,256]{1,0:T(8,128)S(1)} collective-permute-done((f32[128,256]{1,0:T(8,128)S(1)}, f32[128,256]{1,0:T(8,128)S(1)}, u32[]{:S(2)}, u32[]{:S(2)}) %collective-permute-start.14) | collective-permute-done | bytes 131104 | tf_op jit(solution)/shard_map/ppermute | solution.py:304
  107.3 0.5 gram_and_cores.3
  107.9 0.5 collective-permute-start.17
  108.5 1.5 collective-permute-done.17.q2
  110.0 0.4 collective-permute-done.18.q3
  110.4 1.6 %whole_basis.2 = f32[1024,256]{1,0:T(8,128)} custom-call(s32[1]{0:T(128)} %bitcast.place_ref, f32[256,256]{1,0:T(8,128)S(1)} %get-tuple-element.72.inverse_ref, f32[256,256]{1,0:T(8,128)S(1)} %pad_maximum_fusion.2.q0, f32[256,256]{1,0:T(8,128)S(1)} %collective-permute-done.11.q1, f32[256,256]{1,0:T(8,128)S(1)} %collective-permute-done.17.q2, ...), custom_call_target="tpu_custom_call" | custom-call | flops 402653184 | tf_op jit(solution)/shard_map/whole_basis/pallas_call | solution.py:153
  112.1 13.6 %all_to_all.30.tiles_ref = f32[16,24,256]{2,1,0:T(8,128)S(1)} all-to-all(f32[16,24,256]{2,1,0:T(8,128)S(1)} %add.67), channel_id=1, replica_groups=mesh['z'=4,'y_lo'=2,'core'=2,'row'=8] {'y_lo','row'}, dimensions={0} | all-to-all | bytes 786432 | tf_op jit(solution)/shard_map/all_to_all | solution.py:299
  125.7 0.8 owner_sum.3
  126.5 4.8 %all-to-all-start.5 = ((f32[16,24,256]{2,1,0:T(8,128)}), f32[16,24,256]{2,1,0:T(8,128)S(1)}, u32[]{:S(2)}, u32[]{:S(2)}) async-start(f32[16,24,256]{2,1,0:T(8,128)} %owner_sum.3), calls=%async_computation.5 | async-start | bytes 786432 | tf_op jit(solution)/shard_map/all_to_all | solution.py:299
  131.6 7.9 %all-to-all-done.5.mine_ref = f32[16,24,256]{2,1,0:T(8,128)S(1)} async-done(((f32[16,24,256]{2,1,0:T(8,128)}), f32[16,24,256]{2,1,0:T(8,128)S(1)}, u32[]{:S(2)}, u32[]{:S(2)}) %all-to-all-start.5) | async-done | bytes 393248 | tf_op jit(solution)/shard_map/all_to_all | solution.py:299
  139.5 0.5 collective-permute-start.21
  140.0 1.7 %collective-permute-done.20.q1 = f32[256,256]{1,0:T(8,128)S(1)} collective-permute-done((f32[256,256]{1,0:T(8,128)S(1)}, f32[256,256]{1,0:T(8,128)S(1)}, u32[]{:S(2)}, u32[]{:S(2)}) %collective-permute-start.20) | collective-permute-done | bytes 262176 | tf_op jit(solution)/shard_map/ppermute | solution.py:304
  141.7 6.5 %right_cores.1 = (f32[256,256]{1,0:T(8,128)S(1)}, f32[8,16,256]{2,1,0:T(8,128)}) custom-call(s32[1]{0:T(128)} %bitcast.place_ref, f32[16,24,256]{2,1,0:T(8,128)S(1)} %all-to-all-done.5.mine_ref, f32[16,24,256]{2,1,0:T(8,128)S(1)} %collective-permute-done.19.other_ref), custom_call_target="tpu_custom_call" | custom-call | tf_op jit(solution)/shard_map/right_cores/pallas_call | solution.py:153
  148.3 1.6 %whole_basis.3 = f32[1024,256]{1,0:T(8,128)} custom-call(s32[1]{0:T(128)} %bitcast.place_ref, f32[256,256]{1,0:T(8,128)S(1)} %get-tuple-element.77.inverse_ref, f32[256,256]{1,0:T(8,128)S(1)} %pad_maximum_fusion.3.q0, f32[256,256]{1,0:T(8,128)S(1)} %collective-permute-done.20.q1, f32[256,256]{1,0:T(8,128)S(1)} %collective-permute-done.21.q2, ...), custom_call_target="tpu_custom_call" | custom-call | flops 402653184 | tf_op jit(solution)/shard_map/whole_basis/pallas_call | solution.py:153
  (41 shorter events, 1.6 us)
Async XLA Ops:
  1.7 18.5 %collective-permute-start = (f32[128,512]{1,0:T(8,128)S(1)}, f32[128,512]{1,0:T(8,128)S(1)}, u32[]{:S(2)}, u32[]{:S(2)}) collective-permute-start(f32[128,512]{1,0:T(8,128)S(1)} %get-tuple-element.82), channel_id=1, source_target_pairs={{0,16},{16,0},{1,17},{17,1},{2,18},{18,2},{3,19},{19,3},{4,20},{20... | collective-permute-start | bytes 786440 | tf_op jit(solution)/shard_map/ppermute | solution.py:304
  5.3 14.9 %all-to-all-start = ((f32[8,32,256]{2,1,0:T(8,128)}), f32[8,32,256]{2,1,0:T(8,128)S(1)}, u32[]{:S(2)}, u32[]{:S(2)}) async-start(f32[8,32,256]{2,1,0:T(8,128)} %projections.1), calls=%async_computation | async-start | bytes 524288 | tf_op jit(solution)/shard_map/all_to_all | solution.py:299
  21.3 14.0 %all-to-all-start.1 = ((f32[16,32,256]{2,1,0:T(8,128)}), f32[16,32,256]{2,1,0:T(8,128)S(1)}, u32[]{:S(2)}, u32[]{:S(2)}) async-start(f32[16,32,256]{2,1,0:T(8,128)} %owner_coefficients.1), calls=%async_computation.1 | async-start | bytes 1048576 | tf_op jit(solution)/shard_map/all_to_all | solution.py:299
  26.7 1.6 %collective-permute-start.1 = (f32[256,256]{1,0:T(8,128)S(1)}, f32[256,256]{1,0:T(8,128)S(1)}, u32[]{:S(2)}, u32[]{:S(2)}) collective-permute-start(f32[256,256]{1,0:T(8,128)S(1)} %pad_maximum_fusion), channel_id=1, source_target_pairs={{0,8},{8,0},{1,9},{9,1},{2,10},{10,2},{3,11},{11,3},{4,12},{12,4},... | collective-permute-start | bytes 786440 | tf_op jit(solution)/shard_map/ppermute | solution.py:304
  35.3 1.9 %collective-permute-start.2 = (f32[16,32,256]{2,1,0:T(8,128)S(1)}, f32[16,32,256]{2,1,0:T(8,128)S(1)}, u32[]{:S(2)}, u32[]{:S(2)}) collective-permute-start(f32[16,32,256]{2,1,0:T(8,128)S(1)} %all-to-all-done.1.mine_ref.pair_ref), channel_id=1, source_target_pairs={{0,8},{8,0},{1,9},{9,1},{2,10},{10,2},{3,11},{11,3},{4,12},{12,4},... | collective-permute-start | bytes 1572872 | tf_op jit(solution)/shard_map/ppermute | solution.py:304
  37.2 5.0 %copy-start = (f32[8,16,1024]{2,1,0:T(8,128)S(1)}, f32[8,16,1024]{2,1,0:T(8,128)}, u32[]{:S(2)}) copy-start(f32[8,16,1024]{2,1,0:T(8,128)} %param.5) | copy-start | bytes 1572868
  37.6 6.1 %collective-permute-start.3 = (f32[128,256]{1,0:T(8,128)S(1)}, f32[128,256]{1,0:T(8,128)S(1)}, u32[]{:S(2)}, u32[]{:S(2)}) collective-permute-start(f32[128,256]{1,0:T(8,128)S(1)} %get-tuple-element.49), channel_id=1, source_target_pairs={{0,32},{32,0},{64,96},{96,64},{1,33},{33,1},{65,97},{97,65},{2,34}... | collective-permute-start | bytes 393224 | tf_op jit(solution)/shard_map/ppermute | solution.py:304
  39.6 6.5 %collective-permute-start.4 = (f32[128,256]{1,0:T(8,128)S(1)}, f32[128,256]{1,0:T(8,128)S(1)}, u32[]{:S(2)}, u32[]{:S(2)}) collective-permute-start(f32[128,256]{1,0:T(8,128)S(1)} %get-tuple-element.50), channel_id=1, source_target_pairs={{0,96},{32,64},{64,32},{96,0},{1,97},{33,65},{65,33},{97,1},{2,98}... | collective-permute-start | bytes 393224 | tf_op jit(solution)/shard_map/ppermute | solution.py:304
  42.2 7.9 %collective-permute-start.7 = (f32[128,512]{1,0:T(8,128)S(1)}, f32[128,512]{1,0:T(8,128)S(1)}, u32[]{:S(2)}, u32[]{:S(2)}) collective-permute-start(f32[128,512]{1,0:T(8,128)S(1)} %get-tuple-element.80), channel_id=1, source_target_pairs={{0,16},{16,0},{1,17},{17,1},{2,18},{18,2},{3,19},{19,3},{4,20},{20... | collective-permute-start | bytes 786440 | tf_op jit(solution)/shard_map/ppermute | solution.py:304
  46.1 6.3 %collective-permute-start.5 = (f32[128,256]{1,0:T(8,128)S(1)}, f32[128,256]{1,0:T(8,128)S(1)}, u32[]{:S(2)}, u32[]{:S(2)}) collective-permute-start(f32[128,256]{1,0:T(8,128)S(1)} %add.58), channel_id=1, source_target_pairs={{0,96},{32,64},{64,32},{96,0},{1,97},{33,65},{65,33},{97,1},{2,98}... | collective-permute-start | bytes 393224 | tf_op jit(solution)/shard_map/ppermute | solution.py:304
  48.7 5.0 %collective-permute-start.6 = (f32[128,256]{1,0:T(8,128)S(1)}, f32[128,256]{1,0:T(8,128)S(1)}, u32[]{:S(2)}, u32[]{:S(2)}) collective-permute-start(f32[128,256]{1,0:T(8,128)S(1)} %add.59), channel_id=1, source_target_pairs={{0,32},{32,0},{64,96},{96,64},{1,33},{33,1},{65,97},{97,65},{2,34}... | collective-permute-start | bytes 393224 | tf_op jit(solution)/shard_map/ppermute | solution.py:304
  54.4 1.8 %collective-permute-start.8 = (f32[16,24,256]{2,1,0:T(8,128)S(1)}, f32[16,24,256]{2,1,0:T(8,128)S(1)}, u32[]{:S(2)}, u32[]{:S(2)}) collective-permute-start(f32[16,24,256]{2,1,0:T(8,128)S(1)} %get-tuple-element.56), channel_id=1, source_target_pairs={{0,8},{8,0},{1,9},{9,1},{2,10},{10,2},{3,11},{11,3},{4,12},{12,4},... | collective-permute-start | bytes 1179656 | tf_op jit(solution)/shard_map/ppermute | solution.py:304
  57.0 14.2 %all-to-all-start.2 = ((f32[16,24,256]{2,1,0:T(8,128)}), f32[16,24,256]{2,1,0:T(8,128)S(1)}, u32[]{:S(2)}, u32[]{:S(2)}) async-start(f32[16,24,256]{2,1,0:T(8,128)} %add.62), calls=%async_computation.2 | async-start | bytes 786432 | tf_op jit(solution)/shard_map/all_to_all | solution.py:299
  71.9 13.0 %all-to-all-start.3 = ((f32[16,24,256]{2,1,0:T(8,128)}), f32[16,24,256]{2,1,0:T(8,128)S(1)}, u32[]{:S(2)}, u32[]{:S(2)}) async-start(f32[16,24,256]{2,1,0:T(8,128)} %owner_sum.2), calls=%async_computation.3 | async-start | bytes 786432 | tf_op jit(solution)/shard_map/all_to_all | solution.py:299
  76.7 1.6 %collective-permute-start.9 = (f32[256,256]{1,0:T(8,128)S(1)}, f32[256,256]{1,0:T(8,128)S(1)}, u32[]{:S(2)}, u32[]{:S(2)}) collective-permute-start(f32[256,256]{1,0:T(8,128)S(1)} %pad_maximum_fusion.1), channel_id=1, source_target_pairs={{0,8},{8,0},{1,9},{9,1},{2,10},{10,2},{3,11},{11,3},{4,12},{12,4},... | collective-permute-start | bytes 786440 | tf_op jit(solution)/shard_map/ppermute | solution.py:304
  84.9 1.7 %collective-permute-start.10 = (f32[16,24,256]{2,1,0:T(8,128)S(1)}, f32[16,24,256]{2,1,0:T(8,128)S(1)}, u32[]{:S(2)}, u32[]{:S(2)}) collective-permute-start(f32[16,24,256]{2,1,0:T(8,128)S(1)} %all-to-all-done.3.mine_ref), channel_id=1, source_target_pairs={{0,8},{8,0},{1,9},{9,1},{2,10},{10,2},{3,11},{11,3},{4,12},{12,4},... | collective-permute-start | bytes 1179656 | tf_op jit(solution)/shard_map/ppermute | solution.py:304
  85.0 9.0 %collective-permute-start.11 = (f32[256,256]{1,0:T(8,128)S(1)}, f32[256,256]{1,0:T(8,128)S(1)}, u32[]{:S(2)}, u32[]{:S(2)}) collective-permute-start(f32[256,256]{1,0:T(8,128)S(1)} %pad_maximum_fusion.2.q0), channel_id=1, source_target_pairs={{0,16},{16,0},{1,17},{17,1},{2,18},{18,2},{3,19},{19,3},{4,20},{20... | collective-permute-start | bytes 786440 | tf_op jit(solution)/shard_map/ppermute | solution.py:304
  94.0 5.7 %collective-permute-start.12 = (f32[128,256]{1,0:T(8,128)S(1)}, f32[128,256]{1,0:T(8,128)S(1)}, u32[]{:S(2)}, u32[]{:S(2)}) collective-permute-start(f32[128,256]{1,0:T(8,128)S(1)} %get-tuple-element.65), channel_id=1, source_target_pairs={{0,32},{32,0},{64,96},{96,64},{1,33},{33,1},{65,97},{97,65},{2,34}... | collective-permute-start | bytes 393224 | tf_op jit(solution)/shard_map/ppermute | solution.py:304
  94.1 6.8 %collective-permute-start.13 = (f32[128,256]{1,0:T(8,128)S(1)}, f32[128,256]{1,0:T(8,128)S(1)}, u32[]{:S(2)}, u32[]{:S(2)}) collective-permute-start(f32[128,256]{1,0:T(8,128)S(1)} %get-tuple-element.66), channel_id=1, source_target_pairs={{0,96},{32,64},{64,32},{96,0},{1,97},{33,65},{65,33},{97,1},{2,98}... | collective-permute-start | bytes 393224 | tf_op jit(solution)/shard_map/ppermute | solution.py:304
  101.0 6.3 %collective-permute-start.14 = (f32[128,256]{1,0:T(8,128)S(1)}, f32[128,256]{1,0:T(8,128)S(1)}, u32[]{:S(2)}, u32[]{:S(2)}) collective-permute-start(f32[128,256]{1,0:T(8,128)S(1)} %add.63), channel_id=1, source_target_pairs={{0,96},{32,64},{64,32},{96,0},{1,97},{33,65},{65,33},{97,1},{2,98}... | collective-permute-start | bytes 393224 | tf_op jit(solution)/shard_map/ppermute | solution.py:304
  102.2 5.0 %collective-permute-start.15 = (f32[128,256]{1,0:T(8,128)S(1)}, f32[128,256]{1,0:T(8,128)S(1)}, u32[]{:S(2)}, u32[]{:S(2)}) collective-permute-start(f32[128,256]{1,0:T(8,128)S(1)} %add.64), channel_id=1, source_target_pairs={{0,32},{32,0},{64,96},{96,64},{1,33},{33,1},{65,97},{97,65},{2,34}... | collective-permute-start | bytes 393224 | tf_op jit(solution)/shard_map/ppermute | solution.py:304
  107.8 4.2 %collective-permute-start.16 = (f32[16,24,256]{2,1,0:T(8,128)S(1)}, f32[16,24,256]{2,1,0:T(8,128)S(1)}, u32[]{:S(2)}, u32[]{:S(2)}) collective-permute-start(f32[16,24,256]{2,1,0:T(8,128)S(1)} %get-tuple-element.71), channel_id=1, source_target_pairs={{0,8},{8,0},{1,9},{9,1},{2,10},{10,2},{3,11},{11,3},{4,12},{12,4},... | collective-permute-start | bytes 1179656 | tf_op jit(solution)/shard_map/ppermute | solution.py:304
  107.9 2.1 %collective-permute-start.17 = (f32[256,256]{1,0:T(8,128)S(1)}, f32[256,256]{1,0:T(8,128)S(1)}, u32[]{:S(2)}, u32[]{:S(2)}) collective-permute-start(f32[256,256]{1,0:T(8,128)S(1)} %pad_maximum_fusion.2.q0), channel_id=1, source_target_pairs={{0,8},{8,0},{1,9},{9,1},{2,10},{10,2},{3,11},{11,3},{4,12},{12,4},... | collective-permute-start | bytes 786440 | tf_op jit(solution)/shard_map/ppermute | solution.py:304
  108.4 2.0 %collective-permute-start.18 = (f32[256,256]{1,0:T(8,128)S(1)}, f32[256,256]{1,0:T(8,128)S(1)}, u32[]{:S(2)}, u32[]{:S(2)}) collective-permute-start(f32[256,256]{1,0:T(8,128)S(1)} %collective-permute-done.11.q1), channel_id=1, source_target_pairs={{0,8},{8,0},{1,9},{9,1},{2,10},{10,2},{3,11},{11,3},{4,12},{12,4},... | collective-permute-start | bytes 786440 | tf_op jit(solution)/shard_map/ppermute | solution.py:304
  126.5 13.0 %all-to-all-start.5 = ((f32[16,24,256]{2,1,0:T(8,128)}), f32[16,24,256]{2,1,0:T(8,128)S(1)}, u32[]{:S(2)}, u32[]{:S(2)}) async-start(f32[16,24,256]{2,1,0:T(8,128)} %owner_sum.3), calls=%async_computation.5 | async-start | bytes 786432 | tf_op jit(solution)/shard_map/all_to_all | solution.py:299
  131.4 10.4 %collective-permute-start.20 = (f32[256,256]{1,0:T(8,128)S(1)}, f32[256,256]{1,0:T(8,128)S(1)}, u32[]{:S(2)}, u32[]{:S(2)}) collective-permute-start(f32[256,256]{1,0:T(8,128)S(1)} %pad_maximum_fusion.3.q0), channel_id=1, source_target_pairs={{0,16},{16,0},{1,17},{17,1},{2,18},{18,2},{3,19},{19,3},{4,20},{20... | collective-permute-start | bytes 786440 | tf_op jit(solution)/shard_map/ppermute | solution.py:304
  139.5 2.2 %collective-permute-start.19 = (f32[16,24,256]{2,1,0:T(8,128)S(1)}, f32[16,24,256]{2,1,0:T(8,128)S(1)}, u32[]{:S(2)}, u32[]{:S(2)}) collective-permute-start(f32[16,24,256]{2,1,0:T(8,128)S(1)} %all-to-all-done.5.mine_ref), channel_id=1, source_target_pairs={{0,8},{8,0},{1,9},{9,1},{2,10},{10,2},{3,11},{11,3},{4,12},{12,4},... | collective-permute-start | bytes 1179656 | tf_op jit(solution)/shard_map/ppermute | solution.py:304
  139.5 8.8 %collective-permute-start.21 = (f32[256,256]{1,0:T(8,128)S(1)}, f32[256,256]{1,0:T(8,128)S(1)}, u32[]{:S(2)}, u32[]{:S(2)}) collective-permute-start(f32[256,256]{1,0:T(8,128)S(1)} %pad_maximum_fusion.3.q0), channel_id=1, source_target_pairs={{0,8},{8,0},{1,9},{9,1},{2,10},{10,2},{3,11},{11,3},{4,12},{12,4},... | collective-permute-start | bytes 786440 | tf_op jit(solution)/shard_map/ppermute | solution.py:304
  141.7 6.6 %collective-permute-start.22 = (f32[256,256]{1,0:T(8,128)S(1)}, f32[256,256]{1,0:T(8,128)S(1)}, u32[]{:S(2)}, u32[]{:S(2)}) collective-permute-start(f32[256,256]{1,0:T(8,128)S(1)} %collective-permute-done.20.q1), channel_id=1, source_target_pairs={{0,8},{8,0},{1,9},{9,1},{2,10},{10,2},{3,11},{11,3},{4,12},{12,4},... | collective-permute-start | bytes 786440 | tf_op jit(solution)/shard_map/ppermute | solution.py:304

commit v14 on v12

--- a/solution.py
+++ b/solution.py
@@ -403,8 +403,10 @@
         ],
     )
     copies = (lax.axis_size(ROW), 2 * RANK, rank)
+    tiles, b_half = together(exchanged(partial, "row"), b_half)
     b_quarter = column_quarter(b_half, core)
-    pair = exchanged(call(owner_coefficients, [copies], exchanged(partial, "row")), ROW)
+    pair = exchanged(call(owner_coefficients, [copies], tiles), ROW)
+    pair, b_quarter = together(pair, b_quarter)
     pair_other = from_sibling(pair)
 
     part = (width // 8, rank)

time: 151 us -> 149 us (0.987)
  blocking collectives: 44.6 us -> 27.4 us
  starting transfers between devices: 28.7 us -> 36.1 us
  waiting for transfers between devices: 50 us -> 56.2 us
    all_to_all x3 -> x2, blocking collectives: 44.6 us -> 27.4 us  [exchanged(): return lax.all_to_all(tiles, axis, 0, 0, tiled=True)]
    all_to_all x3 -> x4, starting transfers between devices: 14.6 us -> 21.4 us  [exchanged(): return lax.all_to_all(tiles, axis, 0, 0, tiled=True)]
    all_to_all x3 -> x4, waiting for transfers between devices: 22.9 us -> 29.7 us  [exchanged(): return lax.all_to_all(tiles, axis, 0, 0, tiled=True)]
  transfers between devices with their start and end apart: 26 -> 27, of which waited for: 18 -> 18; matrix products, arithmetic and copies ran while one was open for 0% -> 0% of each run, Pallas kernels for 10% -> 13%
where the time goes in v14:
time: 149 us; the launch traced here: 146 us
  waiting for transfers between devices  56.2 us (38%)
  starting transfers between devices  36.1 us (24%)
  blocking collectives  27.4 us (18%)
  Pallas kernels  24.4 us (16%)
    all_to_all x4, waiting for transfers between devices, exchanged(): return lax.all_to_all(tiles, axis, 0, 0, tiled=True)  29.7 us
    all_to_all x2, blocking collectives, exchanged(): return lax.all_to_all(tiles, axis, 0, 0, tiled=True)  27.4 us
    ppermute x23, waiting for transfers between devices, from_peer(): return lax.ppermute(x, axis, [(i, i ^ step) for i in range(count)])  26.5 us
    pallas_call x11, Pallas kernels, call(): pl.pallas_call(kernel, out_shape=shapes if len(shapes) > 1 else shapes[0]...  24.4 us
    all_to_all x4, starting transfers between devices, exchanged(): return lax.all_to_all(tiles, axis, 0, 0, tiled=True)  21.4 us
    ppermute x23, starting transfers between devices, from_peer(): return lax.ppermute(x, axis, [(i, i ^ step) for i in range(count)])  14.7 us
  transfers between devices with their start and end apart: 27, of which 18 were waited for; matrix products, arithmetic and copies ran while one was open for 0% of the time, Pallas kernels for 13%

profile of v14, /device:TPU:8, one launch (start us, length us, event | category | flops | bytes accessed | tf_op | source)
XLA Modules:
  0.0 146.5 jit_solution(16211105524030621148)
XLA Ops:
  0.6 1.1 constant_dynamic-slice_fusion.10
  1.7 0.4 collective-permute-start
  2.2 3.2 %projections.1 = f32[8,32,256]{2,1,0:T(8,128)} custom-call(f32[128,1024]{1,0:T(8,128)} %bitcast.4, f32[128,1024]{1,0:T(8,128)} %bitcast.5, f32[1024,256]{1,0:T(8,128)} %u_hbm.1, f32[1024,256]{1,0:T(8,128)} %v_hbm.1), custom_call_target="tpu_custom_call" | custom-call | tf_op jit(solution)/shard_map/projections/pallas_call | solution.py:153
  5.3 6.4 %all-to-all-start = ((f32[8,32,256]{2,1,0:T(8,128)}), f32[8,32,256]{2,1,0:T(8,128)S(1)}, u32[]{:S(2)}, u32[]{:S(2)}) async-start(f32[8,32,256]{2,1,0:T(8,128)} %projections.1), calls=%async_computation | async-start | bytes 524288 | tf_op jit(solution)/shard_map/all_to_all | solution.py:299
  11.8 8.4 %all-to-all-done.tiles_ref = f32[8,32,256]{2,1,0:T(8,128)S(1)} async-done(((f32[8,32,256]{2,1,0:T(8,128)}), f32[8,32,256]{2,1,0:T(8,128)S(1)}, u32[]{:S(2)}, u32[]{:S(2)}) %all-to-all-start) | async-done | bytes 262176 | tf_op jit(solution)/shard_map/all_to_all | solution.py:299
  20.2 1.1 owner_coefficients.1
  21.3 5.3 %all-to-all-start.1 = ((f32[16,32,256]{2,1,0:T(8,128)}), f32[16,32,256]{2,1,0:T(8,128)S(1)}, u32[]{:S(2)}, u32[]{:S(2)}) async-start(f32[16,32,256]{2,1,0:T(8,128)} %owner_coefficients.1), calls=%async_computation.1 | async-start | bytes 1048576 | tf_op jit(solution)/shard_map/all_to_all | solution.py:299
  26.7 1.5 %collective-permute-done.1.f2 = f32[256,256]{1,0:T(8,128)S(1)} collective-permute-done((f32[256,256]{1,0:T(8,128)S(1)}, f32[256,256]{1,0:T(8,128)S(1)}, u32[]{:S(2)}, u32[]{:S(2)}) %collective-permute-start.1) | collective-permute-done | bytes 262176 | tf_op jit(solution)/shard_map/ppermute | solution.py:304
  28.3 7.0 %all-to-all-done.1.mine_ref.pair_ref = f32[16,32,256]{2,1,0:T(8,128)S(1)} async-done(((f32[16,32,256]{2,1,0:T(8,128)}), f32[16,32,256]{2,1,0:T(8,128)S(1)}, u32[]{:S(2)}, u32[]{:S(2)}) %all-to-all-start.1) | async-done | bytes 524320 | tf_op jit(solution)/shard_map/all_to_all | solution.py:299
  35.3 1.9 %collective-permute-done.2.other_ref.pair_other_ref = f32[16,32,256]{2,1,0:T(8,128)S(1)} collective-permute-done((f32[16,32,256]{2,1,0:T(8,128)S(1)}, f32[16,32,256]{2,1,0:T(8,128)S(1)}, u32[]{:S(2)}, u32[]{:S(2)}) %collective-permute-start.2) | collective-permute-done | bytes 524320 | tf_op jit(solution)/shard_map/ppermute | solution.py:304
  37.2 0.4 load_sum.1
  37.6 2.0 %collective-permute-start.3 = (f32[128,256]{1,0:T(8,128)S(1)}, f32[128,256]{1,0:T(8,128)S(1)}, u32[]{:S(2)}, u32[]{:S(2)}) collective-permute-start(f32[128,256]{1,0:T(8,128)S(1)} %get-tuple-element.51), channel_id=1, source_target_pairs={{0,32},{32,0},{64,96},{96,64},{1,33},{33,1},{65,97},{97,65},{2,34}... | collective-permute-start | bytes 393224 | tf_op jit(solution)/shard_map/ppermute | solution.py:304
  39.6 2.5 %collective-permute-start.4 = (f32[128,256]{1,0:T(8,128)S(1)}, f32[128,256]{1,0:T(8,128)S(1)}, u32[]{:S(2)}, u32[]{:S(2)}) collective-permute-start(f32[128,256]{1,0:T(8,128)S(1)} %get-tuple-element.52), channel_id=1, source_target_pairs={{0,96},{32,64},{64,32},{96,0},{1,97},{33,65},{65,33},{97,1},{2,98}... | collective-permute-start | bytes 393224 | tf_op jit(solution)/shard_map/ppermute | solution.py:304
  42.2 1.5 %collective-permute-start.7 = (f32[128,512]{1,0:T(8,128)S(1)}, f32[128,512]{1,0:T(8,128)S(1)}, u32[]{:S(2)}, u32[]{:S(2)}) collective-permute-start(f32[128,512]{1,0:T(8,128)S(1)} %get-tuple-element.84), channel_id=1, source_target_pairs={{0,16},{16,0},{1,17},{17,1},{2,18},{18,2},{3,19},{19,3},{4,20},{20... | collective-permute-start | bytes 786440 | tf_op jit(solution)/shard_map/ppermute | solution.py:304
  43.7 2.4 %collective-permute-done.4 = f32[128,256]{1,0:T(8,128)S(1)} collective-permute-done((f32[128,256]{1,0:T(8,128)S(1)}, f32[128,256]{1,0:T(8,128)S(1)}, u32[]{:S(2)}, u32[]{:S(2)}) %collective-permute-start.4) | collective-permute-done | bytes 131104 | tf_op jit(solution)/shard_map/ppermute | solution.py:304
  46.1 2.6 %collective-permute-start.5 = (f32[128,256]{1,0:T(8,128)S(1)}, f32[128,256]{1,0:T(8,128)S(1)}, u32[]{:S(2)}, u32[]{:S(2)}) collective-permute-start(f32[128,256]{1,0:T(8,128)S(1)} %add.58), channel_id=1, source_target_pairs={{0,96},{32,64},{64,32},{96,0},{1,97},{33,65},{65,33},{97,1},{2,98}... | collective-permute-start | bytes 393224 | tf_op jit(solution)/shard_map/ppermute | solution.py:304
  48.8 1.2 collective-permute-done.7
  50.1 2.3 %collective-permute-done.5 = f32[128,256]{1,0:T(8,128)S(1)} collective-permute-done((f32[128,256]{1,0:T(8,128)S(1)}, f32[128,256]{1,0:T(8,128)S(1)}, u32[]{:S(2)}, u32[]{:S(2)}) %collective-permute-start.5) | collective-permute-done | bytes 131104 | tf_op jit(solution)/shard_map/ppermute | solution.py:304
  52.4 1.4 collective-permute-done.6
  53.8 0.5 gram_and_cores.2
  54.5 1.7 %collective-permute-done.8 = f32[16,24,256]{2,1,0:T(8,128)S(1)} collective-permute-done((f32[16,24,256]{2,1,0:T(8,128)S(1)}, f32[16,24,256]{2,1,0:T(8,128)S(1)}, u32[]{:S(2)}, u32[]{:S(2)}) %collective-permute-start.8) | collective-permute-done | bytes 393248 | tf_op jit(solution)/shard_map/ppermute | solution.py:304
  56.2 13.7 %all_to_all.30.tiles_ref = f32[16,24,256]{2,1,0:T(8,128)S(1)} all-to-all(f32[16,24,256]{2,1,0:T(8,128)S(1)} %add.62), channel_id=1, replica_groups=mesh['z'=4,'y_lo'=2,'core'=2,'row'=8] {'y_lo','row'}, dimensions={0} | all-to-all | bytes 786432 | tf_op jit(solution)/shard_map/all_to_all | solution.py:299
  70.0 0.8 owner_sum.2
  70.7 4.8 %all-to-all-start.3 = ((f32[16,24,256]{2,1,0:T(8,128)}), f32[16,24,256]{2,1,0:T(8,128)S(1)}, u32[]{:S(2)}, u32[]{:S(2)}) async-start(f32[16,24,256]{2,1,0:T(8,128)} %owner_sum.2), calls=%async_computation.3 | async-start | bytes 786432 | tf_op jit(solution)/shard_map/all_to_all | solution.py:299
  75.8 1.5 %collective-permute-done.9.f2 = f32[256,256]{1,0:T(8,128)S(1)} collective-permute-done((f32[256,256]{1,0:T(8,128)S(1)}, f32[256,256]{1,0:T(8,128)S(1)}, u32[]{:S(2)}, u32[]{:S(2)}) %collective-permute-start.9) | collective-permute-done | bytes 262176 | tf_op jit(solution)/shard_map/ppermute | solution.py:304
  77.3 6.4 %all-to-all-done.3.mine_ref = f32[16,24,256]{2,1,0:T(8,128)S(1)} async-done(((f32[16,24,256]{2,1,0:T(8,128)}), f32[16,24,256]{2,1,0:T(8,128)S(1)}, u32[]{:S(2)}, u32[]{:S(2)}) %all-to-all-start.3) | async-done | bytes 393248 | tf_op jit(solution)/shard_map/all_to_all | solution.py:299
  83.7 1.5 %collective-permute-start.11 = (f32[256,256]{1,0:T(8,128)S(1)}, f32[256,256]{1,0:T(8,128)S(1)}, u32[]{:S(2)}, u32[]{:S(2)}) collective-permute-start(f32[256,256]{1,0:T(8,128)S(1)} %pad_maximum_fusion.2.q0), channel_id=1, source_target_pairs={{0,16},{16,0},{1,17},{17,1},{2,18},{18,2},{3,19},{19,3},{4,20},{20... | collective-permute-start | bytes 786440 | tf_op jit(solution)/shard_map/ppermute | solution.py:304
  85.2 0.2 collective-permute-start.14
  85.4 7.3 %turn_over.1 = (f32[256,256]{1,0:T(8,128)S(1)}, f32[8,16,256]{2,1,0:T(8,128)}, f32[128,256]{1,0:T(8,128)S(1)}, f32[128,256]{1,0:T(8,128)S(1)}) custom-call(s32[1]{0:T(128)} %bitcast.place_ref, f32[16,24,256]{2,1,0:T(8,128)S(1)} %all-to-all-done.3.mine_ref, f32[16,24,256]{2,1,0:T(8,128)S(1)} %collective-permute-done.10.other_ref, ...), custom_call_target="tpu_custom_call" | custom-call | flops 6442450944 | tf_op jit(solution)/shard_map/turn_over/pallas_call | solution.py:153
  92.8 0.3 collective-permute-start.15
  93.1 1.1 collective-permute-start.13
  94.2 0.1 collective-permute-done.15.q3
  94.3 1.6 %whole_basis.2 = f32[1024,256]{1,0:T(8,128)} custom-call(s32[1]{0:T(128)} %bitcast.place_ref, f32[256,256]{1,0:T(8,128)S(1)} %get-tuple-element.72.inverse_ref, f32[256,256]{1,0:T(8,128)S(1)} %pad_maximum_fusion.2.q0, f32[256,256]{1,0:T(8,128)S(1)} %collective-permute-done.11.q1, f32[256,256]{1,0:T(8,128)S(1)} %collective-permute-done.14.q2, ...), custom_call_target="tpu_custom_call" | custom-call | flops 402653184 | tf_op jit(solution)/shard_map/whole_basis/pallas_call | solution.py:153
  95.9 2.7 %collective-permute-done.12 = f32[128,256]{1,0:T(8,128)S(1)} collective-permute-done((f32[128,256]{1,0:T(8,128)S(1)}, f32[128,256]{1,0:T(8,128)S(1)}, u32[]{:S(2)}, u32[]{:S(2)}) %collective-permute-start.12) | collective-permute-done | bytes 131104 | tf_op jit(solution)/shard_map/ppermute | solution.py:304
  98.7 1.2 collective-permute-done.13
  99.9 1.2 collective-permute-start.16
  101.2 5.0 %collective-permute-done.16 = f32[128,256]{1,0:T(8,128)S(1)} collective-permute-done((f32[128,256]{1,0:T(8,128)S(1)}, f32[128,256]{1,0:T(8,128)S(1)}, u32[]{:S(2)}, u32[]{:S(2)}) %collective-permute-start.16) | collective-permute-done | bytes 131104 | tf_op jit(solution)/shard_map/ppermute | solution.py:304
  106.2 0.5 gram_and_cores.3
  106.8 1.7 %collective-permute-done.18 = f32[16,24,256]{2,1,0:T(8,128)S(1)} collective-permute-done((f32[16,24,256]{2,1,0:T(8,128)S(1)}, f32[16,24,256]{2,1,0:T(8,128)S(1)}, u32[]{:S(2)}, u32[]{:S(2)}) %collective-permute-start.18) | collective-permute-done | bytes 393248 | tf_op jit(solution)/shard_map/ppermute | solution.py:304
  108.6 13.7 %all_to_all.31.tiles_ref = f32[16,24,256]{2,1,0:T(8,128)S(1)} all-to-all(f32[16,24,256]{2,1,0:T(8,128)S(1)} %add.67), channel_id=1, replica_groups=mesh['z'=4,'y_lo'=2,'core'=2,'row'=8] {'y_lo','row'}, dimensions={0} | all-to-all | bytes 786432 | tf_op jit(solution)/shard_map/all_to_all | solution.py:299
  122.3 0.8 owner_sum.3
  123.1 4.8 %all-to-all-start.5 = ((f32[16,24,256]{2,1,0:T(8,128)}), f32[16,24,256]{2,1,0:T(8,128)S(1)}, u32[]{:S(2)}, u32[]{:S(2)}) async-start(f32[16,24,256]{2,1,0:T(8,128)} %owner_sum.3), calls=%async_computation.5 | async-start | bytes 786432 | tf_op jit(solution)/shard_map/all_to_all | solution.py:299
  128.0 0.3 collective-permute-start.20
  128.2 7.9 %all-to-all-done.5.mine_ref = f32[16,24,256]{2,1,0:T(8,128)S(1)} async-done(((f32[16,24,256]{2,1,0:T(8,128)}), f32[16,24,256]{2,1,0:T(8,128)S(1)}, u32[]{:S(2)}, u32[]{:S(2)}) %all-to-all-start.5) | async-done | bytes 393248 | tf_op jit(solution)/shard_map/all_to_all | solution.py:299
  136.1 0.5 collective-permute-start.21
  136.6 1.7 %collective-permute-done.20.q1 = f32[256,256]{1,0:T(8,128)S(1)} collective-permute-done((f32[256,256]{1,0:T(8,128)S(1)}, f32[256,256]{1,0:T(8,128)S(1)}, u32[]{:S(2)}, u32[]{:S(2)}) %collective-permute-start.20) | collective-permute-done | bytes 262176 | tf_op jit(solution)/shard_map/ppermute | solution.py:304
  138.3 6.5 %right_cores.1 = (f32[256,256]{1,0:T(8,128)S(1)}, f32[8,16,256]{2,1,0:T(8,128)}) custom-call(s32[1]{0:T(128)} %bitcast.place_ref, f32[16,24,256]{2,1,0:T(8,128)S(1)} %all-to-all-done.5.mine_ref, f32[16,24,256]{2,1,0:T(8,128)S(1)} %collective-permute-done.19.other_ref), custom_call_target="tpu_custom_call" | custom-call | tf_op jit(solution)/shard_map/right_cores/pallas_call | solution.py:153
  144.9 1.6 %whole_basis.3 = f32[1024,256]{1,0:T(8,128)} custom-call(s32[1]{0:T(128)} %bitcast.place_ref, f32[256,256]{1,0:T(8,128)S(1)} %get-tuple-element.81.inverse_ref, f32[256,256]{1,0:T(8,128)S(1)} %pad_maximum_fusion.3.q0, f32[256,256]{1,0:T(8,128)S(1)} %collective-permute-done.20.q1, f32[256,256]{1,0:T(8,128)S(1)} %collective-permute-done.21.q2, ...), custom_call_target="tpu_custom_call" | custom-call | flops 402653184 | tf_op jit(solution)/shard_map/whole_basis/pallas_call | solution.py:153
  (40 shorter events, 1.0 us)
Async XLA Ops:
  1.7 18.5 %collective-permute-start = (f32[128,512]{1,0:T(8,128)S(1)}, f32[128,512]{1,0:T(8,128)S(1)}, u32[]{:S(2)}, u32[]{:S(2)}) collective-permute-start(f32[128,512]{1,0:T(8,128)S(1)} %get-tuple-element.86), channel_id=1, source_target_pairs={{0,16},{16,0},{1,17},{17,1},{2,18},{18,2},{3,19},{19,3},{4,20},{20... | collective-permute-start | bytes 786440 | tf_op jit(solution)/shard_map/ppermute | solution.py:304
  5.3 14.9 %all-to-all-start = ((f32[8,32,256]{2,1,0:T(8,128)}), f32[8,32,256]{2,1,0:T(8,128)S(1)}, u32[]{:S(2)}, u32[]{:S(2)}) async-start(f32[8,32,256]{2,1,0:T(8,128)} %projections.1), calls=%async_computation | async-start | bytes 524288 | tf_op jit(solution)/shard_map/all_to_all | solution.py:299
  21.3 14.0 %all-to-all-start.1 = ((f32[16,32,256]{2,1,0:T(8,128)}), f32[16,32,256]{2,1,0:T(8,128)S(1)}, u32[]{:S(2)}, u32[]{:S(2)}) async-start(f32[16,32,256]{2,1,0:T(8,128)} %owner_coefficients.1), calls=%async_computation.1 | async-start | bytes 1048576 | tf_op jit(solution)/shard_map/all_to_all | solution.py:299
  26.7 1.6 %collective-permute-start.1 = (f32[256,256]{1,0:T(8,128)S(1)}, f32[256,256]{1,0:T(8,128)S(1)}, u32[]{:S(2)}, u32[]{:S(2)}) collective-permute-start(f32[256,256]{1,0:T(8,128)S(1)} %pad_maximum_fusion), channel_id=1, source_target_pairs={{0,8},{8,0},{1,9},{9,1},{2,10},{10,2},{3,11},{11,3},{4,12},{12,4},... | collective-permute-start | bytes 786440 | tf_op jit(solution)/shard_map/ppermute | solution.py:304
  35.3 1.9 %collective-permute-start.2 = (f32[16,32,256]{2,1,0:T(8,128)S(1)}, f32[16,32,256]{2,1,0:T(8,128)S(1)}, u32[]{:S(2)}, u32[]{:S(2)}) collective-permute-start(f32[16,32,256]{2,1,0:T(8,128)S(1)} %all-to-all-done.1.mine_ref.pair_ref), channel_id=1, source_target_pairs={{0,8},{8,0},{1,9},{9,1},{2,10},{10,2},{3,11},{11,3},{4,12},{12,4},... | collective-permute-start | bytes 1572872 | tf_op jit(solution)/shard_map/ppermute | solution.py:304
  37.2 5.0 %copy-start = (f32[8,16,1024]{2,1,0:T(8,128)S(1)}, f32[8,16,1024]{2,1,0:T(8,128)}, u32[]{:S(2)}) copy-start(f32[8,16,1024]{2,1,0:T(8,128)} %param.5) | copy-start | bytes 1572868
  37.6 6.1 %collective-permute-start.3 = (f32[128,256]{1,0:T(8,128)S(1)}, f32[128,256]{1,0:T(8,128)S(1)}, u32[]{:S(2)}, u32[]{:S(2)}) collective-permute-start(f32[128,256]{1,0:T(8,128)S(1)} %get-tuple-element.51), channel_id=1, source_target_pairs={{0,32},{32,0},{64,96},{96,64},{1,33},{33,1},{65,97},{97,65},{2,34}... | collective-permute-start | bytes 393224 | tf_op jit(solution)/shard_map/ppermute | solution.py:304
  39.6 6.5 %collective-permute-start.4 = (f32[128,256]{1,0:T(8,128)S(1)}, f32[128,256]{1,0:T(8,128)S(1)}, u32[]{:S(2)}, u32[]{:S(2)}) collective-permute-start(f32[128,256]{1,0:T(8,128)S(1)} %get-tuple-element.52), channel_id=1, source_target_pairs={{0,96},{32,64},{64,32},{96,0},{1,97},{33,65},{65,33},{97,1},{2,98}... | collective-permute-start | bytes 393224 | tf_op jit(solution)/shard_map/ppermute | solution.py:304
  42.2 7.9 %collective-permute-start.7 = (f32[128,512]{1,0:T(8,128)S(1)}, f32[128,512]{1,0:T(8,128)S(1)}, u32[]{:S(2)}, u32[]{:S(2)}) collective-permute-start(f32[128,512]{1,0:T(8,128)S(1)} %get-tuple-element.84), channel_id=1, source_target_pairs={{0,16},{16,0},{1,17},{17,1},{2,18},{18,2},{3,19},{19,3},{4,20},{20... | collective-permute-start | bytes 786440 | tf_op jit(solution)/shard_map/ppermute | solution.py:304
  46.1 6.3 %collective-permute-start.5 = (f32[128,256]{1,0:T(8,128)S(1)}, f32[128,256]{1,0:T(8,128)S(1)}, u32[]{:S(2)}, u32[]{:S(2)}) collective-permute-start(f32[128,256]{1,0:T(8,128)S(1)} %add.58), channel_id=1, source_target_pairs={{0,96},{32,64},{64,32},{96,0},{1,97},{33,65},{65,33},{97,1},{2,98}... | collective-permute-start | bytes 393224 | tf_op jit(solution)/shard_map/ppermute | solution.py:304
  48.7 5.0 %collective-permute-start.6 = (f32[128,256]{1,0:T(8,128)S(1)}, f32[128,256]{1,0:T(8,128)S(1)}, u32[]{:S(2)}, u32[]{:S(2)}) collective-permute-start(f32[128,256]{1,0:T(8,128)S(1)} %add.59), channel_id=1, source_target_pairs={{0,32},{32,0},{64,96},{96,64},{1,33},{33,1},{65,97},{97,65},{2,34}... | collective-permute-start | bytes 393224 | tf_op jit(solution)/shard_map/ppermute | solution.py:304
  54.4 1.8 %collective-permute-start.8 = (f32[16,24,256]{2,1,0:T(8,128)S(1)}, f32[16,24,256]{2,1,0:T(8,128)S(1)}, u32[]{:S(2)}, u32[]{:S(2)}) collective-permute-start(f32[16,24,256]{2,1,0:T(8,128)S(1)} %get-tuple-element.58), channel_id=1, source_target_pairs={{0,8},{8,0},{1,9},{9,1},{2,10},{10,2},{3,11},{11,3},{4,12},{12,4},... | collective-permute-start | bytes 1179656 | tf_op jit(solution)/shard_map/ppermute | solution.py:304
  70.7 12.9 %all-to-all-start.3 = ((f32[16,24,256]{2,1,0:T(8,128)}), f32[16,24,256]{2,1,0:T(8,128)S(1)}, u32[]{:S(2)}, u32[]{:S(2)}) async-start(f32[16,24,256]{2,1,0:T(8,128)} %owner_sum.2), calls=%async_computation.3 | async-start | bytes 786432 | tf_op jit(solution)/shard_map/all_to_all | solution.py:299
  75.7 1.6 %collective-permute-start.9 = (f32[256,256]{1,0:T(8,128)S(1)}, f32[256,256]{1,0:T(8,128)S(1)}, u32[]{:S(2)}, u32[]{:S(2)}) collective-permute-start(f32[256,256]{1,0:T(8,128)S(1)} %pad_maximum_fusion.1), channel_id=1, source_target_pairs={{0,8},{8,0},{1,9},{9,1},{2,10},{10,2},{3,11},{11,3},{4,12},{12,4},... | collective-permute-start | bytes 786440 | tf_op jit(solution)/shard_map/ppermute | solution.py:304
  83.7 1.7 %collective-permute-start.10 = (f32[16,24,256]{2,1,0:T(8,128)S(1)}, f32[16,24,256]{2,1,0:T(8,128)S(1)}, u32[]{:S(2)}, u32[]{:S(2)}) collective-permute-start(f32[16,24,256]{2,1,0:T(8,128)S(1)} %all-to-all-done.3.mine_ref), channel_id=1, source_target_pairs={{0,8},{8,0},{1,9},{9,1},{2,10},{10,2},{3,11},{11,3},{4,12},{12,4},... | collective-permute-start | bytes 1179656 | tf_op jit(solution)/shard_map/ppermute | solution.py:304
  83.7 9.0 %collective-permute-start.11 = (f32[256,256]{1,0:T(8,128)S(1)}, f32[256,256]{1,0:T(8,128)S(1)}, u32[]{:S(2)}, u32[]{:S(2)}) collective-permute-start(f32[256,256]{1,0:T(8,128)S(1)} %pad_maximum_fusion.2.q0), channel_id=1, source_target_pairs={{0,16},{16,0},{1,17},{17,1},{2,18},{18,2},{3,19},{19,3},{4,20},{20... | collective-permute-start | bytes 786440 | tf_op jit(solution)/shard_map/ppermute | solution.py:304
  85.2 9.0 %collective-permute-start.14 = (f32[256,256]{1,0:T(8,128)S(1)}, f32[256,256]{1,0:T(8,128)S(1)}, u32[]{:S(2)}, u32[]{:S(2)}) collective-permute-start(f32[256,256]{1,0:T(8,128)S(1)} %pad_maximum_fusion.2.q0), channel_id=1, source_target_pairs={{0,8},{8,0},{1,9},{9,1},{2,10},{10,2},{3,11},{11,3},{4,12},{12,4},... | collective-permute-start | bytes 786440 | tf_op jit(solution)/shard_map/ppermute | solution.py:304
  92.8 1.5 %collective-permute-start.15 = (f32[256,256]{1,0:T(8,128)S(1)}, f32[256,256]{1,0:T(8,128)S(1)}, u32[]{:S(2)}, u32[]{:S(2)}) collective-permute-start(f32[256,256]{1,0:T(8,128)S(1)} %collective-permute-done.11.q1), channel_id=1, source_target_pairs={{0,8},{8,0},{1,9},{9,1},{2,10},{10,2},{3,11},{11,3},{4,12},{12,4},... | collective-permute-start | bytes 786440 | tf_op jit(solution)/shard_map/ppermute | solution.py:304
  93.0 5.6 %collective-permute-start.12 = (f32[128,256]{1,0:T(8,128)S(1)}, f32[128,256]{1,0:T(8,128)S(1)}, u32[]{:S(2)}, u32[]{:S(2)}) collective-permute-start(f32[128,256]{1,0:T(8,128)S(1)} %get-tuple-element.70), channel_id=1, source_target_pairs={{0,32},{32,0},{64,96},{96,64},{1,33},{33,1},{65,97},{97,65},{2,34}... | collective-permute-start | bytes 393224 | tf_op jit(solution)/shard_map/ppermute | solution.py:304
  93.1 6.8 %collective-permute-start.13 = (f32[128,256]{1,0:T(8,128)S(1)}, f32[128,256]{1,0:T(8,128)S(1)}, u32[]{:S(2)}, u32[]{:S(2)}) collective-permute-start(f32[128,256]{1,0:T(8,128)S(1)} %get-tuple-element.71), channel_id=1, source_target_pairs={{0,96},{32,64},{64,32},{96,0},{1,97},{33,65},{65,33},{97,1},{2,98}... | collective-permute-start | bytes 393224 | tf_op jit(solution)/shard_map/ppermute | solution.py:304
  99.9 6.3 %collective-permute-start.16 = (f32[128,256]{1,0:T(8,128)S(1)}, f32[128,256]{1,0:T(8,128)S(1)}, u32[]{:S(2)}, u32[]{:S(2)}) collective-permute-start(f32[128,256]{1,0:T(8,128)S(1)} %add.63), channel_id=1, source_target_pairs={{0,96},{32,64},{64,32},{96,0},{1,97},{33,65},{65,33},{97,1},{2,98}... | collective-permute-start | bytes 393224 | tf_op jit(solution)/shard_map/ppermute | solution.py:304
  101.1 5.0 %collective-permute-start.17 = (f32[128,256]{1,0:T(8,128)S(1)}, f32[128,256]{1,0:T(8,128)S(1)}, u32[]{:S(2)}, u32[]{:S(2)}) collective-permute-start(f32[128,256]{1,0:T(8,128)S(1)} %add.64), channel_id=1, source_target_pairs={{0,32},{32,0},{64,96},{96,64},{1,33},{33,1},{65,97},{97,65},{2,34}... | collective-permute-start | bytes 393224 | tf_op jit(solution)/shard_map/ppermute | solution.py:304
  106.7 1.8 %collective-permute-start.18 = (f32[16,24,256]{2,1,0:T(8,128)S(1)}, f32[16,24,256]{2,1,0:T(8,128)S(1)}, u32[]{:S(2)}, u32[]{:S(2)}) collective-permute-start(f32[16,24,256]{2,1,0:T(8,128)S(1)} %get-tuple-element.80), channel_id=1, source_target_pairs={{0,8},{8,0},{1,9},{9,1},{2,10},{10,2},{3,11},{11,3},{4,12},{12,4},... | collective-permute-start | bytes 1179656 | tf_op jit(solution)/shard_map/ppermute | solution.py:304
  123.1 13.0 %all-to-all-start.5 = ((f32[16,24,256]{2,1,0:T(8,128)}), f32[16,24,256]{2,1,0:T(8,128)S(1)}, u32[]{:S(2)}, u32[]{:S(2)}) async-start(f32[16,24,256]{2,1,0:T(8,128)} %owner_sum.3), calls=%async_computation.5 | async-start | bytes 786432 | tf_op jit(solution)/shard_map/all_to_all | solution.py:299
  128.0 10.4 %collective-permute-start.20 = (f32[256,256]{1,0:T(8,128)S(1)}, f32[256,256]{1,0:T(8,128)S(1)}, u32[]{:S(2)}, u32[]{:S(2)}) collective-permute-start(f32[256,256]{1,0:T(8,128)S(1)} %pad_maximum_fusion.3.q0), channel_id=1, source_target_pairs={{0,16},{16,0},{1,17},{17,1},{2,18},{18,2},{3,19},{19,3},{4,20},{20... | collective-permute-start | bytes 786440 | tf_op jit(solution)/shard_map/ppermute | solution.py:304
  136.1 2.2 %collective-permute-start.19 = (f32[16,24,256]{2,1,0:T(8,128)S(1)}, f32[16,24,256]{2,1,0:T(8,128)S(1)}, u32[]{:S(2)}, u32[]{:S(2)}) collective-permute-start(f32[16,24,256]{2,1,0:T(8,128)S(1)} %all-to-all-done.5.mine_ref), channel_id=1, source_target_pairs={{0,8},{8,0},{1,9},{9,1},{2,10},{10,2},{3,11},{11,3},{4,12},{12,4},... | collective-permute-start | bytes 1179656 | tf_op jit(solution)/shard_map/ppermute | solution.py:304
  136.1 8.8 %collective-permute-start.21 = (f32[256,256]{1,0:T(8,128)S(1)}, f32[256,256]{1,0:T(8,128)S(1)}, u32[]{:S(2)}, u32[]{:S(2)}) collective-permute-start(f32[256,256]{1,0:T(8,128)S(1)} %pad_maximum_fusion.3.q0), channel_id=1, source_target_pairs={{0,8},{8,0},{1,9},{9,1},{2,10},{10,2},{3,11},{11,3},{4,12},{12,4},... | collective-permute-start | bytes 786440 | tf_op jit(solution)/shard_map/ppermute | solution.py:304
  138.3 6.6 %collective-permute-start.22 = (f32[256,256]{1,0:T(8,128)S(1)}, f32[256,256]{1,0:T(8,128)S(1)}, u32[]{:S(2)}, u32[]{:S(2)}) collective-permute-start(f32[256,256]{1,0:T(8,128)S(1)} %collective-permute-done.20.q1), channel_id=1, source_target_pairs={{0,8},{8,0},{1,9},{9,1},{2,10},{10,2},{3,11},{11,3},{4,12},{12,4},... | collective-permute-start | bytes 786440 | tf_op jit(solution)/shard_map/ppermute | solution.py:304
